TPU v7x, 32 devices: a whole 2x2x4 slice. The times are simulated.
32 devices in a mesh: dp: 16 (over z, x, core), tensor: 2 (over y).
Axes of the slice: x: 2, y: 2, z: 4, core: 2. Of those that a mesh axis runs over, the one named last changes fastest.
Arguments:
- features: bfloat16 [512, 16, 4096], P('tensor', 'dp'), may hold values from -6 to 6
- cotangent: bfloat16 [512, 16, 4096], P('tensor', 'dp'), may hold values from -6 to 6
- embedding: bfloat16 [16, 2048], P('dp'), may hold values from -6 to 6
- context: bfloat16 [16, 260, 2048], P('dp'), may hold values from -6 to 6
- lengths: int32 [16], P('dp'), may hold values from 5 to 256, as said below
- norm1_gain: float32 [512], P('tensor'), may hold values from 0.25 to 1.75
- norm1_bias: float32 [512], P('tensor'), may hold values from -2 to 2
- conv1_weight: bfloat16 [512, 4608], P('tensor'), may hold values from -0.09375 to 0.09375
- conv1_bias: float32 [512], P('tensor'), may hold values from -2 to 2
- emb_weight: bfloat16 [2, 2048, 512], P(None, None, 'tensor'), may hold values from -0.125 to 0.125
- emb_bias: float32 [2, 512], P(None, 'tensor'), may hold values from -2 to 2
- norm2_gain: float32 [512], P('tensor'), may hold values from 0.25 to 1.75
- norm2_bias: float32 [512], P('tensor'), may hold values from -2 to 2
- conv2_weight: bfloat16 [512, 4608], P('tensor'), may hold values from -0.09375 to 0.09375
- conv2_bias: float32 [512], P('tensor'), may hold values from -2 to 2
- norm3_gain: float32 [512], P('tensor'), may hold values from 0.25 to 1.75
- norm3_bias: float32 [512], P('tensor'), may hold values from -2 to 2
- qkv_weight: bfloat16 [3, 512, 512], P(None, 'tensor'), may hold values from -0.25 to 0.25
- qkv_bias: float32 [3, 512], P(None, 'tensor'), may hold values from -2 to 2
- context_weight: bfloat16 [2, 512, 2048], P(None, 'tensor'), may hold values from -0.125 to 0.125
- context_bias: float32 [2, 512], P(None, 'tensor'), may hold values from -2 to 2
- out_weight: bfloat16 [512, 512], P('tensor'), may hold values from -2 to 2
- out_bias: float32 [512], P('tensor'), may hold values from -2 to 2
Outputs:
- output: bfloat16 [512, 16, 4096], P('tensor', 'dp')
- input_grad: float32 [512, 16, 4096], P('tensor', 'dp')
- norm1_gain_grad: float32 [512], P('tensor')
- norm1_bias_grad: float32 [512], P('tensor')
- conv1_weight_grad: float32 [512, 4608], P('tensor')
- conv1_bias_grad: float32 [512], P('tensor')
- emb_weight_grad: float32 [2, 2048, 512], P(None, None, 'tensor')
- emb_bias_grad: float32 [2, 512], P(None, 'tensor')
- norm2_gain_grad: float32 [512], P('tensor')
- norm2_bias_grad: float32 [512], P('tensor')
- conv2_weight_grad: float32 [512, 4608], P('tensor')
- conv2_bias_grad: float32 [512], P('tensor')
- norm3_gain_grad: float32 [512], P('tensor')
- norm3_bias_grad: float32 [512], P('tensor')
- qkv_weight_grad: float32 [3, 512, 512], P(None, 'tensor')
- qkv_bias_grad: float32 [3, 512], P(None, 'tensor')
- context_weight_grad: float32 [2, 512, 2048], P(None, 'tensor')
- context_bias_grad: float32 [2, 512], P(None, 'tensor')
- out_weight_grad: float32 [512, 512], P('tensor')
- out_bias_grad: float32 [512], P('tensor')
Inputs may be any that keep to these rules, and one draw needn't show every extreme that they name: `lengths`: each image's number of real text tokens; some image has 256.
All inputs are finite; a program needn't handle non-finite values.
Results may differ from a plain program's by a relative error of at most 0.025.
Values may be sent and summed in bfloat16 or wider, within the bound.
No kernel may reach another device: no remote copies, remote signals or barrier semaphores. Data moves between devices by JAX's collectives and lax.ppermute only.
A program may use at most 384 MiB of HBM per device.

v0:
```python
import jax
import jax.numpy as jnp
from jax import lax
from jax.sharding import PartitionSpec as P

C = 512
HEAD_DIM = 64
GROUPS = 32
SIDE = 64
HW = 4096
CTX = 260


EPSILON = 1e-05
NEG_FILL = -1e30


def group_norm(values, gain_vec, bias_vec):
    channels, images, pixels = values.shape
    per_group = C // GROUPS
    grouped = values.reshape(channels // per_group, per_group, images, pixels)
    group_mean = jnp.mean(grouped, axis=(1, 3), keepdims=True)
    group_var = jnp.mean(jnp.square(grouped - group_mean), axis=(1, 3), keepdims=True)
    normal_vals = ((grouped - group_mean) * lax.rsqrt(group_var + EPSILON)).reshape(values.shape)
    return normal_vals * gain_vec[:, None, None] + bias_vec[:, None, None]


def shifted(values, kernel_tap):
    row_off, col_off = (kernel_tap // 3, kernel_tap % 3)
    channels, images, pixels = values.shape
    padded = jnp.pad(values.reshape(channels, images, SIDE, SIDE), ((0, 0), (0, 0), (1, 1), (1, 1)))
    return padded[:, :, row_off : row_off + SIDE, col_off : col_off + SIDE].reshape(
        channels, images, pixels
    )


def convolve(full_act, weight, bias_vec):
    kernel = weight.reshape(weight.shape[0], 9, C)
    result = (
        jnp.zeros((weight.shape[0],) + full_act.shape[1:], jnp.float32) + bias_vec[:, None, None]
    )
    for kernel_tap in range(9):
        result = result + jnp.einsum(
            "oc,cip->oip",
            kernel[:, kernel_tap],
            shifted(full_act, kernel_tap),
            preferred_element_type=jnp.float32,
        )
    return result


def kernel_grad(grad_low, full_act):
    pieces = [
        jnp.einsum(
            "oip,cip->oc",
            grad_low,
            shifted(full_act, kernel_tap),
            preferred_element_type=jnp.float32,
        )
        for kernel_tap in range(9)
    ]
    return jnp.stack(pieces, axis=1).reshape(grad_low.shape[0], 9 * C)


def conv_input_grad(grad_low, weight):
    channels = grad_low.shape[0]
    kernel = weight.reshape(channels, 9, C)
    moved_grads = [shifted(grad_low, 8 - kernel_tap) for kernel_tap in range(9)]
    result = jnp.zeros((lax.axis_size("tensor") * channels,) + grad_low.shape[1:], jnp.float32)
    for kernel_tap in range(9):
        cols_part = kernel[:, kernel_tap]
        result = result + jnp.einsum(
            "oc,oip->cip", cols_part, moved_grads[kernel_tap], preferred_element_type=jnp.float32
        )
    return lax.psum_scatter(
        result.astype(jnp.bfloat16), "tensor", scatter_dimension=0, tiled=True
    ).astype(jnp.float32)


def to_heads(values):
    channels, images, length_n = values.shape
    return (
        values.reshape(channels // HEAD_DIM, HEAD_DIM, images, length_n)
        .transpose(2, 0, 1, 3)
        .reshape(-1, HEAD_DIM, length_n)
    )


def from_heads(values, images):
    groups_n, head_dims, length_n = values.shape
    heads_here = groups_n // images
    return (
        values.reshape(images, heads_here, head_dims, length_n)
        .transpose(1, 2, 0, 3)
        .reshape(heads_here * head_dims, images, length_n)
    )


def masked_scores(q_block, key_rows, key_valid):
    scores = jnp.einsum(
        "gdi,gdj->gij", q_block, key_rows, preferred_element_type=jnp.float32
    ) * HEAD_DIM ** (-0.5)
    return jnp.where(key_valid[:, None, :], scores, NEG_FILL)


def attend_forward(queries, key_rows, value_rows, key_valid):
    groups_n = queries.shape[0]
    block_len = min(512, HW)
    blocks_q = queries.reshape(groups_n, HEAD_DIM, HW // block_len, block_len).transpose(2, 0, 1, 3)

    def one_block(q_block):
        scores = masked_scores(q_block, key_rows, key_valid)
        row_top = jnp.max(scores, axis=-1, keepdims=True)
        raised = jnp.exp(scores - row_top)
        row_total = jnp.sum(raised, axis=-1, keepdims=True)
        probs_low = (raised / row_total).astype(jnp.bfloat16)
        mixed_out = jnp.einsum(
            "gdj,gij->gdi", value_rows, probs_low, preferred_element_type=jnp.float32
        )
        return (mixed_out.astype(jnp.bfloat16), row_top, row_total)

    mixed_out, row_top, row_total = lax.map(one_block, blocks_q)
    merged = mixed_out.transpose(1, 2, 0, 3).reshape(groups_n, HEAD_DIM, HW)
    return (merged, row_top, row_total)


def attend_backward(queries, key_rows, value_rows, key_valid, grad_mixed, row_top, row_total):
    groups_n = queries.shape[0]
    block_len = min(512, HW)
    count_b = HW // block_len
    blocks_q = queries.reshape(groups_n, HEAD_DIM, count_b, block_len).transpose(2, 0, 1, 3)
    blocks_g = grad_mixed.reshape(groups_n, HEAD_DIM, count_b, block_len).transpose(2, 0, 1, 3)
    scale_val = HEAD_DIM ** (-0.5)

    def one_block(carried, packed):
        key_acc, value_acc = carried
        q_block, g_block, block_top, block_total = packed
        scores = masked_scores(q_block, key_rows, key_valid)
        prob_f32 = jnp.exp(scores - block_top) / block_total
        probs_low = prob_f32.astype(jnp.bfloat16)
        value_acc = value_acc + jnp.einsum(
            "gdi,gij->gdj", g_block, probs_low, preferred_element_type=jnp.float32
        )
        grad_probs = jnp.einsum(
            "gdi,gdj->gij", g_block, value_rows, preferred_element_type=jnp.float32
        )
        delta_row = jnp.sum(prob_f32 * grad_probs, axis=-1, keepdims=True)
        grad_scores = (prob_f32 * (grad_probs - delta_row)).astype(jnp.bfloat16)
        grad_query = (
            jnp.einsum("gij,gdj->gdi", grad_scores, key_rows, preferred_element_type=jnp.float32)
            * scale_val
        )
        key_acc = (
            key_acc
            + jnp.einsum("gij,gdi->gdj", grad_scores, q_block, preferred_element_type=jnp.float32)
            * scale_val
        )
        return ((key_acc, value_acc), grad_query)

    zero_acc = jnp.zeros(key_rows.shape, jnp.float32)
    (key_grad, value_grad), query_grad = lax.scan(
        one_block, (zero_acc, zero_acc), (blocks_q, blocks_g, row_top, row_total)
    )
    query_grad = query_grad.transpose(1, 2, 0, 3).reshape(groups_n, HEAD_DIM, HW)
    return (query_grad, key_grad, value_grad)


def first_section(values, gain_vec, bias_vec):
    return jax.nn.silu(group_norm(values, gain_vec, bias_vec))


def second_section(values, gain_vec, bias_vec, modulation):
    normal_vals = group_norm(values, gain_vec, bias_vec)
    return jax.nn.silu(normal_vals * (1.0 + modulation[0][:, :, None]) + modulation[1][:, :, None])


def local(
    features,
    cotangent,
    embedding,
    context,
    lengths,
    norm1_gain,
    norm1_bias,
    conv1_weight,
    conv1_bias,
    emb_weight,
    emb_bias,
    norm2_gain,
    norm2_bias,
    conv2_weight,
    conv2_bias,
    norm3_gain,
    norm3_bias,
    qkv_weight,
    qkv_bias,
    context_weight,
    context_bias,
    out_weight,
    out_bias,
):
    channels, images, pixels = features.shape
    feat_f32 = features.astype(jnp.float32)
    act_one = first_section(feat_f32, norm1_gain, norm1_bias).astype(jnp.bfloat16)
    full_one = lax.all_gather(act_one, "tensor", axis=0, tiled=True)
    conv_one = convolve(full_one, conv1_weight, conv1_bias)
    emb_act = jax.nn.silu(embedding.astype(jnp.float32)).astype(jnp.bfloat16)
    scale_shift = (
        jnp.einsum("ie,teo->toi", emb_act, emb_weight, preferred_element_type=jnp.float32)
        + emb_bias[:, :, None]
    )
    act_two = second_section(conv_one, norm2_gain, norm2_bias, scale_shift).astype(jnp.bfloat16)
    full_two = lax.all_gather(act_two, "tensor", axis=0, tiled=True)
    hidden = feat_f32 + convolve(full_two, conv2_weight, conv2_bias)
    normed = group_norm(hidden, norm3_gain, norm3_bias).astype(jnp.bfloat16)
    full_three = lax.all_gather(normed, "tensor", axis=0, tiled=True)
    qkv_low = (
        jnp.einsum("toc,cip->toip", qkv_weight, full_three, preferred_element_type=jnp.float32)
        + qkv_bias[:, :, None, None]
    ).astype(jnp.bfloat16)
    ctx_low = (
        jnp.einsum("toe,ine->toin", context_weight, context, preferred_element_type=jnp.float32)
        + context_bias[:, :, None, None]
    ).astype(jnp.bfloat16)
    queries = to_heads(qkv_low[0])
    key_rows = jnp.concatenate([to_heads(qkv_low[1]), to_heads(ctx_low[0])], axis=2)
    value_rows = jnp.concatenate([to_heads(qkv_low[2]), to_heads(ctx_low[1])], axis=2)
    key_limit = HW + 4 + lengths
    key_valid = jnp.repeat(
        jnp.arange(HW + CTX, dtype=jnp.int32)[None, :] < key_limit[:, None],
        channels // HEAD_DIM,
        axis=0,
    )
    heads_mixed, row_top, row_total = attend_forward(queries, key_rows, value_rows, key_valid)
    heads_out = from_heads(heads_mixed, images)
    full_heads = lax.all_gather(heads_out, "tensor", axis=0, tiled=True)
    output = (
        hidden
        + jnp.einsum("oc,cip->oip", out_weight, full_heads, preferred_element_type=jnp.float32)
        + out_bias[:, None, None]
    ).astype(jnp.bfloat16)
    grad_top = cotangent.astype(jnp.float32)
    out_weight_grad = jnp.einsum(
        "oip,cip->oc", cotangent, full_heads, preferred_element_type=jnp.float32
    )
    out_bias_grad = jnp.sum(grad_top, axis=(1, 2))
    cols_part = out_weight
    grad_heads = lax.psum_scatter(
        jnp.einsum("oc,oip->cip", cols_part, cotangent, preferred_element_type=jnp.float32).astype(
            jnp.bfloat16
        ),
        "tensor",
        scatter_dimension=0,
        tiled=True,
    )
    query_grad, key_grad, value_grad = attend_backward(
        queries, key_rows, value_rows, key_valid, to_heads(grad_heads), row_top, row_total
    )
    grad_qkv = jnp.stack(
        [
            from_heads(query_grad, images),
            from_heads(key_grad[:, :, :HW], images),
            from_heads(value_grad[:, :, :HW], images),
        ]
    ).astype(jnp.bfloat16)
    grad_ctx = jnp.stack(
        [from_heads(key_grad[:, :, HW:], images), from_heads(value_grad[:, :, HW:], images)]
    ).astype(jnp.bfloat16)
    qkv_weight_grad = jnp.einsum(
        "toip,cip->toc", grad_qkv, full_three, preferred_element_type=jnp.float32
    )
    qkv_bias_grad = jnp.sum(grad_qkv.astype(jnp.float32), axis=(2, 3))
    context_weight_grad = jnp.einsum(
        "toin,ine->toe", grad_ctx, context, preferred_element_type=jnp.float32
    )
    context_bias_grad = jnp.sum(grad_ctx.astype(jnp.float32), axis=(2, 3))
    cols_part = qkv_weight
    grad_normed = lax.psum_scatter(
        jnp.einsum("toc,toip->cip", cols_part, grad_qkv, preferred_element_type=jnp.float32).astype(
            jnp.bfloat16
        ),
        "tensor",
        scatter_dimension=0,
        tiled=True,
    ).astype(jnp.float32)
    unused_three, pull_three = jax.vjp(group_norm, hidden, norm3_gain, norm3_bias)
    grad_branch, norm3_gain_grad, norm3_bias_grad = pull_three(grad_normed)
    grad_hidden = grad_top + grad_branch
    attention_grads = (
        lax.psum(out_weight_grad.astype(jnp.bfloat16), "dp").astype(jnp.float32),
        lax.psum(out_bias_grad.astype(jnp.bfloat16), "dp").astype(jnp.float32),
        lax.psum(qkv_weight_grad.astype(jnp.bfloat16), "dp").astype(jnp.float32),
        lax.psum(qkv_bias_grad.astype(jnp.bfloat16), "dp").astype(jnp.float32),
        lax.psum(context_weight_grad.astype(jnp.bfloat16), "dp").astype(jnp.float32),
        lax.psum(context_bias_grad.astype(jnp.bfloat16), "dp").astype(jnp.float32),
        lax.psum(norm3_gain_grad.astype(jnp.bfloat16), "dp").astype(jnp.float32),
        lax.psum(norm3_bias_grad.astype(jnp.bfloat16), "dp").astype(jnp.float32),
    )
    grad_conv_two = grad_hidden.astype(jnp.bfloat16)
    conv2_bias_grad = jnp.sum(grad_conv_two.astype(jnp.float32), axis=(1, 2))
    conv2_weight_grad = kernel_grad(grad_conv_two, full_two)
    grad_act_two = conv_input_grad(grad_conv_two, conv2_weight)
    unused_two, pull_two = jax.vjp(second_section, conv_one, norm2_gain, norm2_bias, scale_shift)
    grad_conv_one, norm2_gain_grad, norm2_bias_grad, grad_modulation = pull_two(grad_act_two)
    grad_mod_low = grad_modulation.astype(jnp.bfloat16)
    emb_weight_grad = jnp.einsum(
        "ie,toi->teo", emb_act, grad_mod_low, preferred_element_type=jnp.float32
    )
    emb_bias_grad = jnp.sum(grad_mod_low.astype(jnp.float32), axis=2)
    grad_conv_low = grad_conv_one.astype(jnp.bfloat16)
    conv1_bias_grad = jnp.sum(grad_conv_low.astype(jnp.float32), axis=(1, 2))
    conv1_weight_grad = kernel_grad(grad_conv_low, full_one)
    grad_act_one = conv_input_grad(grad_conv_low, conv1_weight)
    unused_one, pull_one = jax.vjp(first_section, feat_f32, norm1_gain, norm1_bias)
    grad_feat, norm1_gain_grad, norm1_bias_grad = pull_one(grad_act_one)
    input_grad = grad_hidden + grad_feat
    residual_grads = (
        lax.psum(norm1_gain_grad.astype(jnp.bfloat16), "dp").astype(jnp.float32),
        lax.psum(norm1_bias_grad.astype(jnp.bfloat16), "dp").astype(jnp.float32),
        lax.psum(conv1_weight_grad.astype(jnp.bfloat16), "dp").astype(jnp.float32),
        lax.psum(conv1_bias_grad.astype(jnp.bfloat16), "dp").astype(jnp.float32),
        lax.psum(emb_weight_grad.astype(jnp.bfloat16), "dp").astype(jnp.float32),
        lax.psum(emb_bias_grad.astype(jnp.bfloat16), "dp").astype(jnp.float32),
        lax.psum(norm2_gain_grad.astype(jnp.bfloat16), "dp").astype(jnp.float32),
        lax.psum(norm2_bias_grad.astype(jnp.bfloat16), "dp").astype(jnp.float32),
        lax.psum(conv2_weight_grad.astype(jnp.bfloat16), "dp").astype(jnp.float32),
        lax.psum(conv2_bias_grad.astype(jnp.bfloat16), "dp").astype(jnp.float32),
    )
    return (
        output,
        input_grad,
        residual_grads[0],
        residual_grads[1],
        residual_grads[2],
        residual_grads[3],
        residual_grads[4],
        residual_grads[5],
        residual_grads[6],
        residual_grads[7],
        residual_grads[8],
        residual_grads[9],
        attention_grads[6],
        attention_grads[7],
        attention_grads[2],
        attention_grads[3],
        attention_grads[4],
        attention_grads[5],
        attention_grads[0],
        attention_grads[1],
    )


def solution(mesh):
    placed = (
        P("tensor", "dp", None),
        P("tensor", "dp", None),
        P("dp", None),
        P("dp", None, None),
        P("dp"),
        P("tensor"),
        P("tensor"),
        P("tensor", None),
        P("tensor"),
        P(None, None, "tensor"),
        P(None, "tensor"),
        P("tensor"),
        P("tensor"),
        P("tensor", None),
        P("tensor"),
        P("tensor"),
        P("tensor"),
        P(None, "tensor", None),
        P(None, "tensor"),
        P(None, "tensor", None),
        P(None, "tensor"),
        P("tensor", None),
        P("tensor"),
    )
    return jax.shard_map(
        local,
        mesh=mesh,
        in_specs=placed,
        out_specs=(
            P("tensor", "dp", None),
            P("tensor", "dp", None),
            P("tensor"),
            P("tensor"),
            P("tensor", None),
            P("tensor"),
            P(None, None, "tensor"),
            P(None, "tensor"),
            P("tensor"),
            P("tensor"),
            P("tensor", None),
            P("tensor"),
            P("tensor"),
            P("tensor"),
            P(None, "tensor", None),
            P(None, "tensor"),
            P(None, "tensor", None),
            P(None, "tensor"),
            P("tensor", None),
            P("tensor"),
        ),
        check_vma=False,
    )
```

profile of v0, /device:TPU:5, one launch (start us, length us, event | category | flops | bytes accessed | tf_op | source)
XLA Modules:
  0.0 2255.2 jit_solution(17377600485982242379)
XLA Ops:
  27.8 50.7 %all-gather.6.cloned.1.call-done = bf16[512,1,4096]{0,2,1:T(8,128)(2,1)} async-done(((bf16[256,1,4096]{0,2,1:T(8,128)(2,1)}), bf16[512,1,4096]{0,2,1:T(8,128)(2,1)}) %all-gather.6.cloned.1.call-update) | async-done | bytes 4194320 | tf_op jit(solution)/shard_map/all_gather | solution.py:205
  78.5 22.1 pad_slice_fusion.8
  144.4 47.6 %all-gather.12.cloned.1.call-done = bf16[512,4096]{0,1:T(8,128)(2,1)} async-done(((bf16[256,4096]{0,1:T(8,128)(2,1)}), bf16[512,4096]{0,1:T(8,128)(2,1)}) %all-gather.12.cloned.1.call-update) | async-done | bytes 4194320 | tf_op jit(solution)/shard_map/all_gather | solution.py:213
  192.0 21.8 pad_slice_fusion
  255.1 51.7 %all-gather.8.cloned.1.call-done = bf16[512,1,4096]{0,2,1:T(8,128)(2,1)} async-done(((bf16[256,1,4096]{0,2,1:T(8,128)(2,1)}), bf16[512,1,4096]{0,2,1:T(8,128)(2,1)}) %all-gather.8.cloned.1.call-update) | async-done | bytes 4194320 | tf_op jit(solution)/shard_map/all_gather | solution.py:216
  320.3 393.9 %while.30 = (s32[]{:T(128)}, bf16[8,4,64,512]{3,2,1,0:T(8,128)(2,1)}, f32[8,4,512,1]{2,1,3,0:T(4,128)S(1)}, f32[8,4,512,1]{2,1,3,0:T(4,128)S(1)}, bf16[8,4,64,51...) while((s32[]{:T(128)}, ...), condition=%wide.region_15.16_spmd.clone, body=%wide.region_12.15_spmd.clone.sunk | while | flops 2390978560 | bytes 121079936 | solution.py:122
  320.3 16.9 fusion.444
  337.2 16.3 fusion.445
  353.6 15.9 fusion.446
  369.5 16.9 fusion.444
  386.5 16.3 fusion.445
  402.8 15.9 fusion.446
  418.8 16.9 fusion.444
  435.7 16.3 fusion.445
  468.0 16.9 fusion.444
  484.9 16.3 fusion.445
  517.2 16.9 fusion.444
  534.2 16.3 fusion.445
  550.5 15.9 fusion.446
  566.5 16.9 fusion.444
  583.4 16.3 fusion.445
  599.8 15.9 fusion.446
  615.7 16.9 fusion.444
  632.7 16.3 fusion.445
  664.9 16.9 fusion.444
  681.9 16.3 fusion.445
  714.2 922.0 %while.31 = (s32[]{:T(128)}, f32[4,64,4356]{2,1,0:T(8,128)}, f32[4,64,4356]{2,1,0:T(8,128)}, bf16[8,4,64,512]{3,2,1,0:T(8,128)(2,1)}, bf16[8,4,64,512]{3,2,1,0:T...) while((s32[]{:T(128)}, f32[4,64,4356]{2,1,0:T(8,128)}, ...), condition=%wide.region_19.20_spmd.clone, body=%wide.region_17.19_spmd.clone.sunk | while | flops 5804411904 | bytes 302971552 | solution.py:161
  714.3 18.3 fusion.456
  732.7 30.3 %multiply_reduce_fusion.7 = (f32[4,512]{1,0:T(4,128)S(1)}, f32[4,512,4356]{1,2,0:T(8,128)}) fusion(f32[4,512,4356]{1,2,0:T(8,128)} %fusion.456, f32[4,512]{1,0:T(4,128)S(1)} %get-tuple-element.508, f32[4,512]{1,0:T(4,128)S(1)} %get-tuple-element.509, bf16[4,64,4356]{2,1,0:T(8,128)(2,1)} %get-tuple-element.570, ...), kind=kOutput, calls=%fused_computation.20.clone.1 | convolution fusion | flops 1195423744 | bytes 73890816 | tf_op jit(solution)/shard_map/while/body/eval_jaxpr/gdi,gdj->gij/dot_general | solution.py:100
  763.0 29.7 %multiply_convert_fusion.4 = bf16[4,512,4356]{1,2,0:T(8,128)(2,1)} fusion(f32[4,512,4356]{1,2,0:T(8,128)} %get-tuple-element.510, f32[4,512,4356]{1,2,0:T(8,128)} %fusion.456, f32[4,512]{1,0:T(4,128)S(1)} %get-tuple-element.511), kind=kLoop, calls=%fused_computation.19.clone.1 | loop fusion | flops 26763264 | bytes 89219072 | tf_op jit(solution)/shard_map/while/body/eval_jaxpr/convert_element_type | solution.py:148
  827.0 18.3 fusion.456
  845.4 30.3 %multiply_reduce_fusion.7 = (f32[4,512]{1,0:T(4,128)S(1)}, f32[4,512,4356]{1,2,0:T(8,128)}) fusion(f32[4,512,4356]{1,2,0:T(8,128)} %fusion.456, f32[4,512]{1,0:T(4,128)S(1)} %get-tuple-element.508, f32[4,512]{1,0:T(4,128)S(1)} %get-tuple-element.509, bf16[4,64,4356]{2,1,0:T(8,128)(2,1)} %get-tuple-element.570, ...), kind=kOutput, calls=%fused_computation.20.clone.1 | convolution fusion | flops 1195423744 | bytes 73890816 | tf_op jit(solution)/shard_map/while/body/eval_jaxpr/gdi,gdj->gij/dot_general | solution.py:100
  875.6 29.7 %multiply_convert_fusion.4 = bf16[4,512,4356]{1,2,0:T(8,128)(2,1)} fusion(f32[4,512,4356]{1,2,0:T(8,128)} %get-tuple-element.510, f32[4,512,4356]{1,2,0:T(8,128)} %fusion.456, f32[4,512]{1,0:T(4,128)S(1)} %get-tuple-element.511), kind=kLoop, calls=%fused_computation.19.clone.1 | loop fusion | flops 26763264 | bytes 89219072 | tf_op jit(solution)/shard_map/while/body/eval_jaxpr/convert_element_type | solution.py:148
  925.6 17.0 fusion.458
  942.6 18.3 fusion.456
  960.9 30.3 %multiply_reduce_fusion.7 = (f32[4,512]{1,0:T(4,128)S(1)}, f32[4,512,4356]{1,2,0:T(8,128)}) fusion(f32[4,512,4356]{1,2,0:T(8,128)} %fusion.456, f32[4,512]{1,0:T(4,128)S(1)} %get-tuple-element.508, f32[4,512]{1,0:T(4,128)S(1)} %get-tuple-element.509, bf16[4,64,4356]{2,1,0:T(8,128)(2,1)} %get-tuple-element.570, ...), kind=kOutput, calls=%fused_computation.20.clone.1 | convolution fusion | flops 1195423744 | bytes 73890816 | tf_op jit(solution)/shard_map/while/body/eval_jaxpr/gdi,gdj->gij/dot_general | solution.py:100
  991.2 29.7 %multiply_convert_fusion.4 = bf16[4,512,4356]{1,2,0:T(8,128)(2,1)} fusion(f32[4,512,4356]{1,2,0:T(8,128)} %get-tuple-element.510, f32[4,512,4356]{1,2,0:T(8,128)} %fusion.456, f32[4,512]{1,0:T(4,128)S(1)} %get-tuple-element.511), kind=kLoop, calls=%fused_computation.19.clone.1 | loop fusion | flops 26763264 | bytes 89219072 | tf_op jit(solution)/shard_map/while/body/eval_jaxpr/convert_element_type | solution.py:148
  1041.1 17.0 fusion.458
  1058.1 18.3 fusion.456
  1076.5 30.3 %multiply_reduce_fusion.7 = (f32[4,512]{1,0:T(4,128)S(1)}, f32[4,512,4356]{1,2,0:T(8,128)}) fusion(f32[4,512,4356]{1,2,0:T(8,128)} %fusion.456, f32[4,512]{1,0:T(4,128)S(1)} %get-tuple-element.508, f32[4,512]{1,0:T(4,128)S(1)} %get-tuple-element.509, bf16[4,64,4356]{2,1,0:T(8,128)(2,1)} %get-tuple-element.570, ...), kind=kOutput, calls=%fused_computation.20.clone.1 | convolution fusion | flops 1195423744 | bytes 73890816 | tf_op jit(solution)/shard_map/while/body/eval_jaxpr/gdi,gdj->gij/dot_general | solution.py:100
  1106.7 29.7 %multiply_convert_fusion.4 = bf16[4,512,4356]{1,2,0:T(8,128)(2,1)} fusion(f32[4,512,4356]{1,2,0:T(8,128)} %get-tuple-element.510, f32[4,512,4356]{1,2,0:T(8,128)} %fusion.456, f32[4,512]{1,0:T(4,128)S(1)} %get-tuple-element.511), kind=kLoop, calls=%fused_computation.19.clone.1 | loop fusion | flops 26763264 | bytes 89219072 | tf_op jit(solution)/shard_map/while/body/eval_jaxpr/convert_element_type | solution.py:148
  1156.7 17.0 fusion.458
  1173.7 18.3 fusion.456
  1192.0 30.3 %multiply_reduce_fusion.7 = (f32[4,512]{1,0:T(4,128)S(1)}, f32[4,512,4356]{1,2,0:T(8,128)}) fusion(f32[4,512,4356]{1,2,0:T(8,128)} %fusion.456, f32[4,512]{1,0:T(4,128)S(1)} %get-tuple-element.508, f32[4,512]{1,0:T(4,128)S(1)} %get-tuple-element.509, bf16[4,64,4356]{2,1,0:T(8,128)(2,1)} %get-tuple-element.570, ...), kind=kOutput, calls=%fused_computation.20.clone.1 | convolution fusion | flops 1195423744 | bytes 73890816 | tf_op jit(solution)/shard_map/while/body/eval_jaxpr/gdi,gdj->gij/dot_general | solution.py:100
  1222.3 29.7 %multiply_convert_fusion.4 = bf16[4,512,4356]{1,2,0:T(8,128)(2,1)} fusion(f32[4,512,4356]{1,2,0:T(8,128)} %get-tuple-element.510, f32[4,512,4356]{1,2,0:T(8,128)} %fusion.456, f32[4,512]{1,0:T(4,128)S(1)} %get-tuple-element.511), kind=kLoop, calls=%fused_computation.19.clone.1 | loop fusion | flops 26763264 | bytes 89219072 | tf_op jit(solution)/shard_map/while/body/eval_jaxpr/convert_element_type | solution.py:148
  1272.2 17.0 fusion.458
  1289.2 18.3 fusion.456
  1307.6 30.3 %multiply_reduce_fusion.7 = (f32[4,512]{1,0:T(4,128)S(1)}, f32[4,512,4356]{1,2,0:T(8,128)}) fusion(f32[4,512,4356]{1,2,0:T(8,128)} %fusion.456, f32[4,512]{1,0:T(4,128)S(1)} %get-tuple-element.508, f32[4,512]{1,0:T(4,128)S(1)} %get-tuple-element.509, bf16[4,64,4356]{2,1,0:T(8,128)(2,1)} %get-tuple-element.570, ...), kind=kOutput, calls=%fused_computation.20.clone.1 | convolution fusion | flops 1195423744 | bytes 73890816 | tf_op jit(solution)/shard_map/while/body/eval_jaxpr/gdi,gdj->gij/dot_general | solution.py:100
  1337.8 29.7 %multiply_convert_fusion.4 = bf16[4,512,4356]{1,2,0:T(8,128)(2,1)} fusion(f32[4,512,4356]{1,2,0:T(8,128)} %get-tuple-element.510, f32[4,512,4356]{1,2,0:T(8,128)} %fusion.456, f32[4,512]{1,0:T(4,128)S(1)} %get-tuple-element.511), kind=kLoop, calls=%fused_computation.19.clone.1 | loop fusion | flops 26763264 | bytes 89219072 | tf_op jit(solution)/shard_map/while/body/eval_jaxpr/convert_element_type | solution.py:148
  1387.7 17.0 fusion.458
  1404.7 18.3 fusion.456
  1423.1 30.3 %multiply_reduce_fusion.7 = (f32[4,512]{1,0:T(4,128)S(1)}, f32[4,512,4356]{1,2,0:T(8,128)}) fusion(f32[4,512,4356]{1,2,0:T(8,128)} %fusion.456, f32[4,512]{1,0:T(4,128)S(1)} %get-tuple-element.508, f32[4,512]{1,0:T(4,128)S(1)} %get-tuple-element.509, bf16[4,64,4356]{2,1,0:T(8,128)(2,1)} %get-tuple-element.570, ...), kind=kOutput, calls=%fused_computation.20.clone.1 | convolution fusion | flops 1195423744 | bytes 73890816 | tf_op jit(solution)/shard_map/while/body/eval_jaxpr/gdi,gdj->gij/dot_general | solution.py:100
  1453.4 29.7 %multiply_convert_fusion.4 = bf16[4,512,4356]{1,2,0:T(8,128)(2,1)} fusion(f32[4,512,4356]{1,2,0:T(8,128)} %get-tuple-element.510, f32[4,512,4356]{1,2,0:T(8,128)} %fusion.456, f32[4,512]{1,0:T(4,128)S(1)} %get-tuple-element.511), kind=kLoop, calls=%fused_computation.19.clone.1 | loop fusion | flops 26763264 | bytes 89219072 | tf_op jit(solution)/shard_map/while/body/eval_jaxpr/convert_element_type | solution.py:148
  1503.3 17.0 fusion.458
  1520.3 18.3 fusion.456
  1538.6 30.3 %multiply_reduce_fusion.7 = (f32[4,512]{1,0:T(4,128)S(1)}, f32[4,512,4356]{1,2,0:T(8,128)}) fusion(f32[4,512,4356]{1,2,0:T(8,128)} %fusion.456, f32[4,512]{1,0:T(4,128)S(1)} %get-tuple-element.508, f32[4,512]{1,0:T(4,128)S(1)} %get-tuple-element.509, bf16[4,64,4356]{2,1,0:T(8,128)(2,1)} %get-tuple-element.570, ...), kind=kOutput, calls=%fused_computation.20.clone.1 | convolution fusion | flops 1195423744 | bytes 73890816 | tf_op jit(solution)/shard_map/while/body/eval_jaxpr/gdi,gdj->gij/dot_general | solution.py:100
  1568.9 29.7 %multiply_convert_fusion.4 = bf16[4,512,4356]{1,2,0:T(8,128)(2,1)} fusion(f32[4,512,4356]{1,2,0:T(8,128)} %get-tuple-element.510, f32[4,512,4356]{1,2,0:T(8,128)} %fusion.456, f32[4,512]{1,0:T(4,128)S(1)} %get-tuple-element.511), kind=kLoop, calls=%fused_computation.19.clone.1 | loop fusion | flops 26763264 | bytes 89219072 | tf_op jit(solution)/shard_map/while/body/eval_jaxpr/convert_element_type | solution.py:148
  1618.8 17.0 fusion.458
  1680.8 45.2 %reduce-scatter.7.cloned.1.call-done = bf16[256,1,4096]{0,2,1:T(8,128)(2,1)} async-done(((bf16[512,1,4096]{0,2,1:T(8,128)(2,1)}), bf16[256,1,4096]{0,2,1:T(8,128)(2,1)}) %reduce-scatter.7.cloned.1.call-update) | async-done | bytes 2097168 | tf_op jit(solution)/shard_map/reduce_scatter | solution.py:278
  1786.9 24.4 %fusion.43 = bf16[512,1,4096]{0,2,1:T(8,128)(2,1)} fusion(bf16[256,4096]{0,1:T(8,128)(2,1)} %bitcast.785, f32[4096,512]{1,0:T(8,128)} %fusion.338, f32[4096,512]{1,0:T(8,128)} %fusion.337, f32[4096,512]{1,0:T(8,128)} %fusion.336, f32[4096,512]{1,0:T(8,128)} %fusion.133, f32[4096,512]{1,0:T(8,128)} %fusion.335, f32[4096,512]{1,0:T(8,128)} %fusion.334, ...), kind=kOutput, calls=%fused_computation.63 | convolution fusion | flops 1092616192 | bytes 73662464 | tf_op jit(solution)/shard_map/oc,oip->cip/dot_general | solution.py:72
  1962.5 25.4 %fusion.44 = bf16[512,1,4096]{0,2,1:T(8,128)(2,1)} fusion(bf16[256,4096]{0,1:T(8,128)(2,1)} %bitcast.784, f32[4096,512]{1,0:T(8,128)} %fusion.331, f32[4096,512]{1,0:T(8,128)} %fusion.330, f32[4096,512]{1,0:T(8,128)} %fusion.329, f32[4096,512]{1,0:T(8,128)} %fusion.113, f32[4096,512]{1,0:T(8,128)} %fusion.328, f32[4096,512]{1,0:T(8,128)} %fusion.327, ...), kind=kOutput, calls=%fused_computation.64 | convolution fusion | flops 1092616192 | bytes 73662464 | tf_op jit(solution)/shard_map/oc,oip->cip/dot_general | solution.py:72
  2008.9 120.8 %all-reduce.10.cloned.1.call-done = (bf16[256,4608]{0,1:T(8,128)(2,1)}, bf16[256,4608]{0,1:T(8,128)(2,1)}, bf16[256,512]{0,1:T(8,128)(2,1)}, bf16[2,2048,256]{2,...) async-done(((bf16[256,4608]{0,1:T(8,128)(2,1)}, bf16[256,4608]{0,1:T(8,128)(2,1)}, bf16[256,512]{0,1:T(8,128)(2,1)}, ...) | async-done | bytes 9961488 | tf_op jit(solution)/shard_map/psum | solution.py:320
  2146.7 39.1 %reduce-scatter.11.cloned.1.call-done = bf16[256,1,4096]{0,2,1:T(8,128)(2,1)} async-done(((bf16[512,1,4096]{0,2,1:T(8,128)(2,1)}), bf16[256,1,4096]{0,2,1:T(8,128)(2,1)}) %reduce-scatter.11.cloned.1.call-update) | async-done | bytes 2097168 | tf_op jit(solution)/shard_map/reduce_scatter | solution.py:75
  2191.6 30.4 %all-reduce.6 = (bf16[256]{0:T(256)(128)(2,1)S(1)}, bf16[256]{0:T(256)(128)(2,1)S(1)}, bf16[256]{0:T(256)(128)(2,1)S(1)}, bf16[2,256]{1,0:T(2,128)(2,1)S(1)}, bf...) all-reduce(bf16[256]{0:T(256)(128)(2,1)S(1)} %get-tuple-element.252, ...), channel_id=1, replica_groups=mesh['dp'=16,'tensor'=2] {'dp'}, use_global_device_ids=true, to_apply=%region_42.43 | all-reduce | flops 4096 | bytes 16384 | tf_op jit(solution)/shard_map/psum | solution.py:318
  (523 shorter events, 683.7 us)
Async XLA Ops:
  7.2 240.9 %copy-start = (bf16[2,256,2048]{2,1,0:T(8,128)(2,1)S(1)}, bf16[2,256,2048]{2,1,0:T(8,128)(2,1)}, u32[]{:S(2)}) copy-start(bf16[2,256,2048]{2,1,0:T(8,128)(2,1)} %param.46) | copy-start | bytes 6291460
  7.2 71.3 %all-gather.6.cloned.1.call-start = ((), (), s32[]{:S(2)}) async-start(), calls=%async_computation.4 | async-start | bytes 6291456 | tf_op jit(solution)/shard_map/all_gather | solution.py:205
  21.5 170.5 %all-gather.12.cloned.1.call-start = ((), (), s32[]{:S(2)}) async-start(), calls=%async_computation.11 | async-start | bytes 6291456 | tf_op jit(solution)/shard_map/all_gather | solution.py:213
  27.8 101.9 %copy-start.72 = (f32[1,256]{1,0:T(1,128)}, f32[1,256]{1,0:T(1,128)S(1)}, u32[]{:S(2)}) copy-start(f32[1,256]{1,0:T(1,128)S(1)} %get-tuple-element.370) | copy-start | bytes 3076
  27.8 101.9 %copy-start.88 = (f32[1,256]{1,0:T(1,128)}, f32[1,256]{1,0:T(1,128)S(1)}, u32[]{:S(2)}) copy-start(f32[1,256]{1,0:T(1,128)S(1)} %get-tuple-element.371) | copy-start | bytes 3076
  78.5 22.1 copy-start.97
  100.6 17.8 copy-start.17
  100.6 19.1 copy-start.15
  100.6 20.5 copy-start.13
  100.6 21.8 copy-start.11
  135.1 116.2 %reduce-scatter.5.cloned.1.call-start = ((), (), s32[]{:S(2)}) async-start(), calls=%async_computation.7 | async-start | bytes 6291456 | tf_op jit(solution)/shard_map/reduce_scatter | solution.py:248
  140.0 166.8 %all-gather.8.cloned.1.call-start = ((), (), s32[]{:S(2)}) async-start(), calls=%async_computation.5 | async-start | bytes 6291456 | tf_op jit(solution)/shard_map/all_gather | solution.py:216
  192.0 21.8 copy-start.98
  213.8 18.0 copy-start.31
  213.8 19.4 copy-start.29
  213.8 20.7 copy-start.27
  213.8 21.9 copy-start.7
  248.0 1478.0 %reduce-scatter.7.cloned.1.call-start = ((), (), s32[]{:S(2)}) async-start(), calls=%async_computation.8 | async-start | bytes 6291456 | tf_op jit(solution)/shard_map/reduce_scatter | solution.py:278
  248.1 58.7 %copy-start.110 = (bf16[3,256,512]{2,1,0:T(8,128)(2,1)S(1)}, bf16[3,256,512]{2,1,0:T(8,128)(2,1)}, u32[]{:S(2)}) copy-start(bf16[3,256,512]{2,1,0:T(8,128)(2,1)} %param.44) | copy-start | bytes 2359300
  248.1 58.7 %copy-start.112 = (f32[3,256]{1,0:T(4,128)S(1)}, f32[3,256]{1,0:T(4,128)}, u32[]{:S(2)}) copy-start(f32[3,256]{1,0:T(4,128)} %param.45) | copy-start | bytes 9220
  337.2 16.3 copy-start.6
  386.5 16.3 copy-start.6
  435.7 16.3 copy-start.6
  484.9 16.3 copy-start.6
  534.2 16.3 copy-start.6
  583.4 16.3 copy-start.6
  632.7 16.3 copy-start.6
  681.9 16.3 copy-start.6
  905.4 11.7 copy-start.3
  1020.9 11.7 copy-start.3
  1136.5 11.7 copy-start.3
  1252.0 11.7 copy-start.3
  1367.6 11.7 copy-start.3
  1483.1 11.7 copy-start.3
  1671.5 155.7 %all-gather.10.cloned.1.call-start = ((), (), s32[]{:S(2)}) async-start(), calls=%async_computation.6 | async-start | bytes 6291456 | tf_op jit(solution)/shard_map/all_gather | solution.py:236
  1678.3 47.7 %copy-start.62 = (f32[256]{0:T(256)S(1)}, f32[256]{0:T(256)}, u32[]{:S(2)}) copy-start(f32[256]{0:T(256)} %copy-done.61) | copy-start | bytes 3076
  1678.3 47.7 %copy-start.75 = (f32[256]{0:T(256)S(1)}, f32[256]{0:T(256)}, u32[]{:S(2)}) copy-start(f32[256]{0:T(256)} %copy-done.74) | copy-start | bytes 3076
  1678.3 47.7 %copy-start.84 = (f32[256]{0:T(256)S(1)}, f32[256]{0:T(256)}, u32[]{:S(2)}) copy-start(f32[256]{0:T(256)} %param.42) | copy-start | bytes 3076
  1680.7 50.2 %copy-start.109 = (f32[16]{0:T(128)S(1)}, f32[16]{0:T(128)}, u32[]{:S(2)}) copy-start(f32[16]{0:T(128)} %copy-done.108) | copy-start | bytes 196
  1680.7 185.0 %reduce-scatter.9.cloned.1.call-start = ((), (), s32[]{:S(2)}) async-start(), calls=%async_computation.9 | async-start | bytes 6291456 | tf_op jit(solution)/shard_map/reduce_scatter | solution.py:75
  1811.3 318.3 %all-reduce.10.cloned.1.call-start = ((), (), s32[]{:S(2)}) async-start(), calls=%async_computation.12 | async-start | bytes 19922944 | tf_op jit(solution)/shard_map/psum | solution.py:320
  1852.7 13.1 copy-start.67
  1852.7 13.1 copy-start.71
  1852.7 13.1 copy-start.73
  1852.7 13.1 copy-start.80
  1852.7 13.1 copy-start.89
  1852.7 13.1 copy-start.93
  1857.0 16.2 copy-start.107
  1933.0 252.7 %reduce-scatter.11.cloned.1.call-start = ((), (), s32[]{:S(2)}) async-start(), calls=%async_computation.10 | async-start | bytes 6291456 | tf_op jit(solution)/shard_map/reduce_scatter | solution.py:75
  2141.7 44.0 %copy-start.5 = (bf16[256,1,4096]{0,2,1:T(8,128)(2,1)S(1)}, bf16[256,1,4096]{0,2,1:T(8,128)(2,1)}, u32[]{:S(2)}) copy-start(bf16[256,1,4096]{0,2,1:T(8,128)(2,1)} %copy.104) | copy-start | bytes 6291460
  2141.7 44.0 %copy-start.65 = (f32[256]{0:T(256)S(1)}, f32[256]{0:T(256)}, u32[]{:S(2)}) copy-start(f32[256]{0:T(256)} %copy-done.64) | copy-start | bytes 3076
  2141.7 44.0 %copy-start.78 = (f32[256]{0:T(256)S(1)}, f32[256]{0:T(256)}, u32[]{:S(2)}) copy-start(f32[256]{0:T(256)} %copy-done.77) | copy-start | bytes 3076
  2141.7 44.0 %copy-start.87 = (f32[256]{0:T(256)S(1)}, f32[256]{0:T(256)}, u32[]{:S(2)}) copy-start(f32[256]{0:T(256)} %param.32) | copy-start | bytes 3076
  2141.7 44.0 %copy-start.96 = (f32[256]{0:T(256)S(1)}, f32[256]{0:T(256)}, u32[]{:S(2)}) copy-start(f32[256]{0:T(256)} %param.33) | copy-start | bytes 3076
  2146.6 45.0 %copy-start.99 = (bf16[256]{0:T(256)(128)(2,1)S(1)}, bf16[256]{0:T(256)(128)(2,1)}, u32[]{:S(2)}) copy-start(bf16[256]{0:T(256)(128)(2,1)} %get-tuple-element.250) | copy-start | bytes 1540
  2146.6 45.0 %copy-start.101 = (bf16[256]{0:T(256)(128)(2,1)S(1)}, bf16[256]{0:T(256)(128)(2,1)}, u32[]{:S(2)}) copy-start(bf16[256]{0:T(256)(128)(2,1)} %get-tuple-element.318) | copy-start | bytes 1540
  2146.6 45.0 %copy-start.102 = (bf16[256]{0:T(256)(128)(2,1)S(1)}, bf16[256]{0:T(256)(128)(2,1)}, u32[]{:S(2)}) copy-start(bf16[256]{0:T(256)(128)(2,1)} %get-tuple-element.351) | copy-start | bytes 1540
  2146.6 82.5 %copy-start.105 = (f32[16]{0:T(128)S(1)}, f32[16]{0:T(128)}, u32[]{:S(2)}) copy-start(f32[16]{0:T(128)} %copy-done.104) | copy-start | bytes 196
  2146.6 83.8 %copy-start.63 = (f32[256]{0:T(256)S(1)}, f32[256]{0:T(256)}, u32[]{:S(2)}) copy-start(f32[256]{0:T(256)} %copy-done.61) | copy-start | bytes 3076
  2146.6 83.8 %copy-start.76 = (f32[256]{0:T(256)S(1)}, f32[256]{0:T(256)}, u32[]{:S(2)}) copy-start(f32[256]{0:T(256)} %copy-done.74) | copy-start | bytes 3076
  2146.6 83.8 %copy-start.82 = (f32[256]{0:T(256)S(1)}, f32[256]{0:T(256)}, u32[]{:S(2)}) copy-start(f32[256]{0:T(256)} %copy-done.81) | copy-start | bytes 3076
  2146.6 83.8 %copy-start.85 = (f32[256]{0:T(256)S(1)}, f32[256]{0:T(256)}, u32[]{:S(2)}) copy-start(f32[256]{0:T(256)} %param.42) | copy-start | bytes 3076
  2146.7 83.8 %copy-start.91 = (f32[256]{0:T(256)S(1)}, f32[256]{0:T(256)}, u32[]{:S(2)}) copy-start(f32[256]{0:T(256)} %copy-done.90) | copy-start | bytes 3076
  2230.5 18.0 copy-start.1
  (73 other events, 334.6 us)
Sparse Core Ops, SparseCore 0:
  21.6 56.9 all-gather.5
  135.2 56.7 all-gather.11
  194.3 54.2 reduce-scatter.4
  250.0 56.7 all-gather.7
  1671.6 54.3 reduce-scatter.6
  1728.0 56.7 all-gather.9
  1811.4 54.2 reduce-scatter.8
  1933.1 196.5 all-reduce.9
  2132.5 53.1 reduce-scatter.10
where the time goes:
time: 2270 us; the launch traced here: 2260 us
  matrix products  1190 us (52%)
  other arithmetic  460 us (20%)
  waiting for transfers between devices  364 us (16%)
  local copies, waits for them, and re-layouts  189 us (8%)
  blocking collectives  30.4 us (1%)
    dot_general x16, matrix products, masked_scores(): jnp.einsum('gdi,gdj->gij', q_block, key_rows, preferred_element_type=jnp....  378 us
    convert_element_type x8, other arithmetic, one_block(): grad_scores = (prob_f32 * (grad_probs - delta_row)).astype(jnp.bfloat16)  238 us
    dot_general x8, matrix products, one_block(): jnp.einsum('gdi,gdj->gij', g_block, value_rows, preferred_element_type=jn...  147 us
    dot_general x8, matrix products, one_block(): jnp.einsum('gdi,gij->gdj', g_block, probs_low, preferred_element_type=jnp...  134 us
    reduce_sum x8, other arithmetic, one_block(): row_total = jnp.sum(raised, axis=-1, keepdims=True)  130 us
    dot_general x18, matrix products, conv_input_grad(): jnp.einsum('oc,oip->cip', cols_part, moved_grads[kernel_tap], preferred_e...  130 us
    dot_general x8, matrix products, one_block(): jnp.einsum('gdj,gij->gdi', value_rows, probs_low, preferred_element_type=...  128 us
    psum x1, waiting for transfers between devices, local(): lax.psum(conv1_weight_grad.astype(jnp.bfloat16), 'dp').astype(jnp.float32)  121 us
  transfers between devices with their start and end apart: 9, of which 7 were waited for; matrix products, arithmetic and copies ran while one was open for 13% of the time, Pallas kernels for 0%

commit v1 on v0

--- a/solution.py
+++ b/solution.py
@@ -1,6 +1,10 @@
+import functools
+
 import jax
 import jax.numpy as jnp
 from jax import lax
+from jax.experimental import pallas as pl
+from jax.experimental.pallas import tpu as pltpu
 from jax.sharding import PartitionSpec as P
 
 C = 512
@@ -96,73 +100,81 @@
     )
 
 
-def masked_scores(q_block, key_rows, key_valid):
-    scores = jnp.einsum(
-        "gdi,gdj->gij", q_block, key_rows, preferred_element_type=jnp.float32
-    ) * HEAD_DIM ** (-0.5)
-    return jnp.where(key_valid[:, None, :], scores, NEG_FILL)
-
-
-def attend_forward(queries, key_rows, value_rows, key_valid):
-    groups_n = queries.shape[0]
-    block_len = min(512, HW)
-    blocks_q = queries.reshape(groups_n, HEAD_DIM, HW // block_len, block_len).transpose(2, 0, 1, 3)
-
-    def one_block(q_block):
-        scores = masked_scores(q_block, key_rows, key_valid)
-        row_top = jnp.max(scores, axis=-1, keepdims=True)
-        raised = jnp.exp(scores - row_top)
-        row_total = jnp.sum(raised, axis=-1, keepdims=True)
-        probs_low = (raised / row_total).astype(jnp.bfloat16)
-        mixed_out = jnp.einsum(
-            "gdj,gij->gdi", value_rows, probs_low, preferred_element_type=jnp.float32
-        )
-        return (mixed_out.astype(jnp.bfloat16), row_top, row_total)
-
-    mixed_out, row_top, row_total = lax.map(one_block, blocks_q)
-    merged = mixed_out.transpose(1, 2, 0, 3).reshape(groups_n, HEAD_DIM, HW)
-    return (merged, row_top, row_total)
-
-
-def attend_backward(queries, key_rows, value_rows, key_valid, grad_mixed, row_top, row_total):
-    groups_n = queries.shape[0]
-    block_len = min(512, HW)
-    count_b = HW // block_len
-    blocks_q = queries.reshape(groups_n, HEAD_DIM, count_b, block_len).transpose(2, 0, 1, 3)
-    blocks_g = grad_mixed.reshape(groups_n, HEAD_DIM, count_b, block_len).transpose(2, 0, 1, 3)
-    scale_val = HEAD_DIM ** (-0.5)
-
-    def one_block(carried, packed):
-        key_acc, value_acc = carried
-        q_block, g_block, block_top, block_total = packed
-        scores = masked_scores(q_block, key_rows, key_valid)
-        prob_f32 = jnp.exp(scores - block_top) / block_total
-        probs_low = prob_f32.astype(jnp.bfloat16)
-        value_acc = value_acc + jnp.einsum(
-            "gdi,gij->gdj", g_block, probs_low, preferred_element_type=jnp.float32
-        )
-        grad_probs = jnp.einsum(
-            "gdi,gdj->gij", g_block, value_rows, preferred_element_type=jnp.float32
-        )
-        delta_row = jnp.sum(prob_f32 * grad_probs, axis=-1, keepdims=True)
-        grad_scores = (prob_f32 * (grad_probs - delta_row)).astype(jnp.bfloat16)
-        grad_query = (
-            jnp.einsum("gij,gdj->gdi", grad_scores, key_rows, preferred_element_type=jnp.float32)
-            * scale_val
-        )
-        key_acc = (
-            key_acc
-            + jnp.einsum("gij,gdi->gdj", grad_scores, q_block, preferred_element_type=jnp.float32)
-            * scale_val
-        )
-        return ((key_acc, value_acc), grad_query)
-
-    zero_acc = jnp.zeros(key_rows.shape, jnp.float32)
-    (key_grad, value_grad), query_grad = lax.scan(
-        one_block, (zero_acc, zero_acc), (blocks_q, blocks_g, row_top, row_total)
-    )
-    query_grad = query_grad.transpose(1, 2, 0, 3).reshape(groups_n, HEAD_DIM, HW)
-    return (query_grad, key_grad, value_grad)
+CTXP = 384
+KP = HW + CTXP
+
+
+def chunks(ck):
+    out=[(c,ck,False) for c in range(0,HW,ck)]
+    out.append((HW,CTXP,True))
+    return out
+
+def attn_kernel(lim_ref,q_ref,k_ref,v_ref,g_ref,o_ref,dq_ref,dk_ref,dv_ref,kt,vt,s_sc,p_sc,dka,dva,*,ck):
+    i=pl.program_id(1); n=pl.num_programs(1)
+    bq=q_ref.shape[2]
+    @pl.when(i==0)
+    def _():
+        kt[...]=k_ref[0].astype(jnp.float32).T.astype(jnp.bfloat16)
+        vt[...]=v_ref[0].astype(jnp.float32).T.astype(jnp.bfloat16)
+        dka[...]=jnp.zeros_like(dka); dva[...]=jnp.zeros_like(dva)
+    scale=HEAD_DIM**-0.5
+    q=(q_ref[0].astype(jnp.float32)*scale).astype(jnp.bfloat16)
+    g=g_ref[0]
+    f32=jnp.float32
+    lim=lim_ref[0]
+    m=jnp.full((8,bq),-jnp.inf,f32)
+    for c,w,masked in chunks(ck):
+        s=jnp.dot(kt[c:c+w,:],q,preferred_element_type=f32)
+        if masked:
+            row=lax.broadcasted_iota(jnp.int32,(w,bq),0)
+            s=jnp.where(row<lim,s,-1e30)
+        s_sc[c:c+w,:]=s
+        m=jnp.maximum(m,jnp.max(s.reshape(w//8,8,bq),axis=0))
+    mm=jnp.max(m,axis=0,keepdims=True)
+    l=jnp.zeros((8,bq),f32)
+    o=jnp.zeros((HEAD_DIM,bq),f32)
+    for c,w,_ in chunks(ck):
+        p=jnp.exp(s_sc[c:c+w,:]-mm)
+        l=l+jnp.sum(p.reshape(w//8,8,bq),axis=0)
+        pb=p.astype(jnp.bfloat16)
+        p_sc[c:c+w,:]=pb
+        o=o+jnp.dot(v_ref[0,:,c:c+w],pb,preferred_element_type=f32)
+    inv=1.0/jnp.sum(l,axis=0,keepdims=True)
+    o=o*inv
+    o_ref[0]=o.astype(jnp.bfloat16)
+    gf=g.astype(f32)
+    delta=jnp.sum(gf*o,axis=0,keepdims=True)*inv
+    gs=(gf*inv).astype(jnp.bfloat16)
+    dq=jnp.zeros((HEAD_DIM,bq),f32)
+    nt=(((1,),(1,)),((),()))
+    for c,w,_ in chunks(ck):
+        dp=jnp.dot(vt[c:c+w,:],gs,preferred_element_type=f32)
+        pb=p_sc[c:c+w,:]
+        ds=(dp-delta).astype(jnp.bfloat16)*pb
+        dq=dq+jnp.dot(k_ref[0,:,c:c+w],ds,preferred_element_type=f32)
+        dka[:,c:c+w]+=lax.dot_general(q,ds,nt,preferred_element_type=f32)
+        dva[:,c:c+w]+=lax.dot_general(gs,pb,nt,preferred_element_type=f32)
+    dq_ref[0]=(dq*scale).astype(jnp.bfloat16)
+    @pl.when(i==n-1)
+    def _():
+        dk_ref[0]=dka[...].astype(jnp.bfloat16)
+        dv_ref[0]=dva[...].astype(jnp.bfloat16)
+
+def attention(lim,q,k,v,g,bq=1024, ck=512):
+    H=q.shape[0]
+    bs=lambda w,im: pl.BlockSpec((1,HEAD_DIM,w),im)
+    qm=lambda h,i:(h,0,i); km=lambda h,i:(h,0,0)
+    sd=jax.ShapeDtypeStruct
+    fl=6*2*H*HW*KP*HEAD_DIM
+    return pl.pallas_call(functools.partial(attn_kernel,ck=ck),
+        grid=(H,HW//bq),
+        in_specs=[pl.BlockSpec(memory_space=pltpu.SMEM),bs(bq,qm),bs(KP,km),bs(KP,km),bs(bq,qm)],
+        out_specs=[bs(bq,qm),bs(bq,qm),bs(KP,km),bs(KP,km)],
+        out_shape=[sd((H,HEAD_DIM,HW),jnp.bfloat16)]*2+[sd((H,HEAD_DIM,KP),jnp.bfloat16)]*2,
+        scratch_shapes=[pltpu.VMEM((KP,HEAD_DIM),jnp.bfloat16)]*2+[pltpu.VMEM((KP,bq),jnp.float32),pltpu.VMEM((KP,bq),jnp.bfloat16)]+[pltpu.VMEM((HEAD_DIM,KP),jnp.float32)]*2,
+        compiler_params=pltpu.CompilerParams(vmem_limit_bytes=60<<20,dimension_semantics=("arbitrary","arbitrary")),
+        cost_estimate=pl.CostEstimate(flops=fl,transcendentals=H*HW*KP,bytes_accessed=H*64*(4*HW+4*KP)*2),
+    )(lim,q,k,v,g)
 
 
 def first_section(values, gain_vec, bias_vec):
@@ -223,15 +235,20 @@
         + context_bias[:, :, None, None]
     ).astype(jnp.bfloat16)
     queries = to_heads(qkv_low[0])
-    key_rows = jnp.concatenate([to_heads(qkv_low[1]), to_heads(ctx_low[0])], axis=2)
-    value_rows = jnp.concatenate([to_heads(qkv_low[2]), to_heads(ctx_low[1])], axis=2)
-    key_limit = HW + 4 + lengths
-    key_valid = jnp.repeat(
-        jnp.arange(HW + CTX, dtype=jnp.int32)[None, :] < key_limit[:, None],
-        channels // HEAD_DIM,
-        axis=0,
-    )
-    heads_mixed, row_top, row_total = attend_forward(queries, key_rows, value_rows, key_valid)
+    pad = ((0, 0), (0, 0), (0, CTXP - CTX))
+    key_rows = jnp.concatenate([to_heads(qkv_low[1]), jnp.pad(to_heads(ctx_low[0]), pad)], axis=2)
+    value_rows = jnp.concatenate([to_heads(qkv_low[2]), jnp.pad(to_heads(ctx_low[1]), pad)], axis=2)
+    grad_heads = lax.psum_scatter(
+        jnp.einsum("oc,oip->cip", out_weight, cotangent, preferred_element_type=jnp.float32).astype(
+            jnp.bfloat16
+        ),
+        "tensor",
+        scatter_dimension=0,
+        tiled=True,
+    )
+    heads_mixed, query_grad, key_grad, value_grad = attention(
+        4 + lengths, queries, key_rows, value_rows, to_heads(grad_heads)
+    )
     heads_out = from_heads(heads_mixed, images)
     full_heads = lax.all_gather(heads_out, "tensor", axis=0, tiled=True)
     output = (
@@ -244,18 +261,6 @@
         "oip,cip->oc", cotangent, full_heads, preferred_element_type=jnp.float32
     )
     out_bias_grad = jnp.sum(grad_top, axis=(1, 2))
-    cols_part = out_weight
-    grad_heads = lax.psum_scatter(
-        jnp.einsum("oc,oip->cip", cols_part, cotangent, preferred_element_type=jnp.float32).astype(
-            jnp.bfloat16
-        ),
-        "tensor",
-        scatter_dimension=0,
-        tiled=True,
-    )
-    query_grad, key_grad, value_grad = attend_backward(
-        queries, key_rows, value_rows, key_valid, to_heads(grad_heads), row_top, row_total
-    )
     grad_qkv = jnp.stack(
         [
             from_heads(query_grad, images),
@@ -264,7 +269,7 @@
         ]
     ).astype(jnp.bfloat16)
     grad_ctx = jnp.stack(
-        [from_heads(key_grad[:, :, HW:], images), from_heads(value_grad[:, :, HW:], images)]
+        [from_heads(key_grad[:, :, HW : HW + CTX], images), from_heads(value_grad[:, :, HW : HW + CTX], images)]
     ).astype(jnp.bfloat16)
     qkv_weight_grad = jnp.einsum(
         "toip,cip->toc", grad_qkv, full_three, preferred_element_type=jnp.float32

time: 2270 us -> 1250 us (0.55)
  matrix products: 1190 us -> 247 us
  other arithmetic: 460 us -> 95.6 us
  Pallas kernels: 0 us -> 265 us
  waiting for transfers between devices: 364 us -> 422 us
  local copies, waits for them, and re-layouts: 189 us -> 158 us
    dot_general x57 -> x1, matrix products: 951 us -> 4.82 us  [local(): jnp.einsum('oc,oip->cip', out_weight, cotangent, preferred_element_type=j...]
    pallas_call x0 -> x1, Pallas kernels: none -> 265 us  [attention(): pl.pallas_call(functools.partial(attn_kernel, ck=ck), grid=(H, HW // bq),...]
    convert_element_type x8 -> x0, other arithmetic: 238 us -> none  [one_block(): grad_scores = (prob_f32 * (grad_probs - delta_row)).astype(jnp.bfloat16)]
    reduce_sum x8 -> x0, other arithmetic: 130 us -> none  [one_block(): row_total = jnp.sum(raised, axis=-1, keepdims=True)]
    reduce_scatter x1, waiting for transfers between devices: 0.02 us -> 46.1 us  [local(): lax.psum_scatter(jnp.einsum('oc,oip->cip', out_weight, cotangent, preferr...]
    unnamed x235 -> x209, local copies, waits for them, and re-layouts: 68.5 us -> 61.6 us
  transfers between devices with their start and end apart: 9 -> 9, of which waited for: 7 -> 8; matrix products, arithmetic and copies ran while one was open for 13% -> 20% of each run, Pallas kernels for 0% -> 0%
where the time goes in v1:
time: 1250 us; the launch traced here: 1230 us
  waiting for transfers between devices  422 us (34%)
  Pallas kernels  265 us (21%)
  matrix products  247 us (20%)
  local copies, waits for them, and re-layouts  158 us (13%)
  other arithmetic  95.6 us (8%)
  blocking collectives  30.4 us (2%)
  between operations  15.8 us (1%)
    pallas_call x1, Pallas kernels, attention(): pl.pallas_call(functools.partial(attn_kernel, ck=ck), grid=(H, HW // bq),...  265 us
    dot_general x18, matrix products, conv_input_grad(): jnp.einsum('oc,oip->cip', cols_part, moved_grads[kernel_tap], preferred_e...  130 us
    psum x1, waiting for transfers between devices, local(): lax.psum(conv1_weight_grad.astype(jnp.bfloat16), 'dp').astype(jnp.float32)  129 us
    slice x4, local copies, waits for them, and re-layouts, shifted(): padded[:, :, row_off:row_off + SIDE, col_off:col_off + SIDE]  61.9 us
    unnamed x209, local copies, waits for them, and re-layouts  61.6 us
    all_gather x1, waiting for transfers between devices, local(): full_two = lax.all_gather(act_two, 'tensor', axis=0, tiled=True)  52.5 us
    all_gather x1, waiting for transfers between devices, local(): full_one = lax.all_gather(act_one, 'tensor', axis=0, tiled=True)  50.7 us
    reduce_scatter x1, waiting for transfers between devices, local(): lax.psum_scatter(jnp.einsum('toc,toip->cip', cols_part, grad_qkv, preferr...  50.3 us
  transfers between devices with their start and end apart: 9, of which 8 were waited for; matrix products, arithmetic and copies ran while one was open for 20% of the time, Pallas kernels for 0%

profile of v1, /device:TPU:5, one launch (start us, length us, event | category | flops | bytes accessed | tf_op | source)
XLA Modules:
  0.0 1234.8 jit_solution(17657651292623115212)
XLA Ops:
  7.3 4.2 copy.97
  17.1 4.3 fusion.36
  21.5 4.3 copy.98
  27.8 50.7 %all-gather.6.cloned.1.call-done = bf16[512,1,4096]{0,2,1:T(8,128)(2,1)} async-done(((bf16[256,1,4096]{0,2,1:T(8,128)(2,1)}), bf16[512,1,4096]{0,2,1:T(8,128)(2,1)}) %all-gather.6.cloned.1.call-update) | async-done | bytes 4194320 | tf_op jit(solution)/shard_map/all_gather | solution.py:217
  78.5 22.0 %pad_slice_fusion.8 = (bf16[512,1,64,64]{0,3,2,1:T(8,128)(2,1)S(1)}, bf16[512,1,64,64]{0,3,2,1:T(8,128)(2,1)}, bf16[512,1,64,64]{0,3,2,1:T(8,128)(2,1)}, bf16[51...) fusion(bf16[512,1,64,64]{0,3,2,1:T(8,128)(2,1)} %bitcast.606), kind=kLoop, calls=%fused_computation.125 | loop fusion | bytes 37748736 | tf_op jit(solution)/shard_map/slice | solution.py:36
  100.6 6.8 convolution_add_fusion.17
  122.4 3.3 fusion.330
  129.7 5.3 multiply_convert_fusion.1
  135.1 4.3 copy.108
  139.4 52.5 %all-gather.12.cloned.1.call-done = bf16[512,4096]{0,1:T(8,128)(2,1)} async-done(((bf16[256,4096]{0,1:T(8,128)(2,1)}), bf16[512,4096]{0,1:T(8,128)(2,1)}) %all-gather.12.cloned.1.call-update) | async-done | bytes 4194320 | tf_op jit(solution)/shard_map/all_gather | solution.py:225
  191.9 21.8 %pad_slice_fusion = (bf16[512,1,64,64]{0,3,2,1:T(8,128)(2,1)S(1)}, bf16[512,1,64,64]{0,3,2,1:T(8,128)(2,1)}, bf16[512,1,64,64]{0,3,2,1:T(8,128)(2,1)}, bf16[512,...) fusion(bf16[512,1,64,64]{0,3,2,1:T(8,128)(2,1)} %bitcast.621), kind=kLoop, calls=%fused_computation.117 | loop fusion | bytes 37748736 | tf_op jit(solution)/shard_map/slice | solution.py:36
  213.8 6.8 convolution_add_fusion.8
  242.5 4.6 add_convert_fusion.3
  247.2 4.8 fusion.8
  255.2 48.8 %all-gather.8.cloned.1.call-done = bf16[512,1,4096]{0,2,1:T(8,128)(2,1)} async-done(((bf16[256,1,4096]{0,2,1:T(8,128)(2,1)}), bf16[512,1,4096]{0,2,1:T(8,128)(2,1)}) %all-gather.8.cloned.1.call-update) | async-done | bytes 4194320 | tf_op jit(solution)/shard_map/all_gather | solution.py:228
  304.0 5.9 fusion.7
  314.4 46.1 %reduce-scatter.5.cloned.1.call-done = bf16[256,1,4096]{2,0,1:T(8,128)(2,1)} async-done(((bf16[512,1,4096]{2,0,1:T(8,128)(2,1)}), bf16[256,1,4096]{2,0,1:T(8,128)(2,1)}) %reduce-scatter.5.cloned.1.call-update) | async-done | bytes 2097168 | tf_op jit(solution)/shard_map/reduce_scatter | solution.py:241
  360.5 265.1 %shard_map.374 = (bf16[4,64,4096]{2,1,0:T(8,128)(2,1)}, bf16[4,64,4096]{2,1,0:T(8,128)(2,1)}, bf16[4,64,4480]{2,1,0:T(8,128)(2,1)}, bf16[4,64,4480]{2,1,0:T(8,128)(2,1)}) custom-call(s32[1]{0:T(128)S(6)} %add.455.lim_ref, bf16[4,64,4096]{2,1,0:T(8,128)(2,1)} %bitcast.700, bf16[4,64,4480]{2,1,0:T(8,128)(2,1)} %get-tuple-element.171.k_ref, ...), custom_call_target="tpu_custom_call" | custom-call | flops 56371445760 | bytes 17563648 | tf_op jit(solution)/shard_map/pallas_call | solution.py:169
  628.9 3.9 slice.273
  632.8 4.1 copy.123
  640.0 4.1 copy.124
  644.1 7.6 fusion.11
  655.8 50.3 %reduce-scatter.7.cloned.1.call-done = bf16[256,1,4096]{0,2,1:T(8,128)(2,1)} async-done(((bf16[512,1,4096]{0,2,1:T(8,128)(2,1)}), bf16[256,1,4096]{0,2,1:T(8,128)(2,1)}) %reduce-scatter.7.cloned.1.call-update) | async-done | bytes 2097168 | tf_op jit(solution)/shard_map/reduce_scatter | solution.py:283
  706.2 4.7 fusion.41
  714.6 7.7 fusion.322
  722.3 4.5 fusion.104
  726.8 8.7 pad_slice_fusion.30
  735.5 4.5 fusion.305
  739.9 4.5 fusion.304
  744.4 4.5 fusion.306
  748.9 4.5 fusion.307
  753.4 4.5 fusion.308
  757.9 4.5 fusion.309
  762.4 4.5 fusion.303
  766.9 24.3 %fusion.9 = bf16[512,1,4096]{0,2,1:T(8,128)(2,1)} fusion(bf16[256,4096]{0,1:T(8,128)(2,1)} %bitcast.693, f32[4096,512]{1,0:T(8,128)} %fusion.309, f32[4096,512]{1,0:T(8,128)} %fusion.308, f32[4096,512]{1,0:T(8,128)} %fusion.307, f32[4096,512]{1,0:T(8,128)} %fusion.104, f32[4096,512]{1,0:T(8,128)} %fusion.306, f32[4096,512]{1,0:T(8,128)} %fusion.305, ...), kind=kOutput, calls=%fused_computation.20 | convolution fusion | flops 1092616192 | bytes 73662464 | tf_op jit(solution)/shard_map/oc,oip->cip/dot_general | solution.py:76
  794.1 3.9 convolution_convert_fusion.1
  798.0 9.1 fusion.108
  807.0 5.0 fusion.175
  832.5 4.3 copy.126
  836.8 8.8 reduce-scatter.9.cloned.1.call-done
  845.6 7.3 fusion.52
  856.7 4.8 fusion.324
  863.4 5.6 fusion.84
  886.3 4.3 copy.125
  890.6 9.4 pad_slice_fusion.22
  900.0 5.4 fusion.298
  905.4 5.5 fusion.297
  914.1 5.6 fusion.299
  919.7 5.7 fusion.300
  925.4 5.6 fusion.301
  931.0 5.6 fusion.302
  936.6 5.4 fusion.296
  942.0 25.3 %fusion.10 = bf16[512,1,4096]{0,2,1:T(8,128)(2,1)} fusion(bf16[256,4096]{0,1:T(8,128)(2,1)} %bitcast.692, f32[4096,512]{1,0:T(8,128)} %fusion.302, f32[4096,512]{1,0:T(8,128)} %fusion.301, f32[4096,512]{1,0:T(8,128)} %fusion.300, f32[4096,512]{1,0:T(8,128)} %fusion.84, f32[4096,512]{1,0:T(8,128)} %fusion.299, f32[4096,512]{1,0:T(8,128)} %fusion.298, ...), kind=kOutput, calls=%fused_computation.21 | convolution fusion | flops 1092616192 | bytes 73662464 | tf_op jit(solution)/shard_map/oc,oip->cip/dot_general | solution.py:76
  969.5 4.3 fusion.319
  973.8 3.6 fusion.17
  980.3 129.0 %all-reduce.12.cloned.1.call-done = (bf16[256,4608]{0,1:T(8,128)(2,1)}, bf16[256,4608]{0,1:T(8,128)(2,1)}, bf16[256,512]{0,1:T(8,128)(2,1)}, bf16[2,2048,256]{2,...) async-done(((bf16[256,4608]{0,1:T(8,128)(2,1)}, bf16[256,4608]{0,1:T(8,128)(2,1)}, bf16[256,512]{0,1:T(8,128)(2,1)}, ...) | async-done | bytes 9961488 | tf_op jit(solution)/shard_map/psum | solution.py:325
  1113.6 4.5 copy.133
  1118.1 4.5 convert_element_type.294
  1125.2 4.8 copy.134
  1130.0 35.3 %reduce-scatter.11.cloned.1.call-done = bf16[256,1,4096]{0,2,1:T(8,128)(2,1)} async-done(((bf16[512,1,4096]{0,2,1:T(8,128)(2,1)}), bf16[256,1,4096]{0,2,1:T(8,128)(2,1)}) %reduce-scatter.11.cloned.1.call-update) | async-done | bytes 2097168 | tf_op jit(solution)/shard_map/reduce_scatter | solution.py:79
  1165.3 5.8 fusion.37
  1171.2 30.4 %all-reduce.8 = (bf16[256]{0:T(256)(128)(2,1)S(1)}, bf16[256]{0:T(256)(128)(2,1)S(1)}, bf16[256]{0:T(256)(128)(2,1)S(1)}, bf16[2,256]{1,0:T(2,128)(2,1)S(1)}, bf...) all-reduce(bf16[256]{0:T(256)(128)(2,1)S(1)} %get-tuple-element.93,, ...), channel_id=1, replica_groups=mesh['dp'=16,'tensor'=2] {'dp'}, use_global_device_ids=true, to_apply=%region_35.36 | all-reduce | flops 4096 | bytes 16384 | tf_op jit(solution)/shard_map/psum | solution.py:323
  1210.0 7.9 fusion.29
  1217.9 10.1 copy.132
  (363 shorter events, 139.4 us)
Async XLA Ops:
  7.2 245.7 %copy-start = (bf16[2,256,2048]{2,1,0:T(8,128)(2,1)S(1)}, bf16[2,256,2048]{2,1,0:T(8,128)(2,1)}, u32[]{:S(2)}) copy-start(bf16[2,256,2048]{2,1,0:T(8,128)(2,1)} %param.42) | copy-start | bytes 6291460
  7.2 9.9 copy-start.75
  7.2 9.9 copy-start.84
  7.2 71.3 %all-gather.6.cloned.1.call-start = ((), (), s32[]{:S(2)}) async-start(), calls=%async_computation.4 | async-start | bytes 6291456 | tf_op jit(solution)/shard_map/all_gather | solution.py:217
  14.0 7.5 copy-start.55
  17.1 8.7 copy-start.67
  21.4 6.3 copy-start.89
  21.5 170.4 %all-gather.12.cloned.1.call-start = ((), (), s32[]{:S(2)}) async-start(), calls=%async_computation.11 | async-start | bytes 6291456 | tf_op jit(solution)/shard_map/all_gather | solution.py:225
  27.8 101.9 %copy-start.63 = (f32[1,256]{1,0:T(1,128)}, f32[1,256]{1,0:T(1,128)S(1)}, u32[]{:S(2)}) copy-start(f32[1,256]{1,0:T(1,128)S(1)} %get-tuple-element.165) | copy-start | bytes 3076
  27.8 101.9 %copy-start.77 = (f32[1,256]{1,0:T(1,128)}, f32[1,256]{1,0:T(1,128)S(1)}, u32[]{:S(2)}) copy-start(f32[1,256]{1,0:T(1,128)S(1)} %get-tuple-element.166) | copy-start | bytes 3076
  78.5 22.1 %copy-start.86 = (f32[256]{0:T(256)S(1)}, f32[256]{0:T(256)}, u32[]{:S(2)}) copy-start(f32[256]{0:T(256)} %param.31) | copy-start | bytes 3076
  100.6 17.8 %copy-start.15 = (bf16[512,1,64,64]{0,3,2,1:T(8,128)(2,1)}, bf16[512,1,64,64]{0,3,2,1:T(8,128)(2,1)S(1)}, u32[]{:S(2)}) copy-start(bf16[512,1,64,64]{0,3,2,1:T(8,128)(2,1)S(1)} %get-tuple-element.142) | copy-start | bytes 12582916
  100.6 19.1 %copy-start.13 = (bf16[512,1,64,64]{0,3,2,1:T(8,128)(2,1)}, bf16[512,1,64,64]{0,3,2,1:T(8,128)(2,1)S(1)}, u32[]{:S(2)}) copy-start(bf16[512,1,64,64]{0,3,2,1:T(8,128)(2,1)S(1)} %get-tuple-element.143) | copy-start | bytes 12582916
  100.6 20.4 %copy-start.11 = (bf16[512,1,64,64]{0,3,2,1:T(8,128)(2,1)}, bf16[512,1,64,64]{0,3,2,1:T(8,128)(2,1)S(1)}, u32[]{:S(2)}) copy-start(bf16[512,1,64,64]{0,3,2,1:T(8,128)(2,1)S(1)} %get-tuple-element.144) | copy-start | bytes 12582916
  100.6 21.8 %copy-start.9 = (bf16[512,1,64,64]{0,3,2,1:T(8,128)(2,1)}, bf16[512,1,64,64]{0,3,2,1:T(8,128)(2,1)S(1)}, u32[]{:S(2)}) copy-start(bf16[512,1,64,64]{0,3,2,1:T(8,128)(2,1)S(1)} %get-tuple-element.138) | copy-start | bytes 12582916
  100.6 9.2 copy-start.21
  100.6 9.9 copy-start.37
  126.1 8.9 copy-start.57
  135.0 169.0 %all-gather.8.cloned.1.call-start = ((), (), s32[]{:S(2)}) async-start(), calls=%async_computation.5 | async-start | bytes 6291456 | tf_op jit(solution)/shard_map/all_gather | solution.py:228
  191.9 21.8 %copy-start.87 = (f32[256]{0:T(256)S(1)}, f32[256]{0:T(256)}, u32[]{:S(2)}) copy-start(f32[256]{0:T(256)} %param.37) | copy-start | bytes 3076
  213.7 17.8 %copy-start.29 = (bf16[512,1,64,64]{0,3,2,1:T(8,128)(2,1)}, bf16[512,1,64,64]{0,3,2,1:T(8,128)(2,1)S(1)}, u32[]{:S(2)}) copy-start(bf16[512,1,64,64]{0,3,2,1:T(8,128)(2,1)S(1)} %get-tuple-element.134) | copy-start | bytes 12582916
  213.7 19.1 %copy-start.27 = (bf16[512,1,64,64]{0,3,2,1:T(8,128)(2,1)}, bf16[512,1,64,64]{0,3,2,1:T(8,128)(2,1)S(1)}, u32[]{:S(2)}) copy-start(bf16[512,1,64,64]{0,3,2,1:T(8,128)(2,1)S(1)} %get-tuple-element.135) | copy-start | bytes 12582916
  213.7 20.5 %copy-start.25 = (bf16[512,1,64,64]{0,3,2,1:T(8,128)(2,1)}, bf16[512,1,64,64]{0,3,2,1:T(8,128)(2,1)S(1)}, u32[]{:S(2)}) copy-start(bf16[512,1,64,64]{0,3,2,1:T(8,128)(2,1)S(1)} %get-tuple-element.136) | copy-start | bytes 12582916
  213.7 21.7 %copy-start.5 = (bf16[512,1,64,64]{0,3,2,1:T(8,128)(2,1)}, bf16[512,1,64,64]{0,3,2,1:T(8,128)(2,1)S(1)}, u32[]{:S(2)}) copy-start(bf16[512,1,64,64]{0,3,2,1:T(8,128)(2,1)S(1)} %get-tuple-element.130) | copy-start | bytes 12582916
  213.7 9.2 copy-start.35
  213.7 9.9 copy-start.38
  239.3 475.2 %copy-start.53 = (f32[256]{0:T(256)}, f32[256]{0:T(256)S(1)}, u32[]{:S(2)}) copy-start(f32[256]{0:T(256)S(1)} %sub.143) | copy-start | bytes 3076
  242.5 472.1 %copy-start.65 = (f32[256]{0:T(256)}, f32[256]{0:T(256)S(1)}, u32[]{:S(2)}) copy-start(f32[256]{0:T(256)S(1)} %mul.393) | copy-start | bytes 3076
  247.2 5.7 copy-start.99
  247.2 113.4 %reduce-scatter.5.cloned.1.call-start = ((), (), s32[]{:S(2)}) async-start(), calls=%async_computation.6 | async-start | bytes 6291456 | tf_op jit(solution)/shard_map/reduce_scatter | solution.py:241
  252.1 52.0 %copy-start.97 = (bf16[3,256,512]{2,1,0:T(8,128)(2,1)S(1)}, bf16[3,256,512]{2,1,0:T(8,128)(2,1)}, u32[]{:S(2)}) copy-start(bf16[3,256,512]{2,1,0:T(8,128)(2,1)} %param.40) | copy-start | bytes 2359300
  252.1 52.0 %copy-start.98 = (f32[3,256]{1,0:T(4,128)S(1)}, f32[3,256]{1,0:T(4,128)}, u32[]{:S(2)}) copy-start(f32[3,256]{1,0:T(4,128)} %param.41) | copy-start | bytes 9220
  252.1 454.1 %reduce-scatter.7.cloned.1.call-start = ((), (), s32[]{:S(2)}) async-start(), calls=%async_computation.8 | async-start | bytes 6291456 | tf_op jit(solution)/shard_map/reduce_scatter | solution.py:283
  628.9 15.2 %copy-start.49 = (bf16[1,256,1,4096]{1,3,0,2:T(8,128)(2,1)}, bf16[1,256,1,4096]{1,3,0,2:T(8,128)(2,1)S(1)}, u32[]{:S(2)}) copy-start(bf16[1,256,1,4096]{1,3,0,2:T(8,128)(2,1)S(1)} %copy.122) | copy-start | bytes 6291460
  651.7 155.3 %all-gather.10.cloned.1.call-start = ((), (), s32[]{:S(2)}) async-start(), calls=%async_computation.7 | async-start | bytes 6291456 | tf_op jit(solution)/shard_map/all_gather | solution.py:253
  655.8 189.8 %reduce-scatter.9.cloned.1.call-start = ((), (), s32[]{:S(2)}) async-start(), calls=%async_computation.9 | async-start | bytes 6291456 | tf_op jit(solution)/shard_map/reduce_scatter | solution.py:79
  711.2 11.1 copy-start.71
  714.6 7.7 copy-start.79
  714.6 7.7 copy-start.39
  791.2 318.0 %all-reduce.12.cloned.1.call-start = ((), (), s32[]{:S(2)}) async-start(), calls=%async_computation.12 | async-start | bytes 19922944 | tf_op jit(solution)/shard_map/psum | solution.py:325
  832.5 13.1 %copy-start.58 = (f32[256]{0:T(256)S(1)}, f32[256]{0:T(256)}, u32[]{:S(2)}) copy-start(f32[256]{0:T(256)} %copy-done.57) | copy-start | bytes 3076
  832.5 13.1 %copy-start.62 = (f32[256]{0:T(256)S(1)}, f32[256]{0:T(256)}, u32[]{:S(2)}) copy-start(f32[256]{0:T(256)} %copy-done.61) | copy-start | bytes 3076
  832.5 13.1 %copy-start.64 = (f32[1,256]{1,0:T(1,128)S(1)}, f32[1,256]{1,0:T(1,128)}, u32[]{:S(2)}) copy-start(f32[1,256]{1,0:T(1,128)} %copy-done.63) | copy-start | bytes 3076
  832.5 13.1 %copy-start.70 = (f32[256]{0:T(256)S(1)}, f32[256]{0:T(256)}, u32[]{:S(2)}) copy-start(f32[256]{0:T(256)} %param.34) | copy-start | bytes 3076
  832.5 13.1 %copy-start.78 = (f32[1,256]{1,0:T(1,128)S(1)}, f32[1,256]{1,0:T(1,128)}, u32[]{:S(2)}) copy-start(f32[1,256]{1,0:T(1,128)} %copy-done.77) | copy-start | bytes 3076
  832.5 13.1 %copy-start.82 = (f32[256]{0:T(256)S(1)}, f32[256]{0:T(256)}, u32[]{:S(2)}) copy-start(f32[256]{0:T(256)} %param.35) | copy-start | bytes 3076
  836.8 16.3 %copy-start.96 = (f32[16]{0:T(128)S(1)}, f32[16]{0:T(128)}, u32[]{:S(2)}) copy-start(f32[16]{0:T(128)} %copy-done.95) | copy-start | bytes 196
  912.6 252.7 %reduce-scatter.11.cloned.1.call-start = ((), (), s32[]{:S(2)}) async-start(), calls=%async_computation.10 | async-start | bytes 6291456 | tf_op jit(solution)/shard_map/reduce_scatter | solution.py:79
  919.7 5.7 copy-start.46
  1125.1 40.1 %copy-start.4 = (bf16[256,1,4096]{0,2,1:T(8,128)(2,1)S(1)}, bf16[256,1,4096]{0,2,1:T(8,128)(2,1)}, u32[]{:S(2)}) copy-start(bf16[256,1,4096]{0,2,1:T(8,128)(2,1)} %copy.97) | copy-start | bytes 6291460
  1125.1 40.1 %copy-start.56 = (f32[256]{0:T(256)S(1)}, f32[256]{0:T(256)}, u32[]{:S(2)}) copy-start(f32[256]{0:T(256)} %copy-done.55) | copy-start | bytes 3076
  1125.2 40.1 %copy-start.68 = (f32[256]{0:T(256)S(1)}, f32[256]{0:T(256)}, u32[]{:S(2)}) copy-start(f32[256]{0:T(256)} %copy-done.67) | copy-start | bytes 3076
  1125.2 40.1 %copy-start.76 = (f32[256]{0:T(256)S(1)}, f32[256]{0:T(256)}, u32[]{:S(2)}) copy-start(f32[256]{0:T(256)} %param.28) | copy-start | bytes 3076
  1125.2 40.1 %copy-start.85 = (f32[256]{0:T(256)S(1)}, f32[256]{0:T(256)}, u32[]{:S(2)}) copy-start(f32[256]{0:T(256)} %param.29) | copy-start | bytes 3076
  1129.9 41.2 %copy-start.88 = (bf16[256]{0:T(256)(128)(2,1)S(1)}, bf16[256]{0:T(256)(128)(2,1)}, u32[]{:S(2)}) copy-start(bf16[256]{0:T(256)(128)(2,1)} %get-tuple-element.91) | copy-start | bytes 1540
  1129.9 41.2 %copy-start.90 = (bf16[256]{0:T(256)(128)(2,1)S(1)}, bf16[256]{0:T(256)(128)(2,1)}, u32[]{:S(2)}) copy-start(bf16[256]{0:T(256)(128)(2,1)} %get-tuple-element.121) | copy-start | bytes 1540
  1129.9 41.2 %copy-start.91 = (bf16[256]{0:T(256)(128)(2,1)S(1)}, bf16[256]{0:T(256)(128)(2,1)}, u32[]{:S(2)}) copy-start(bf16[256]{0:T(256)(128)(2,1)} %get-tuple-element.146) | copy-start | bytes 1540
  1129.9 78.7 %copy-start.94 = (f32[16]{0:T(128)S(1)}, f32[16]{0:T(128)}, u32[]{:S(2)}) copy-start(f32[16]{0:T(128)} %copy-done.93) | copy-start | bytes 196
  1130.0 80.0 %copy-start.54 = (f32[256]{0:T(256)S(1)}, f32[256]{0:T(256)}, u32[]{:S(2)}) copy-start(f32[256]{0:T(256)} %copy-done.53) | copy-start | bytes 3076
  1130.0 80.0 %copy-start.66 = (f32[256]{0:T(256)S(1)}, f32[256]{0:T(256)}, u32[]{:S(2)}) copy-start(f32[256]{0:T(256)} %copy-done.65) | copy-start | bytes 3076
  1130.0 80.0 %copy-start.72 = (f32[256]{0:T(256)S(1)}, f32[256]{0:T(256)}, u32[]{:S(2)}) copy-start(f32[256]{0:T(256)} %copy-done.71) | copy-start | bytes 3076
  1130.0 80.0 %copy-start.74 = (f32[256]{0:T(256)S(1)}, f32[256]{0:T(256)}, u32[]{:S(2)}) copy-start(f32[256]{0:T(256)} %param.38) | copy-start | bytes 3076
  1130.0 80.0 %copy-start.80 = (f32[256]{0:T(256)S(1)}, f32[256]{0:T(256)}, u32[]{:S(2)}) copy-start(f32[256]{0:T(256)} %copy-done.79) | copy-start | bytes 3076
  1210.0 18.0 %copy-start.1 = (bf16[2,256,2048]{2,1,0:T(8,128)(2,1)S(1)}, bf16[2,256,2048]{2,1,0:T(8,128)(2,1)}, u32[]{:S(2)}) copy-start(bf16[2,256,2048]{2,1,0:T(8,128)(2,1)} %param.42) | copy-start | bytes 6291460
  (45 other events, 135.1 us)
Sparse Core Ops, SparseCore 0:
  21.6 56.9 all-gather.5
  135.2 56.7 all-gather.11
  247.3 56.6 all-gather.7
  306.2 54.3 reduce-scatter.4
  651.8 54.2 reduce-scatter.6
  707.5 56.7 all-gather.9
  791.3 54.1 reduce-scatter.8
  912.7 196.4 all-reduce.11
  1112.1 53.1 reduce-scatter.10

commit v2 on v0

v2 whole, which is shorter than its diff:
```python
import functools

import jax
import jax.numpy as jnp
from jax import lax
from jax.experimental import pallas as pl
from jax.experimental.pallas import tpu as pltpu
from jax.sharding import PartitionSpec as P

C = 512
HEAD_DIM = 64
PER_GROUP = 16
SIDE = 64
HW = 4096
CTX = 260
CTXP = 384
PAD = 128
EPSILON = 1e-05
NEG_FILL = -1e30
F32 = jnp.float32
BF = jnp.bfloat16
NT = (((1,), (1,)), ((), ()))
VMEM_BYTES = 62 << 20


def dot(a, b):
    return jnp.dot(a, b, preferred_element_type=F32)


def dot_nt(a, b):
    return lax.dot_general(a, b, NT, preferred_element_type=F32)


def whole():
    return pl.BlockSpec(memory_space=pltpu.VMEM)


def params(**kwargs):
    return pltpu.CompilerParams(vmem_limit_bytes=VMEM_BYTES, **kwargs)


def cost(flops, nbytes, transcendentals=0):
    return pl.CostEstimate(flops=flops, bytes_accessed=nbytes, transcendentals=transcendentals)


def struct(shape, dtype):
    return jax.ShapeDtypeStruct(shape, dtype)


def group_scalar(column):
    return jnp.sum(column, axis=0, keepdims=True) * (1.0 / (PER_GROUP * HW))


def group_stats(vals):
    mean = group_scalar(jnp.sum(vals, axis=1, keepdims=True))
    centred = vals - mean
    var = group_scalar(jnp.sum(centred * centred, axis=1, keepdims=True))
    rstd = lax.rsqrt(var + EPSILON)
    return mean, rstd


def norm_backward(dy_sum, dyx_sum, gain):
    return group_scalar(dy_sum * gain), group_scalar(dyx_sum * gain)


def for_groups(channels, body):
    def step(g, carry):
        body(pl.ds(pl.multiple_of(g * PER_GROUP, PER_GROUP), PER_GROUP))
        return carry

    lax.fori_loop(0, channels // PER_GROUP, step, 0)


def columns(values):
    lane = lax.broadcasted_iota(jnp.int32, (PER_GROUP, 128), 1)
    tile = jnp.zeros((PER_GROUP, 128), F32)
    for at, val in enumerate(values):
        tile = jnp.where(lane == at, val, tile)
    return tile


def act_one_kernel(x_ref, par_ref, act_ref, stat_ref):
    def body(rows):
        vals = x_ref[rows, :].astype(F32)
        mean, rstd = group_stats(vals)
        par = par_ref[rows, :]
        out = (vals - mean) * rstd * par[:, 0:1] + par[:, 1:2]
        act_ref[rows, :] = (out * jax.nn.sigmoid(out)).astype(BF)
        stat_ref[rows, :] = columns([mean, rstd])

    for_groups(x_ref.shape[0], body)


def first_activation(x, par):
    ch = x.shape[0]
    return pl.pallas_call(
        act_one_kernel,
        out_shape=[struct((ch, HW), BF), struct((ch, 128), F32)],
        in_specs=[whole()] * 2,
        out_specs=[whole()] * 2,
        compiler_params=params(),
        cost_estimate=cost(20 * ch * HW, 4 * ch * HW, ch * HW),
    )(x, par)


def fill_shifted(xs, pieces):
    row = 0
    for x_ref in pieces:
        rows = x_ref.shape[0]
        for r in range(0, rows, 64):
            x = x_ref[r : r + 64, :].astype(F32)
            col = lax.broadcasted_iota(jnp.int32, x.shape, 1) % SIDE
            zero = jnp.zeros_like(x)
            at = slice(row + r, row + r + 64)
            for d in range(3):
                if d == 0:
                    y = jnp.where(col == 0, zero, pltpu.roll(x, 1, 1))
                elif d == 1:
                    y = x
                else:
                    y = jnp.where(col == SIDE - 1, zero, pltpu.roll(x, HW - 1, 1))
                xs[2 * d, at, PAD : PAD + HW] = y.astype(BF)
                turned = pltpu.roll(y, 64, 1)
                lane = lax.broadcasted_iota(jnp.int32, x.shape, 1)
                xs[2 * d + 1, at, PAD : PAD + HW] = jnp.where(lane < 64, zero, turned).astype(BF)
                tail = turned[:, :128]
                xs[2 * d + 1, at, PAD + HW :] = jnp.where(
                    lane[:, :128] < 64, tail, jnp.zeros_like(tail)
                ).astype(BF)
        row += rows
    edge = jnp.zeros((xs.shape[1], PAD), BF)
    for d in range(3):
        xs[2 * d, :, :PAD] = edge
        xs[2 * d, :, PAD + HW :] = edge
        xs[2 * d + 1, :, :PAD] = edge


def window(xs, tap, start, width):
    row_off, col_off = tap // 3, tap % 3
    off = (row_off - 1) * SIDE
    if off == 0:
        return xs[2 * col_off, :, PAD + start : PAD + start + width]
    first = PAD + start + off + 64
    return xs[2 * col_off + 1, :, first : first + width]


def convolve(xs, w_ref, out_ref, add, width=1024):
    depth = xs.shape[1]
    for p in range(0, HW, width):
        acc = dot(w_ref[:, :depth], window(xs, 0, p, width))
        for tap in range(1, 9):
            acc = acc + dot(w_ref[:, tap * depth : (tap + 1) * depth], window(xs, tap, p, width))
        out_ref[:, p : p + width] = add(acc, slice(p, p + width))


def conv_call(kernel, weight, pieces, others, outs, scratch, name):
    out_ch, depth = weight.shape[0], C
    nbytes = weight.size * 2 + sum(a.size * a.dtype.itemsize for a in tuple(pieces) + tuple(others))
    return pl.pallas_call(
        functools.partial(kernel, len(pieces)),
        out_shape=outs,
        in_specs=[whole()] * (1 + len(pieces) + len(others)),
        out_specs=[whole()] * len(outs),
        scratch_shapes=[pltpu.VMEM((6, depth, HW + 2 * PAD), BF)] + scratch,
        compiler_params=params(),
        cost_estimate=cost(2 * out_ch * 9 * depth * HW, nbytes, out_ch * HW),
        name=name,
    )(weight, *pieces, *others)


def conv_one_kernel(n, w_ref, *refs):
    pieces, (par_ref, conv_ref, act_ref, stat_ref, xs) = refs[:n], refs[n:]
    fill_shifted(xs, pieces)
    bias = par_ref[:, 0:1]
    convolve(xs, w_ref, conv_ref, lambda acc, at: acc + bias)

    def body(rows):
        vals = conv_ref[rows, :]
        mean, rstd = group_stats(vals)
        par = par_ref[rows, :]
        normal = (vals - mean) * rstd * par[:, 1:2] + par[:, 2:3]
        mid = normal * (1.0 + par[:, 3:4]) + par[:, 4:5]
        act_ref[rows, :] = (mid * jax.nn.sigmoid(mid)).astype(BF)
        stat_ref[rows, :] = columns([mean, rstd])

    for_groups(conv_ref.shape[0], body)


def conv_two_kernel(n, w_ref, *refs):
    pieces, (par_ref, feat_ref, hidden_ref, normed_ref, stat_ref, xs) = refs[:n], refs[n:]
    fill_shifted(xs, pieces)
    bias = par_ref[:, 0:1]
    convolve(xs, w_ref, hidden_ref, lambda acc, at: acc + bias + feat_ref[:, at].astype(F32))

    def body(rows):
        vals = hidden_ref[rows, :]
        mean, rstd = group_stats(vals)
        par = par_ref[rows, :]
        normed_ref[rows, :] = ((vals - mean) * rstd * par[:, 1:2] + par[:, 2:3]).astype(BF)
        stat_ref[rows, :] = columns([mean, rstd])

    for_groups(hidden_ref.shape[0], body)


def silu_slope(mid):
    sig = jax.nn.sigmoid(mid)
    return sig * (1.0 + mid * (1.0 - sig))


def conv_two_back_kernel(n, w_ref, *refs):
    pieces, (par_ref, conv_ref, stat_ref, grad_ref, sums_ref, xs, acc_ref) = refs[:n], refs[n:]
    fill_shifted(xs, pieces)
    convolve(xs, w_ref, acc_ref, lambda acc, at: acc)

    def body(rows):
        par, stat = par_ref[rows, :], stat_ref[rows, :]
        gain, shift, factor = par[:, 1:2], par[:, 2:3], 1.0 + par[:, 3:4]
        rstd = stat[:, 1:2]
        hat = (conv_ref[rows, :] - stat[:, 0:1]) * rstd
        mid = (hat * gain + shift) * factor + par[:, 4:5]
        grad = acc_ref[rows, :] * silu_slope(mid)
        total = jnp.sum(grad, axis=1, keepdims=True)
        total_hat = jnp.sum(grad * hat, axis=1, keepdims=True)
        mean_u, mean_uhat = norm_backward(total * factor, total_hat * factor, gain)
        out = ((grad * (factor * gain) - mean_u - hat * mean_uhat) * rstd).astype(BF)
        grad_ref[rows, :] = out
        bias_grad = jnp.sum(out.astype(F32), axis=1, keepdims=True)
        sums_ref[rows, :] = columns(
            [
                total_hat * factor,
                total * factor,
                total_hat * gain + total * shift,
                total,
                bias_grad,
            ]
        )

    for_groups(acc_ref.shape[0], body)


def conv_one_back_kernel(n, w_ref, *refs):
    pieces, (par_ref, feat_ref, stat_ref, hid_ref, grad_ref, sums_ref, xs, acc_ref) = (
        refs[:n],
        refs[n:],
    )
    fill_shifted(xs, pieces)
    convolve(xs, w_ref, acc_ref, lambda acc, at: acc)

    def body(rows):
        par, stat = par_ref[rows, :], stat_ref[rows, :]
        gain, shift = par[:, 0:1], par[:, 1:2]
        rstd = stat[:, 1:2]
        hat = (feat_ref[rows, :].astype(F32) - stat[:, 0:1]) * rstd
        grad = acc_ref[rows, :] * silu_slope(hat * gain + shift)
        total = jnp.sum(grad, axis=1, keepdims=True)
        total_hat = jnp.sum(grad * hat, axis=1, keepdims=True)
        mean_u, mean_uhat = norm_backward(total, total_hat, gain)
        out = hid_ref[rows, :] + (grad * gain - mean_u - hat * mean_uhat) * rstd
        grad_ref[rows, :] = out.astype(grad_ref.dtype)
        sums_ref[rows, :] = columns([total_hat, total])

    for_groups(acc_ref.shape[0], body)


def weight_grad_kernel(n, grad_ref, *refs):
    pieces, (out_ref, gs) = refs[:n], refs[n:]
    fill_shifted(gs, (grad_ref,))
    for tap in range(9):
        moved = window(gs, 8 - tap, 0, HW)
        at = tap * C
        for x_ref in pieces:
            rows = x_ref.shape[0]
            out_ref[:, at : at + rows] = dot_nt(moved, x_ref[...]).astype(BF)
            at += rows


def conv_weight_grad(grad, pieces, name):
    out_ch = grad.shape[0]
    return pl.pallas_call(
        functools.partial(weight_grad_kernel, len(pieces)),
        out_shape=struct((out_ch, 9 * C), BF),
        in_specs=[whole()] * (1 + len(pieces)),
        out_specs=whole(),
        scratch_shapes=[pltpu.VMEM((6, out_ch, HW + 2 * PAD), BF)],
        compiler_params=params(),
        cost_estimate=cost(2 * out_ch * 9 * C * HW, (out_ch + C) * HW * 2 + out_ch * 9 * C * 2),
        name=name,
    )(grad, *pieces)


def norm_three_back_kernel(n, *refs):
    addends, (hidden_ref, stat_ref, par_ref, cot_ref, hid_ref, grad_ref, sums_ref) = (
        refs[:n],
        refs[n:],
    )

    def body(rows):
        dy = addends[0][rows, :].astype(F32)
        for extra in addends[1:]:
            dy = dy + extra[rows, :].astype(F32)
        par, stat = par_ref[rows, :], stat_ref[rows, :]
        gain, rstd = par[:, 1:2], stat[:, 1:2]
        hat = (hidden_ref[rows, :] - stat[:, 0:1]) * rstd
        total = jnp.sum(dy, axis=1, keepdims=True)
        total_hat = jnp.sum(dy * hat, axis=1, keepdims=True)
        mean_u, mean_uhat = norm_backward(total, total_hat, gain)
        top = cot_ref[rows, :].astype(F32)
        out = top + (dy * gain - mean_u - hat * mean_uhat) * rstd
        hid_ref[rows, :] = out
        low = out.astype(BF)
        grad_ref[rows, :] = low
        sums_ref[rows, :] = columns(
            [
                total_hat,
                total,
                jnp.sum(low.astype(F32), axis=1, keepdims=True),
                jnp.sum(top, axis=1, keepdims=True),
            ]
        )

    for_groups(hidden_ref.shape[0], body)


def norm_three_back(addends, hidden, stat, par, cot):
    ch = hidden.shape[0]
    return pl.pallas_call(
        functools.partial(norm_three_back_kernel, len(addends)),
        out_shape=[struct((ch, HW), F32), struct((ch, HW), BF), struct((ch, 128), F32)],
        in_specs=[whole()] * (len(addends) + 4),
        out_specs=[whole()] * 3,
        compiler_params=params(),
        cost_estimate=cost(20 * ch * HW, 16 * ch * HW),
    )(*addends, hidden, stat, par, cot)


def product_kernel(n, w_ref, *refs):
    pieces, (bias_ref, out_ref) = refs[:n], refs[n:]
    acc = bias_ref[...]
    at = 0
    for x_ref in pieces:
        rows = x_ref.shape[0]
        acc = acc + dot(w_ref[:, at : at + rows], x_ref[...])
        at += rows
    out_ref[...] = acc.astype(BF)


def product(weight, pieces, bias, width=1024, name=None):
    rows, depth = weight.shape
    return pl.pallas_call(
        functools.partial(product_kernel, len(pieces)),
        grid=(HW // width,),
        out_shape=struct((rows, HW), BF),
        in_specs=[pl.BlockSpec((rows, depth), lambda p: (0, 0))]
        + [pl.BlockSpec((x.shape[0], width), lambda p: (0, p)) for x in pieces]
        + [pl.BlockSpec((rows, 1), lambda p: (0, 0))],
        out_specs=pl.BlockSpec((rows, width), lambda p: (0, p)),
        compiler_params=params(),
        cost_estimate=cost(2 * rows * depth * HW, (rows + depth) * HW * 2),
        name=name,
    )(weight, *pieces, bias)


def output_kernel(n, w_ref, *refs):
    pieces, (bias_ref, hidden_ref, out_ref) = refs[:n], refs[n:]
    acc = hidden_ref[...] + bias_ref[...]
    at = 0
    for x_ref in pieces:
        rows = x_ref.shape[0]
        acc = acc + dot(w_ref[:, at : at + rows], x_ref[...])
        at += rows
    out_ref[...] = acc.astype(BF)


def output_product(weight, pieces, bias, hidden, width=1024):
    rows, depth = weight.shape
    return pl.pallas_call(
        functools.partial(output_kernel, len(pieces)),
        grid=(HW // width,),
        out_shape=struct((rows, HW), BF),
        in_specs=[pl.BlockSpec((rows, depth), lambda p: (0, 0))]
        + [pl.BlockSpec((x.shape[0], width), lambda p: (0, p)) for x in pieces]
        + [
            pl.BlockSpec((rows, 1), lambda p: (0, 0)),
            pl.BlockSpec((rows, width), lambda p: (0, p)),
        ],
        out_specs=pl.BlockSpec((rows, width), lambda p: (0, p)),
        compiler_params=params(),
        cost_estimate=cost(2 * rows * depth * HW, (rows * 3 + depth) * HW * 2),
    )(weight, *pieces, bias, hidden)


def outer_kernel(n_left, n_right, *refs):
    lefts, rights = refs[:n_left], refs[n_left : n_left + n_right]
    out_ref, sums_ref = refs[n_left + n_right : n_left + n_right + 2]
    acc_ref, tot_ref = refs[n_left + n_right + 2 :]
    step = pl.program_id(0)

    @pl.when(step == 0)
    def _():
        acc_ref[...] = jnp.zeros_like(acc_ref)
        tot_ref[...] = jnp.zeros_like(tot_ref)

    row = 0
    for left in lefts:
        rows = left.shape[0]
        val = left[...]
        at = 0
        for right in rights:
            cols = right.shape[0]
            acc_ref[row : row + rows, at : at + cols] += dot_nt(val, right[...])
            at += cols
        tot_ref[row : row + rows, :] += jnp.sum(val.astype(F32), axis=1, keepdims=True)
        row += rows

    @pl.when(step == pl.num_programs(0) - 1)
    def _():
        out_ref[...] = acc_ref[...].astype(BF)
        sums_ref[...] = tot_ref[...]


def outer(lefts, rights, width=1024, name=None):
    rows, cols = sum(a.shape[0] for a in lefts), sum(a.shape[0] for a in rights)
    fixed = lambda p: (0, 0)
    return pl.pallas_call(
        functools.partial(outer_kernel, len(lefts), len(rights)),
        grid=(HW // width,),
        out_shape=[struct((rows, cols), BF), struct((rows, 128), F32)],
        in_specs=[pl.BlockSpec((a.shape[0], width), lambda p: (0, p)) for a in (*lefts, *rights)],
        out_specs=[pl.BlockSpec((rows, cols), fixed), pl.BlockSpec((rows, 128), fixed)],
        scratch_shapes=[pltpu.VMEM((rows, cols), F32), pltpu.VMEM((rows, 128), F32)],
        compiler_params=params(),
        cost_estimate=cost(2 * rows * cols * HW, (rows + cols) * HW * 2),
        name=name,
    )(*lefts, *rights)


def key_chunks(width):
    return [(c, width, False) for c in range(0, HW, width)] + [(0, CTXP, True)]


def attention_kernel(
    lim_ref, q_ref, k_ref, v_ref, kc_ref, vc_ref, g_ref,
    o_ref, dq_ref, dk_ref, dv_ref, dkc_ref, dvc_ref,
    kt, vt, s_sc, p_sc, dk_acc, dv_acc, *, chunk,
):
    step, last = pl.program_id(1), pl.num_programs(1) - 1
    width = q_ref.shape[-1]

    @pl.when(step == 0)
    def _():
        kt[:HW, :] = k_ref[0, 0].astype(F32).T.astype(BF)
        kt[HW:, :] = kc_ref[0, 0].astype(F32).T.astype(BF)
        vt[:HW, :] = v_ref[0, 0].astype(F32).T.astype(BF)
        vt[HW:, :] = vc_ref[0, 0].astype(F32).T.astype(BF)
        dk_acc[...] = jnp.zeros_like(dk_acc)
        dv_acc[...] = jnp.zeros_like(dv_acc)

    scale = HEAD_DIM ** (-0.5)
    q = (q_ref[0, 0].astype(F32) * scale).astype(BF)
    limit = lim_ref[0]
    top = jnp.full((8, width), -jnp.inf, F32)
    for c, w, masked in key_chunks(chunk):
        at = slice(c + HW, c + HW + w) if masked else slice(c, c + w)
        scores = dot(kt[at, :], q)
        if masked:
            key = lax.broadcasted_iota(jnp.int32, (w, width), 0)
            scores = jnp.where(key < limit, scores, NEG_FILL)
        s_sc[at, :] = scores
        top = jnp.maximum(top, jnp.max(scores.reshape(w // 8, 8, width), axis=0))
    row_top = jnp.max(top, axis=0, keepdims=True)
    total = jnp.zeros((8, width), F32)
    mixed = jnp.zeros((HEAD_DIM, width), F32)
    for c, w, masked in key_chunks(chunk):
        at = slice(c + HW, c + HW + w) if masked else slice(c, c + w)
        vals = vc_ref[0, 0, :, c : c + w] if masked else v_ref[0, 0, :, c : c + w]
        raised = jnp.exp(s_sc[at, :] - row_top)
        total = total + jnp.sum(raised.reshape(w // 8, 8, width), axis=0)
        low = raised.astype(BF)
        p_sc[at, :] = low
        mixed = mixed + dot(vals, low)
    inverse = 1.0 / jnp.sum(total, axis=0, keepdims=True)
    mixed = mixed * inverse
    o_ref[0] = mixed.astype(BF)
    grad = g_ref[0].astype(F32)
    delta = jnp.sum(grad * mixed, axis=0, keepdims=True) * inverse
    grad_low = (grad * inverse).astype(BF)
    dq = jnp.zeros((HEAD_DIM, width), F32)
    for c, w, masked in key_chunks(chunk):
        at = slice(c + HW, c + HW + w) if masked else slice(c, c + w)
        keys = kc_ref[0, 0, :, c : c + w] if masked else k_ref[0, 0, :, c : c + w]
        probs = p_sc[at, :]
        slope = (dot(vt[at, :], grad_low) - delta).astype(BF) * probs
        dq = dq + dot(keys, slope)
        dk_acc[:, at] += dot_nt(q, slope)
        dv_acc[:, at] += dot_nt(grad_low, probs)
    dq_ref[0] = (dq * scale).astype(BF)

    @pl.when(step == last)
    def _():
        dk_ref[0] = dk_acc[:, :HW].astype(BF)
        dv_ref[0] = dv_acc[:, :HW].astype(BF)
        dkc_ref[0] = dk_acc[:, HW:].astype(BF)
        dvc_ref[0] = dv_acc[:, HW:].astype(BF)


def attention(limit, qkv, ctx_kv, grads, width=1024, chunk=512):
    heads = qkv.shape[1]
    keys = HW + CTXP

    def part(t, w, moving):
        return pl.BlockSpec(
            (1, 1, HEAD_DIM, w), (lambda h, i: (t, h, 0, i)) if moving else (lambda h, i: (t, h, 0, 0))
        )

    def row(w, moving):
        return pl.BlockSpec(
            (1, HEAD_DIM, w), (lambda h, i: (h, 0, i)) if moving else (lambda h, i: (h, 0, 0))
        )

    big, small = struct((heads, HEAD_DIM, HW), BF), struct((heads, HEAD_DIM, CTXP), BF)
    return pl.pallas_call(
        functools.partial(attention_kernel, chunk=chunk),
        grid=(heads, HW // width),
        in_specs=[
            pl.BlockSpec(memory_space=pltpu.SMEM),
            part(0, width, True),
            part(1, HW, False),
            part(2, HW, False),
            part(0, CTXP, False),
            part(1, CTXP, False),
            row(width, True),
        ],
        out_specs=[
            row(width, True),
            row(width, True),
            row(HW, False),
            row(HW, False),
            row(CTXP, False),
            row(CTXP, False),
        ],
        out_shape=[big, big, big, big, small, small],
        scratch_shapes=[
            pltpu.VMEM((keys, HEAD_DIM), BF),
            pltpu.VMEM((keys, HEAD_DIM), BF),
            pltpu.VMEM((keys, width), F32),
            pltpu.VMEM((keys, width), BF),
            pltpu.VMEM((HEAD_DIM, keys), F32),
            pltpu.VMEM((HEAD_DIM, keys), F32),
        ],
        compiler_params=params(dimension_semantics=("arbitrary", "arbitrary")),
        cost_estimate=cost(
            24 * heads * HW * keys * HEAD_DIM, heads * HEAD_DIM * 8 * HW * 2, heads * HW * keys
        ),
        name="attention",
    )(limit, qkv, qkv, qkv, ctx_kv, ctx_kv, grads)


class Alone:
    def __init__(self, mesh):
        self.size = mesh.shape["tensor"]

    def move(self, x):
        return x

    def gather(self, x):
        return (lax.all_gather(x, "tensor", axis=0, tiled=True),)

    def scatter(self, x):
        return (lax.psum_scatter(x, "tensor", scatter_dimension=0, tiled=True),)

    def arrange(self, x, axis):
        return x

    def restore(self, x, axis):
        return x

    def turn(self, w):
        return lax.all_to_all(w, "tensor", split_axis=2, concat_axis=0, tiled=True)


class Paired:
    def __init__(self, mesh):
        dp = mesh.shape["dp"]
        self.near = [(i, i ^ 1) for i in range(dp)]
        self.far = [
            ((2 * k + core) * 2 + t, (2 * k + t) * 2 + core)
            for k in range(dp // 2)
            for core in range(2)
            for t in range(2)
        ]

    def half(self):
        return lax.axis_index("dp") % 2

    def move(self, x):
        return lax.ppermute(x, ("dp", "tensor"), self.far)

    def trade(self, x):
        return lax.ppermute(x, "dp", self.near)

    def gather(self, x):
        return (x, self.trade(x))

    def scatter(self, x):
        rows = x.shape[0] // 2
        return (x[:rows], self.trade(x[rows:]))

    def arrange(self, x, axis):
        size = x.shape[axis] // 2
        own = lax.dynamic_slice_in_dim(x, self.half() * size, size, axis)
        other = lax.dynamic_slice_in_dim(x, (1 - self.half()) * size, size, axis)
        return jnp.concatenate([own, other], axis)

    def restore(self, x, axis):
        size = x.shape[axis] // 2
        low = lax.slice_in_dim(x, 0, size, axis=axis)
        high = lax.slice_in_dim(x, size, 2 * size, axis=axis)
        return jnp.where(lax.axis_index("tensor") == 0, x, jnp.concatenate([high, low], axis))

    def turn(self, w):
        size = w.shape[2] // 2
        own = lax.dynamic_slice_in_dim(w, self.half() * size, size, 2)
        other = lax.dynamic_slice_in_dim(w, (1 - self.half()) * size, size, 2)
        return jnp.concatenate([own, self.trade(other)], 0)


def after(first, *later):
    held = lax.optimization_barrier((first, *later))
    return held[1:] if len(later) > 1 else held[1]


def local(plan, features, cotangent, embedding, context, lengths, norm1_gain, norm1_bias,
    conv1_weight, conv1_bias, emb_weight, emb_bias, norm2_gain, norm2_bias, conv2_weight,
    conv2_bias, norm3_gain, norm3_bias, qkv_weight, qkv_bias, context_weight, context_bias,
    out_weight, out_bias,
):
    ch, images, pixels = features.shape
    heads = ch // HEAD_DIM
    features = plan.move(features.reshape(ch, pixels))
    w1 = plan.move(conv1_weight)

    emb_act = jax.nn.silu(embedding.astype(F32)).astype(BF)
    scale_shift = (
        jnp.einsum("ie,teo->to", emb_act, emb_weight, preferred_element_type=F32) + emb_bias
    )
    ctx_kv = (
        jnp.einsum("toe,ne->ton", context_weight, context[0], preferred_element_type=F32)
        + context_bias[:, :, None]
    ).astype(BF)
    ctx_kv = jnp.pad(ctx_kv, ((0, 0), (0, 0), (0, CTXP - CTX)))
    length_row = jnp.broadcast_to(lengths.astype(F32)[:, None], (1, ch))
    vectors = jnp.concatenate(
        [
            jnp.stack([norm1_gain, norm1_bias, conv1_bias, norm2_gain, norm2_bias]),
            scale_shift,
            jnp.stack([conv2_bias, norm3_gain, norm3_bias, out_bias]),
            qkv_bias,
            length_row,
        ]
    )
    vectors = plan.move(vectors)
    w2 = plan.move(after(features, conv2_weight))
    cot = plan.move(after(w1, cotangent.reshape(ch, pixels)))
    w_out = plan.move(after(w1, out_weight))
    w_qkv = plan.move(after(w1, qkv_weight))
    ctx_kv = plan.move(after(w1, ctx_kv))

    length = vectors[14, :1].astype(jnp.int32)
    par = jnp.pad(vectors[:14].T, ((0, 0), (0, 2)))
    par_one, par_two, par_three = par[:, 0:2], par[:, 2:7], par[:, 7:10]
    bias_out, bias_qkv = par[:, 10:11], vectors[11:14].reshape(3 * ch, 1)

    def conv_weight(w):
        return plan.arrange(w.reshape(ch, 9, C), 2).reshape(ch, 9 * C)

    def turned_weight(w):
        return plan.turn(w.reshape(ch, 9, C))[:, ::-1].transpose(2, 1, 0).reshape(ch, 9 * C)

    act_one, stat_one = first_activation(features, par_one)
    full_one = plan.gather(act_one)
    conv_one, act_two, stat_two = conv_call(
        conv_one_kernel, conv_weight(w1), full_one, (par_two,),
        [struct((ch, HW), F32), struct((ch, HW), BF), struct((ch, 128), F32)], [], "conv_one",
    )
    full_two = plan.gather(act_two)
    hidden, normed, stat_three = conv_call(
        conv_two_kernel, conv_weight(w2), full_two, (par_three, features),
        [struct((ch, HW), F32), struct((ch, HW), BF), struct((ch, 128), F32)], [], "conv_two",
    )
    full_three = plan.gather(normed)
    zeros = jnp.zeros((C, 1), F32)
    grad_heads = product(plan.arrange(w_out, 1).T, (cot,), zeros, name="grad_heads")
    grad_heads = sum(a.astype(F32) for a in plan.scatter(grad_heads)).astype(BF)
    w_in = plan.arrange(w_qkv, 2)
    qkv = product(w_in.reshape(3 * ch, C), full_three, bias_qkv, name="qkv")
    mixed, dq, dk, dv, dkc, dvc = attention(
        4 + length,
        qkv.reshape(3, heads, HEAD_DIM, HW),
        ctx_kv.reshape(2, heads, HEAD_DIM, CTXP),
        grad_heads.reshape(heads, HEAD_DIM, HW),
    )

    flat = lambda a: a.reshape(ch, HW)
    dq, dk, dv = flat(dq), flat(dk), flat(dv)
    grad_normed = product(w_in.reshape(3 * ch, C).T, (dq, dk, dv), zeros, name="grad_normed")
    addends = plan.scatter(grad_normed)
    full_heads = plan.gather(flat(mixed))
    dw_qkv, db_qkv = outer((dq, dk, dv), full_three, name="qkv_grad")
    grad_hidden, grad_two, sums_three = norm_three_back(addends, hidden, stat_three, par_three, cot)
    full_grad_two = plan.gather(grad_two)
    dw_two = conv_weight_grad(grad_two, full_two, "conv_two_weight_grad")
    output = output_product(plan.arrange(w_out, 1), full_heads, bias_out, hidden)
    output = plan.move(output)
    dw_out, _ = outer((cot,), full_heads, name="out_grad")
    grad_one, sums_two = conv_call(
        conv_two_back_kernel, turned_weight(w2), full_grad_two, (par_two, conv_one, stat_two),
        [struct((ch, HW), BF), struct((ch, 128), F32)], [pltpu.VMEM((ch, HW), F32)], "conv_two_back",
    )
    full_grad_one = plan.gather(grad_one)
    dw_one = conv_weight_grad(grad_one, full_one, "conv_one_weight_grad")
    moved = isinstance(plan, Paired)
    input_grad, sums_one = conv_call(
        conv_one_back_kernel, turned_weight(w1), full_grad_one,
        (par_one, features, stat_one, grad_hidden),
        [struct((ch, HW), BF if moved else F32), struct((ch, 128), F32)],
        [pltpu.VMEM((ch, HW), F32)], "conv_one_back",
    )
    input_grad = plan.move(input_grad).astype(F32)

    grad_ctx = jnp.stack([flat_ctx.reshape(ch, CTXP) for flat_ctx in (dkc, dvc)])
    grad_ctx = plan.move(grad_ctx)[:, :, :CTX]
    small = jnp.concatenate(
        [
            sums_three[:, :4].T,
            db_qkv[:, 0].reshape(3, ch),
            sums_two[:, :5].T,
        ]
    )
    small = plan.move(small)
    last = plan.move(sums_one[:, :2].T)
    grad_mod = small[9:11].astype(BF)
    dw_emb = emb_act.astype(F32).reshape(1, -1, 1) * grad_mod.astype(F32)[:, None, :]
    dw_ctx = jnp.einsum("ton,ne->toe", grad_ctx, context[0], preferred_element_type=F32)
    db_ctx = jnp.sum(grad_ctx.astype(F32), axis=2)
    moved_grads = [plan.move(a) for a in (dw_out, dw_qkv.reshape(3, ch, C), dw_two)]
    dw_one = plan.move(dw_one)
    early = lax.psum((dw_ctx.astype(BF), *moved_grads, dw_emb.astype(BF)), "dp")
    rest = jnp.concatenate([small[:7], small[7:9], grad_mod.astype(F32), small[11:12], db_ctx, last])
    late = lax.psum((after(early[-1], dw_one), rest), "dp")
    dw_ctx, dw_out, dw_qkv, dw_two, dw_emb = early
    dw_one, rest = late

    def restored(a, axis):
        return plan.restore(a, axis).astype(F32)

    def conv_grad(a):
        return restored(a.reshape(ch, 9, C), 2).reshape(ch, 9 * C)

    return (
        output.reshape(ch, images, pixels),
        input_grad.reshape(ch, images, pixels),
        rest[14],
        rest[15],
        conv_grad(dw_one),
        rest[11],
        dw_emb.astype(F32),
        rest[9:11],
        rest[7],
        rest[8],
        conv_grad(dw_two),
        rest[2],
        rest[0],
        rest[1],
        restored(dw_qkv, 2),
        rest[4:7],
        dw_ctx.astype(F32),
        rest[12:14],
        restored(dw_out, 1),
        rest[3],
    )


def solution(mesh):
    paired = mesh.shape["tensor"] == 2 and mesh.shape["dp"] % 2 == 0
    plan = Paired(mesh) if paired else Alone(mesh)
    placed = (
        P("tensor", "dp", None),
        P("tensor", "dp", None),
        P("dp", None),
        P("dp", None, None),
        P("dp"),
        P("tensor"),
        P("tensor"),
        P("tensor", None),
        P("tensor"),
        P(None, None, "tensor"),
        P(None, "tensor"),
        P("tensor"),
        P("tensor"),
        P("tensor", None),
        P("tensor"),
        P("tensor"),
        P("tensor"),
        P(None, "tensor", None),
        P(None, "tensor"),
        P(None, "tensor", None),
        P(None, "tensor"),
        P("tensor", None),
        P("tensor"),
    )
    return jax.shard_map(
        functools.partial(local, plan),
        mesh=mesh,
        in_specs=placed,
        out_specs=(
            P("tensor", "dp", None),
            P("tensor", "dp", None),
            P("tensor"),
            P("tensor"),
            P("tensor", None),
            P("tensor"),
            P(None, None, "tensor"),
            P(None, "tensor"),
            P("tensor"),
            P("tensor"),
            P("tensor", None),
            P("tensor"),
            P("tensor"),
            P("tensor"),
            P(None, "tensor", None),
            P(None, "tensor"),
            P(None, "tensor", None),
            P(None, "tensor"),
            P("tensor", None),
            P("tensor"),
        ),
        check_vma=False,
    )
```

time: 2270 us -> 970 us (0.43)
  matrix products: 1190 us -> 6.37 us
  Pallas kernels: 0 us -> 459 us
  other arithmetic: 460 us -> 34.3 us
  waiting for transfers between devices: 364 us -> 96.1 us
  starting transfers between devices: 0.78 us -> 201 us
  local copies, waits for them, and re-layouts: 189 us -> 80.7 us
  blocking collectives: 30.4 us -> 60.7 us
    dot_general x119 -> x3, matrix products: 1190 us -> 6.37 us  [the longest x1 3.64 us: local(): jnp.einsum('ton,ne->toe', grad_ctx, context[0], preferred_element_type=F32)]
    pallas_call x0 -> x15, Pallas kernels: none -> 459 us  [the longest x1 267 us: attention(): pl.pallas_call(functools.partial(attention_kernel, chunk=chunk), grid=(he...]
    convert_element_type x28 -> x9, other arithmetic: 267 us -> 23.9 us  [the longest x3 11.2 us: restored(): return plan.restore(a, axis).astype(F32)]
    ppermute x0 -> x27, starting transfers between devices: none -> 201 us  [the longest x17 170 us: move(): return lax.ppermute(x, ('dp', 'tensor'), self.far)]
    reduce_sum x38 -> x1, other arithmetic: 183 us -> 1.02 us  [local(): db_ctx = jnp.sum(grad_ctx.astype(F32), axis=2)]
    all_gather x4 -> x0, waiting for transfers between devices: 150 us -> none  [the longest x1 51.7 us: local(): full_three = lax.all_gather(normed, 'tensor', axis=0, tiled=True)]
    reduce_scatter x4 -> x0, waiting for transfers between devices: 93 us -> none  [the longest x2 47.8 us: conv_input_grad(): lax.psum_scatter(result.astype(jnp.bfloat16), 'tensor', scatter_dimension...]
    slice x12 -> x17, local copies, waits for them, and re-layouts: 71.7 us -> 17.4 us  [the longest x2 7.16 us: scatter(): return (x[:rows], self.trade(x[rows:]))]
  transfers between devices with their start and end apart: 9 -> 29, of which waited for: 7 -> 3; matrix products, arithmetic and copies ran while one was open for 13% -> 9% of each run, Pallas kernels for 0% -> 18%
where the time goes in v2:
time: 970 us; the launch traced here: 954 us
  Pallas kernels  459 us (47%)
  starting transfers between devices  201 us (21%)
  waiting for transfers between devices  96.1 us (10%)
  local copies, waits for them, and re-layouts  80.7 us (8%)
  blocking collectives  60.7 us (6%)
  other arithmetic  34.3 us (4%)
  between operations  16.3 us (2%)
    pallas_call x1, Pallas kernels, attention(): pl.pallas_call(functools.partial(attention_kernel, chunk=chunk), grid=(he...  267 us
    ppermute x17, starting transfers between devices, move(): return lax.ppermute(x, ('dp', 'tensor'), self.far)  170 us
    pallas_call x4, Pallas kernels, conv_call(): pl.pallas_call(functools.partial(kernel, len(pieces)), out_shape=outs, in...  97 us
    psum x1, blocking collectives, local(): late = lax.psum((after(early[-1], dw_one), rest), 'dp')  60.7 us
    psum x1, waiting for transfers between devices, local(): late = lax.psum((after(early[-1], dw_one), rest), 'dp')  48.7 us
    psum x1, waiting for transfers between devices, local(): early = lax.psum((dw_ctx.astype(BF), *moved_grads, dw_emb.astype(BF)), 'dp')  41.7 us
    pallas_call x2, Pallas kernels, conv_weight_grad(): pl.pallas_call(functools.partial(weight_grad_kernel, len(pieces)), out_sh...  32.1 us
    ppermute x10, starting transfers between devices, trade(): return lax.ppermute(x, 'dp', self.near)  30.7 us
  transfers between devices with their start and end apart: 29, of which 3 were waited for; matrix products, arithmetic and copies ran while one was open for 9% of the time, Pallas kernels for 18%

profile of v2, /device:TPU:5, one launch (start us, length us, event | category | flops | bytes accessed | tf_op | source)
XLA Modules:
  0.0 953.9 jit_solution(535531602237102849)
XLA Ops:
  7.4 17.3 %collective-permute-start.4 = (bf16[256,4096]{1,0:T(8,128)(2,1)}, bf16[256,4096]{1,0:T(8,128)(2,1)}, u32[]{:S(2)}, u32[]{:S(2)}) collective-permute-start(bf16[256,4096]{1,0:T(8,128)(2,1)} %bitcast.124), channel_id=1, source_target_pairs={{0,0},{1,2},{2,1},{3,3},{4,4},{5,6},{6,5},{7,7},{8,8},{9,10},{10,9... | collective-permute-start | bytes 6291464 | tf_op jit(solution)/shard_map/ppermute | solution.py:596
  24.6 4.3 copy.99
  28.9 19.2 %collective-permute-start = (bf16[256,4608]{0,1:T(8,128)(2,1)}, bf16[256,4608]{0,1:T(8,128)(2,1)}, u32[]{:S(2)}, u32[]{:S(2)}) collective-permute-start(bf16[256,4608]{0,1:T(8,128)(2,1)} %copy.99), channel_id=1, source_target_pairs={{0,0},{1,2},{2,1},{3,3},{4,4},{5,6},{6,5},{7,7},{8,8},{9,10},{10,9... | collective-permute-start | bytes 7077896 | tf_op jit(solution)/shard_map/ppermute | solution.py:596
  51.4 8.2 shard_map.374
  59.6 12.5 %collective-permute-start.6 = (bf16[256,4096]{1,0:T(8,128)(2,1)}, bf16[256,4096]{1,0:T(8,128)(2,1)}, u32[]{:S(2)}, u32[]{:S(2)}) collective-permute-start(bf16[256,4096]{1,0:T(8,128)(2,1)} %get-tuple-element.53.refs_0_), channel_id=1, source_target_pairs={{0,2},{2,0},{4,6},{6,4},{8,10},{10,8},{12,14},{14,12},{16,18},{18,... | collective-permute-start | bytes 6291464 | tf_op jit(solution)/shard_map/ppermute | solution.py:599
  72.9 4.3 copy.101
  77.1 19.2 %collective-permute-start.5 = (bf16[256,4608]{0,1:T(8,128)(2,1)}, bf16[256,4608]{0,1:T(8,128)(2,1)}, u32[]{:S(2)}, u32[]{:S(2)}) collective-permute-start(bf16[256,4608]{0,1:T(8,128)(2,1)} %copy.101), channel_id=1, source_target_pairs={{0,0},{1,2},{2,1},{3,3},{4,4},{5,6},{6,5},{7,7},{8,8},{9,10},{10,9... | collective-permute-start | bytes 7077896 | tf_op jit(solution)/shard_map/ppermute | solution.py:596
  96.3 17.1 %collective-permute-start.10 = (bf16[256,4096]{1,0:T(8,128)(2,1)}, bf16[256,4096]{1,0:T(8,128)(2,1)}, u32[]{:S(2)}, u32[]{:S(2)}) collective-permute-start(bf16[256,4096]{1,0:T(8,128)(2,1)} %bitcast.24), channel_id=1, source_target_pairs={{0,0},{1,2},{2,1},{3,3},{4,4},{5,6},{6,5},{7,7},{8,8},{9,10},{10,9... | collective-permute-start | bytes 6291464 | tf_op jit(solution)/shard_map/ppermute | solution.py:596
  113.4 1.8 constant_dynamic-slice_fusion.1
  116.6 2.6 copy.102.w_ref
  119.2 22.8 %conv_one.1 = (f32[256,4096]{1,0:T(8,128)}, bf16[256,4096]{1,0:T(8,128)(2,1)}, f32[256,128]{1,0:T(8,128)}) custom-call(bf16[256,4608]{1,0:T(8,128)(2,1)} %copy.102.w_ref, bf16[256,4096]{1,0:T(8,128)(2,1)} %get-tuple-element.53.refs_0_, bf16[256,4096]{1,0:T(8,128)(2,1)} %collective-permute-done.6.refs_1_, f32[256,5]{1,0:T(8,128)} %slice.166.refs_2_), custom_call_target="tpu_custom_call" | custom-call | flops 9663676416 | bytes 6558720 | tf_op jit(solution)/shard_map/conv_one/pallas_call | solution.py:159
  143.5 7.4 collective-permute-start.3
  153.2 5.1 grad_heads.1
  158.3 3.1 slice.170
  161.5 2.8 constant_dynamic-slice_fusion.3
  164.3 1.8 pad_maximum_fusion
  166.2 2.8 copy.103.w_ref
  169.0 22.9 %conv_two.1 = (f32[256,4096]{1,0:T(8,128)}, bf16[256,4096]{1,0:T(8,128)(2,1)}, f32[256,128]{1,0:T(8,128)}) custom-call(bf16[256,4608]{1,0:T(8,128)(2,1)} %copy.103.w_ref, bf16[256,4096]{1,0:T(8,128)(2,1)} %get-tuple-element.54.refs_0_, bf16[256,4096]{1,0:T(8,128)(2,1)} %collective-permute-done.7.refs_1_, f32[256,3]{1,0:T(8,128)} %slice.167.refs_2_.refs_4_, ...), custom_call_target="tpu_custom_call" | custom-call | flops 9663676416 | bytes 8653824 | tf_op jit(solution)/shard_map/conv_two/pallas_call | solution.py:159
  192.4 2.4 fusion
  201.3 4.3 add_convert_fusion
  205.6 7.7 qkv.1
  213.4 267.3 %attention.1 = (bf16[4,64,4096]{2,1,0:T(8,128)(2,1)}, bf16[4,64,4096]{2,1,0:T(8,128)(2,1)}, bf16[4,64,4096]{2,1,0:T(8,128)(2,1)}, bf16[4,64,4096]{2,1,0:T(8,128)...) custom-call(s32[1]{0:T(128)} %bitcast.11.lim_ref, bf16[3,4,64,4096]{3,2,1,0:T(8,128)(2,1)} %bitcast.126, ...), custom_call_target="tpu_custom_call" | custom-call | flops 112742891520 | bytes 16777216 | tf_op jit(solution)/shard_map/attention/pallas_call | solution.py:521
  480.6 7.7 grad_normed.1
  488.3 4.0 fusion.11
  492.3 6.0 collective-permute-start.16
  498.4 5.6 collective-permute-done.16.refs_1_
  504.0 14.1 %shard_map.376 = (f32[256,4096]{1,0:T(8,128)}, bf16[256,4096]{1,0:T(8,128)(2,1)}, f32[256,128]{1,0:T(8,128)}) custom-call(bf16[256,4096]{1,0:T(8,128)(2,1)} %get-tuple-element.146.refs_0_, bf16[256,4096]{1,0:T(8,128)(2,1)} %collective-permute-done.16.refs_1_, f32[256,4096]{1,0:T(8,128)} %get-tuple-element.59.refs_3_.refs_2_, ...), custom_call_target="tpu_custom_call" | custom-call | flops 20971520 | bytes 16777216 | tf_op jit(solution)/shard_map/pallas_call | solution.py:326
  518.5 1.8 pad_maximum_fusion.3
  520.5 2.4 copy.109
  522.9 4.3 copy.111.w_ref
  527.2 8.1 qkv_grad.1
  536.8 16.1 %conv_two_weight_grad.1 = bf16[256,4608]{1,0:T(8,128)(2,1)} custom-call(bf16[256,4096]{1,0:T(8,128)(2,1)} %get-tuple-element.64.refs_0_.grad_ref, bf16[256,4096]{1,0:T(8,128)(2,1)} %get-tuple-element.54.refs_0_, bf16[256,4096]{1,0:T(8,128)(2,1)} %collective-permute-done.7.refs_1_), custom_call_target="tpu_custom_call" | custom-call | flops 9663676416 | bytes 8650752 | tf_op jit(solution)/shard_map/conv_two_weight_grad/pallas_call | solution.py:279
  552.8 19.3 %collective-permute-start.24 = (bf16[256,4608]{1,0:T(8,128)(2,1)}, bf16[256,4608]{1,0:T(8,128)(2,1)}, u32[]{:S(2)}, u32[]{:S(2)}) collective-permute-start(bf16[256,4608]{1,0:T(8,128)(2,1)} %conv_two_weight_grad.1), channel_id=1, source_target_pairs={{0,0},{1,2},{2,1},{3,3},{4,4},{5,6},{6,5},{7,7},{8,8},{9,10},{10,9... | collective-permute-start | bytes 7077896 | tf_op jit(solution)/shard_map/ppermute | solution.py:596
  572.1 26.4 %conv_two_back.1 = (bf16[256,4096]{1,0:T(8,128)(2,1)}, f32[256,128]{1,0:T(8,128)}) custom-call(bf16[256,4608]{1,0:T(8,128)(2,1)} %copy.111.w_ref, bf16[256,4096]{1,0:T(8,128)(2,1)} %get-tuple-element.64.refs_0_.grad_ref, bf16[256,4096]{1,0:T(8,128)(2,1)} %collective-permute-done.17.refs_1_, f32[256,5]{1,0:T(8,128)} %slice.166.refs_2_, ...), custom_call_target="tpu_custom_call" | custom-call | flops 9663676416 | bytes 10884096 | tf_op jit(solution)/shard_map/conv_two_back/pallas_call | solution.py:159
  598.6 16.0 %conv_one_weight_grad.1 = bf16[256,4608]{1,0:T(8,128)(2,1)} custom-call(bf16[256,4096]{1,0:T(8,128)(2,1)} %get-tuple-element.67.refs_0_.grad_ref, bf16[256,4096]{1,0:T(8,128)(2,1)} %get-tuple-element.53.refs_0_, bf16[256,4096]{1,0:T(8,128)(2,1)} %collective-permute-done.6.refs_1_), custom_call_target="tpu_custom_call" | custom-call | flops 9663676416 | bytes 8650752 | tf_op jit(solution)/shard_map/conv_one_weight_grad/pallas_call | solution.py:279
  614.7 19.3 %collective-permute-start.23 = (bf16[256,4608]{1,0:T(8,128)(2,1)}, bf16[256,4608]{1,0:T(8,128)(2,1)}, u32[]{:S(2)}, u32[]{:S(2)}) collective-permute-start(bf16[256,4608]{1,0:T(8,128)(2,1)} %conv_one_weight_grad.1), channel_id=1, source_target_pairs={{0,0},{1,2},{2,1},{3,3},{4,4},{5,6},{6,5},{7,7},{8,8},{9,10},{10,9... | collective-permute-start | bytes 7077896 | tf_op jit(solution)/shard_map/ppermute | solution.py:596
  634.8 11.1 %collective-permute-start.14 = (bf16[256,9,256]{0,2,1:T(8,128)(2,1)}, bf16[256,9,256]{0,2,1:T(8,128)(2,1)}, u32[]{:S(2)}, u32[]{:S(2)}) collective-permute-start(bf16[256,9,256]{0,2,1:T(8,128)(2,1)} %copy-done.5), channel_id=1, source_target_pairs={{0,2},{2,0},{4,6},{6,4},{8,10},{10,8},{12,14},{14,12},{16,18},{18,... | collective-permute-start | bytes 3538952 | tf_op jit(solution)/shard_map/ppermute | solution.py:599
  649.6 4.5 collective-permute-start.21
  654.1 7.4 collective-permute-start.25
  663.2 2.4 copy.108
  665.6 4.3 copy.112.w_ref
  669.9 5.2 out_grad.1
  676.6 3.6 convolution_convert_fusion
  680.3 6.2 shard_map.375
  686.5 17.3 %collective-permute-start.13 = (bf16[256,4096]{1,0:T(8,128)(2,1)}, bf16[256,4096]{1,0:T(8,128)(2,1)}, u32[]{:S(2)}, u32[]{:S(2)}) collective-permute-start(bf16[256,4096]{1,0:T(8,128)(2,1)} %shard_map.375), channel_id=1, source_target_pairs={{0,0},{1,2},{2,1},{3,3},{4,4},{5,6},{6,5},{7,7},{8,8},{9,10},{10,9... | collective-permute-start | bytes 6291464 | tf_op jit(solution)/shard_map/ppermute | solution.py:596
  703.8 41.7 %all-reduce.5.cloned.1.call-done = bf16[2,2048,256]{2,1,0:T(8,128)(2,1)} async-done(((bf16[2,2048,256]{2,1,0:T(8,128)(2,1)}), bf16[2,2048,256]{2,1,0:T(8,128)(2,1)}) %all-reduce.5.cloned.1.call-update) | async-done | bytes 2097168 | tf_op jit(solution)/shard_map/psum | solution.py:747
  746.2 24.9 %conv_one_back.1 = (bf16[256,4096]{1,0:T(8,128)(2,1)}, f32[256,128]{1,0:T(8,128)}) custom-call(bf16[256,4608]{1,0:T(8,128)(2,1)} %copy.112.w_ref, bf16[256,4096]{1,0:T(8,128)(2,1)} %get-tuple-element.67.refs_0_.grad_ref, bf16[256,4096]{1,0:T(8,128)(2,1)} %collective-permute-done.18.refs_1_, f32[256,2]{1,0:T(8,128)} %bitcast.93, ...), custom_call_target="tpu_custom_call" | custom-call | flops 9663676416 | bytes 12978176 | tf_op jit(solution)/shard_map/conv_one_back/pallas_call | solution.py:159
  771.0 17.1 %collective-permute-start.19 = (bf16[256,4096]{1,0:T(8,128)(2,1)}, bf16[256,4096]{1,0:T(8,128)(2,1)}, u32[]{:S(2)}, u32[]{:S(2)}) collective-permute-start(bf16[256,4096]{1,0:T(8,128)(2,1)} %get-tuple-element.70), channel_id=1, source_target_pairs={{0,0},{1,2},{2,1},{3,3},{4,4},{5,6},{6,5},{7,7},{8,8},{9,10},{10,9... | collective-permute-start | bytes 6291464 | tf_op jit(solution)/shard_map/ppermute | solution.py:596
  790.8 4.0 convert_element_type.78
  794.9 60.7 %psum.49 = f32[16,256]{1,0:T(8,128)S(1)} all-reduce(f32[16,256]{1,0:T(8,128)S(1)} %concatenate.53), channel_id=1, replica_groups=mesh['dp'=16,'tensor'=2] {'dp'}, use_global_device_ids=true, to_apply=%region_1.2 | all-reduce | flops 4096 | bytes 32768 | tf_op jit(solution)/shard_map/psum | solution.py:749
  857.4 2.1 bitcast_convert_fusion
  859.5 6.3 copy.122
  865.8 48.7 %all-reduce.7.cloned.1.call-done = (bf16[256,4608]{1,0:T(8,128)(2,1)}, bf16[256,4608]{1,0:T(8,128)(2,1)}, bf16[3,256,512]{2,1,0:T(8,128)(2,1)}, bf16[2,256,2048]{2,1,0:T(8,128)(2,1)}, bf16[256,512]{1,0:T(8,128)(2,1)}) async-done(((bf16[256,4608]{1,0:T(8,128)(2,1)}, bf16[256,4608]{1,0:T(8,128)(2,1)}, bf16[3,256,512]{2,1,0:T(8,128)(2,1)}, bf16[2,256,2048]{2,1,0:T(8,128)(2,1)}, bf16[256,512]{1,0:T(8,128)(2,1)}), ...) | async-done | bytes 7864336 | tf_op jit(solution)/shard_map/psum | solution.py:749
  914.5 1.8 fusion.15
  916.4 2.0 fusion.14
  918.4 2.5 convert_element_type.82
  921.0 2.8 copy.118
  924.2 2.5 copy.119
  926.7 2.8 copy.120
  929.9 2.5 copy.121
  932.5 2.0 fusion.4
  934.5 2.5 fusion.3
  937.0 6.7 select_convert_fusion
  943.7 3.1 copy.135
  (164 shorter events, 30.7 us)
Async XLA Ops:
  7.2 185.2 %copy-start = (bf16[1,260,2048]{2,1,0:T(8,128)(2,1)S(1)}, bf16[1,260,2048]{2,1,0:T(8,128)(2,1)}, u32[]{:S(2)}) copy-start(bf16[1,260,2048]{2,1,0:T(8,128)(2,1)} %param.26) | copy-start | bytes 3194884
  7.2 738.2 %all-reduce.5.cloned.1.call-start = ((), (), s32[]{:S(2)}) async-start(), calls=%async_computation | async-start | bytes 4194304 | tf_op jit(solution)/shard_map/psum | solution.py:747
  7.3 40.8 %copy-start.11 = (bf16[2,2048,256]{2,1,0:T(8,128)(2,1)S(1)}, bf16[2,2048,256]{2,1,0:T(8,128)(2,1)}, u32[]{:S(2)}) copy-start(bf16[2,2048,256]{2,1,0:T(8,128)(2,1)} %param.32) | copy-start | bytes 6291460
  7.3 40.8 %copy-start.19 = (bf16[1,2048]{1,0:T(2,128)(2,1)S(1)}, bf16[1,2048]{1,0:T(2,128)(2,1)}, u32[]{:S(2)}) copy-start(bf16[1,2048]{1,0:T(2,128)(2,1)} %param.25) | copy-start | bytes 12292
  7.3 41.8 %copy-start.22 = (f32[2,256]{1,0:T(2,128)S(1)}, f32[2,256]{1,0:T(2,128)}, u32[]{:S(2)}) copy-start(f32[2,256]{1,0:T(2,128)} %param.33) | copy-start | bytes 6148
  7.3 41.9 %copy-start.21 = (f32[3,256]{1,0:T(4,128)S(1)}, f32[3,256]{1,0:T(4,128)}, u32[]{:S(2)}) copy-start(f32[3,256]{1,0:T(4,128)} %param.41) | copy-start | bytes 9220
  7.3 41.9 %copy-start.23 = (f32[256]{0:T(256)S(1)}, f32[256]{0:T(256)}, u32[]{:S(2)}) copy-start(f32[256]{0:T(256)} %param.28) | copy-start | bytes 3076
  7.3 41.9 %copy-start.24 = (f32[256]{0:T(256)S(1)}, f32[256]{0:T(256)}, u32[]{:S(2)}) copy-start(f32[256]{0:T(256)} %param.29) | copy-start | bytes 3076
  7.3 41.9 %copy-start.25 = (f32[256]{0:T(256)S(1)}, f32[256]{0:T(256)}, u32[]{:S(2)}) copy-start(f32[256]{0:T(256)} %param.31) | copy-start | bytes 3076
  7.3 41.9 %copy-start.26 = (f32[256]{0:T(256)S(1)}, f32[256]{0:T(256)}, u32[]{:S(2)}) copy-start(f32[256]{0:T(256)} %param.34) | copy-start | bytes 3076
  7.3 41.9 %copy-start.27 = (f32[256]{0:T(256)S(1)}, f32[256]{0:T(256)}, u32[]{:S(2)}) copy-start(f32[256]{0:T(256)} %param.35) | copy-start | bytes 3076
  7.3 41.9 %copy-start.28 = (f32[256]{0:T(256)S(1)}, f32[256]{0:T(256)}, u32[]{:S(2)}) copy-start(f32[256]{0:T(256)} %param.37) | copy-start | bytes 3076
  7.4 41.9 %copy-start.29 = (f32[256]{0:T(256)S(1)}, f32[256]{0:T(256)}, u32[]{:S(2)}) copy-start(f32[256]{0:T(256)} %param.38) | copy-start | bytes 3076
  7.4 41.9 %copy-start.30 = (f32[256]{0:T(256)S(1)}, f32[256]{0:T(256)}, u32[]{:S(2)}) copy-start(f32[256]{0:T(256)} %param.39) | copy-start | bytes 3076
  7.4 41.9 %copy-start.31 = (f32[256]{0:T(256)S(1)}, f32[256]{0:T(256)}, u32[]{:S(2)}) copy-start(f32[256]{0:T(256)} %param.45) | copy-start | bytes 3076
  7.4 44.0 %collective-permute-start.4 = (bf16[256,4096]{1,0:T(8,128)(2,1)}, bf16[256,4096]{1,0:T(8,128)(2,1)}, u32[]{:S(2)}, u32[]{:S(2)}) collective-permute-start(bf16[256,4096]{1,0:T(8,128)(2,1)} %bitcast.124), channel_id=1, source_target_pairs={{0,0},{1,2},{2,1},{3,3},{4,4},{5,6},{6,5},{7,7},{8,8},{9,10},{10,9... | collective-permute-start | bytes 6291464 | tf_op jit(solution)/shard_map/ppermute | solution.py:596
  28.9 67.4 %collective-permute-start = (bf16[256,4608]{0,1:T(8,128)(2,1)}, bf16[256,4608]{0,1:T(8,128)(2,1)}, u32[]{:S(2)}, u32[]{:S(2)}) collective-permute-start(bf16[256,4608]{0,1:T(8,128)(2,1)} %copy.99), channel_id=1, source_target_pairs={{0,0},{1,2},{2,1},{3,3},{4,4},{5,6},{6,5},{7,7},{8,8},{9,10},{10,9... | collective-permute-start | bytes 7077896 | tf_op jit(solution)/shard_map/ppermute | solution.py:596
  49.4 0.7 collective-permute-start.2
  50.1 0.7 copy-start.12
  51.4 20.7 %copy-start.6 = (f32[256,14]{1,0:T(8,128)S(1)}, f32[256,14]{1,0:T(8,128)}, u32[]{:S(2)}) copy-start(f32[256,14]{1,0:T(8,128)} %slice_bitcast_fusion) | copy-start | bytes 43012
  59.6 59.6 %collective-permute-start.6 = (bf16[256,4096]{1,0:T(8,128)(2,1)}, bf16[256,4096]{1,0:T(8,128)(2,1)}, u32[]{:S(2)}, u32[]{:S(2)}) collective-permute-start(bf16[256,4096]{1,0:T(8,128)(2,1)} %get-tuple-element.53.refs_0_), channel_id=1, source_target_pairs={{0,2},{2,0},{4,6},{6,4},{8,10},{10,8},{12,14},{14,12},{16,18},{18,... | collective-permute-start | bytes 6291464 | tf_op jit(solution)/shard_map/ppermute | solution.py:599
  77.1 84.3 %collective-permute-start.5 = (bf16[256,4608]{0,1:T(8,128)(2,1)}, bf16[256,4608]{0,1:T(8,128)(2,1)}, u32[]{:S(2)}, u32[]{:S(2)}) collective-permute-start(bf16[256,4608]{0,1:T(8,128)(2,1)} %copy.101), channel_id=1, source_target_pairs={{0,0},{1,2},{2,1},{3,3},{4,4},{5,6},{6,5},{7,7},{8,8},{9,10},{10,9... | collective-permute-start | bytes 7077896 | tf_op jit(solution)/shard_map/ppermute | solution.py:596
  96.3 56.2 %collective-permute-start.10 = (bf16[256,4096]{1,0:T(8,128)(2,1)}, bf16[256,4096]{1,0:T(8,128)(2,1)}, u32[]{:S(2)}, u32[]{:S(2)}) collective-permute-start(bf16[256,4096]{1,0:T(8,128)(2,1)} %bitcast.24), channel_id=1, source_target_pairs={{0,0},{1,2},{2,1},{3,3},{4,4},{5,6},{6,5},{7,7},{8,8},{9,10},{10,9... | collective-permute-start | bytes 6291464 | tf_op jit(solution)/shard_map/ppermute | solution.py:596
  115.2 1.1 copy-start.1
  115.2 1.4 copy-start.5
  119.2 22.8 %copy-start.32 = (bf16[256,512]{1,0:T(8,128)(2,1)S(1)}, bf16[256,512]{1,0:T(8,128)(2,1)}, u32[]{:S(2)}) copy-start(bf16[256,512]{1,0:T(8,128)(2,1)} %param.44) | copy-start | bytes 786436
  119.2 23.5 %copy-start.7 = (f32[256,14]{1,0:T(8,128)S(1)}, f32[256,14]{1,0:T(8,128)}, u32[]{:S(2)}) copy-start(f32[256,14]{1,0:T(8,128)} %slice_bitcast_fusion) | copy-start | bytes 43012
  142.0 27.0 %collective-permute-start.7 = (bf16[256,4096]{1,0:T(8,128)(2,1)}, bf16[256,4096]{1,0:T(8,128)(2,1)}, u32[]{:S(2)}, u32[]{:S(2)}) collective-permute-start(bf16[256,4096]{1,0:T(8,128)(2,1)} %get-tuple-element.54.refs_0_), channel_id=1, source_target_pairs={{0,2},{2,0},{4,6},{6,4},{8,10},{10,8},{12,14},{14,12},{16,18},{18,... | collective-permute-start | bytes 6291464 | tf_op jit(solution)/shard_map/ppermute | solution.py:599
  142.0 8.9 collective-permute-start.1
  143.5 55.4 %collective-permute-start.3 = (bf16[3,256,512]{2,1,0:T(8,128)(2,1)}, bf16[3,256,512]{2,1,0:T(8,128)(2,1)}, u32[]{:S(2)}, u32[]{:S(2)}) collective-permute-start(bf16[3,256,512]{2,1,0:T(8,128)(2,1)} %param.40), channel_id=1, source_target_pairs={{0,0},{1,2},{2,1},{3,3},{4,4},{5,6},{6,5},{7,7},{8,8},{9,10},{10,9... | collective-permute-start | bytes 2359304 | tf_op jit(solution)/shard_map/ppermute | solution.py:596
  161.5 39.9 %collective-permute-start.11 = (bf16[256,4096]{1,0:T(8,128)(2,1)}, bf16[256,4096]{1,0:T(8,128)(2,1)}, u32[]{:S(2)}, u32[]{:S(2)}) collective-permute-start(bf16[256,4096]{1,0:T(8,128)(2,1)} %slice.170), channel_id=1, source_target_pairs={{0,2},{2,0},{4,6},{6,4},{8,10},{10,8},{12,14},{14,12},{16,18},{18,... | collective-permute-start | bytes 6291464 | tf_op jit(solution)/shard_map/ppermute | solution.py:599
  164.3 1.9 copy-start.3
  169.0 23.4 %copy-start.33 = (f32[2,256]{1,0:T(2,128)S(1)}, f32[2,256]{1,0:T(2,128)}, u32[]{:S(2)}) copy-start(f32[2,256]{1,0:T(2,128)} %param.43) | copy-start | bytes 6148
  191.9 3.6 copy-start.13
  191.9 13.7 %collective-permute-start.8 = (bf16[256,4096]{1,0:T(8,128)(2,1)}, bf16[256,4096]{1,0:T(8,128)(2,1)}, u32[]{:S(2)}, u32[]{:S(2)}) collective-permute-start(bf16[256,4096]{1,0:T(8,128)(2,1)} %get-tuple-element.55.refs_0_.refs_3_), channel_id=1, source_target_pairs={{0,2},{2,0},{4,6},{6,4},{8,10},{10,8},{12,14},{14,12},{16,18},{18,... | collective-permute-start | bytes 6291464 | tf_op jit(solution)/shard_map/ppermute | solution.py:599
  194.8 3.1 collective-permute-start.9
  200.1 5.6 copy-start.9
  492.3 11.7 %collective-permute-start.16 = (bf16[256,4096]{1,0:T(8,128)(2,1)S(1)}, bf16[256,4096]{1,0:T(8,128)(2,1)}, u32[]{:S(2)}, u32[]{:S(2)}) collective-permute-start(bf16[256,4096]{1,0:T(8,128)(2,1)S(1)} %get-tuple-element.145), channel_id=1, source_target_pairs={{0,2},{2,0},{4,6},{6,4},{8,10},{10,8},{12,14},{14,12},{16,18},{18,... | collective-permute-start | bytes 6291464 | tf_op jit(solution)/shard_map/ppermute | solution.py:599
  498.4 20.1 %collective-permute-start.15 = (bf16[256,9,256]{0,2,1:T(8,128)(2,1)}, bf16[256,9,256]{0,2,1:T(8,128)(2,1)}, u32[]{:S(2)}, u32[]{:S(2)}) collective-permute-start(bf16[256,9,256]{0,2,1:T(8,128)(2,1)} %get-tuple-element.154), channel_id=1, source_target_pairs={{0,2},{2,0},{4,6},{6,4},{8,10},{10,8},{12,14},{14,12},{16,18},{18,... | collective-permute-start | bytes 3538952 | tf_op jit(solution)/shard_map/ppermute | solution.py:599
  518.1 54.0 %collective-permute-start.17 = (bf16[256,4096]{1,0:T(8,128)(2,1)}, bf16[256,4096]{1,0:T(8,128)(2,1)}, u32[]{:S(2)}, u32[]{:S(2)}) collective-permute-start(bf16[256,4096]{1,0:T(8,128)(2,1)} %get-tuple-element.64.refs_0_.grad_ref), channel_id=1, source_target_pairs={{0,2},{2,0},{4,6},{6,4},{8,10},{10,8},{12,14},{14,12},{16,18},{18,... | collective-permute-start | bytes 6291464 | tf_op jit(solution)/shard_map/ppermute | solution.py:599
  527.2 9.5 copy-start.17
  536.5 117.6 %collective-permute-start.12 = (bf16[256,4096]{1,0:T(8,128)(2,1)}, bf16[256,4096]{1,0:T(8,128)(2,1)}, u32[]{:S(2)}, u32[]{:S(2)}) collective-permute-start(bf16[256,4096]{1,0:T(8,128)(2,1)} %bitcast.89), channel_id=1, source_target_pairs={{0,2},{2,0},{4,6},{6,4},{8,10},{10,8},{12,14},{14,12},{16,18},{18,... | collective-permute-start | bytes 6291464 | tf_op jit(solution)/shard_map/ppermute | solution.py:599
  552.8 192.6 %collective-permute-start.24 = (bf16[256,4608]{1,0:T(8,128)(2,1)}, bf16[256,4608]{1,0:T(8,128)(2,1)}, u32[]{:S(2)}, u32[]{:S(2)}) collective-permute-start(bf16[256,4608]{1,0:T(8,128)(2,1)} %conv_two_weight_grad.1), channel_id=1, source_target_pairs={{0,0},{1,2},{2,1},{3,3},{4,4},{5,6},{6,5},{7,7},{8,8},{9,10},{10,9... | collective-permute-start | bytes 7077896 | tf_op jit(solution)/shard_map/ppermute | solution.py:596
  598.6 35.4 %copy-start.18 = (f32[256,128]{1,0:T(8,128)S(1)}, f32[256,128]{1,0:T(8,128)}, u32[]{:S(2)}) copy-start(f32[256,128]{1,0:T(8,128)} %get-tuple-element.73) | copy-start | bytes 393220
  598.6 47.3 %copy-start.20 = (bf16[1,2048]{1,0:T(2,128)(2,1)S(1)}, bf16[1,2048]{1,0:T(2,128)(2,1)}, u32[]{:S(2)}) copy-start(bf16[1,2048]{1,0:T(2,128)(2,1)} %param.25) | copy-start | bytes 12292
  598.6 147.6 %collective-permute-start.18 = (bf16[256,4096]{1,0:T(8,128)(2,1)}, bf16[256,4096]{1,0:T(8,128)(2,1)}, u32[]{:S(2)}, u32[]{:S(2)}) collective-permute-start(bf16[256,4096]{1,0:T(8,128)(2,1)} %get-tuple-element.67.refs_0_.grad_ref), channel_id=1, source_target_pairs={{0,2},{2,0},{4,6},{6,4},{8,10},{10,8},{12,14},{14,12},{16,18},{18,... | collective-permute-start | bytes 6291464 | tf_op jit(solution)/shard_map/ppermute | solution.py:599
  614.7 33.1 %copy-start.8 = (f32[256,14]{1,0:T(8,128)S(1)}, f32[256,14]{1,0:T(8,128)}, u32[]{:S(2)}) copy-start(f32[256,14]{1,0:T(8,128)} %slice_bitcast_fusion) | copy-start | bytes 43012
  614.7 71.8 %collective-permute-start.23 = (bf16[256,4608]{1,0:T(8,128)(2,1)}, bf16[256,4608]{1,0:T(8,128)(2,1)}, u32[]{:S(2)}, u32[]{:S(2)}) collective-permute-start(bf16[256,4608]{1,0:T(8,128)(2,1)} %conv_one_weight_grad.1), channel_id=1, source_target_pairs={{0,0},{1,2},{2,1},{3,3},{4,4},{5,6},{6,5},{7,7},{8,8},{9,10},{10,9... | collective-permute-start | bytes 7077896 | tf_op jit(solution)/shard_map/ppermute | solution.py:596
  634.0 14.5 %copy-start.16 = (bf16[4,64,384]{2,1,0:T(8,128)(2,1)S(1)}, bf16[4,64,384]{2,1,0:T(8,128)(2,1)}, u32[]{:S(2)}) copy-start(bf16[4,64,384]{2,1,0:T(8,128)(2,1)} %get-tuple-element.74) | copy-start | bytes 589828
  634.1 0.7 collective-permute-start.20
  634.8 14.8 %collective-permute-start.14 = (bf16[256,9,256]{0,2,1:T(8,128)(2,1)}, bf16[256,9,256]{0,2,1:T(8,128)(2,1)}, u32[]{:S(2)}, u32[]{:S(2)}) collective-permute-start(bf16[256,9,256]{0,2,1:T(8,128)(2,1)} %copy-done.5), channel_id=1, source_target_pairs={{0,2},{2,0},{4,6},{6,4},{8,10},{10,8},{12,14},{14,12},{16,18},{18,... | collective-permute-start | bytes 3538952 | tf_op jit(solution)/shard_map/ppermute | solution.py:599
  645.9 2.8 copy-start.15
  647.7 13.8 %copy-start.2 = (bf16[256,9,256]{0,2,1:T(8,128)(2,1)S(1)}, bf16[256,9,256]{0,2,1:T(8,128)(2,1)}, u32[]{:S(2)}) copy-start(bf16[256,9,256]{0,2,1:T(8,128)(2,1)} %copy-done.1) | copy-start | bytes 3538948
  647.7 266.9 %all-reduce.7.cloned.1.call-start = ((), (), s32[]{:S(2)}) async-start(), calls=%async_computation.1 | async-start | bytes 15728640 | tf_op jit(solution)/shard_map/psum | solution.py:749
  649.6 25.4 %collective-permute-start.21 = (bf16[2,256,384]{1,2,0:T(8,128)(2,1)}, bf16[2,256,384]{1,2,0:T(8,128)(2,1)}, u32[]{:S(2)}, u32[]{:S(2)}) collective-permute-start(bf16[2,256,384]{1,2,0:T(8,128)(2,1)} %pad_maximum_fusion.7), channel_id=1, source_target_pairs={{0,0},{1,2},{2,1},{3,3},{4,4},{5,6},{6,5},{7,7},{8,8},{9,10},{10,9... | collective-permute-start | bytes 1179656 | tf_op jit(solution)/shard_map/ppermute | solution.py:596
  654.1 91.4 %collective-permute-start.25 = (bf16[3,256,512]{2,1,0:T(8,128)(2,1)}, bf16[3,256,512]{2,1,0:T(8,128)(2,1)}, u32[]{:S(2)}, u32[]{:S(2)}) collective-permute-start(bf16[3,256,512]{2,1,0:T(8,128)(2,1)} %bitcast.125), channel_id=1, source_target_pairs={{0,0},{1,2},{2,1},{3,3},{4,4},{5,6},{6,5},{7,7},{8,8},{9,10},{10,9... | collective-permute-start | bytes 2359304 | tf_op jit(solution)/shard_map/ppermute | solution.py:596
  675.0 70.4 %collective-permute-start.26 = (bf16[256,512]{1,0:T(8,128)(2,1)}, bf16[256,512]{1,0:T(8,128)(2,1)S(1)}, u32[]{:S(2)}, u32[]{:S(2)}) collective-permute-start(bf16[256,512]{1,0:T(8,128)(2,1)} %get-tuple-element.79), channel_id=1, source_target_pairs={{0,0},{1,2},{2,1},{3,3},{4,4},{5,6},{6,5},{7,7},{8,8},{9,10},{10,9... | collective-permute-start | bytes 786440 | tf_op jit(solution)/shard_map/ppermute | solution.py:596
  686.5 104.3 %collective-permute-start.13 = (bf16[256,4096]{1,0:T(8,128)(2,1)}, bf16[256,4096]{1,0:T(8,128)(2,1)}, u32[]{:S(2)}, u32[]{:S(2)}) collective-permute-start(bf16[256,4096]{1,0:T(8,128)(2,1)} %shard_map.375), channel_id=1, source_target_pairs={{0,0},{1,2},{2,1},{3,3},{4,4},{5,6},{6,5},{7,7},{8,8},{9,10},{10,9... | collective-permute-start | bytes 6291464 | tf_op jit(solution)/shard_map/ppermute | solution.py:596
  745.4 0.7 copy-start.14
  771.0 86.4 %collective-permute-start.19 = (bf16[256,4096]{1,0:T(8,128)(2,1)}, bf16[256,4096]{1,0:T(8,128)(2,1)}, u32[]{:S(2)}, u32[]{:S(2)}) collective-permute-start(bf16[256,4096]{1,0:T(8,128)(2,1)} %get-tuple-element.70), channel_id=1, source_target_pairs={{0,0},{1,2},{2,1},{3,3},{4,4},{5,6},{6,5},{7,7},{8,8},{9,10},{10,9... | collective-permute-start | bytes 6291464 | tf_op jit(solution)/shard_map/ppermute | solution.py:596
  789.1 5.7 collective-permute-start.22
  914.5 3.9 copy-start.10
  932.5 4.5 copy-start.4
Sparse Core Ops, SparseCore 0:
  647.8 97.5 all-reduce.4
  750.8 163.6 all-reduce.6

commit v3 on v2

v3 whole, which is shorter than its diff:
```python
import functools

import jax
import jax.numpy as jnp
from jax import lax
from jax.experimental import pallas as pl
from jax.experimental.pallas import tpu as pltpu
from jax.sharding import PartitionSpec as P

C = 512
HEAD_DIM = 64
PER_GROUP = 16
SIDE = 64
HW = 4096
CTX = 260
CTXP = 384
BLOCK = 256
KEYS = 4608
PAD = 128
FILL = 32
EPSILON = 1e-05
NEG_FILL = -1e30
F32 = jnp.float32
BF = jnp.bfloat16
NT = (((1,), (1,)), ((), ()))
VMEM_BYTES = 62 << 20


def dot(a, b):
    return jnp.dot(a, b, preferred_element_type=F32)


def dot_nt(a, b):
    return lax.dot_general(a, b, NT, preferred_element_type=F32)


def whole():
    return pl.BlockSpec(memory_space=pltpu.VMEM)


def placed():
    return pl.BlockSpec(memory_space=pl.ANY)


def scalars():
    return pl.BlockSpec(memory_space=pltpu.SMEM)


def params(**kwargs):
    return pltpu.CompilerParams(vmem_limit_bytes=VMEM_BYTES, **kwargs)


def cost(flops, nbytes, transcendentals=0):
    return pl.CostEstimate(flops=flops, bytes_accessed=nbytes, transcendentals=transcendentals)


def struct(shape, dtype):
    return jax.ShapeDtypeStruct(shape, dtype)


def fetch(meta, own_ref, got_ref, buf, sem):
    @pl.when(meta[1] == 1)
    def _():
        pltpu.make_async_copy(own_ref, buf, sem).start()

    @pl.when(meta[1] != 1)
    def _():
        pltpu.make_async_copy(got_ref, buf, sem).start()


def arrive(own_ref, buf, sem):
    pltpu.make_async_copy(own_ref, buf, sem).wait()


def group_scalar(column):
    return jnp.sum(column, axis=0, keepdims=True) * (1.0 / (PER_GROUP * HW))


def group_stats(vals):
    mean = group_scalar(jnp.sum(vals, axis=1, keepdims=True))
    centred = vals - mean
    var = group_scalar(jnp.sum(centred * centred, axis=1, keepdims=True))
    rstd = lax.rsqrt(var + EPSILON)
    return mean, rstd


def norm_backward(dy_sum, dyx_sum, gain):
    return group_scalar(dy_sum * gain), group_scalar(dyx_sum * gain)


def for_groups(channels, body, together=2):
    def step(g, carry):
        for u in range(together):
            first = pl.multiple_of((g * together + u) * PER_GROUP, PER_GROUP)
            body(pl.ds(first, PER_GROUP))
        return carry

    lax.fori_loop(0, channels // PER_GROUP // together, step, 0)


def columns(values):
    lane = lax.broadcasted_iota(jnp.int32, (PER_GROUP, 128), 1)
    tile = jnp.zeros((PER_GROUP, 128), F32)
    for at, val in enumerate(values):
        tile = jnp.where(lane == at, val, tile)
    return tile


ROWS = SIDE // 2


def lanes(x, n):
    return x[:, 128 * n : 128 * n + 128]


def low_lanes(x):
    return lax.broadcasted_iota(jnp.int32, (x.shape[0], 128), 1) < SIDE


def fold(x):
    low = low_lanes(x)
    out = []
    for r in range(ROWS):
        upper, lower = lanes(x, r // 2), lanes(x, r // 2 + ROWS // 2)
        if r % 2 == 0:
            out.append(jnp.where(low, upper, pltpu.roll(lower, SIDE, 1)))
        else:
            out.append(jnp.where(low, pltpu.roll(upper, SIDE, 1), lower))
    return jnp.concatenate(out, 1)


def unfold(x):
    low = low_lanes(x)
    pairs = range(x.shape[1] // 256)
    top = [jnp.where(low, lanes(x, 2 * n), pltpu.roll(lanes(x, 2 * n + 1), SIDE, 1)) for n in pairs]
    bottom = [
        jnp.where(low, pltpu.roll(lanes(x, 2 * n), SIDE, 1), lanes(x, 2 * n + 1)) for n in pairs
    ]
    return jnp.concatenate(top, 1), jnp.concatenate(bottom, 1)


def fold_kernel(meta, own_ref, got_ref, out_ref, x_buf, sem):
    fetch(meta, own_ref, got_ref, x_buf, sem)
    arrive(own_ref, x_buf, sem)

    def body(rows):
        out_ref[rows, :] = fold(x_buf[rows, :].astype(F32)).astype(BF)

    for_groups(out_ref.shape[0], body)


def folded(meta, own, got):
    return pl.pallas_call(
        fold_kernel,
        out_shape=struct(own.shape, BF),
        in_specs=[scalars(), placed(), placed()],
        out_specs=whole(),
        scratch_shapes=[pltpu.VMEM(own.shape, BF), pltpu.SemaphoreType.DMA(())],
        compiler_params=params(),
        cost_estimate=cost(8 * own.size, 4 * own.size),
        name="fold",
    )(meta, own, got)


def act_one_kernel(meta, own_ref, got_ref, par_ref, act_ref, stat_ref, fold_ref, x_buf, sem):
    fetch(meta, own_ref, got_ref, x_buf, sem)
    arrive(own_ref, x_buf, sem)

    def body(rows):
        vals = fold(x_buf[rows, :].astype(F32))
        fold_ref[rows, :] = vals.astype(BF)
        mean, rstd = group_stats(vals)
        par = par_ref[rows, :]
        out = (vals - mean) * (rstd * par[:, 0:1]) + par[:, 1:2]
        act_ref[rows, :] = (out * jax.nn.sigmoid(out)).astype(BF)
        stat_ref[rows, :] = columns([mean, rstd])

    for_groups(act_ref.shape[0], body)


def first_activation(meta, own, got, par):
    ch = own.shape[0]
    return pl.pallas_call(
        act_one_kernel,
        out_shape=[struct((ch, HW), BF), struct((ch, 128), F32), struct((ch, HW), BF)],
        in_specs=[scalars(), placed(), placed(), whole()],
        out_specs=[whole()] * 3,
        scratch_shapes=[pltpu.VMEM((ch, HW), BF), pltpu.SemaphoreType.DMA(())],
        compiler_params=params(),
        cost_estimate=cost(20 * ch * HW, 6 * ch * HW, ch * HW),
        name="act_one",
    )(meta, own, got, par)


def fill_shifted(xs, pieces, first):
    start = first
    for x_ref in pieces:
        rows = x_ref.shape[0]

        def step(r, carry, x_ref=x_ref, start=start):
            off = pl.multiple_of(r * FILL, FILL)
            at = pl.ds(pl.multiple_of(start + off, FILL), FILL)
            lane = lax.broadcasted_iota(jnp.int32, (FILL, 128), 1)
            low = lane < SIDE
            left, right = lane % SIDE == 0, lane % SIDE == SIDE - 1
            zero = jnp.zeros((FILL, 128), F32)
            here = pl.ds(off, FILL)
            for n in range(ROWS):
                x = x_ref[here, 128 * n : 128 * n + 128].astype(F32)
                kinds = (
                    jnp.where(left, zero, pltpu.roll(x, 1, 1)),
                    x,
                    jnp.where(right, zero, pltpu.roll(x, 127, 1)),
                )
                for d, y in enumerate(kinds):
                    xs[d, at, PAD + 128 * n : PAD + 128 * n + 128] = y.astype(BF)
                    if n == ROWS - 1:
                        xs[d, at, :PAD] = jnp.where(low, zero, pltpu.roll(y, SIDE, 1)).astype(BF)
                    if n == 0:
                        xs[d, at, PAD + HW :] = jnp.where(
                            low, pltpu.roll(y, SIDE, 1), zero
                        ).astype(BF)
            return carry

        lax.fori_loop(0, rows // FILL, step, 0)
        start = xs.shape[1] - rows - start if len(pieces) == 2 else start + rows


def window(xs, tap, start, width):
    first = PAD + start + (tap // 3 - 1) * 128
    if not isinstance(start, int):
        first = pl.multiple_of(first, 128)
    return xs[tap % 3, :, pl.ds(first, width)]


def convolve(xs, w_ref, out_ref, add, width=1024):
    depth = xs.shape[1]

    def step(n, carry):
        p = n * width
        acc = dot(w_ref[:, :depth], window(xs, 0, p, width))
        for tap in range(1, 9):
            acc = acc + dot(w_ref[:, tap * depth : (tap + 1) * depth], window(xs, tap, p, width))
        at = pl.ds(pl.multiple_of(p, width), width)
        out_ref[:, at] = add(acc, at)
        return carry

    lax.fori_loop(0, HW // width, step, 0)


def conv_call(kernel, meta, weights, pieces, vmem_in, any_in, outs, any_outs, scratch, name):
    out_ch, depth = weights[0].shape[0], C
    arrays = (weights[0], *pieces, *vmem_in, *any_in)
    nbytes = sum(a.size * a.dtype.itemsize for a in arrays) + out_ch * HW * 4
    return pl.pallas_call(
        functools.partial(kernel, len(pieces)),
        out_shape=[*outs, *any_outs],
        in_specs=[scalars(), placed(), placed()]
        + [whole()] * (len(pieces) + len(vmem_in))
        + [placed()] * len(any_in),
        out_specs=[whole()] * len(outs) + [placed()] * len(any_outs),
        scratch_shapes=[
            pltpu.VMEM((3, depth, HW + 2 * PAD), BF),
            pltpu.VMEM((out_ch, 9 * depth), BF),
            pltpu.VMEM((out_ch, HW), F32),
            pltpu.SemaphoreType.DMA((4,)),
            *scratch,
        ],
        compiler_params=params(),
        cost_estimate=cost(2 * out_ch * 9 * depth * HW, nbytes, out_ch * HW),
        name=name,
    )(meta, *weights, *pieces, *vmem_in, *any_in)


def conv_one_kernel(n, meta, w_own, w_got, *refs):
    pieces, refs = refs[:n], refs[n:]
    par_ref, act_ref, stat_ref, conv_ref, w_ref, xs, w_buf, acc, sems = refs
    fetch(meta, w_own, w_got, w_buf, sems.at[0])
    fill_shifted(xs, pieces, meta[0])
    arrive(w_own, w_buf, sems.at[0])
    keep = pltpu.make_async_copy(w_buf, w_ref, sems.at[2])
    keep.start()
    bias = par_ref[:, 0:1]
    convolve(xs, w_buf, acc, lambda val, at: val + bias)
    store = pltpu.make_async_copy(acc, conv_ref, sems.at[1])
    store.start()

    def body(rows):
        vals = acc[rows, :]
        mean, rstd = group_stats(vals)
        par = par_ref[rows, :]
        gain, shift, factor = par[:, 1:2], par[:, 2:3], 1.0 + par[:, 3:4]
        mid = (vals - mean) * (rstd * gain * factor) + (shift * factor + par[:, 4:5])
        act_ref[rows, :] = (mid * jax.nn.sigmoid(mid)).astype(BF)
        stat_ref[rows, :] = columns([mean, rstd])

    for_groups(acc.shape[0], body)
    store.wait()
    keep.wait()


def conv_two_kernel(n, meta, w_own, w_got, *refs):
    pieces, refs = refs[:n], refs[n:]
    par_ref, f_ref, normed_ref, stat_ref, hidden_ref, w_ref, xs, w_buf, acc, sems = refs
    fetch(meta, w_own, w_got, w_buf, sems.at[0])
    fill_shifted(xs, pieces, meta[0])
    arrive(w_own, w_buf, sems.at[0])
    keep = pltpu.make_async_copy(w_buf, w_ref, sems.at[2])
    keep.start()
    bias = par_ref[:, 0:1]
    convolve(xs, w_buf, acc, lambda val, at: val + bias + f_ref[:, at].astype(F32))
    store = pltpu.make_async_copy(acc, hidden_ref, sems.at[1])
    store.start()

    def body(rows):
        vals = acc[rows, :]
        mean, rstd = group_stats(vals)
        par = par_ref[rows, :]
        normed_ref[rows, :] = ((vals - mean) * (rstd * par[:, 1:2]) + par[:, 2:3]).astype(BF)
        stat_ref[rows, :] = columns([mean, rstd])

    for_groups(acc.shape[0], body)
    store.wait()
    keep.wait()


def silu_slope(mid):
    sig = jax.nn.sigmoid(mid)
    return sig * (1.0 + mid * (1.0 - sig))


def conv_two_back_kernel(n, meta, w_own, w_got, *refs):
    pieces, refs = refs[:n], refs[n:]
    par_ref, stat_ref, conv_ref, grad_ref, sums_ref, xs, w_buf, acc, sems, conv_buf = refs
    fetch(meta, w_own, w_got, w_buf, sems.at[0])
    load = pltpu.make_async_copy(conv_ref, conv_buf, sems.at[1])
    load.start()
    fill_shifted(xs, pieces, meta[0])
    arrive(w_own, w_buf, sems.at[0])
    convolve(xs, w_buf, acc, lambda val, at: val)
    load.wait()

    def body(rows):
        par, stat = par_ref[rows, :], stat_ref[rows, :]
        gain, shift, factor = par[:, 1:2], par[:, 2:3], 1.0 + par[:, 3:4]
        rstd = stat[:, 1:2]
        hat = (conv_buf[rows, :] - stat[:, 0:1]) * rstd
        mid = hat * (gain * factor) + (shift * factor + par[:, 4:5])
        grad = acc[rows, :] * silu_slope(mid)
        total = jnp.sum(grad, axis=1, keepdims=True)
        total_hat = jnp.sum(grad * hat, axis=1, keepdims=True)
        mean_u, mean_uhat = norm_backward(total * factor, total_hat * factor, gain)
        out = ((grad * (factor * gain) - mean_u - hat * mean_uhat) * rstd).astype(BF)
        grad_ref[rows, :] = out
        bias_grad = jnp.sum(out.astype(F32), axis=1, keepdims=True)
        sums_ref[rows, :] = columns(
            [
                total_hat * factor,
                total * factor,
                total_hat * gain + total * shift,
                total,
                bias_grad,
            ]
        )

    for_groups(acc.shape[0], body)


def conv_one_back_kernel(n, meta, w_own, w_got, *refs):
    pieces, refs = refs[:n], refs[n:]
    par_ref, stat_ref, f_ref, hid_ref, grad_ref, sums_ref, xs, w_buf, acc, sems, hid_buf = refs
    fetch(meta, w_own, w_got, w_buf, sems.at[0])
    load = pltpu.make_async_copy(hid_ref, hid_buf, sems.at[1])
    load.start()
    fill_shifted(xs, pieces, meta[0])
    arrive(w_own, w_buf, sems.at[0])
    convolve(xs, w_buf, acc, lambda val, at: val)
    load.wait()

    def body(rows):
        par, stat = par_ref[rows, :], stat_ref[rows, :]
        gain, shift = par[:, 0:1], par[:, 1:2]
        rstd = stat[:, 1:2]
        hat = (f_ref[rows, :].astype(F32) - stat[:, 0:1]) * rstd
        grad = acc[rows, :] * silu_slope(hat * gain + shift)
        total = jnp.sum(grad, axis=1, keepdims=True)
        total_hat = jnp.sum(grad * hat, axis=1, keepdims=True)
        mean_u, mean_uhat = norm_backward(total, total_hat, gain)
        out = hid_buf[rows, :] + (grad * gain - mean_u - hat * mean_uhat) * rstd
        top, bottom = unfold(out)
        grad_ref[rows, : HW // 2] = top.astype(grad_ref.dtype)
        grad_ref[rows, HW // 2 :] = bottom.astype(grad_ref.dtype)
        sums_ref[rows, :] = columns([total_hat, total])

    for_groups(acc.shape[0], body)


def weight_grad_kernel(n, meta, grad_ref, *refs):
    pieces, (out_ref, gs) = refs[:n], refs[n:]
    fill_shifted(gs, (grad_ref,), 0)
    for tap in range(9):
        moved = window(gs, 8 - tap, 0, HW)
        first = meta[0]
        for x_ref in pieces:
            rows = x_ref.shape[0]
            at = pl.ds(pl.multiple_of(tap * C + first, rows), rows)
            out_ref[:, at] = dot_nt(moved, x_ref[...]).astype(BF)
            first = C - rows - first


def conv_weight_grad(meta, grad, pieces, name):
    out_ch = grad.shape[0]
    return pl.pallas_call(
        functools.partial(weight_grad_kernel, len(pieces)),
        out_shape=struct((out_ch, 9 * C), BF),
        in_specs=[scalars()] + [whole()] * (1 + len(pieces)),
        out_specs=whole(),
        scratch_shapes=[pltpu.VMEM((3, out_ch, HW + 2 * PAD), BF)],
        compiler_params=params(),
        cost_estimate=cost(2 * out_ch * 9 * C * HW, (out_ch + C) * HW * 2 + out_ch * 9 * C * 2),
        name=name,
    )(meta, grad, *pieces)


def turn_kernel(meta, own_ref, other_ref, out_ref):
    half = own_ref.shape[0]
    for tap in range(9):
        at = pl.ds(pl.multiple_of(tap * C + meta[0], half), half)
        row = meta[0]
        for ref in (own_ref, other_ref):
            to = pl.ds(pl.multiple_of((8 - tap) * C + row, half), half)
            out_ref[:, to] = ref[:, at].astype(F32).T.astype(BF)
            row = half - row


def turned_pair(meta, own, other):
    return pl.pallas_call(
        turn_kernel,
        out_shape=struct(own.shape, BF),
        in_specs=[scalars(), whole(), whole()],
        out_specs=whole(),
        compiler_params=params(),
        cost_estimate=cost(0, 3 * own.size * 2),
        name="turn",
    )(meta, own, other)


def norm_three_back_kernel(n, *refs):
    addends, (hidden_ref, stat_ref, par_ref, cot_ref, hid_ref, grad_ref, sums_ref) = (
        refs[:n],
        refs[n:],
    )

    def body(rows):
        dy = addends[0][rows, :].astype(F32)
        for extra in addends[1:]:
            dy = dy + extra[rows, :].astype(F32)
        par, stat = par_ref[rows, :], stat_ref[rows, :]
        gain, rstd = par[:, 1:2], stat[:, 1:2]
        hat = (hidden_ref[rows, :] - stat[:, 0:1]) * rstd
        total = jnp.sum(dy, axis=1, keepdims=True)
        total_hat = jnp.sum(dy * hat, axis=1, keepdims=True)
        mean_u, mean_uhat = norm_backward(total, total_hat, gain)
        top = cot_ref[rows, :].astype(F32)
        out = top + (dy * gain - mean_u - hat * mean_uhat) * rstd
        hid_ref[rows, :] = out
        low = out.astype(BF)
        grad_ref[rows, :] = low
        sums_ref[rows, :] = columns(
            [
                total_hat,
                total,
                jnp.sum(low.astype(F32), axis=1, keepdims=True),
                jnp.sum(top, axis=1, keepdims=True),
            ]
        )

    for_groups(hidden_ref.shape[0], body)


def norm_three_back(addends, hidden, stat, par, cot):
    ch = hidden.shape[0]
    rows = 32

    def part(a):
        return pl.BlockSpec((rows, a.shape[1]), lambda r: (r, 0))

    outs = [struct((ch, HW), F32), struct((ch, HW), BF), struct((ch, 128), F32)]
    ins = (*addends, hidden, stat, par, cot)
    return pl.pallas_call(
        functools.partial(norm_three_back_kernel, len(addends)),
        grid=(ch // rows,),
        out_shape=outs,
        in_specs=[part(a) for a in ins],
        out_specs=[part(a) for a in outs],
        compiler_params=params(),
        cost_estimate=cost(20 * ch * HW, 16 * ch * HW),
        name="norm_three_back",
    )(*ins)


def piece_columns(meta, w_ref, pieces):
    first = meta[0]
    acc = None
    for x_ref in pieces:
        rows = x_ref.shape[0]
        term = dot(w_ref[:, pl.ds(pl.multiple_of(first, rows), rows)], x_ref[...])
        acc = term if acc is None else acc + term
        first = w_ref.shape[1] - rows - first
    return acc


def inputs_kernel(n, meta, w_ref, *refs):
    pieces, (bias_ref, out_ref) = refs[:n], refs[n:]
    out_ref[...] = (piece_columns(meta, w_ref, pieces) + bias_ref[...]).astype(BF)


def inputs_product(meta, weight, pieces, bias, width=1024, name=None):
    rows, depth = weight.shape
    return pl.pallas_call(
        functools.partial(inputs_kernel, len(pieces)),
        grid=(HW // width,),
        out_shape=struct((rows, HW), BF),
        in_specs=[scalars(), pl.BlockSpec((rows, depth), lambda p: (0, 0))]
        + [pl.BlockSpec((x.shape[0], width), lambda p: (0, p)) for x in pieces]
        + [pl.BlockSpec((rows, 1), lambda p: (0, 0))],
        out_specs=pl.BlockSpec((rows, width), lambda p: (0, p)),
        compiler_params=params(),
        cost_estimate=cost(2 * rows * depth * HW, (rows + depth) * HW * 2),
        name=name,
    )(meta, weight, *pieces, bias)


def parts_kernel(n, meta, w_ref, *refs):
    pieces, outs = refs[:n], refs[n:]
    first = meta[0]
    for out_ref in outs:
        rows = out_ref.shape[0]
        row = pl.ds(pl.multiple_of(first, rows), rows)
        acc = None
        at = 0
        for x_ref in pieces:
            depth = x_ref.shape[0]
            term = dot(w_ref[row, at : at + depth], x_ref[...])
            acc = term if acc is None else acc + term
            at += depth
        out_ref[...] = acc.astype(BF)
        first = w_ref.shape[0] - rows - first


def parts_product(meta, weight, pieces, count, width=1024, name=None):
    rows, depth = weight.shape
    part = struct((rows // count, HW), BF)
    return pl.pallas_call(
        functools.partial(parts_kernel, len(pieces)),
        grid=(HW // width,),
        out_shape=[part] * count,
        in_specs=[scalars(), pl.BlockSpec((rows, depth), lambda p: (0, 0))]
        + [pl.BlockSpec((x.shape[0], width), lambda p: (0, p)) for x in pieces],
        out_specs=[pl.BlockSpec((rows // count, width), lambda p: (0, p))] * count,
        compiler_params=params(),
        cost_estimate=cost(2 * rows * depth * HW, (rows + depth) * HW * 2),
        name=name,
    )(meta, weight, *pieces)


def output_kernel(n, meta, w_ref, *refs):
    pieces, (bias_ref, hidden_ref, out_ref) = refs[:n], refs[n:]
    acc = hidden_ref[...] + bias_ref[...] + piece_columns(meta, w_ref, pieces)
    half = acc.shape[1] // 2
    for base, val in zip((0, HW // 2), unfold(acc)):
        first = pl.multiple_of(base + pl.program_id(0) * half, half)
        out_ref[:, pl.ds(first, half)] = val.astype(BF)


def output_product(meta, weight, pieces, bias, hidden, width=1024):
    rows, depth = weight.shape
    return pl.pallas_call(
        functools.partial(output_kernel, len(pieces)),
        grid=(HW // width,),
        out_shape=struct((rows, HW), BF),
        in_specs=[scalars(), pl.BlockSpec((rows, depth), lambda p: (0, 0))]
        + [pl.BlockSpec((x.shape[0], width), lambda p: (0, p)) for x in pieces]
        + [
            pl.BlockSpec((rows, 1), lambda p: (0, 0)),
            pl.BlockSpec((rows, width), lambda p: (0, p)),
        ],
        out_specs=pl.BlockSpec((rows, HW), lambda p: (0, 0)),
        compiler_params=params(),
        cost_estimate=cost(2 * rows * depth * HW, (rows * 3 + depth) * HW * 2),
        name="output",
    )(meta, weight, *pieces, bias, hidden)


def outer_kernel(n_left, n_right, meta, *refs):
    lefts, rights = refs[:n_left], refs[n_left : n_left + n_right]
    out_ref, sums_ref = refs[n_left + n_right : n_left + n_right + 2]
    acc_ref, tot_ref = refs[n_left + n_right + 2 :]
    step = pl.program_id(0)

    @pl.when(step == 0)
    def _():
        acc_ref[...] = jnp.zeros_like(acc_ref)
        tot_ref[...] = jnp.zeros_like(tot_ref)

    row = 0
    for left in lefts:
        rows = left.shape[0]
        val = left[...]
        first = meta[0]
        for right in rights:
            cols = right.shape[0]
            at = pl.ds(pl.multiple_of(first, cols), cols)
            acc_ref[row : row + rows, at] += dot_nt(val, right[...])
            first = acc_ref.shape[1] - cols - first
        tot_ref[row : row + rows, :] += jnp.sum(val.astype(F32), axis=1, keepdims=True)
        row += rows

    @pl.when(step == pl.num_programs(0) - 1)
    def _():
        out_ref[...] = acc_ref[...].astype(BF)
        sums_ref[...] = tot_ref[...]


def outer(meta, lefts, rights, width=1024, name=None):
    rows, cols = sum(a.shape[0] for a in lefts), sum(a.shape[0] for a in rights)
    fixed = lambda p: (0, 0)
    return pl.pallas_call(
        functools.partial(outer_kernel, len(lefts), len(rights)),
        grid=(HW // width,),
        out_shape=[struct((rows, cols), BF), struct((rows, 128), F32)],
        in_specs=[scalars()]
        + [pl.BlockSpec((a.shape[0], width), lambda p: (0, p)) for a in (*lefts, *rights)],
        out_specs=[pl.BlockSpec((rows, cols), fixed), pl.BlockSpec((rows, 128), fixed)],
        scratch_shapes=[pltpu.VMEM((rows, cols), F32), pltpu.VMEM((rows, 128), F32)],
        compiler_params=params(),
        cost_estimate=cost(2 * rows * cols * HW, (rows + cols) * HW * 2),
        name=name,
    )(meta, *lefts, *rights)


def attention_kernel(
    lim_ref, q_ref, k_ref, v_ref, kc_ref, vc_ref, g_ref,
    o_ref, dq_ref, dk_ref, dv_ref, dkc_ref, dvc_ref,
    kt, vt, kn, vn, s_even, s_odd, p_sc, tops, o_acc, dk_acc, dv_acc, *, unroll, back,
):
    step, last = pl.program_id(1), pl.num_programs(1) - 1
    width = q_ref.shape[-1]
    blocks = KEYS // BLOCK

    @pl.when(step == 0)
    def _():
        spare = jnp.zeros((HEAD_DIM, KEYS - HW - CTXP), BF)
        for ref, own, ctx in ((kn, k_ref, kc_ref), (vn, v_ref, vc_ref)):
            ref[:, :HW] = own[0, 0]
            ref[:, HW : HW + CTXP] = ctx[0, 0]
            ref[:, HW + CTXP :] = spare
        row = lax.broadcasted_iota(jnp.int32, (HEAD_DIM, BLOCK), 0)
        for n in range(blocks):
            at = slice(n * BLOCK, (n + 1) * BLOCK)
            key = lax.broadcasted_iota(jnp.int32, (HEAD_DIM, BLOCK), 1) + n * BLOCK
            fill = jnp.where((row == 0) & (key >= HW + lim_ref[0]), NEG_FILL, 0.0)
            kt[at, :] = jnp.concatenate([kn[:, at].astype(F32), fill], 0).T.astype(BF)
            vt[at, :] = jnp.concatenate([vn[:, at].astype(F32), jnp.zeros_like(fill)], 0).T.astype(BF)
        dk_acc[...] = jnp.zeros_like(dk_acc)
        dv_acc[...] = jnp.zeros_like(dv_acc)

    def keys_at(n):
        return pl.ds(pl.multiple_of(n * BLOCK, BLOCK), BLOCK)

    scale = HEAD_DIM ** (-0.5)
    q = (q_ref[0, 0].astype(F32) * scale).astype(BF)
    one = jnp.where(lax.broadcasted_iota(jnp.int32, (HEAD_DIM, width), 0) == 0, 1.0, 0.0).astype(BF)
    q_more = jnp.concatenate([q, one], 0)

    def score(n, held):
        scores = dot(kt[keys_at(n), :], q_more)
        held[...] = scores
        return jnp.max(jnp.max(scores.reshape(BLOCK // 8, 8, width), axis=0), axis=0, keepdims=True)

    o_acc[...] = jnp.zeros_like(o_acc)

    def forward(n, held, top, total, shrink):
        raised = jnp.exp(held[...] - top)
        low = raised.astype(BF)
        p_sc[keys_at(n), :] = low
        tops[n, 0:1, :] = top
        sums = jnp.sum(raised.reshape(BLOCK // 8, 8, width), axis=0)
        o_acc[...] = o_acc[...] * shrink + dot(vn[:, keys_at(n)], low)
        return total * shrink + sums

    def forward_step(n, held, ahead_held, carry):
        top, total, shrink = carry
        ahead = jnp.maximum(top, score(n + 1, ahead_held))
        total = forward(n, held, top, total, shrink)
        return ahead, total, jnp.exp(top - ahead)

    held = (s_even, s_odd)

    def forward_run(j, carry):
        for u in range(unroll):
            carry = forward_step(unroll * j + u, held[u % 2], held[1 - u % 2], carry)
        return carry

    carry = (score(0, s_even), jnp.zeros((8, width), F32), jnp.ones((1, width), F32))
    carry = lax.fori_loop(0, blocks // unroll - 1, forward_run, carry)
    for n in range(blocks - unroll, blocks - 1):
        carry = forward_step(n, held[n % 2], held[1 - n % 2], carry)
    top, total, shrink = carry
    total = forward(blocks - 1, s_odd, top, total, shrink)

    inverse = 1.0 / jnp.sum(total, axis=0, keepdims=True)
    mixed = o_acc[...] * inverse
    o_ref[0] = mixed.astype(BF)
    grad = g_ref[0].astype(F32)
    delta = jnp.sum(grad * mixed, axis=0, keepdims=True)
    dq = jnp.zeros((HEAD_DIM, width), F32)
    none = jnp.zeros((HEAD_DIM, width), BF)
    for c in range(0, KEYS, back):
        at = slice(c, c + back)
        slopes = []
        for n in range(c // BLOCK, (c + back) // BLOCK):
            sub = slice(n * BLOCK, (n + 1) * BLOCK)
            factor = inverse * jnp.exp(tops[n, 0:1, :] - top)
            grad_low = (grad * factor).astype(BF)
            both = jnp.concatenate([grad_low, none], 0)
            probs = p_sc[sub, :]
            slope = (dot(vt[sub, :], both) - delta * factor).astype(BF) * probs
            slopes.append(slope)
            dv_acc[:, sub] += dot_nt(grad_low, probs)
        slope = jnp.concatenate(slopes, 0)
        dq = dq + dot(kn[:, at], slope)
        dk_acc[:, at] += dot_nt(q, slope)
    dq_ref[0] = (dq * scale).astype(BF)

    @pl.when(step == last)
    def _():
        dk_ref[0] = dk_acc[:, :HW].astype(BF)
        dv_ref[0] = dv_acc[:, :HW].astype(BF)
        dkc_ref[0] = dk_acc[:, HW : HW + CTXP].astype(BF)
        dvc_ref[0] = dv_acc[:, HW : HW + CTXP].astype(BF)


def attention(limit, qkv, ctx_kv, grads, width=1024, unroll=6, back=512):
    heads = qkv.shape[1]
    keys = KEYS

    def part(t, w, moving):
        return pl.BlockSpec(
            (1, 1, HEAD_DIM, w), (lambda h, i: (t, h, 0, i)) if moving else (lambda h, i: (t, h, 0, 0))
        )

    def row(w, moving):
        return pl.BlockSpec(
            (1, HEAD_DIM, w), (lambda h, i: (h, 0, i)) if moving else (lambda h, i: (h, 0, 0))
        )

    big, small = struct((heads, HEAD_DIM, HW), BF), struct((heads, HEAD_DIM, CTXP), BF)
    return pl.pallas_call(
        functools.partial(attention_kernel, unroll=unroll, back=back),
        grid=(heads, HW // width),
        in_specs=[
            pl.BlockSpec(memory_space=pltpu.SMEM),
            part(0, width, True),
            part(1, HW, False),
            part(2, HW, False),
            part(0, CTXP, False),
            part(1, CTXP, False),
            row(width, True),
        ],
        out_specs=[
            row(width, True),
            row(width, True),
            row(HW, False),
            row(HW, False),
            row(CTXP, False),
            row(CTXP, False),
        ],
        out_shape=[big, big, big, big, small, small],
        scratch_shapes=[
            pltpu.VMEM((keys, 2 * HEAD_DIM), BF),
            pltpu.VMEM((keys, 2 * HEAD_DIM), BF),
            pltpu.VMEM((HEAD_DIM, keys), BF),
            pltpu.VMEM((HEAD_DIM, keys), BF),
            pltpu.VMEM((BLOCK, width), F32),
            pltpu.VMEM((BLOCK, width), F32),
            pltpu.VMEM((keys, width), BF),
            pltpu.VMEM((keys // BLOCK, 8, width), F32),
            pltpu.VMEM((HEAD_DIM, width), F32),
            pltpu.VMEM((HEAD_DIM, keys), F32),
            pltpu.VMEM((HEAD_DIM, keys), F32),
        ],
        compiler_params=params(dimension_semantics=("arbitrary", "arbitrary")),
        cost_estimate=cost(
            24 * heads * HW * keys * HEAD_DIM, heads * HEAD_DIM * 8 * HW * 2, heads * HW * keys
        ),
        name="attention",
    )(limit, qkv, qkv, qkv, ctx_kv, ctx_kv, grads)


class Alone:
    parts = 1

    def __init__(self, mesh):
        self.images = mesh.shape["dp"]

    def meta(self):
        return jnp.array([0, 1], jnp.int32)

    def image(self):
        return lax.axis_index("dp")

    def got(self, x):
        return x

    def pick(self, own, got):
        return own

    def gather(self, x):
        return (lax.all_gather(x, "tensor", axis=0, tiled=True),)

    def scatter(self, parts):
        return (lax.psum_scatter(parts[0], "tensor", scatter_dimension=0, tiled=True),)

    def turn(self, meta, w):
        ch = w.shape[0]
        cut = w.reshape(ch, 9, C)
        turned = lax.all_to_all(cut, "tensor", split_axis=2, concat_axis=0, tiled=True)
        return turned[:, ::-1].transpose(2, 1, 0).reshape(ch, 9 * C)

    def total(self, x):
        return lax.psum(x, "dp")

    def everywhere(self, x):
        return lax.psum(x, "dp")

    def sum_owned(self, x):
        return lax.psum(x, "dp")


class Paired:
    parts = 2

    def __init__(self, mesh):
        dp = mesh.shape["dp"]
        self.images = dp
        self.far = [
            ((2 * k + core) * 2 + 1 - core, (2 * k + 1 - core) * 2 + core)
            for k in range(dp // 2)
            for core in range(2)
        ]
        self.bits = [1 << b for b in range((dp - 1).bit_length())]

    def half(self):
        return lax.axis_index("dp") % 2

    def stays(self):
        return self.half() == lax.axis_index("tensor")

    def meta(self):
        return jnp.stack([self.half() * (C // 2), self.stays().astype(jnp.int32)]).astype(jnp.int32)

    def image(self):
        return lax.axis_index("dp") // 2 * 2 + lax.axis_index("tensor")

    def got(self, x):
        return lax.ppermute(x, ("dp", "tensor"), self.far)

    def pick(self, own, got):
        return jnp.where(self.stays(), own, got)

    def over(self, x, bit):
        return lax.ppermute(x, "dp", [(i, i ^ bit) for i in range(self.images)])

    def gather(self, x):
        return (x, self.over(x, 1))

    def scatter(self, parts):
        return (parts[0], self.over(parts[1], 1))

    def turn(self, meta, w):
        return turned_pair(meta, w, self.over(w, 1))

    def total(self, x):
        x = x + lax.ppermute(x, "tensor", [(0, 1), (1, 0)])
        for bit in self.bits[1:]:
            x = x + self.over(x, bit)
        return self.pick(x, self.over(x, 1))

    def everywhere(self, x):
        for bit in self.bits:
            x = x + self.over(x, bit)
        return x

    def sum_owned(self, x):
        rows = x.shape[0] // 2
        done = []
        for at, order in enumerate((self.bits, [self.bits[0], *self.bits[2:], self.bits[1]])):
            part = lax.slice_in_dim(x, at * rows, (at + 1) * rows)
            size = rows
            for bit in order:
                size //= 2
                upper = (lax.axis_index("dp") // bit) % 2
                keep = lax.dynamic_slice_in_dim(part, upper * size, size)
                send = lax.dynamic_slice_in_dim(part, (1 - upper) * size, size)
                part = (keep.astype(F32) + self.over(send, bit).astype(F32)).astype(BF)
            for bit in reversed(order):
                upper = (lax.axis_index("dp") // bit) % 2
                other = self.over(part, bit)
                part = jnp.where(
                    upper == 0,
                    jnp.concatenate([part, other]),
                    jnp.concatenate([other, part]),
                )
            done.append(part)
        return jnp.concatenate(done)


def after(first, *later):
    held = lax.optimization_barrier((first, *later))
    return held[1:] if len(later) > 1 else held[1]


def local(plan, features, cotangent, embedding, context, lengths, norm1_gain, norm1_bias,
    conv1_weight, conv1_bias, emb_weight, emb_bias, norm2_gain, norm2_bias, conv2_weight,
    conv2_bias, norm3_gain, norm3_bias, qkv_weight, qkv_bias, context_weight, context_bias,
    out_weight, out_bias,
):
    ch, images, pixels = features.shape
    heads = ch // HEAD_DIM
    meta = plan.meta()
    moved = plan.parts == 2

    length_row = jnp.broadcast_to(lengths.astype(F32)[:, None], (1, ch))
    vectors = jnp.concatenate(
        [
            jnp.stack([norm1_gain, norm1_bias, conv1_bias, norm2_gain, norm2_bias]),
            jnp.stack([conv2_bias, norm3_gain, norm3_bias, out_bias]),
            qkv_bias,
            length_row,
        ]
    )
    vectors = plan.pick(vectors, plan.got(vectors))
    f_own = features.reshape(ch, pixels)
    f_got = plan.got(f_own)
    w1_got = plan.got(conv1_weight)
    emb_act = jax.nn.silu(embedding.astype(F32)).astype(BF)
    scale_shift = (
        jnp.einsum("ie,teo->to", emb_act, emb_weight, preferred_element_type=F32) + emb_bias
    )
    ctx_kv = (
        jnp.einsum("toe,ne->ton", context_weight, context[0], preferred_element_type=F32)
        + context_bias[:, :, None]
    ).astype(BF)
    ctx_kv = jnp.pad(ctx_kv, ((0, 0), (0, 0), (0, CTXP - CTX)))
    vectors, ctx_kv = after(scale_shift, vectors, ctx_kv)
    scale_shift = plan.pick(scale_shift, plan.got(scale_shift))
    length = vectors[12, :1].astype(jnp.int32)
    par_one = vectors[0:2].T
    act_one, stat_one, f_low = first_activation(meta, f_own, f_got, par_one)
    full_one = plan.gather(act_one)
    w2_got = plan.got(after(act_one, conv2_weight))
    mats_own = jnp.concatenate([qkv_weight.reshape(3 * ch, C), out_weight])
    mats_own, ctx_own, cot_own = after(
        full_one[-1], mats_own, ctx_kv, cotangent.reshape(ch, pixels)
    )
    mats_got, ctx_got = plan.got(mats_own), plan.got(ctx_own)
    cot_got = plan.got(cot_own)

    par_two = jnp.concatenate([vectors[2:5], scale_shift]).T
    low, stat, wide = struct((ch, HW), BF), struct((ch, 128), F32), struct((ch, HW), F32)
    weight = struct((ch, 9 * C), BF)
    act_two, stat_two, conv_one, w1 = conv_call(
        conv_one_kernel, meta, (conv1_weight, w1_got), full_one, (par_two,), (),
        [low, stat], [wide, weight], [], "conv_one",
    )
    full_two = plan.gather(act_two)
    par_three = vectors[5:8].T
    normed, stat_three, hidden, w2 = conv_call(
        conv_two_kernel, meta, (conv2_weight, w2_got), full_two, (par_three, f_low), (),
        [low, stat], [wide, weight], [], "conv_two",
    )
    full_three = plan.gather(normed)
    mats = plan.pick(mats_own, mats_got)
    w_qkv, w_out = mats[: 3 * ch], mats[3 * ch :]
    qkv = inputs_product(meta, w_qkv, full_three, vectors[9:12].reshape(3 * ch, 1), name="qkv")
    cot = folded(meta, *after(normed, cot_own, cot_got))
    grad_heads = plan.scatter(
        parts_product(meta, w_out.T, (cot,), plan.parts, name="grad_heads")
    )
    turned_one = plan.turn(meta, w1)
    turned_two = plan.turn(meta, w2)
    grad_heads = sum(a.astype(F32) for a in grad_heads).astype(BF)
    ctx_kv = plan.pick(ctx_own, ctx_got)
    mixed, dq, dk, dv, dkc, dvc = attention(
        4 + length,
        qkv.reshape(3, heads, HEAD_DIM, HW),
        ctx_kv.reshape(2, heads, HEAD_DIM, CTXP),
        grad_heads.reshape(heads, HEAD_DIM, HW),
    )

    flat = lambda a: a.reshape(ch, HW)
    dq, dk, dv = flat(dq), flat(dk), flat(dv)
    addends = plan.scatter(
        parts_product(meta, w_qkv.T, (dq, dk, dv), plan.parts, name="grad_normed")
    )
    full_heads = plan.gather(flat(mixed))
    ctx_own = jnp.concatenate([a.reshape(1, ch, CTXP) for a in (dkc, dvc)])
    ctx_got = plan.got(ctx_own)
    dw_qkv, db_qkv = outer(meta, (dq, dk, dv), full_three, name="qkv_grad")
    dw_out, _ = outer(meta, (cot,), full_heads, name="out_grad")
    mats_own = jnp.concatenate([dw_qkv, dw_out])
    mats_got = plan.got(mats_own)
    grad_hidden, grad_two, sums_three = norm_three_back(addends, hidden, stat_three, par_three, cot)
    full_grad_two = plan.gather(grad_two)
    dw_two = conv_weight_grad(meta, grad_two, full_two, "conv_two_weight_grad")
    two_got = plan.got(dw_two)
    ctx_grad = plan.pick(ctx_own, ctx_got)[:, :, :CTX]
    dw_ctx = jnp.einsum("ton,ne->toe", ctx_grad, context[0], preferred_element_type=F32).astype(BF)
    full_grad_two = after(dw_two, *full_grad_two) if moved else full_grad_two
    grad_one, sums_two = conv_call(
        conv_two_back_kernel, meta, (turned_two, turned_two), full_grad_two, (par_two, stat_two),
        (conv_one,), [low, stat], [], [pltpu.VMEM((ch, HW), F32)], "conv_two_back",
    )
    full_grad_one = plan.gather(grad_one)
    mats = plan.pick(mats_own, after(dw_two, mats_got))
    early = (dw_ctx, mats, plan.pick(dw_two, after(grad_one, two_got)))
    held = after(early, grad_one)
    dw_one = conv_weight_grad(meta, held, full_one, "conv_one_weight_grad")
    early = lax.psum(early, "dp")
    one_got = plan.got(dw_one)
    full_grad_one = after(dw_one, *full_grad_one) if moved else full_grad_one
    input_grad, sums_one = conv_call(
        conv_one_back_kernel, meta, (turned_one, turned_one), full_grad_one,
        (par_one, stat_one, f_low), (grad_hidden,),
        [struct((ch, HW), BF if moved else F32), stat], [],
        [pltpu.VMEM((ch, HW), F32)], "conv_one_back",
    )
    input_got = plan.got(input_grad)
    output = output_product(
        meta, w_out, full_heads, vectors[8].reshape(ch, 1), after(grad_hidden, hidden)
    )
    output = plan.pick(output, plan.got(output))

    dw_one = plan.sum_owned(plan.pick(dw_one, one_got))
    emb_all = jnp.where(
        jnp.arange(plan.images)[:, None] == lax.axis_index("dp"), emb_act, jnp.zeros_like(emb_act)
    )
    emb_all = plan.everywhere(emb_all)
    ctx_sums = jnp.sum(ctx_own.astype(F32), axis=2)
    sums_two = sums_two[:, :5].T
    own_mod = sums_two[2:4].astype(BF).astype(F32)
    mods = jnp.where(
        (jnp.arange(plan.images) == plan.image())[:, None, None], own_mod, jnp.zeros_like(own_mod)
    ).reshape(2 * plan.images, ch)
    small = plan.total(
        jnp.concatenate(
            [
                sums_three[:, :4].T,
                db_qkv[:, 0].reshape(3, ch),
                sums_two[:2],
                sums_two[4:5],
                ctx_sums,
                mods,
            ]
        )
    )
    mods = small[12:].reshape(plan.images, 2, ch)
    mods_low = mods.astype(BF)
    dw_emb = jnp.stack(
        [
            jnp.einsum("ie,io->eo", emb_all, mods_low[:, t], preferred_element_type=F32)
            for t in range(2)
        ]
    )
    last = plan.total(sums_one[:, :2].T)
    input_grad = plan.pick(input_grad, input_got).astype(F32)
    dw_ctx, mats, dw_two = after((dw_one, last, input_grad), *early)

    return (
        output.reshape(ch, images, pixels),
        input_grad.reshape(ch, images, pixels),
        last[0],
        last[1],
        dw_one.astype(F32),
        small[9],
        dw_emb,
        jnp.sum(mods, axis=0),
        small[7],
        small[8],
        dw_two.astype(F32),
        small[2],
        small[0],
        small[1],
        mats[: 3 * ch].astype(F32).reshape(3, ch, C),
        small[4:7],
        dw_ctx.astype(F32),
        small[10:12],
        mats[3 * ch :].astype(F32),
        small[3],
    )


def solution(mesh):
    paired = mesh.shape["tensor"] == 2 and mesh.shape["dp"] % 2 == 0
    plan = Paired(mesh) if paired else Alone(mesh)
    specs = (
        P("tensor", "dp", None),
        P("tensor", "dp", None),
        P("dp", None),
        P("dp", None, None),
        P("dp"),
        P("tensor"),
        P("tensor"),
        P("tensor", None),
        P("tensor"),
        P(None, None, "tensor"),
        P(None, "tensor"),
        P("tensor"),
        P("tensor"),
        P("tensor", None),
        P("tensor"),
        P("tensor"),
        P("tensor"),
        P(None, "tensor", None),
        P(None, "tensor"),
        P(None, "tensor", None),
        P(None, "tensor"),
        P("tensor", None),
        P("tensor"),
    )
    return jax.shard_map(
        functools.partial(local, plan),
        mesh=mesh,
        in_specs=specs,
        out_specs=(
            P("tensor", "dp", None),
            P("tensor", "dp", None),
            P("tensor"),
            P("tensor"),
            P("tensor", None),
            P("tensor"),
            P(None, None, "tensor"),
            P(None, "tensor"),
            P("tensor"),
            P("tensor"),
            P("tensor", None),
            P("tensor"),
            P("tensor"),
            P("tensor"),
            P(None, "tensor", None),
            P(None, "tensor"),
            P(None, "tensor", None),
            P(None, "tensor"),
            P("tensor", None),
            P("tensor"),
        ),
        check_vma=False,
    )
```

time: 970 us -> 813 us (0.84)
  starting transfers between devices: 201 us -> 133 us
  blocking collectives: 60.7 us -> 0 us
  local copies, waits for them, and re-layouts: 80.7 us -> 32.5 us
  waiting for transfers between devices: 96.1 us -> 139 us
  Pallas kernels: 459 us -> 433 us
    ppermute x27 -> x54, starting transfers between devices: 201 us -> 133 us  [the longest x38 101 us: over(): return lax.ppermute(x, 'dp', [(i, i ^ bit) for i in range(self.images)])]
    psum x1 -> x0, blocking collectives: 60.7 us -> none  [local(): late = lax.psum((after(early[-1], dw_one), rest), 'dp')]
    ppermute x27 -> x54, waiting for transfers between devices: 5.67 us -> 52.6 us  [the longest x38 48.2 us: over(): return lax.ppermute(x, 'dp', [(i, i ^ bit) for i in range(self.images)])]
    pallas_call x9 -> x12, Pallas kernels: 399 us -> 371 us  [the longest x1 233 us: attention(): pl.pallas_call(functools.partial(attention_kernel, unroll=unroll, back=ba...]
    reshape x5 -> x3, local copies, waits for them, and re-layouts: 15.2 us -> 1.68 us  [the longest x1 1.39 us: local(): mods = small[12:].reshape(plan.images, 2, ch)]
    slice x16 -> x14, local copies, waits for them, and re-layouts: 16.2 us -> 5.12 us  [the longest x2 0.88 us: local(): vectors[9:12].reshape(3 * ch, 1)]
    convert_element_type x7 -> x14, other arithmetic: 21.3 us -> 14.5 us  [the longest x1 4.33 us: local(): grad_heads = sum((a.astype(F32) for a in grad_heads)).astype(BF)]
    psum x2 -> x1, waiting for transfers between devices: 90.4 us -> 86.6 us  [local(): early = lax.psum(early, 'dp')]
  transfers between devices with their start and end apart: 29 -> 55, of which waited for: 3 -> 19; matrix products, arithmetic and copies ran while one was open for 9% -> 9% of each run, Pallas kernels for 18% -> 22%
where the time goes in v3:
time: 813 us; the launch traced here: 802 us
  Pallas kernels  433 us (53%)
  waiting for transfers between devices  139 us (17%)
  starting transfers between devices  133 us (16%)
  other arithmetic  37 us (5%)
  local copies, waits for them, and re-layouts  32.5 us (4%)
  between operations  16.3 us (2%)
  matrix products  10.7 us (1%)
    pallas_call x1, Pallas kernels, attention(): pl.pallas_call(functools.partial(attention_kernel, unroll=unroll, back=ba...  233 us
    ppermute x38, starting transfers between devices, over(): return lax.ppermute(x, 'dp', [(i, i ^ bit) for i in range(self.images)])  101 us
    pallas_call x4, Pallas kernels, conv_call(): pl.pallas_call(functools.partial(kernel, len(pieces)), out_shape=[*outs,...  93.9 us
    psum x1, waiting for transfers between devices, local(): early = lax.psum(early, 'dp')  86.6 us
    ppermute x38, waiting for transfers between devices, over(): return lax.ppermute(x, 'dp', [(i, i ^ bit) for i in range(self.images)])  48.2 us
    pallas_call x2, Pallas kernels, conv_weight_grad(): pl.pallas_call(functools.partial(weight_grad_kernel, len(pieces)), out_sh...  32.8 us
    ppermute x14, starting transfers between devices, got(): return lax.ppermute(x, ('dp', 'tensor'), self.far)  22.1 us
  transfers between devices with their start and end apart: 55, of which 19 were waited for; matrix products, arithmetic and copies ran while one was open for 9% of the time, Pallas kernels for 22%

profile of v3, /device:TPU:5, one launch (start us, length us, event | category | flops | bytes accessed | tf_op | source)
XLA Modules:
  0.0 802.2 jit_solution(7615098942631743552)
XLA Ops:
  7.3 2.1 collective-permute-start
  12.4 2.2 collective-permute-start.5
  14.5 2.0 fusion.15
  16.9 2.4 fusion
  20.6 9.0 %act_one.1 = (bf16[256,4096]{1,0:T(8,128)(2,1)}, f32[256,128]{1,0:T(8,128)}, bf16[256,4096]{1,0:T(8,128)(2,1)}) custom-call(s32[2]{0:T(128)} %pad_add_fusion.meta, bf16[256,4096]{1,0:T(8,128)(2,1)} %bitcast.92, bf16[256,4096]{1,0:T(8,128)(2,1)} %collective-permute-done.got_ref, f32[256,2]{1,0:T(8,128)} %slice_bitcast_fusion.5.par_ref.refs_2_), custom_call_target="tpu_custom_call" | custom-call | flops 20971520 | bytes 6291456 | tf_op jit(solution)/shard_map/act_one/pallas_call | solution.py:183
  29.5 17.2 %collective-permute-start.2 = (bf16[256,4096]{1,0:T(8,128)(2,1)}, bf16[256,4096]{1,0:T(8,128)(2,1)}, u32[]{:S(2)}, u32[]{:S(2)}) collective-permute-start(bf16[256,4096]{1,0:T(8,128)(2,1)} %get-tuple-element.71.refs_0_), channel_id=1, source_target_pairs={{0,2},{2,0},{4,6},{6,4},{8,10},{10,8},{12,14},{14,12},{16,18},{18,... | collective-permute-start | bytes 6291464 | tf_op jit(solution)/shard_map/ppermute | solution.py:873
  49.0 2.2 collective-permute-start.4
  51.2 21.9 %conv_one.1 = (bf16[256,4096]{1,0:T(8,128)(2,1)}, f32[256,128]{1,0:T(8,128)}, f32[256,4096]{1,0:T(8,128)}, bf16[256,4608]{1,0:T(8,128)(2,1)}) custom-call(s32[2]{0:T(128)} %pad_add_fusion.meta, bf16[256,4608]{1,0:T(8,128)(2,1)} %w_own.2, bf16[256,4608]{1,0:T(8,128)(2,1)} %collective-permute-done.5.w_got, bf16[256,4096]{1,0:T(8,128)(2,1)} %get-tuple-element.71.refs_0_, ...), custom_call_target="tpu_custom_call" | custom-call | flops 9663676416 | bytes 10753024 | tf_op jit(solution)/shard_map/conv_one/pallas_call | solution.py:255
  73.1 16.2 %collective-permute-start.7 = (bf16[256,4096]{1,0:T(8,128)(2,1)}, bf16[256,4096]{1,0:T(8,128)(2,1)}, u32[]{:S(2)}, u32[]{:S(2)}) collective-permute-start(bf16[256,4096]{1,0:T(8,128)(2,1)} %get-tuple-element.75.refs_0_), channel_id=1, source_target_pairs={{0,2},{2,0},{4,6},{6,4},{8,10},{10,8},{12,14},{14,12},{16,18},{18,... | collective-permute-start | bytes 6291464 | tf_op jit(solution)/shard_map/ppermute | solution.py:873
  91.3 2.0 collective-permute-start.10
  96.0 22.3 %conv_two.1 = (bf16[256,4096]{1,0:T(8,128)(2,1)}, f32[256,128]{1,0:T(8,128)}, f32[256,4096]{1,0:T(8,128)}, bf16[256,4608]{1,0:T(8,128)(2,1)}) custom-call(s32[2]{0:T(128)} %pad_add_fusion.meta, bf16[256,4608]{1,0:T(8,128)(2,1)} %w_own.3, bf16[256,4608]{1,0:T(8,128)(2,1)} %collective-permute-done.4.w_got, bf16[256,4096]{1,0:T(8,128)(2,1)} %get-tuple-element.75.refs_0_, ...), custom_call_target="tpu_custom_call" | custom-call | flops 9663676416 | bytes 12848128 | tf_op jit(solution)/shard_map/conv_two/pallas_call | solution.py:255
  118.3 4.7 fold.1.refs_0_.refs_5_
  123.0 4.9 grad_heads.1
  127.9 13.7 %collective-permute-start.11 = (bf16[256,4096]{1,0:T(8,128)(2,1)}, bf16[256,4096]{1,0:T(8,128)(2,1)}, u32[]{:S(2)}, u32[]{:S(2)}) collective-permute-start(bf16[256,4096]{1,0:T(8,128)(2,1)} %get-tuple-element.83), channel_id=1, source_target_pairs={{0,2},{2,0},{4,6},{6,4},{8,10},{10,8},{12,14},{14,12},{16,18},{18,... | collective-permute-start | bytes 6291464 | tf_op jit(solution)/shard_map/ppermute | solution.py:873
  148.5 4.3 add_convert_fusion
  152.8 7.7 qkv.1
  160.5 233.2 %attention.1 = (bf16[4,64,4096]{2,1,0:T(8,128)(2,1)}, bf16[4,64,4096]{2,1,0:T(8,128)(2,1)}, bf16[4,64,4096]{2,1,0:T(8,128)(2,1)}, bf16[4,64,4096]{2,1,0:T(8,128)...) custom-call(s32[1]{0:T(128)} %bitcast.19.lim_ref, bf16[3,4,64,4096]{3,2,1,0:T(8,128)(2,1)} %bitcast.118, ...), custom_call_target="tpu_custom_call" | custom-call | flops 115964116992 | bytes 16777216 | tf_op jit(solution)/shard_map/attention/pallas_call | solution.py:759
  393.8 7.5 grad_normed.1
  401.3 6.9 collective-permute-start.13
  409.2 3.0 collective-permute-done.50
  416.9 1.8 collective-permute-start.15
  418.7 10.2 %norm_three_back.1 = (f32[256,4096]{1,0:T(8,128)}, bf16[256,4096]{1,0:T(8,128)(2,1)}, f32[256,128]{1,0:T(8,128)}) custom-call(bf16[256,4096]{1,0:T(8,128)(2,1)} %get-tuple-element.88.refs_0_, bf16[256,4096]{1,0:T(8,128)(2,1)} %collective-permute-done.13.refs_1_, f32[256,4096]{1,0:T(8,128)} %get-tuple-element.93.refs_2_.refs_3_, ...), custom_call_target="tpu_custom_call" | custom-call | flops 20971520 | bytes 16777216 | tf_op jit(solution)/shard_map/norm_three_back/pallas_call | solution.py:490
  429.0 8.4 %qkv_grad.1 = (bf16[768,512]{1,0:T(8,128)(2,1)}, f32[768,128]{1,0:T(8,128)}) custom-call(s32[2]{0:T(128)} %pad_add_fusion.meta, bf16[256,4096]{1,0:T(8,128)(2,1)} %bitcast.122, bf16[256,4096]{1,0:T(8,128)(2,1)} %bitcast.124, bf16[256,4096]{1,0:T(8,128)(2,1)} %bitcast.126, bf16[256,4096]{1,0:T(8,128)(2,1)} %get-tuple-element.77.refs_0_.refs_3_, ...), custom_call_target="tpu_custom_call" | custom-call | flops 3221225472 | bytes 10485760 | tf_op jit(solution)/shard_map/qkv_grad/pallas_call | solution.py:628
  441.4 4.5 turn.3.w_own.w_got
  446.9 5.2 out_grad.1
  453.8 1.7 collective-permute-start.17
  455.5 6.5 output.1
  462.1 16.3 %conv_two_weight_grad.1 = bf16[256,4608]{1,0:T(8,128)(2,1)} custom-call(s32[2]{0:T(128)} %pad_add_fusion.meta, bf16[256,4096]{1,0:T(8,128)(2,1)} %get-tuple-element.102.grad_ref.refs_0_, bf16[256,4096]{1,0:T(8,128)(2,1)} %get-tuple-element.75.refs_0_, bf16[256,4096]{1,0:T(8,128)(2,1)} %collective-permute-done.7.refs_1_), custom_call_target="tpu_custom_call" | custom-call | flops 9663676416 | bytes 8650752 | tf_op jit(solution)/shard_map/conv_two_weight_grad/pallas_call | solution.py:413
  478.4 2.0 collective-permute-start.14
  480.4 25.1 %conv_two_back.1 = (bf16[256,4096]{1,0:T(8,128)(2,1)}, f32[256,128]{1,0:T(8,128)}) custom-call(s32[2]{0:T(128)} %pad_add_fusion.meta, bf16[256,4608]{1,0:T(8,128)(2,1)} %turn.3.w_own.w_got, bf16[256,4608]{1,0:T(8,128)(2,1)} %turn.3.w_own.w_got, bf16[256,4096]{1,0:T(8,128)(2,1)} %get-tuple-element.102.grad_ref.refs_0_, ...), custom_call_target="tpu_custom_call" | custom-call | flops 9663676416 | bytes 15078400 | tf_op jit(solution)/shard_map/conv_two_back/pallas_call | solution.py:255
  507.2 4.3 collective-permute-start.45
  513.1 2.0 collective-permute-start.20
  517.3 4.5 turn.2.w_own.w_got
  521.7 2.3 collective-permute-start.53
  525.1 3.8 convolution_convert_fusion
  530.1 4.9 collective-permute-start.21
  535.1 2.2 collective-permute-start.49
  540.9 2.0 fusion.25
  544.6 16.5 %conv_one_weight_grad.1 = bf16[256,4608]{1,0:T(8,128)(2,1)} custom-call(s32[2]{0:T(128)} %pad_add_fusion.meta, bf16[256,4096]{1,0:T(8,128)(2,1)} %get-tuple-element.109.grad_ref.refs_0_, bf16[256,4096]{1,0:T(8,128)(2,1)} %get-tuple-element.71.refs_0_, bf16[256,4096]{1,0:T(8,128)(2,1)} %collective-permute-done.2.refs_1_), custom_call_target="tpu_custom_call" | custom-call | flops 9663676416 | bytes 8650752 | tf_op jit(solution)/shard_map/conv_one_weight_grad/pallas_call | solution.py:413
  561.1 2.1 collective-permute-start.28
  563.2 24.7 %conv_one_back.1 = (bf16[256,4096]{1,0:T(8,128)(2,1)}, f32[256,128]{1,0:T(8,128)}) custom-call(s32[2]{0:T(128)} %pad_add_fusion.meta, bf16[256,4608]{1,0:T(8,128)(2,1)} %turn.2.w_own.w_got, bf16[256,4608]{1,0:T(8,128)(2,1)} %turn.2.w_own.w_got, bf16[256,4096]{1,0:T(8,128)(2,1)} %get-tuple-element.109.grad_ref.refs_0_, ...), custom_call_target="tpu_custom_call" | custom-call | flops 9663676416 | bytes 17172480 | tf_op jit(solution)/shard_map/conv_one_back/pallas_call | solution.py:255
  588.8 5.9 collective-permute-start.23
  594.7 2.8 collective-permute-done.23
  598.5 1.8 collective-permute-start.24
  604.2 2.3 collective-permute-done.25
  606.6 2.6 collective-permute-start.26
  609.2 2.3 pad_maximum_fusion
  613.5 4.7 collective-permute-start.27
  622.4 5.2 collective-permute-start.37
  631.9 12.6 %collective-permute-done.38 = bf16[32,4608]{1,0:T(8,128)(2,1)S(1)} collective-permute-done((bf16[32,4608]{1,0:T(8,128)(2,1)S(1)}, bf16[32,4608]{1,0:T(8,128)(2,1)S(1)}, u32[]{:S(2)}, u32[]{:S(2)}) %collective-permute-start.38) | collective-permute-done | bytes 294944 | tf_op jit(solution)/shard_map/ppermute | solution.py:873
  647.5 9.5 %collective-permute-done.39 = bf16[16,4608]{1,0:T(8,128)(2,1)S(1)} collective-permute-done((bf16[16,4608]{1,0:T(8,128)(2,1)S(1)}, bf16[16,4608]{1,0:T(8,128)(2,1)S(1)}, u32[]{:S(2)}, u32[]{:S(2)}) %collective-permute-start.39) | collective-permute-done | bytes 147488 | tf_op jit(solution)/shard_map/ppermute | solution.py:873
  659.0 2.3 collective-permute-start.32
  662.6 2.5 collective-permute-done.32
  665.1 2.5 collective-permute-start.33
  667.7 3.7 collective-permute-done.33
  671.4 2.2 collective-permute-start.34
  673.6 8.2 %collective-permute-done.42 = bf16[16,4608]{1,0:T(8,128)(2,1)S(1)} collective-permute-done((bf16[16,4608]{1,0:T(8,128)(2,1)S(1)}, bf16[16,4608]{1,0:T(8,128)(2,1)S(1)}, u32[]{:S(2)}, u32[]{:S(2)}) %collective-permute-start.42) | collective-permute-done | bytes 147488 | tf_op jit(solution)/shard_map/ppermute | solution.py:873
  683.4 2.3 select_convert_fusion
  685.7 86.6 %all-reduce.4.cloned.1.call-done = (bf16[2,256,2048]{2,1,0:T(8,128)(2,1)}, bf16[1024,512]{1,0:T(8,128)(2,1)}, bf16[256,4608]{1,0:T(8,128)(2,1)}) async-done(((bf16[2,256,2048]{2,1,0:T(8,128)(2,1)}, bf16[1024,512]{1,0:T(8,128)(2,1)}, bf16[256,4608]{1,0:T(8,128)(2,1)}), (bf16[2,256,2048]{2,1,0:T(8,128)(2,1)}, bf16[1024,512]{1,0:T(8,128)(2,1)}, bf16[256,4608]{1,0:T(8,128)(2,1)})) %all-reduce.4.cloned.1.call-update) | async-done | bytes 5505040 | tf_op jit(solution)/shard_map/psum | solution.py:1030
  773.2 1.8 slice_convert_fusion
  777.2 2.7 convert_element_type.168
  780.0 2.7 convert_element_type.169
  783.7 6.3 copy.148
  792.4 2.7 fusion.21
  (227 shorter events, 73.4 us)
Async XLA Ops:
  7.2 9.7 %copy-start = (bf16[1,260,2048]{2,1,0:T(8,128)(2,1)S(1)}, bf16[1,260,2048]{2,1,0:T(8,128)(2,1)}, u32[]{:S(2)}) copy-start(bf16[1,260,2048]{2,1,0:T(8,128)(2,1)} %param.26) | copy-start | bytes 3194884
  7.2 765.0 %all-reduce.4.cloned.1.call-start = ((), (), s32[]{:S(2)}) async-start(), calls=%async_computation | async-start | bytes 11010048 | tf_op jit(solution)/shard_map/psum | solution.py:1030
  7.3 13.3 %collective-permute-start = (bf16[256,4096]{1,0:T(8,128)(2,1)}, bf16[256,4096]{1,0:T(8,128)(2,1)}, u32[]{:S(2)}, u32[]{:S(2)}) collective-permute-start(bf16[256,4096]{1,0:T(8,128)(2,1)} %bitcast.91), channel_id=1, source_target_pairs={{1,2},{2,1},{5,6},{6,5},{9,10},{10,9},{13,14},{14,13},{17,18},{18,... | collective-permute-start | bytes 6291464 | tf_op jit(solution)/shard_map/ppermute | solution.py:867
  11.7 8.1 %collective-permute-start.1 = (f32[13,256]{0,1:T(8,128)S(1)}, f32[13,256]{0,1:T(8,128)S(1)}, u32[]{:S(2)}, u32[]{:S(2)}) collective-permute-start(f32[13,256]{0,1:T(8,128)S(1)} %copy.136), channel_id=1, source_target_pairs={{1,2},{2,1},{5,6},{6,5},{9,10},{10,9},{13,14},{14,13},{17,18},{18,... | collective-permute-start | bytes 39944 | tf_op jit(solution)/shard_map/ppermute | solution.py:867
  12.4 38.8 %collective-permute-start.5 = (bf16[256,4608]{1,0:T(8,128)(2,1)}, bf16[256,4608]{1,0:T(8,128)(2,1)}, u32[]{:S(2)}, u32[]{:S(2)}) collective-permute-start(bf16[256,4608]{1,0:T(8,128)(2,1)} %w_own.2), channel_id=1, source_target_pairs={{1,2},{2,1},{5,6},{6,5},{9,10},{10,9},{13,14},{14,13},{17,18},{18,... | collective-permute-start | bytes 7077896 | tf_op jit(solution)/shard_map/ppermute | solution.py:867
  29.5 21.7 %collective-permute-start.2 = (bf16[256,4096]{1,0:T(8,128)(2,1)}, bf16[256,4096]{1,0:T(8,128)(2,1)}, u32[]{:S(2)}, u32[]{:S(2)}) collective-permute-start(bf16[256,4096]{1,0:T(8,128)(2,1)} %get-tuple-element.71.refs_0_), channel_id=1, source_target_pairs={{0,2},{2,0},{4,6},{6,4},{8,10},{10,8},{12,14},{14,12},{16,18},{18,... | collective-permute-start | bytes 6291464 | tf_op jit(solution)/shard_map/ppermute | solution.py:873
  46.8 0.7 collective-permute-start.6
  49.0 40.4 %copy-start.14 = (bf16[256,512]{1,0:T(8,128)(2,1)S(1)}, bf16[256,512]{1,0:T(8,128)(2,1)}, u32[]{:S(2)}) copy-start(bf16[256,512]{1,0:T(8,128)(2,1)} %param.44) | copy-start | bytes 786436
  49.0 47.0 %collective-permute-start.4 = (bf16[256,4608]{1,0:T(8,128)(2,1)}, bf16[256,4608]{1,0:T(8,128)(2,1)}, u32[]{:S(2)}, u32[]{:S(2)}) collective-permute-start(bf16[256,4608]{1,0:T(8,128)(2,1)} %w_own.3), channel_id=1, source_target_pairs={{1,2},{2,1},{5,6},{6,5},{9,10},{10,9},{13,14},{14,13},{17,18},{18,... | collective-permute-start | bytes 7077896 | tf_op jit(solution)/shard_map/ppermute | solution.py:867
  73.1 22.9 %collective-permute-start.7 = (bf16[256,4096]{1,0:T(8,128)(2,1)}, bf16[256,4096]{1,0:T(8,128)(2,1)}, u32[]{:S(2)}, u32[]{:S(2)}) collective-permute-start(bf16[256,4096]{1,0:T(8,128)(2,1)} %get-tuple-element.75.refs_0_), channel_id=1, source_target_pairs={{0,2},{2,0},{4,6},{6,4},{8,10},{10,8},{12,14},{14,12},{16,18},{18,... | collective-permute-start | bytes 6291464 | tf_op jit(solution)/shard_map/ppermute | solution.py:873
  90.6 2.8 collective-permute-start.3
  91.3 27.0 %collective-permute-start.10 = (bf16[256,4096]{1,0:T(8,128)(2,1)}, bf16[256,4096]{1,0:T(8,128)(2,1)}, u32[]{:S(2)}, u32[]{:S(2)}) collective-permute-start(bf16[256,4096]{1,0:T(8,128)(2,1)} %bitcast.18.own_ref), channel_id=1, source_target_pairs={{1,2},{2,1},{5,6},{6,5},{9,10},{10,9},{13,14},{14,13},{17,18},{18,... | collective-permute-start | bytes 6291464 | tf_op jit(solution)/shard_map/ppermute | solution.py:867
  127.9 18.5 %copy-start.4 = (bf16[1024,512]{1,0:T(8,128)(2,1)S(1)}, bf16[1024,512]{1,0:T(8,128)(2,1)}, u32[]{:S(2)}) copy-start(bf16[1024,512]{1,0:T(8,128)(2,1)} %copy-done.3) | copy-start | bytes 3145732
  127.9 20.6 %collective-permute-start.11 = (bf16[256,4096]{1,0:T(8,128)(2,1)}, bf16[256,4096]{1,0:T(8,128)(2,1)}, u32[]{:S(2)}, u32[]{:S(2)}) collective-permute-start(bf16[256,4096]{1,0:T(8,128)(2,1)} %get-tuple-element.83), channel_id=1, source_target_pairs={{0,2},{2,0},{4,6},{6,4},{8,10},{10,8},{12,14},{14,12},{16,18},{18,... | collective-permute-start | bytes 6291464 | tf_op jit(solution)/shard_map/ppermute | solution.py:873
  141.6 11.2 %collective-permute-start.8 = (bf16[256,4096]{1,0:T(8,128)(2,1)}, bf16[256,4096]{1,0:T(8,128)(2,1)}, u32[]{:S(2)}, u32[]{:S(2)}) collective-permute-start(bf16[256,4096]{1,0:T(8,128)(2,1)} %get-tuple-element.77.refs_0_.refs_3_), channel_id=1, source_target_pairs={{0,2},{2,0},{4,6},{6,4},{8,10},{10,8},{12,14},{14,12},{16,18},{18,... | collective-permute-start | bytes 6291464 | tf_op jit(solution)/shard_map/ppermute | solution.py:873
  141.6 3.7 collective-permute-start.9
  393.8 14.4 %copy-start.19 = (bf16[1,2048]{1,0:T(2,128)(2,1)S(1)}, bf16[1,2048]{1,0:T(2,128)(2,1)}, u32[]{:S(2)}) copy-start(bf16[1,2048]{1,0:T(2,128)(2,1)} %param.25) | copy-start | bytes 12292
  401.3 17.4 %collective-permute-start.13 = (bf16[256,4096]{1,0:T(8,128)(2,1)}, bf16[256,4096]{1,0:T(8,128)(2,1)}, u32[]{:S(2)}, u32[]{:S(2)}) collective-permute-start(bf16[256,4096]{1,0:T(8,128)(2,1)} %get-tuple-element.89), channel_id=1, source_target_pairs={{0,2},{2,0},{4,6},{6,4},{8,10},{10,8},{12,14},{14,12},{16,18},{18,... | collective-permute-start | bytes 6291464 | tf_op jit(solution)/shard_map/ppermute | solution.py:873
  408.2 31.8 %collective-permute-start.18 = (bf16[256,4608]{1,0:T(8,128)(2,1)}, bf16[256,4608]{1,0:T(8,128)(2,1)}, u32[]{:S(2)}, u32[]{:S(2)}) collective-permute-start(bf16[256,4608]{1,0:T(8,128)(2,1)} %get-tuple-element.101.own_ref), channel_id=1, source_target_pairs={{0,2},{2,0},{4,6},{6,4},{8,10},{10,8},{12,14},{14,12},{16,18},{18,... | collective-permute-start | bytes 7077896 | tf_op jit(solution)/shard_map/ppermute | solution.py:873
  408.4 3.8 collective-permute-start.50
  408.9 38.0 %collective-permute-start.12 = (bf16[256,4096]{1,0:T(8,128)(2,1)}, bf16[256,4096]{1,0:T(8,128)(2,1)}, u32[]{:S(2)}, u32[]{:S(2)}) collective-permute-start(bf16[256,4096]{1,0:T(8,128)(2,1)} %bitcast.86), channel_id=1, source_target_pairs={{0,2},{2,0},{4,6},{6,4},{8,10},{10,8},{12,14},{14,12},{16,18},{18,... | collective-permute-start | bytes 6291464 | tf_op jit(solution)/shard_map/ppermute | solution.py:873
  412.2 3.2 collective-permute-start.51
  415.5 13.4 %copy-start.13 = (bf16[16,2048]{1,0:T(8,128)(2,1)}, bf16[16,2048]{1,0:T(8,128)(2,1)S(1)}, u32[]{:S(2)}) copy-start(bf16[16,2048]{1,0:T(8,128)(2,1)S(1)} %fusion.29) | copy-start | bytes 196612
  415.5 91.7 %collective-permute-start.52 = (bf16[16,2048]{1,0:T(8,128)(2,1)S(1)}, bf16[16,2048]{1,0:T(8,128)(2,1)S(1)}, u32[]{:S(2)}, u32[]{:S(2)}) collective-permute-start(bf16[16,2048]{1,0:T(8,128)(2,1)S(1)} %fusion.29), channel_id=1, source_target_pairs={{0,8},{2,10},{4,12},{6,14},{8,0},{10,2},{12,4},{14,6},{16,24},{18,... | collective-permute-start | bytes 196616 | tf_op jit(solution)/shard_map/ppermute | solution.py:873
  416.9 98.2 %collective-permute-start.15 = (bf16[256,4608]{1,0:T(8,128)(2,1)}, bf16[256,4608]{1,0:T(8,128)(2,1)}, u32[]{:S(2)}, u32[]{:S(2)}) collective-permute-start(bf16[256,4608]{1,0:T(8,128)(2,1)} %get-tuple-element.94.own_ref), channel_id=1, source_target_pairs={{0,2},{2,0},{4,6},{6,4},{8,10},{10,8},{12,14},{14,12},{16,18},{18,... | collective-permute-start | bytes 7077896 | tf_op jit(solution)/shard_map/ppermute | solution.py:873
  428.9 9.7 %copy-start.16 = (bf16[4,64,384]{2,1,0:T(8,128)(2,1)S(1)}, bf16[4,64,384]{2,1,0:T(8,128)(2,1)}, u32[]{:S(2)}) copy-start(bf16[4,64,384]{2,1,0:T(8,128)(2,1)} %get-tuple-element.95) | copy-start | bytes 589828
  428.9 9.9 %copy-start.15 = (bf16[4,64,384]{2,1,0:T(8,128)(2,1)S(1)}, bf16[4,64,384]{2,1,0:T(8,128)(2,1)}, u32[]{:S(2)}) copy-start(bf16[4,64,384]{2,1,0:T(8,128)(2,1)} %get-tuple-element.96) | copy-start | bytes 589828
  428.9 49.5 %collective-permute-start.19 = (bf16[256,4096]{1,0:T(8,128)(2,1)}, bf16[256,4096]{1,0:T(8,128)(2,1)}, u32[]{:S(2)}, u32[]{:S(2)}) collective-permute-start(bf16[256,4096]{1,0:T(8,128)(2,1)} %get-tuple-element.102.grad_ref.refs_0_), channel_id=1, source_target_pairs={{0,2},{2,0},{4,6},{6,4},{8,10},{10,8},{12,14},{14,12},{16,18},{18,... | collective-permute-start | bytes 6291464 | tf_op jit(solution)/shard_map/ppermute | solution.py:873
  440.0 84.9 %collective-permute-start.16 = (bf16[2,256,384]{1,2,0:T(8,128)(2,1)S(1)}, bf16[2,256,384]{1,2,0:T(8,128)(2,1)}, u32[]{:S(2)}, u32[]{:S(2)}) collective-permute-start(bf16[2,256,384]{1,2,0:T(8,128)(2,1)S(1)} %pad_maximum_fusion.3), channel_id=1, source_target_pairs={{1,2},{2,1},{5,6},{6,5},{9,10},{10,9},{13,14},{14,13},{17,18},{18,... | collective-permute-start | bytes 1179656 | tf_op jit(solution)/shard_map/ppermute | solution.py:867
  453.8 75.0 %collective-permute-start.17 = (bf16[1024,512]{1,0:T(8,128)(2,1)}, bf16[1024,512]{1,0:T(8,128)(2,1)}, u32[]{:S(2)}, u32[]{:S(2)}) collective-permute-start(bf16[1024,512]{1,0:T(8,128)(2,1)} %constant_dynamic-update-slice_fusion), channel_id=1, source_target_pairs={{1,2},{2,1},{5,6},{6,5},{9,10},{10,9},{13,14},{14,13},{17,18},{18,... | collective-permute-start | bytes 3145736 | tf_op jit(solution)/shard_map/ppermute | solution.py:867
  478.4 58.8 %collective-permute-start.14 = (bf16[256,4096]{1,0:T(8,128)(2,1)}, bf16[256,4096]{1,0:T(8,128)(2,1)}, u32[]{:S(2)}, u32[]{:S(2)}) collective-permute-start(bf16[256,4096]{1,0:T(8,128)(2,1)} %output.1), channel_id=1, source_target_pairs={{1,2},{2,1},{5,6},{6,5},{9,10},{10,9},{13,14},{14,13},{17,18},{18,... | collective-permute-start | bytes 6291464 | tf_op jit(solution)/shard_map/ppermute | solution.py:867
  507.2 5.8 collective-permute-start.45
  513.1 29.9 %collective-permute-start.20 = (bf16[256,4608]{1,0:T(8,128)(2,1)}, bf16[256,4608]{1,0:T(8,128)(2,1)}, u32[]{:S(2)}, u32[]{:S(2)}) collective-permute-start(bf16[256,4608]{1,0:T(8,128)(2,1)} %conv_two_weight_grad.1), channel_id=1, source_target_pairs={{1,2},{2,1},{5,6},{6,5},{9,10},{10,9},{13,14},{14,13},{17,18},{18,... | collective-permute-start | bytes 7077896 | tf_op jit(solution)/shard_map/ppermute | solution.py:867
  515.1 6.6 collective-permute-start.46
  521.7 78.5 %collective-permute-start.53 = (bf16[16,2048]{1,0:T(8,128)(2,1)S(1)}, bf16[16,2048]{1,0:T(8,128)(2,1)}, u32[]{:S(2)}, u32[]{:S(2)}) collective-permute-start(bf16[16,2048]{1,0:T(8,128)(2,1)S(1)} %add.225), channel_id=1, source_target_pairs={{0,16},{2,18},{4,20},{6,22},{8,24},{10,26},{12,28},{14,30},{16,0},... | collective-permute-start | bytes 196616 | tf_op jit(solution)/shard_map/ppermute | solution.py:873
  524.9 4.0 collective-permute-start.47
  528.9 6.2 collective-permute-start.48
  530.1 33.1 %collective-permute-start.21 = (bf16[256,4096]{1,0:T(8,128)(2,1)}, bf16[256,4096]{1,0:T(8,128)(2,1)}, u32[]{:S(2)}, u32[]{:S(2)}) collective-permute-start(bf16[256,4096]{1,0:T(8,128)(2,1)} %get-tuple-element.109.grad_ref.refs_0_), channel_id=1, source_target_pairs={{0,2},{2,0},{4,6},{6,4},{8,10},{10,8},{12,14},{14,12},{16,18},{18,... | collective-permute-start | bytes 6291464 | tf_op jit(solution)/shard_map/ppermute | solution.py:873
  535.1 3.8 collective-permute-start.49
  561.1 60.7 %collective-permute-start.28 = (bf16[256,4608]{1,0:T(8,128)(2,1)}, bf16[256,4608]{1,0:T(8,128)(2,1)}, u32[]{:S(2)}, u32[]{:S(2)}) collective-permute-start(bf16[256,4608]{1,0:T(8,128)(2,1)} %conv_one_weight_grad.1), channel_id=1, source_target_pairs={{1,2},{2,1},{5,6},{6,5},{9,10},{10,9},{13,14},{14,13},{17,18},{18,... | collective-permute-start | bytes 7077896 | tf_op jit(solution)/shard_map/ppermute | solution.py:867
  563.2 31.5 %copy-start.17 = (bf16[16,2,256]{2,1,0:T(2,128)(2,1)S(1)}, bf16[16,2,256]{2,1,0:T(2,128)(2,1)}, u32[]{:S(2)}) copy-start(bf16[16,2,256]{2,1,0:T(2,128)(2,1)} %get-tuple-element.262) | copy-start | bytes 49156
  588.8 8.8 %collective-permute-start.23 = (f32[2,256]{0,1:T(8,128)S(1)}, f32[2,256]{0,1:T(8,128)S(1)}, u32[]{:S(2)}, u32[]{:S(2)}) collective-permute-start(f32[2,256]{0,1:T(8,128)S(1)} %slice_bitcast_fusion.2), channel_id=1, source_target_pairs={{0,1},{1,0},{2,3},{3,2},{4,5},{5,4},{6,7},{7,6},{8,9},{9,8},{10,11... | collective-permute-start | bytes 6152 | tf_op jit(solution)/shard_map/ppermute | solution.py:885
  598.5 4.1 collective-permute-start.24
  602.7 3.9 collective-permute-start.25
  606.6 6.3 collective-permute-start.26
  613.5 7.4 collective-permute-start.27
  620.0 63.4 %collective-permute-start.22 = (bf16[256,4096]{1,0:T(8,128)(2,1)}, bf16[256,4096]{1,0:T(8,128)(2,1)S(1)}, u32[]{:S(2)}, u32[]{:S(2)}) collective-permute-start(bf16[256,4096]{1,0:T(8,128)(2,1)} %get-tuple-element.112), channel_id=1, source_target_pairs={{1,2},{2,1},{5,6},{6,5},{9,10},{10,9},{13,14},{14,13},{17,18},{18,... | collective-permute-start | bytes 6291464 | tf_op jit(solution)/shard_map/ppermute | solution.py:867
  622.4 6.8 collective-permute-start.37
  628.3 2.1 collective-permute-start.29
  629.3 15.2 %collective-permute-start.38 = (bf16[32,4608]{1,0:T(8,128)(2,1)S(1)}, bf16[32,4608]{1,0:T(8,128)(2,1)S(1)}, u32[]{:S(2)}, u32[]{:S(2)}) collective-permute-start(bf16[32,4608]{1,0:T(8,128)(2,1)S(1)} %constant_dynamic-slice_fusion.2), channel_id=1, source_target_pairs={{0,8},{2,10},{4,12},{6,14},{8,0},{10,2},{12,4},{14,6},{16,24},{18,... | collective-permute-start | bytes 884744 | tf_op jit(solution)/shard_map/ppermute | solution.py:873
  630.6 15.4 %collective-permute-start.30 = (bf16[32,4608]{1,0:T(8,128)(2,1)S(1)}, bf16[32,4608]{1,0:T(8,128)(2,1)S(1)}, u32[]{:S(2)}, u32[]{:S(2)}) collective-permute-start(bf16[32,4608]{1,0:T(8,128)(2,1)S(1)} %constant_dynamic-slice_fusion.6), channel_id=1, source_target_pairs={{0,4},{2,6},{4,0},{6,2},{8,12},{10,14},{12,8},{14,10},{16,20},{18,... | collective-permute-start | bytes 884744 | tf_op jit(solution)/shard_map/ppermute | solution.py:873
  644.6 38.7 %copy-start.10 = (bf16[256,4096]{1,0:T(8,128)(2,1)S(1)}, bf16[256,4096]{1,0:T(8,128)(2,1)}, u32[]{:S(2)}) copy-start(bf16[256,4096]{1,0:T(8,128)(2,1)} %get-tuple-element.112) | copy-start | bytes 6291460
  644.7 12.4 %collective-permute-start.39 = (bf16[16,4608]{1,0:T(8,128)(2,1)S(1)}, bf16[16,4608]{1,0:T(8,128)(2,1)S(1)}, u32[]{:S(2)}, u32[]{:S(2)}) collective-permute-start(bf16[16,4608]{1,0:T(8,128)(2,1)S(1)} %constant_dynamic-slice_fusion.1), channel_id=1, source_target_pairs={{0,16},{2,18},{4,20},{6,22},{8,24},{10,26},{12,28},{14,30},{16,0},... | collective-permute-start | bytes 442376 | tf_op jit(solution)/shard_map/ppermute | solution.py:873
  646.1 12.8 %collective-permute-start.31 = (bf16[16,4608]{1,0:T(8,128)(2,1)S(1)}, bf16[16,4608]{1,0:T(8,128)(2,1)S(1)}, u32[]{:S(2)}, u32[]{:S(2)}) collective-permute-start(bf16[16,4608]{1,0:T(8,128)(2,1)S(1)} %constant_dynamic-slice_fusion.5), channel_id=1, source_target_pairs={{0,8},{2,10},{4,12},{6,14},{8,0},{10,2},{12,4},{14,6},{16,24},{18,... | collective-permute-start | bytes 442376 | tf_op jit(solution)/shard_map/ppermute | solution.py:873
  657.1 4.1 collective-permute-start.40
  659.0 6.1 collective-permute-start.32
  661.3 6.3 collective-permute-start.41
  665.1 6.3 collective-permute-start.33
  667.6 14.2 %collective-permute-start.42 = (bf16[16,4608]{1,0:T(8,128)(2,1)S(1)}, bf16[16,4608]{1,0:T(8,128)(2,1)S(1)}, u32[]{:S(2)}, u32[]{:S(2)}) collective-permute-start(bf16[16,4608]{1,0:T(8,128)(2,1)S(1)} %maximum_select_fusion.7), channel_id=1, source_target_pairs={{0,16},{2,18},{4,20},{6,22},{8,24},{10,26},{12,28},{14,30},{16,0},... | collective-permute-start | bytes 442376 | tf_op jit(solution)/shard_map/ppermute | solution.py:873
  671.4 10.6 %collective-permute-start.34 = (bf16[16,4608]{1,0:T(8,128)(2,1)S(1)}, bf16[16,4608]{1,0:T(8,128)(2,1)S(1)}, u32[]{:S(2)}, u32[]{:S(2)}) collective-permute-start(bf16[16,4608]{1,0:T(8,128)(2,1)S(1)} %maximum_select_fusion.6), channel_id=1, source_target_pairs={{0,8},{2,10},{4,12},{6,14},{8,0},{10,2},{12,4},{14,6},{16,24},{18,... | collective-permute-start | bytes 442376 | tf_op jit(solution)/shard_map/ppermute | solution.py:873
  681.9 90.4 %collective-permute-start.43 = (bf16[32,4608]{1,0:T(8,128)(2,1)S(1)}, bf16[32,4608]{1,0:T(8,128)(2,1)S(1)}, u32[]{:S(2)}, u32[]{:S(2)}) collective-permute-start(bf16[32,4608]{1,0:T(8,128)(2,1)S(1)} %maximum_select_fusion.5), channel_id=1, source_target_pairs={{0,8},{2,10},{4,12},{6,14},{8,0},{10,2},{12,4},{14,6},{16,24},{18,... | collective-permute-start | bytes 884744 | tf_op jit(solution)/shard_map/ppermute | solution.py:873
  682.1 107.9 %collective-permute-start.35 = (bf16[32,4608]{1,0:T(8,128)(2,1)S(1)}, bf16[32,4608]{1,0:T(8,128)(2,1)S(1)}, u32[]{:S(2)}, u32[]{:S(2)}) collective-permute-start(bf16[32,4608]{1,0:T(8,128)(2,1)S(1)} %maximum_select_fusion.4), channel_id=1, source_target_pairs={{0,4},{2,6},{4,0},{6,2},{8,12},{10,14},{12,8},{14,10},{16,20},{18,... | collective-permute-start | bytes 884744 | tf_op jit(solution)/shard_map/ppermute | solution.py:873
  772.4 17.9 %collective-permute-start.44 = (bf16[64,4608]{1,0:T(8,128)(2,1)S(1)}, bf16[64,4608]{1,0:T(8,128)(2,1)}, u32[]{:S(2)}, u32[]{:S(2)}) collective-permute-start(bf16[64,4608]{1,0:T(8,128)(2,1)S(1)} %maximum_select_fusion.3), channel_id=1, source_target_pairs={{0,2},{2,0},{4,6},{6,4},{8,10},{10,8},{12,14},{14,12},{16,18},{18,... | collective-permute-start | bytes 1769480 | tf_op jit(solution)/shard_map/ppermute | solution.py:873
  790.1 2.1 collective-permute-start.36
  (13 other events, 64.7 us)
Sparse Core Ops, SparseCore 0:
  620.1 152.1 all-reduce.3

commit v4 on v3

--- a/solution.py
+++ b/solution.py
@@ -14,10 +14,12 @@
 HW = 4096
 CTX = 260
 CTXP = 384
+CTX_EMB = 2048
 BLOCK = 256
 KEYS = 4608
 PAD = 128
 FILL = 32
+SCALE = 100
 EPSILON = 1e-05
 NEG_FILL = -1e30
 F32 = jnp.float32
@@ -51,7 +53,9 @@
 
 
 def cost(flops, nbytes, transcendentals=0):
-    return pl.CostEstimate(flops=flops, bytes_accessed=nbytes, transcendentals=transcendentals)
+    return pl.CostEstimate(
+        flops=flops // SCALE, bytes_accessed=nbytes // SCALE, transcendentals=transcendentals // SCALE
+    )
 
 
 def struct(shape, dtype):
@@ -640,10 +644,11 @@
 
 
 def attention_kernel(
-    lim_ref, q_ref, k_ref, v_ref, kc_ref, vc_ref, g_ref,
-    o_ref, dq_ref, dk_ref, dv_ref, dkc_ref, dvc_ref,
-    kt, vt, kn, vn, s_even, s_odd, p_sc, tops, o_acc, dk_acc, dv_acc, *, unroll, back,
+    n_grads, lim_ref, q_ref, k_ref, v_ref, kc_ref, vc_ref, *refs, unroll, back,
 ):
+    g_refs, refs = refs[:n_grads], refs[n_grads:]
+    o_ref, dq_ref, dk_ref, dv_ref, dkc_ref, dvc_ref = refs[:6]
+    kt, vt, kn, vn, s_even, s_odd, p_sc, tops, o_acc, dk_acc, dv_acc = refs[6:]
     step, last = pl.program_id(1), pl.num_programs(1) - 1
     width = q_ref.shape[-1]
     blocks = KEYS // BLOCK
@@ -712,7 +717,9 @@
     inverse = 1.0 / jnp.sum(total, axis=0, keepdims=True)
     mixed = o_acc[...] * inverse
     o_ref[0] = mixed.astype(BF)
-    grad = g_ref[0].astype(F32)
+    grad = sum(g_ref[0].astype(F32) for g_ref in g_refs)
+    if n_grads > 1:
+        grad = grad.astype(BF).astype(F32)
     delta = jnp.sum(grad * mixed, axis=0, keepdims=True)
     dq = jnp.zeros((HEAD_DIM, width), F32)
     none = jnp.zeros((HEAD_DIM, width), BF)
@@ -757,7 +764,7 @@
 
     big, small = struct((heads, HEAD_DIM, HW), BF), struct((heads, HEAD_DIM, CTXP), BF)
     return pl.pallas_call(
-        functools.partial(attention_kernel, unroll=unroll, back=back),
+        functools.partial(attention_kernel, len(grads), unroll=unroll, back=back),
         grid=(heads, HW // width),
         in_specs=[
             pl.BlockSpec(memory_space=pltpu.SMEM),
@@ -766,8 +773,8 @@
             part(2, HW, False),
             part(0, CTXP, False),
             part(1, CTXP, False),
-            row(width, True),
-        ],
+        ]
+        + [row(width, True)] * len(grads),
         out_specs=[
             row(width, True),
             row(width, True),
@@ -795,7 +802,7 @@
             24 * heads * HW * keys * HEAD_DIM, heads * HEAD_DIM * 8 * HW * 2, heads * HW * keys
         ),
         name="attention",
-    )(limit, qkv, qkv, qkv, ctx_kv, ctx_kv, grads)
+    )(limit, qkv, qkv, qkv, ctx_kv, ctx_kv, *grads)
 
 
 class Alone:
@@ -931,35 +938,39 @@
     meta = plan.meta()
     moved = plan.parts == 2
 
+    emb_act = jax.nn.silu(embedding.astype(F32)).astype(BF)
+    scale_shift = (
+        jnp.einsum("ie,teo->to", emb_act, emb_weight, preferred_element_type=F32) + emb_bias
+    )
     length_row = jnp.broadcast_to(lengths.astype(F32)[:, None], (1, ch))
     vectors = jnp.concatenate(
         [
             jnp.stack([norm1_gain, norm1_bias, conv1_bias, norm2_gain, norm2_bias]),
+            scale_shift,
             jnp.stack([conv2_bias, norm3_gain, norm3_bias, out_bias]),
             qkv_bias,
             length_row,
         ]
     )
-    vectors = plan.pick(vectors, plan.got(vectors))
     f_own = features.reshape(ch, pixels)
     f_got = plan.got(f_own)
-    w1_got = plan.got(conv1_weight)
-    emb_act = jax.nn.silu(embedding.astype(F32)).astype(BF)
-    scale_shift = (
-        jnp.einsum("ie,teo->to", emb_act, emb_weight, preferred_element_type=F32) + emb_bias
-    )
+    vectors, w1_own = after(scale_shift, vectors, conv1_weight)
+    vectors = plan.pick(vectors, plan.got(vectors))
+    w1_got = plan.got(w1_own)
     ctx_kv = (
         jnp.einsum("toe,ne->ton", context_weight, context[0], preferred_element_type=F32)
         + context_bias[:, :, None]
     ).astype(BF)
     ctx_kv = jnp.pad(ctx_kv, ((0, 0), (0, 0), (0, CTXP - CTX)))
-    vectors, ctx_kv = after(scale_shift, vectors, ctx_kv)
-    scale_shift = plan.pick(scale_shift, plan.got(scale_shift))
-    length = vectors[12, :1].astype(jnp.int32)
-    par_one = vectors[0:2].T
+    emb_all = jnp.where(
+        jnp.arange(plan.images)[:, None] == lax.axis_index("dp"), emb_act, jnp.zeros_like(emb_act)
+    )
+    emb_all = plan.everywhere(emb_all)
+    length = vectors[14, :1].astype(jnp.int32)
+    par_one, par_two, par_three = vectors[0:2].T, vectors[2:7].T, vectors[7:10].T
+    w2_got = plan.got(after(vectors, conv2_weight))
     act_one, stat_one, f_low = first_activation(meta, f_own, f_got, par_one)
     full_one = plan.gather(act_one)
-    w2_got = plan.got(after(act_one, conv2_weight))
     mats_own = jnp.concatenate([qkv_weight.reshape(3 * ch, C), out_weight])
     mats_own, ctx_own, cot_own = after(
         full_one[-1], mats_own, ctx_kv, cotangent.reshape(ch, pixels)
@@ -967,7 +978,7 @@
     mats_got, ctx_got = plan.got(mats_own), plan.got(ctx_own)
     cot_got = plan.got(cot_own)
 
-    par_two = jnp.concatenate([vectors[2:5], scale_shift]).T
+    par_two = after(emb_all, par_two)
     low, stat, wide = struct((ch, HW), BF), struct((ch, 128), F32), struct((ch, HW), F32)
     weight = struct((ch, 9 * C), BF)
     act_two, stat_two, conv_one, w1 = conv_call(
@@ -975,28 +986,25 @@
         [low, stat], [wide, weight], [], "conv_one",
     )
     full_two = plan.gather(act_two)
-    par_three = vectors[5:8].T
     normed, stat_three, hidden, w2 = conv_call(
         conv_two_kernel, meta, (conv2_weight, w2_got), full_two, (par_three, f_low), (),
         [low, stat], [wide, weight], [], "conv_two",
     )
     full_three = plan.gather(normed)
+    mats_got, ctx_got, cot_got = after(normed, mats_got, ctx_got, cot_got)
     mats = plan.pick(mats_own, mats_got)
     w_qkv, w_out = mats[: 3 * ch], mats[3 * ch :]
-    qkv = inputs_product(meta, w_qkv, full_three, vectors[9:12].reshape(3 * ch, 1), name="qkv")
-    cot = folded(meta, *after(normed, cot_own, cot_got))
+    cot = folded(meta, cot_own, cot_got)
     grad_heads = plan.scatter(
         parts_product(meta, w_out.T, (cot,), plan.parts, name="grad_heads")
     )
-    turned_one = plan.turn(meta, w1)
-    turned_two = plan.turn(meta, w2)
-    grad_heads = sum(a.astype(F32) for a in grad_heads).astype(BF)
+    qkv = inputs_product(meta, w_qkv, full_three, vectors[11:14].reshape(3 * ch, 1), name="qkv")
     ctx_kv = plan.pick(ctx_own, ctx_got)
     mixed, dq, dk, dv, dkc, dvc = attention(
         4 + length,
         qkv.reshape(3, heads, HEAD_DIM, HW),
         ctx_kv.reshape(2, heads, HEAD_DIM, CTXP),
-        grad_heads.reshape(heads, HEAD_DIM, HW),
+        [a.reshape(heads, HEAD_DIM, HW) for a in grad_heads],
     )
 
     flat = lambda a: a.reshape(ch, HW)
@@ -1007,6 +1015,7 @@
     full_heads = plan.gather(flat(mixed))
     ctx_own = jnp.concatenate([a.reshape(1, ch, CTXP) for a in (dkc, dvc)])
     ctx_got = plan.got(ctx_own)
+    turned_two = plan.turn(meta, after(mixed, w2))
     dw_qkv, db_qkv = outer(meta, (dq, dk, dv), full_three, name="qkv_grad")
     dw_out, _ = outer(meta, (cot,), full_heads, name="out_grad")
     mats_own = jnp.concatenate([dw_qkv, dw_out])
@@ -1023,11 +1032,15 @@
         (conv_one,), [low, stat], [], [pltpu.VMEM((ch, HW), F32)], "conv_two_back",
     )
     full_grad_one = plan.gather(grad_one)
-    mats = plan.pick(mats_own, after(dw_two, mats_got))
-    early = (dw_ctx, mats, plan.pick(dw_two, after(grad_one, two_got)))
+    turned_one = plan.turn(meta, after(mixed, w1))
+    mats = plan.pick(mats_own, mats_got)
+    dw_two = plan.pick(dw_two, after(grad_one, two_got))
+    early = jnp.concatenate(
+        [dw_ctx[0], dw_ctx[1], *(mats[t * ch : (t + 1) * ch] for t in range(4)), dw_two], 1
+    )
     held = after(early, grad_one)
+    early = lax.psum_scatter(early, "dp", scatter_dimension=0, tiled=True)
     dw_one = conv_weight_grad(meta, held, full_one, "conv_one_weight_grad")
-    early = lax.psum(early, "dp")
     one_got = plan.got(dw_one)
     full_grad_one = after(dw_one, *full_grad_one) if moved else full_grad_one
     input_grad, sums_one = conv_call(
@@ -1037,16 +1050,15 @@
         [pltpu.VMEM((ch, HW), F32)], "conv_one_back",
     )
     input_got = plan.got(input_grad)
+
     output = output_product(
-        meta, w_out, full_heads, vectors[8].reshape(ch, 1), after(grad_hidden, hidden)
-    )
-    output = plan.pick(output, plan.got(output))
-
+        meta, w_out, full_heads, vectors[10].reshape(ch, 1), after(input_grad, hidden)
+    )
+    output_got = plan.got(output)
+    early, dw_one, one_got, sums_one = after((output, input_got), early, dw_one, one_got, sums_one)
+    dw_one, one_got, sums_one = after(early, dw_one, one_got, sums_one)
+    early = lax.all_gather(early, "dp", axis=0, tiled=True)
     dw_one = plan.sum_owned(plan.pick(dw_one, one_got))
-    emb_all = jnp.where(
-        jnp.arange(plan.images)[:, None] == lax.axis_index("dp"), emb_act, jnp.zeros_like(emb_act)
-    )
-    emb_all = plan.everywhere(emb_all)
     ctx_sums = jnp.sum(ctx_own.astype(F32), axis=2)
     sums_two = sums_two[:, :5].T
     own_mod = sums_two[2:4].astype(BF).astype(F32)
@@ -1061,11 +1073,12 @@
                 sums_two[:2],
                 sums_two[4:5],
                 ctx_sums,
+                sums_one[:, :2].T,
                 mods,
             ]
         )
     )
-    mods = small[12:].reshape(plan.images, 2, ch)
+    mods = small[14:].reshape(plan.images, 2, ch)
     mods_low = mods.astype(BF)
     dw_emb = jnp.stack(
         [
@@ -1073,15 +1086,19 @@
             for t in range(2)
         ]
     )
-    last = plan.total(sums_one[:, :2].T)
     input_grad = plan.pick(input_grad, input_got).astype(F32)
-    dw_ctx, mats, dw_two = after((dw_one, last, input_grad), *early)
+    output = plan.pick(output, output_got)
+    early = after((dw_one, small, input_grad), early)
+    dw_ctx = jnp.stack([early[:, n * CTX_EMB : (n + 1) * CTX_EMB] for n in range(2)])
+    first = 2 * CTX_EMB
+    mats = [early[:, first + n * C : first + (n + 1) * C].astype(F32) for n in range(4)]
+    dw_two = early[:, first + 4 * C :]
 
     return (
         output.reshape(ch, images, pixels),
         input_grad.reshape(ch, images, pixels),
-        last[0],
-        last[1],
+        small[12],
+        small[13],
         dw_one.astype(F32),
         small[9],
         dw_emb,
@@ -1092,11 +1109,11 @@
         small[2],
         small[0],
         small[1],
-        mats[: 3 * ch].astype(F32).reshape(3, ch, C),
+        jnp.stack(mats[:3]),
         small[4:7],
         dw_ctx.astype(F32),
         small[10:12],
-        mats[3 * ch :].astype(F32),
+        mats[3],
         small[3],
     )
 

time: 813 us -> 784 us (0.964)
  waiting for transfers between devices: 139 us -> 89.1 us
  starting transfers between devices: 133 us -> 156 us
    psum x1 -> x0, waiting for transfers between devices: 86.6 us -> none  [local(): early = lax.psum(early, 'dp')]
    ppermute x38 -> x34, waiting for transfers between devices: 48.2 us -> 65.8 us  [over(): return lax.ppermute(x, 'dp', [(i, i ^ bit) for i in range(self.images)])]
    ppermute x2 -> x1, starting transfers between devices: 10.2 us -> 24.1 us  [total(): x = x + lax.ppermute(x, 'tensor', [(0, 1), (1, 0)])]
    reduce_scatter x0 -> x1, waiting for transfers between devices: none -> 10.2 us  [local(): early = lax.psum_scatter(early, 'dp', scatter_dimension=0, tiled=True)]
    ppermute x2 -> x1, waiting for transfers between devices: 4.35 us -> 13 us  [total(): x = x + lax.ppermute(x, 'tensor', [(0, 1), (1, 0)])]
    ppermute x38 -> x34, starting transfers between devices: 101 us -> 108 us  [over(): return lax.ppermute(x, 'dp', [(i, i ^ bit) for i in range(self.images)])]
    ppermute x14 -> x13, starting transfers between devices: 22.1 us -> 23.6 us  [got(): return lax.ppermute(x, ('dp', 'tensor'), self.far)]
  transfers between devices with their start and end apart: 55 -> 50, of which waited for: 19 -> 17; matrix products, arithmetic and copies ran while one was open for 9% -> 8% of each run, Pallas kernels for 22% -> 25%
where the time goes in v4:
time: 784 us; the launch traced here: 774 us
  Pallas kernels  434 us (55%)
  starting transfers between devices  156 us (20%)
  waiting for transfers between devices  89.1 us (11%)
  other arithmetic  38.4 us (5%)
  local copies, waits for them, and re-layouts  31.9 us (4%)
  between operations  16.7 us (2%)
  matrix products  8.27 us (1%)
    pallas_call x1, Pallas kernels, attention(): pl.pallas_call(functools.partial(attention_kernel, len(grads), unroll=unr...  234 us
    ppermute x34, starting transfers between devices, over(): return lax.ppermute(x, 'dp', [(i, i ^ bit) for i in range(self.images)])  108 us
    pallas_call x4, Pallas kernels, conv_call(): pl.pallas_call(functools.partial(kernel, len(pieces)), out_shape=[*outs,...  93.8 us
    ppermute x34, waiting for transfers between devices, over(): return lax.ppermute(x, 'dp', [(i, i ^ bit) for i in range(self.images)])  65.8 us
    pallas_call x2, Pallas kernels, conv_weight_grad(): pl.pallas_call(functools.partial(weight_grad_kernel, len(pieces)), out_sh...  33.1 us
    ppermute x1, starting transfers between devices, total(): x = x + lax.ppermute(x, 'tensor', [(0, 1), (1, 0)])  24.1 us
    ppermute x13, starting transfers between devices, got(): return lax.ppermute(x, ('dp', 'tensor'), self.far)  23.6 us
  transfers between devices with their start and end apart: 50, of which 17 were waited for; matrix products, arithmetic and copies ran while one was open for 8% of the time, Pallas kernels for 25%

profile of v4, /device:TPU:5, one launch (start us, length us, event | category | flops | bytes accessed | tf_op | source)
XLA Modules:
  0.0 774.3 jit_solution(3476388561934697577)
XLA Ops:
  7.4 2.1 collective-permute-start
  13.1 2.1 collective-permute-start.4
  16.5 9.0 %act_one.1 = (bf16[256,4096]{1,0:T(8,128)(2,1)}, f32[256,128]{1,0:T(8,128)}, bf16[256,4096]{1,0:T(8,128)(2,1)}) custom-call(s32[2]{0:T(128)} %pad_add_fusion.meta, bf16[256,4096]{1,0:T(8,128)(2,1)} %bitcast.121, bf16[256,4096]{1,0:T(8,128)(2,1)} %collective-permute-done.got_ref, f32[256,2]{1,0:T(8,128)} %slice_bitcast_fusion.10.par_ref.refs_2_), custom_call_target="tpu_custom_call" | custom-call | flops 209715 | bytes 62914 | tf_op jit(solution)/shard_map/act_one/pallas_call | solution.py:187
  25.5 21.4 %collective-permute-start.2 = (bf16[256,4096]{1,0:T(8,128)(2,1)}, bf16[256,4096]{1,0:T(8,128)(2,1)}, u32[]{:S(2)}, u32[]{:S(2)}) collective-permute-start(bf16[256,4096]{1,0:T(8,128)(2,1)} %get-tuple-element.79.refs_0_), channel_id=1, source_target_pairs={{0,2},{2,0},{4,6},{6,4},{8,10},{10,8},{12,14},{14,12},{16,18},{18,... | collective-permute-start | bytes 6291464 | tf_op jit(solution)/shard_map/ppermute | solution.py:880
  47.0 3.6 collective-permute-done.5
  52.0 2.4 collective-permute-done.6
  55.9 3.1 fusion
  59.0 2.0 collective-permute-start.3
  61.0 2.4 collective-permute-start.8
  66.3 22.1 %conv_one.1 = (bf16[256,4096]{1,0:T(8,128)(2,1)}, f32[256,128]{1,0:T(8,128)}, f32[256,4096]{1,0:T(8,128)}, bf16[256,4608]{1,0:T(8,128)(2,1)}) custom-call(s32[2]{0:T(128)} %pad_add_fusion.meta, bf16[256,4608]{1,0:T(8,128)(2,1)} %w_own.2, bf16[256,4608]{1,0:T(8,128)(2,1)} %collective-permute-done.4.w_got, bf16[256,4096]{1,0:T(8,128)(2,1)} %get-tuple-element.79.refs_0_, ...), custom_call_target="tpu_custom_call" | custom-call | flops 96636768 | bytes 107530 | tf_op jit(solution)/shard_map/conv_one/pallas_call | solution.py:259
  88.5 2.2 collective-permute-start.9
  90.7 2.0 pad_maximum_fusion.2
  92.8 2.0 collective-permute-start.12
  98.6 22.3 %conv_two.1 = (bf16[256,4096]{1,0:T(8,128)(2,1)}, f32[256,128]{1,0:T(8,128)}, f32[256,4096]{1,0:T(8,128)}, bf16[256,4608]{1,0:T(8,128)(2,1)}) custom-call(s32[2]{0:T(128)} %pad_add_fusion.meta, bf16[256,4608]{1,0:T(8,128)(2,1)} %w_own.3, bf16[256,4608]{1,0:T(8,128)(2,1)} %collective-permute-done.3.w_got, bf16[256,4096]{1,0:T(8,128)(2,1)} %get-tuple-element.84.refs_0_, ...), custom_call_target="tpu_custom_call" | custom-call | flops 96636768 | bytes 128481 | tf_op jit(solution)/shard_map/conv_two/pallas_call | solution.py:259
  120.9 4.1 collective-permute-start.13
  128.1 4.8 fold.1.refs_0_.refs_5_
  133.7 4.8 grad_heads.1
  138.5 10.9 %collective-permute-start.14 = (bf16[256,4096]{1,0:T(8,128)(2,1)}, bf16[256,4096]{1,0:T(8,128)(2,1)}, u32[]{:S(2)}, u32[]{:S(2)}) collective-permute-start(bf16[256,4096]{1,0:T(8,128)(2,1)} %get-tuple-element.93), channel_id=1, source_target_pairs={{0,2},{2,0},{4,6},{6,4},{8,10},{10,8},{12,14},{14,12},{16,18},{18,... | collective-permute-start | bytes 6291464 | tf_op jit(solution)/shard_map/ppermute | solution.py:880
  154.8 7.7 qkv.1
  162.5 233.8 %attention.1 = (bf16[4,64,4096]{2,1,0:T(8,128)(2,1)}, bf16[4,64,4096]{2,1,0:T(8,128)(2,1)}, bf16[4,64,4096]{2,1,0:T(8,128)(2,1)}, bf16[4,64,4096]{2,1,0:T(8,128)...) custom-call(s32[1]{0:T(128)} %bitcast.21.lim_ref, bf16[3,4,64,4096]{3,2,1,0:T(8,128)(2,1)} %bitcast.104, ...), custom_call_target="tpu_custom_call" | custom-call | flops 1159641216 | bytes 167772 | tf_op jit(solution)/shard_map/attention/pallas_call | solution.py:766
  396.3 7.4 grad_normed.1
  406.9 8.7 %qkv_grad.1 = (bf16[768,512]{1,0:T(8,128)(2,1)}, f32[768,128]{1,0:T(8,128)}) custom-call(s32[2]{0:T(128)} %pad_add_fusion.meta, bf16[256,4096]{1,0:T(8,128)(2,1)} %bitcast.112, bf16[256,4096]{1,0:T(8,128)(2,1)} %bitcast.114, bf16[256,4096]{1,0:T(8,128)(2,1)} %bitcast.116, bf16[256,4096]{1,0:T(8,128)(2,1)} %get-tuple-element.86.refs_0_.refs_3_, ...), custom_call_target="tpu_custom_call" | custom-call | flops 32212254 | bytes 104857 | tf_op jit(solution)/shard_map/qkv_grad/pallas_call | solution.py:632
  415.7 2.1 constant_dynamic-update-slice_fusion.1
  417.7 10.2 %norm_three_back.1 = (f32[256,4096]{1,0:T(8,128)}, bf16[256,4096]{1,0:T(8,128)(2,1)}, f32[256,128]{1,0:T(8,128)}) custom-call(bf16[256,4096]{1,0:T(8,128)(2,1)} %get-tuple-element.104.refs_0_, bf16[256,4096]{1,0:T(8,128)(2,1)} %collective-permute-done.19.refs_1_, f32[256,4096]{1,0:T(8,128)} %get-tuple-element.123.refs_2_.refs_3_, ...), custom_call_target="tpu_custom_call" | custom-call | flops 209715 | bytes 167772 | tf_op jit(solution)/shard_map/norm_three_back/pallas_call | solution.py:494
  427.9 16.4 %conv_two_weight_grad.1 = bf16[256,4608]{1,0:T(8,128)(2,1)} custom-call(s32[2]{0:T(128)} %pad_add_fusion.meta, bf16[256,4096]{1,0:T(8,128)(2,1)} %get-tuple-element.111.grad_ref.refs_0_, bf16[256,4096]{1,0:T(8,128)(2,1)} %get-tuple-element.84.refs_0_, bf16[256,4096]{1,0:T(8,128)(2,1)} %collective-permute-done.9.refs_1_), custom_call_target="tpu_custom_call" | custom-call | flops 96636768 | bytes 86507 | tf_op jit(solution)/shard_map/conv_two_weight_grad/pallas_call | solution.py:417
  444.3 2.2 collective-permute-start.22
  446.5 5.2 out_grad.1
  455.2 2.3 convolution_convert_fusion
  457.5 4.1 collective-permute-start.21
  463.8 4.5 turn.3.w_own.w_got
  472.6 24.6 %conv_two_back.1 = (bf16[256,4096]{1,0:T(8,128)(2,1)}, f32[256,128]{1,0:T(8,128)}) custom-call(s32[2]{0:T(128)} %pad_add_fusion.meta, bf16[256,4608]{1,0:T(8,128)(2,1)} %turn.3.w_own.w_got, bf16[256,4608]{1,0:T(8,128)(2,1)} %turn.3.w_own.w_got, bf16[256,4096]{1,0:T(8,128)(2,1)} %get-tuple-element.111.grad_ref.refs_0_, ...), custom_call_target="tpu_custom_call" | custom-call | flops 96636768 | bytes 150784 | tf_op jit(solution)/shard_map/conv_two_back/pallas_call | solution.py:259
  497.2 3.6 select_dynamic-update-slice_fusion
  501.0 20.1 %collective-permute-start.16 = (bf16[256,4608]{1,0:T(8,128)(2,1)}, bf16[256,4608]{1,0:T(8,128)(2,1)}, u32[]{:S(2)}, u32[]{:S(2)}) collective-permute-start(bf16[256,4608]{1,0:T(8,128)(2,1)} %get-tuple-element.96.own_ref), channel_id=1, source_target_pairs={{0,2},{2,0},{4,6},{6,4},{8,10},{10,8},{12,14},{14,12},{16,18},{18,... | collective-permute-start | bytes 7077896 | tf_op jit(solution)/shard_map/ppermute | solution.py:880
  521.1 4.4 collective-permute-done.16.other_ref
  525.6 4.7 turn.2.w_own.w_got
  530.2 16.7 %conv_one_weight_grad.1 = bf16[256,4608]{1,0:T(8,128)(2,1)} custom-call(s32[2]{0:T(128)} %pad_add_fusion.meta, bf16[256,4096]{1,0:T(8,128)(2,1)} %get-tuple-element.118.grad_ref.refs_0_, bf16[256,4096]{1,0:T(8,128)(2,1)} %get-tuple-element.79.refs_0_, bf16[256,4096]{1,0:T(8,128)(2,1)} %collective-permute-done.2.refs_1_), custom_call_target="tpu_custom_call" | custom-call | flops 96636768 | bytes 86507 | tf_op jit(solution)/shard_map/conv_one_weight_grad/pallas_call | solution.py:417
  546.9 24.7 %conv_one_back.1 = (bf16[256,4096]{1,0:T(8,128)(2,1)}, f32[256,128]{1,0:T(8,128)}) custom-call(s32[2]{0:T(128)} %pad_add_fusion.meta, bf16[256,4608]{1,0:T(8,128)(2,1)} %turn.2.w_own.w_got, bf16[256,4608]{1,0:T(8,128)(2,1)} %turn.2.w_own.w_got, bf16[256,4096]{1,0:T(8,128)(2,1)} %get-tuple-element.118.grad_ref.refs_0_, ...), custom_call_target="tpu_custom_call" | custom-call | flops 96636768 | bytes 171724 | tf_op jit(solution)/shard_map/conv_one_back/pallas_call | solution.py:259
  571.6 2.0 collective-permute-start.25
  573.9 2.1 collective-permute-start.26
  577.1 6.7 output.1
  583.8 2.1 collective-permute-start.24
  586.5 3.9 select_convert_fusion
  590.5 10.2 %reduce-scatter.2.cloned.1.call-done = bf16[16,10752]{1,0:T(8,128)(2,1)} async-done(((bf16[256,10752]{1,0:T(8,128)(2,1)}), bf16[16,10752]{1,0:T(8,128)(2,1)}) %reduce-scatter.2.cloned.1.call-update) | async-done | bytes 344080 | tf_op jit(solution)/shard_map/reduce_scatter | solution.py:1042
  601.1 24.1 %collective-permute-start.27 = (f32[46,256]{1,0:T(8,128)S(1)}, f32[46,256]{1,0:T(8,128)S(1)}, u32[]{:S(2)}, u32[]{:S(2)}) collective-permute-start(f32[46,256]{1,0:T(8,128)S(1)} %concatenate.74), channel_id=1, source_target_pairs={{0,1},{1,0},{2,3},{3,2},{4,5},{5,4},{6,7},{7,6},{8,9},{9,8},{10,11... | collective-permute-start | bytes 141320 | tf_op jit(solution)/shard_map/ppermute | solution.py:892
  625.2 3.1 select_bitcast_fusion
  628.3 6.3 copy.133
  634.6 13.0 %collective-permute-done.27 = f32[46,256]{1,0:T(8,128)S(1)} collective-permute-done((f32[46,256]{1,0:T(8,128)S(1)}, f32[46,256]{1,0:T(8,128)S(1)}, u32[]{:S(2)}, u32[]{:S(2)}) %collective-permute-start.27) | collective-permute-done | bytes 47136 | tf_op jit(solution)/shard_map/ppermute | solution.py:892
  651.1 2.8 collective-permute-done.29
  654.9 11.9 %collective-permute-start.32 = (bf16[64,4608]{1,0:T(8,128)(2,1)S(1)}, bf16[64,4608]{1,0:T(8,128)(2,1)}, u32[]{:S(2)}, u32[]{:S(2)}) collective-permute-start(bf16[64,4608]{1,0:T(8,128)(2,1)S(1)} %constant_dynamic-slice_fusion.7), channel_id=1, source_target_pairs={{0,2},{2,0},{4,6},{6,4},{8,10},{10,8},{12,14},{14,12},{16,18},{18,... | collective-permute-start | bytes 1769480 | tf_op jit(solution)/shard_map/ppermute | solution.py:880
  666.9 6.7 collective-permute-start.31
  676.1 2.3 pad_maximum_fusion
  682.2 5.6 collective-permute-done.33
  688.0 7.0 collective-permute-done.41
  696.0 8.7 %collective-permute-done.34 = bf16[16,4608]{1,0:T(8,128)(2,1)S(1)} collective-permute-done((bf16[16,4608]{1,0:T(8,128)(2,1)S(1)}, bf16[16,4608]{1,0:T(8,128)(2,1)S(1)}, u32[]{:S(2)}, u32[]{:S(2)}) %collective-permute-start.34) | collective-permute-done | bytes 147488 | tf_op jit(solution)/shard_map/ppermute | solution.py:880
  706.1 11.9 %collective-permute-done.35 = bf16[8,4608]{1,0:T(8,128)(2,1)S(1)} collective-permute-done((bf16[8,4608]{1,0:T(8,128)(2,1)S(1)}, bf16[8,4608]{1,0:T(8,128)(2,1)S(1)}, u32[]{:S(2)}, u32[]{:S(2)}) %collective-permute-start.35) | collective-permute-done | bytes 73760 | tf_op jit(solution)/shard_map/ppermute | solution.py:880
  718.3 6.6 collective-permute-done.36
  726.7 3.5 collective-permute-done.37
  730.7 2.1 collective-permute-done.45
  733.0 2.8 collective-permute-done.38
  735.9 12.5 %collective-permute-start.39 = (bf16[64,4608]{1,0:T(8,128)(2,1)S(1)}, bf16[64,4608]{1,0:T(8,128)(2,1)S(1)}, u32[]{:S(2)}, u32[]{:S(2)}) collective-permute-start(bf16[64,4608]{1,0:T(8,128)(2,1)S(1)} %maximum_select_fusion.2), channel_id=1, source_target_pairs={{0,2},{2,0},{4,6},{6,4},{8,10},{10,8},{12,14},{14,12},{16,18},{18,... | collective-permute-start | bytes 1769480 | tf_op jit(solution)/shard_map/ppermute | solution.py:880
  752.6 2.7 fusion.20
  757.0 2.1 slice_convert_fusion.1
  759.1 4.4 slice_convert_fusion
  763.5 2.3 maximum_convert_fusion
  (226 shorter events, 61.5 us)
Async XLA Ops:
  7.2 48.7 %copy-start = (bf16[1,260,2048]{2,1,0:T(8,128)(2,1)S(1)}, bf16[1,260,2048]{2,1,0:T(8,128)(2,1)}, u32[]{:S(2)}) copy-start(bf16[1,260,2048]{2,1,0:T(8,128)(2,1)} %param.26) | copy-start | bytes 3194884
  7.2 8.0 %copy-start.14 = (bf16[1,2048]{1,0:T(2,128)(2,1)S(1)}, bf16[1,2048]{1,0:T(2,128)(2,1)}, u32[]{:S(2)}) copy-start(bf16[1,2048]{1,0:T(2,128)(2,1)} %param.25) | copy-start | bytes 12292
  7.2 4.9 copy-start.23
  7.3 593.3 %reduce-scatter.2.cloned.1.call-start = ((), (), s32[]{:S(2)}) async-start(), calls=%async_computation.1 | async-start | bytes 5849088 | tf_op jit(solution)/shard_map/reduce_scatter | solution.py:1042
  7.4 9.1 %collective-permute-start = (bf16[256,4096]{1,0:T(8,128)(2,1)}, bf16[256,4096]{1,0:T(8,128)(2,1)}, u32[]{:S(2)}, u32[]{:S(2)}) collective-permute-start(bf16[256,4096]{1,0:T(8,128)(2,1)} %bitcast.120), channel_id=1, source_target_pairs={{1,2},{2,1},{5,6},{6,5},{9,10},{10,9},{13,14},{14,13},{17,18},{18,... | collective-permute-start | bytes 6291464 | tf_op jit(solution)/shard_map/ppermute | solution.py:874
  12.4 3.4 collective-permute-start.1
  13.1 53.3 %collective-permute-start.4 = (bf16[256,4608]{1,0:T(8,128)(2,1)}, bf16[256,4608]{1,0:T(8,128)(2,1)}, u32[]{:S(2)}, u32[]{:S(2)}) collective-permute-start(bf16[256,4608]{1,0:T(8,128)(2,1)} %w_own.2), channel_id=1, source_target_pairs={{1,2},{2,1},{5,6},{6,5},{9,10},{10,9},{13,14},{14,13},{17,18},{18,... | collective-permute-start | bytes 7077896 | tf_op jit(solution)/shard_map/ppermute | solution.py:874
  16.5 39.4 %copy-start.26 = (f32[2,256]{1,0:T(2,128)S(1)}, f32[2,256]{1,0:T(2,128)}, u32[]{:S(2)}) copy-start(f32[2,256]{1,0:T(2,128)} %param.43) | copy-start | bytes 6148
  25.5 40.9 %collective-permute-start.2 = (bf16[256,4096]{1,0:T(8,128)(2,1)}, bf16[256,4096]{1,0:T(8,128)(2,1)}, u32[]{:S(2)}, u32[]{:S(2)}) collective-permute-start(bf16[256,4096]{1,0:T(8,128)(2,1)} %get-tuple-element.79.refs_0_), channel_id=1, source_target_pairs={{0,2},{2,0},{4,6},{6,4},{8,10},{10,8},{12,14},{14,12},{16,18},{18,... | collective-permute-start | bytes 6291464 | tf_op jit(solution)/shard_map/ppermute | solution.py:880
  47.0 3.7 collective-permute-start.5
  50.7 3.7 collective-permute-start.6
  54.5 6.5 collective-permute-start.7
  59.0 39.6 %collective-permute-start.3 = (bf16[256,4608]{1,0:T(8,128)(2,1)}, bf16[256,4608]{1,0:T(8,128)(2,1)}, u32[]{:S(2)}, u32[]{:S(2)}) collective-permute-start(bf16[256,4608]{1,0:T(8,128)(2,1)} %w_own.3), channel_id=1, source_target_pairs={{1,2},{2,1},{5,6},{6,5},{9,10},{10,9},{13,14},{14,13},{17,18},{18,... | collective-permute-start | bytes 7077896 | tf_op jit(solution)/shard_map/ppermute | solution.py:874
  61.0 4.7 collective-permute-start.8
  66.3 24.4 %copy-start.5 = (bf16[3,256,512]{2,1,0:T(8,128)(2,1)S(1)}, bf16[3,256,512]{2,1,0:T(8,128)(2,1)}, u32[]{:S(2)}) copy-start(bf16[3,256,512]{2,1,0:T(8,128)(2,1)} %param.40) | copy-start | bytes 2359300
  88.5 10.1 %collective-permute-start.9 = (bf16[256,4096]{1,0:T(8,128)(2,1)}, bf16[256,4096]{1,0:T(8,128)(2,1)}, u32[]{:S(2)}, u32[]{:S(2)}) collective-permute-start(bf16[256,4096]{1,0:T(8,128)(2,1)} %get-tuple-element.84.refs_0_), channel_id=1, source_target_pairs={{0,2},{2,0},{4,6},{6,4},{8,10},{10,8},{12,14},{14,12},{16,18},{18,... | collective-permute-start | bytes 6291464 | tf_op jit(solution)/shard_map/ppermute | solution.py:880
  92.8 32.2 %collective-permute-start.12 = (bf16[256,4096]{1,0:T(8,128)(2,1)}, bf16[256,4096]{1,0:T(8,128)(2,1)}, u32[]{:S(2)}, u32[]{:S(2)}) collective-permute-start(bf16[256,4096]{1,0:T(8,128)(2,1)} %bitcast.18.own_ref), channel_id=1, source_target_pairs={{1,2},{2,1},{5,6},{6,5},{9,10},{10,9},{13,14},{14,13},{17,18},{18,... | collective-permute-start | bytes 6291464 | tf_op jit(solution)/shard_map/ppermute | solution.py:874
  94.8 30.2 %collective-permute-start.10 = (bf16[1024,512]{1,0:T(8,128)(2,1)}, bf16[1024,512]{1,0:T(8,128)(2,1)}, u32[]{:S(2)}, u32[]{:S(2)}) collective-permute-start(bf16[1024,512]{1,0:T(8,128)(2,1)} %pad_maximum_fusion.2), channel_id=1, source_target_pairs={{1,2},{2,1},{5,6},{6,5},{9,10},{10,9},{13,14},{14,13},{17,18},{18,... | collective-permute-start | bytes 3145736 | tf_op jit(solution)/shard_map/ppermute | solution.py:874
  96.4 28.6 %collective-permute-start.11 = (bf16[2,256,384]{1,2,0:T(8,128)(2,1)S(1)}, bf16[2,256,384]{1,2,0:T(8,128)(2,1)}, u32[]{:S(2)}, u32[]{:S(2)}) collective-permute-start(bf16[2,256,384]{1,2,0:T(8,128)(2,1)S(1)} %pad.4), channel_id=1, source_target_pairs={{1,2},{2,1},{5,6},{6,5},{9,10},{10,9},{13,14},{14,13},{17,18},{18,... | collective-permute-start | bytes 1179656 | tf_op jit(solution)/shard_map/ppermute | solution.py:874
  120.9 34.0 %collective-permute-start.13 = (bf16[256,4096]{1,0:T(8,128)(2,1)}, bf16[256,4096]{1,0:T(8,128)(2,1)}, u32[]{:S(2)}, u32[]{:S(2)}) collective-permute-start(bf16[256,4096]{1,0:T(8,128)(2,1)} %get-tuple-element.86.refs_0_.refs_3_), channel_id=1, source_target_pairs={{0,2},{2,0},{4,6},{6,4},{8,10},{10,8},{12,14},{14,12},{16,18},{18,... | collective-permute-start | bytes 6291464 | tf_op jit(solution)/shard_map/ppermute | solution.py:880
  138.5 14.2 %copy-start.4 = (bf16[1024,512]{1,0:T(8,128)(2,1)S(1)}, bf16[1024,512]{1,0:T(8,128)(2,1)}, u32[]{:S(2)}) copy-start(bf16[1024,512]{1,0:T(8,128)(2,1)} %copy-done.3) | copy-start | bytes 3145732
  138.5 24.0 %collective-permute-start.14 = (bf16[256,4096]{1,0:T(8,128)(2,1)}, bf16[256,4096]{1,0:T(8,128)(2,1)}, u32[]{:S(2)}, u32[]{:S(2)}) collective-permute-start(bf16[256,4096]{1,0:T(8,128)(2,1)} %get-tuple-element.93), channel_id=1, source_target_pairs={{0,2},{2,0},{4,6},{6,4},{8,10},{10,8},{12,14},{14,12},{16,18},{18,... | collective-permute-start | bytes 6291464 | tf_op jit(solution)/shard_map/ppermute | solution.py:880
  396.3 8.9 %copy-start.10 = (bf16[4,64,384]{2,1,0:T(8,128)(2,1)S(1)}, bf16[4,64,384]{2,1,0:T(8,128)(2,1)}, u32[]{:S(2)}) copy-start(bf16[4,64,384]{2,1,0:T(8,128)(2,1)} %get-tuple-element.97) | copy-start | bytes 589828
  396.3 9.0 %copy-start.9 = (bf16[4,64,384]{2,1,0:T(8,128)(2,1)S(1)}, bf16[4,64,384]{2,1,0:T(8,128)(2,1)}, u32[]{:S(2)}) copy-start(bf16[4,64,384]{2,1,0:T(8,128)(2,1)} %get-tuple-element.98) | copy-start | bytes 589828
  403.7 14.1 %collective-permute-start.19 = (bf16[256,4096]{1,0:T(8,128)(2,1)}, bf16[256,4096]{1,0:T(8,128)(2,1)}, u32[]{:S(2)}, u32[]{:S(2)}) collective-permute-start(bf16[256,4096]{1,0:T(8,128)(2,1)} %get-tuple-element.105), channel_id=1, source_target_pairs={{0,2},{2,0},{4,6},{6,4},{8,10},{10,8},{12,14},{14,12},{16,18},{18,... | collective-permute-start | bytes 6291464 | tf_op jit(solution)/shard_map/ppermute | solution.py:880
  404.6 41.8 %collective-permute-start.15 = (bf16[256,4096]{1,0:T(8,128)(2,1)}, bf16[256,4096]{1,0:T(8,128)(2,1)}, u32[]{:S(2)}, u32[]{:S(2)}) collective-permute-start(bf16[256,4096]{1,0:T(8,128)(2,1)} %bitcast.108), channel_id=1, source_target_pairs={{0,2},{2,0},{4,6},{6,4},{8,10},{10,8},{12,14},{14,12},{16,18},{18,... | collective-permute-start | bytes 6291464 | tf_op jit(solution)/shard_map/ppermute | solution.py:880
  404.7 59.1 %collective-permute-start.20 = (bf16[256,4608]{1,0:T(8,128)(2,1)}, bf16[256,4608]{1,0:T(8,128)(2,1)}, u32[]{:S(2)}, u32[]{:S(2)}) collective-permute-start(bf16[256,4608]{1,0:T(8,128)(2,1)} %get-tuple-element.110.own_ref), channel_id=1, source_target_pairs={{0,2},{2,0},{4,6},{6,4},{8,10},{10,8},{12,14},{14,12},{16,18},{18,... | collective-permute-start | bytes 7077896 | tf_op jit(solution)/shard_map/ppermute | solution.py:880
  405.5 49.7 %collective-permute-start.17 = (bf16[2,256,384]{1,2,0:T(8,128)(2,1)S(1)}, bf16[2,256,384]{1,2,0:T(8,128)(2,1)}, u32[]{:S(2)}, u32[]{:S(2)}) collective-permute-start(bf16[2,256,384]{1,2,0:T(8,128)(2,1)S(1)} %pad_maximum_fusion.3), channel_id=1, source_target_pairs={{1,2},{2,1},{5,6},{6,5},{9,10},{10,9},{13,14},{14,13},{17,18},{18,... | collective-permute-start | bytes 1179656 | tf_op jit(solution)/shard_map/ppermute | solution.py:874
  444.3 52.9 %collective-permute-start.22 = (bf16[256,4608]{1,0:T(8,128)(2,1)}, bf16[256,4608]{1,0:T(8,128)(2,1)}, u32[]{:S(2)}, u32[]{:S(2)}) collective-permute-start(bf16[256,4608]{1,0:T(8,128)(2,1)} %conv_two_weight_grad.1), channel_id=1, source_target_pairs={{1,2},{2,1},{5,6},{6,5},{9,10},{10,9},{13,14},{14,13},{17,18},{18,... | collective-permute-start | bytes 7077896 | tf_op jit(solution)/shard_map/ppermute | solution.py:874
  453.4 14.8 %collective-permute-start.18 = (bf16[1024,512]{1,0:T(8,128)(2,1)}, bf16[1024,512]{1,0:T(8,128)(2,1)}, u32[]{:S(2)}, u32[]{:S(2)}) collective-permute-start(bf16[1024,512]{1,0:T(8,128)(2,1)} %constant_dynamic-update-slice_fusion), channel_id=1, source_target_pairs={{1,2},{2,1},{5,6},{6,5},{9,10},{10,9},{13,14},{14,13},{17,18},{18,... | collective-permute-start | bytes 3145736 | tf_op jit(solution)/shard_map/ppermute | solution.py:874
  457.5 15.1 %collective-permute-start.21 = (bf16[256,4096]{1,0:T(8,128)(2,1)}, bf16[256,4096]{1,0:T(8,128)(2,1)}, u32[]{:S(2)}, u32[]{:S(2)}) collective-permute-start(bf16[256,4096]{1,0:T(8,128)(2,1)} %get-tuple-element.111.grad_ref.refs_0_), channel_id=1, source_target_pairs={{0,2},{2,0},{4,6},{6,4},{8,10},{10,8},{12,14},{14,12},{16,18},{18,... | collective-permute-start | bytes 6291464 | tf_op jit(solution)/shard_map/ppermute | solution.py:880
  500.9 254.4 %all-gather.2.cloned.1.call-start = ((), (), s32[]{:S(2)}) async-start(), calls=%async_computation.2 | async-start | bytes 5849088 | tf_op jit(solution)/shard_map/all_gather | solution.py:1060
  501.0 24.6 %collective-permute-start.16 = (bf16[256,4608]{1,0:T(8,128)(2,1)}, bf16[256,4608]{1,0:T(8,128)(2,1)}, u32[]{:S(2)}, u32[]{:S(2)}) collective-permute-start(bf16[256,4608]{1,0:T(8,128)(2,1)} %get-tuple-element.96.own_ref), channel_id=1, source_target_pairs={{0,2},{2,0},{4,6},{6,4},{8,10},{10,8},{12,14},{14,12},{16,18},{18,... | collective-permute-start | bytes 7077896 | tf_op jit(solution)/shard_map/ppermute | solution.py:880
  521.1 25.9 %collective-permute-start.23 = (bf16[256,4096]{1,0:T(8,128)(2,1)}, bf16[256,4096]{1,0:T(8,128)(2,1)}, u32[]{:S(2)}, u32[]{:S(2)}) collective-permute-start(bf16[256,4096]{1,0:T(8,128)(2,1)} %get-tuple-element.118.grad_ref.refs_0_), channel_id=1, source_target_pairs={{0,2},{2,0},{4,6},{6,4},{8,10},{10,8},{12,14},{14,12},{16,18},{18,... | collective-permute-start | bytes 6291464 | tf_op jit(solution)/shard_map/ppermute | solution.py:880
  546.9 29.9 %copy-start.7 = (f32[768,128]{1,0:T(8,128)S(1)}, f32[768,128]{1,0:T(8,128)}, u32[]{:S(2)}) copy-start(f32[768,128]{1,0:T(8,128)} %get-tuple-element.125) | copy-start | bytes 1179652
  571.6 14.9 %collective-permute-start.25 = (bf16[256,4096]{1,0:T(8,128)(2,1)}, bf16[256,4096]{1,0:T(8,128)(2,1)}, u32[]{:S(2)}, u32[]{:S(2)}) collective-permute-start(bf16[256,4096]{1,0:T(8,128)(2,1)} %get-tuple-element.122), channel_id=1, source_target_pairs={{1,2},{2,1},{5,6},{6,5},{9,10},{10,9},{13,14},{14,13},{17,18},{18,... | collective-permute-start | bytes 6291464 | tf_op jit(solution)/shard_map/ppermute | solution.py:874
  573.9 16.6 %collective-permute-start.26 = (bf16[256,4608]{1,0:T(8,128)(2,1)}, bf16[256,4608]{1,0:T(8,128)(2,1)}, u32[]{:S(2)}, u32[]{:S(2)}) collective-permute-start(bf16[256,4608]{1,0:T(8,128)(2,1)} %conv_one_weight_grad.1), channel_id=1, source_target_pairs={{1,2},{2,1},{5,6},{6,5},{9,10},{10,9},{13,14},{14,13},{17,18},{18,... | collective-permute-start | bytes 7077896 | tf_op jit(solution)/shard_map/ppermute | solution.py:874
  577.1 8.8 %copy-start.11 = (f32[256,128]{1,0:T(8,128)S(1)}, f32[256,128]{1,0:T(8,128)}, u32[]{:S(2)}) copy-start(f32[256,128]{1,0:T(8,128)} %get-tuple-element.124) | copy-start | bytes 393220
  577.1 8.9 %copy-start.12 = (f32[256,128]{1,0:T(8,128)S(1)}, f32[256,128]{1,0:T(8,128)}, u32[]{:S(2)}) copy-start(f32[256,128]{1,0:T(8,128)} %get-tuple-element.126) | copy-start | bytes 393220
  583.8 41.4 %collective-permute-start.24 = (bf16[256,4096]{1,0:T(8,128)(2,1)}, bf16[256,4096]{1,0:T(8,128)(2,1)}, u32[]{:S(2)}, u32[]{:S(2)}) collective-permute-start(bf16[256,4096]{1,0:T(8,128)(2,1)} %output.1), channel_id=1, source_target_pairs={{1,2},{2,1},{5,6},{6,5},{9,10},{10,9},{13,14},{14,13},{17,18},{18,... | collective-permute-start | bytes 6291464 | tf_op jit(solution)/shard_map/ppermute | solution.py:874
  586.5 14.2 %copy-start.13 = (f32[256,128]{1,0:T(8,128)S(1)}, f32[256,128]{1,0:T(8,128)}, u32[]{:S(2)}) copy-start(f32[256,128]{1,0:T(8,128)} %get-tuple-element.132) | copy-start | bytes 393220
  601.1 27.2 %copy-start.2 = (f32[256,4096]{1,0:T(8,128)S(1)}, f32[256,4096]{1,0:T(8,128)}, u32[]{:S(2)}) copy-start(f32[256,4096]{1,0:T(8,128)} %select_convert_fusion) | copy-start | bytes 12582916
  601.1 46.6 %collective-permute-start.27 = (f32[46,256]{1,0:T(8,128)S(1)}, f32[46,256]{1,0:T(8,128)S(1)}, u32[]{:S(2)}, u32[]{:S(2)}) collective-permute-start(f32[46,256]{1,0:T(8,128)S(1)} %concatenate.74), channel_id=1, source_target_pairs={{0,1},{1,0},{2,3},{3,2},{4,5},{5,4},{6,7},{7,6},{8,9},{9,8},{10,11... | collective-permute-start | bytes 141320 | tf_op jit(solution)/shard_map/ppermute | solution.py:892
  647.7 3.2 collective-permute-start.28
  650.9 3.0 collective-permute-start.29
  651.1 24.0 %copy-start.6 = (bf16[16,2048]{1,0:T(8,128)(2,1)S(1)}, bf16[16,2048]{1,0:T(8,128)(2,1)}, u32[]{:S(2)}) copy-start(bf16[16,2048]{1,0:T(8,128)(2,1)} %add.168) | copy-start | bytes 196612
  653.9 13.0 %collective-permute-start.30 = (f32[46,256]{1,0:T(8,128)S(1)}, f32[46,256]{1,0:T(8,128)S(1)}, u32[]{:S(2)}, u32[]{:S(2)}) collective-permute-start(f32[46,256]{1,0:T(8,128)S(1)} %add.174), channel_id=1, source_target_pairs={{0,16},{2,18},{4,20},{6,22},{8,24},{10,26},{12,28},{14,30},{16,0},... | collective-permute-start | bytes 141320 | tf_op jit(solution)/shard_map/ppermute | solution.py:880
  654.9 23.5 %collective-permute-start.32 = (bf16[64,4608]{1,0:T(8,128)(2,1)S(1)}, bf16[64,4608]{1,0:T(8,128)(2,1)}, u32[]{:S(2)}, u32[]{:S(2)}) collective-permute-start(bf16[64,4608]{1,0:T(8,128)(2,1)S(1)} %constant_dynamic-slice_fusion.7), channel_id=1, source_target_pairs={{0,2},{2,0},{4,6},{6,4},{8,10},{10,8},{12,14},{14,12},{16,18},{18,... | collective-permute-start | bytes 1769480 | tf_op jit(solution)/shard_map/ppermute | solution.py:880
  666.9 7.6 collective-permute-start.31
  674.4 6.5 collective-permute-start.40
  679.6 8.2 %collective-permute-start.33 = (bf16[32,4608]{1,0:T(8,128)(2,1)S(1)}, bf16[32,4608]{1,0:T(8,128)(2,1)S(1)}, u32[]{:S(2)}, u32[]{:S(2)}) collective-permute-start(bf16[32,4608]{1,0:T(8,128)(2,1)S(1)} %constant_dynamic-slice_fusion.6), channel_id=1, source_target_pairs={{0,4},{2,6},{4,0},{6,2},{8,12},{10,14},{12,8},{14,10},{16,20},{18,... | collective-permute-start | bytes 884744 | tf_op jit(solution)/shard_map/ppermute | solution.py:880
  682.1 12.8 %collective-permute-start.41 = (bf16[32,4608]{1,0:T(8,128)(2,1)S(1)}, bf16[32,4608]{1,0:T(8,128)(2,1)S(1)}, u32[]{:S(2)}, u32[]{:S(2)}) collective-permute-start(bf16[32,4608]{1,0:T(8,128)(2,1)S(1)} %constant_dynamic-slice_fusion.2), channel_id=1, source_target_pairs={{0,8},{2,10},{4,12},{6,14},{8,0},{10,2},{12,4},{14,6},{16,24},{18,... | collective-permute-start | bytes 884744 | tf_op jit(solution)/shard_map/ppermute | solution.py:880
  687.9 16.8 %collective-permute-start.34 = (bf16[16,4608]{1,0:T(8,128)(2,1)S(1)}, bf16[16,4608]{1,0:T(8,128)(2,1)S(1)}, u32[]{:S(2)}, u32[]{:S(2)}) collective-permute-start(bf16[16,4608]{1,0:T(8,128)(2,1)S(1)} %constant_dynamic-slice_fusion.5), channel_id=1, source_target_pairs={{0,8},{2,10},{4,12},{6,14},{8,0},{10,2},{12,4},{14,6},{16,24},{18,... | collective-permute-start | bytes 442376 | tf_op jit(solution)/shard_map/ppermute | solution.py:880
  695.1 10.9 %collective-permute-start.42 = (bf16[16,4608]{1,0:T(8,128)(2,1)S(1)}, bf16[16,4608]{1,0:T(8,128)(2,1)S(1)}, u32[]{:S(2)}, u32[]{:S(2)}) collective-permute-start(bf16[16,4608]{1,0:T(8,128)(2,1)S(1)} %constant_dynamic-slice_fusion.1), channel_id=1, source_target_pairs={{0,16},{2,18},{4,20},{6,22},{8,24},{10,26},{12,28},{14,30},{16,0},... | collective-permute-start | bytes 442376 | tf_op jit(solution)/shard_map/ppermute | solution.py:880
  704.8 13.2 %collective-permute-start.35 = (bf16[8,4608]{1,0:T(8,128)(2,1)S(1)}, bf16[8,4608]{1,0:T(8,128)(2,1)S(1)}, u32[]{:S(2)}, u32[]{:S(2)}) collective-permute-start(bf16[8,4608]{1,0:T(8,128)(2,1)S(1)} %constant_dynamic-slice_fusion.4), channel_id=1, source_target_pairs={{0,16},{2,18},{4,20},{6,22},{8,24},{10,26},{12,28},{14,30},{16,0},... | collective-permute-start | bytes 221192 | tf_op jit(solution)/shard_map/ppermute | solution.py:880
  706.0 12.0 %collective-permute-start.43 = (bf16[8,4608]{1,0:T(8,128)(2,1)S(1)}, bf16[8,4608]{1,0:T(8,128)(2,1)S(1)}, u32[]{:S(2)}, u32[]{:S(2)}) collective-permute-start(bf16[8,4608]{1,0:T(8,128)(2,1)S(1)} %constant_dynamic-slice_fusion), channel_id=1, source_target_pairs={{0,4},{2,6},{4,0},{6,2},{8,12},{10,14},{12,8},{14,10},{16,20},{18,... | collective-permute-start | bytes 221192 | tf_op jit(solution)/shard_map/ppermute | solution.py:880
  718.0 7.0 collective-permute-start.36
  718.1 7.0 collective-permute-start.44
  725.0 5.2 collective-permute-start.37
  725.1 7.8 %collective-permute-start.45 = (bf16[16,4608]{1,0:T(8,128)(2,1)S(1)}, bf16[16,4608]{1,0:T(8,128)(2,1)S(1)}, u32[]{:S(2)}, u32[]{:S(2)}) collective-permute-start(bf16[16,4608]{1,0:T(8,128)(2,1)S(1)} %maximum_select_fusion.7), channel_id=1, source_target_pairs={{0,16},{2,18},{4,20},{6,22},{8,24},{10,26},{12,28},{14,30},{16,0},... | collective-permute-start | bytes 442376 | tf_op jit(solution)/shard_map/ppermute | solution.py:880
  730.2 5.6 collective-permute-start.38
  732.9 17.3 %collective-permute-start.46 = (bf16[32,4608]{1,0:T(8,128)(2,1)S(1)}, bf16[32,4608]{1,0:T(8,128)(2,1)S(1)}, u32[]{:S(2)}, u32[]{:S(2)}) collective-permute-start(bf16[32,4608]{1,0:T(8,128)(2,1)S(1)} %maximum_select_fusion.5), channel_id=1, source_target_pairs={{0,8},{2,10},{4,12},{6,14},{8,0},{10,2},{12,4},{14,6},{16,24},{18,... | collective-permute-start | bytes 884744 | tf_op jit(solution)/shard_map/ppermute | solution.py:880
  735.9 14.5 %collective-permute-start.39 = (bf16[64,4608]{1,0:T(8,128)(2,1)S(1)}, bf16[64,4608]{1,0:T(8,128)(2,1)S(1)}, u32[]{:S(2)}, u32[]{:S(2)}) collective-permute-start(bf16[64,4608]{1,0:T(8,128)(2,1)S(1)} %maximum_select_fusion.2), channel_id=1, source_target_pairs={{0,2},{2,0},{4,6},{6,4},{8,10},{10,8},{12,14},{14,12},{16,18},{18,... | collective-permute-start | bytes 1769480 | tf_op jit(solution)/shard_map/ppermute | solution.py:880
  750.3 2.1 collective-permute-start.47
  (13 other events, 57.8 us)
Sparse Core Ops, SparseCore 0:
  501.0 99.6 reduce-scatter.1
  634.8 91.8 all-gather.1

commit v5 on v4

--- a/solution.py
+++ b/solution.py
@@ -901,26 +901,29 @@
 
     def sum_owned(self, x):
         rows = x.shape[0] // 2
-        done = []
-        for at, order in enumerate((self.bits, [self.bits[0], *self.bits[2:], self.bits[1]])):
-            part = lax.slice_in_dim(x, at * rows, (at + 1) * rows)
-            size = rows
-            for bit in order:
-                size //= 2
-                upper = (lax.axis_index("dp") // bit) % 2
-                keep = lax.dynamic_slice_in_dim(part, upper * size, size)
-                send = lax.dynamic_slice_in_dim(part, (1 - upper) * size, size)
-                part = (keep.astype(F32) + self.over(send, bit).astype(F32)).astype(BF)
-            for bit in reversed(order):
-                upper = (lax.axis_index("dp") // bit) % 2
-                other = self.over(part, bit)
-                part = jnp.where(
-                    upper == 0,
-                    jnp.concatenate([part, other]),
-                    jnp.concatenate([other, part]),
+        order = (self.bits, [self.bits[0], *self.bits[2:], self.bits[1]])
+        parts = [lax.slice_in_dim(x, at * rows, (at + 1) * rows) for at in range(2)]
+
+        def upper(bit):
+            return (lax.axis_index("dp") // bit) % 2
+
+        for step in range(len(self.bits)):
+            size = parts[0].shape[0] // 2
+            for at in range(2):
+                bit = order[at][step]
+                keep = lax.dynamic_slice_in_dim(parts[at], upper(bit) * size, size)
+                send = lax.dynamic_slice_in_dim(parts[at], (1 - upper(bit)) * size, size)
+                parts[at] = (keep.astype(F32) + self.over(send, bit).astype(F32)).astype(BF)
+        for step in reversed(range(len(self.bits))):
+            for at in range(2):
+                bit = order[at][step]
+                other = self.over(parts[at], bit)
+                parts[at] = jnp.where(
+                    upper(bit) == 0,
+                    jnp.concatenate([parts[at], other]),
+                    jnp.concatenate([other, parts[at]]),
                 )
-            done.append(part)
-        return jnp.concatenate(done)
+        return jnp.concatenate(parts)
 
 
 def after(first, *later):
@@ -968,17 +971,17 @@
     emb_all = plan.everywhere(emb_all)
     length = vectors[14, :1].astype(jnp.int32)
     par_one, par_two, par_three = vectors[0:2].T, vectors[2:7].T, vectors[7:10].T
+    par_one = after(emb_all, par_one)
     w2_got = plan.got(after(vectors, conv2_weight))
     act_one, stat_one, f_low = first_activation(meta, f_own, f_got, par_one)
     full_one = plan.gather(act_one)
     mats_own = jnp.concatenate([qkv_weight.reshape(3 * ch, C), out_weight])
     mats_own, ctx_own, cot_own = after(
-        full_one[-1], mats_own, ctx_kv, cotangent.reshape(ch, pixels)
+        act_one, mats_own, ctx_kv, cotangent.reshape(ch, pixels)
     )
     mats_got, ctx_got = plan.got(mats_own), plan.got(ctx_own)
     cot_got = plan.got(cot_own)
 
-    par_two = after(emb_all, par_two)
     low, stat, wide = struct((ch, HW), BF), struct((ch, 128), F32), struct((ch, HW), F32)
     weight = struct((ch, 9 * C), BF)
     act_two, stat_two, conv_one, w1 = conv_call(
@@ -986,6 +989,8 @@
         [low, stat], [wide, weight], [], "conv_one",
     )
     full_two = plan.gather(act_two)
+    if moved:
+        full_two = after(cot_got, *full_two)
     normed, stat_three, hidden, w2 = conv_call(
         conv_two_kernel, meta, (conv2_weight, w2_got), full_two, (par_three, f_low), (),
         [low, stat], [wide, weight], [], "conv_two",
@@ -1024,8 +1029,6 @@
     full_grad_two = plan.gather(grad_two)
     dw_two = conv_weight_grad(meta, grad_two, full_two, "conv_two_weight_grad")
     two_got = plan.got(dw_two)
-    ctx_grad = plan.pick(ctx_own, ctx_got)[:, :, :CTX]
-    dw_ctx = jnp.einsum("ton,ne->toe", ctx_grad, context[0], preferred_element_type=F32).astype(BF)
     full_grad_two = after(dw_two, *full_grad_two) if moved else full_grad_two
     grad_one, sums_two = conv_call(
         conv_two_back_kernel, meta, (turned_two, turned_two), full_grad_two, (par_two, stat_two),
@@ -1033,8 +1036,11 @@
     )
     full_grad_one = plan.gather(grad_one)
     turned_one = plan.turn(meta, after(mixed, w1))
+    mats_got, ctx_got, two_got = after(grad_one, mats_got, ctx_got, two_got)
+    ctx_grad = plan.pick(ctx_own, ctx_got)[:, :, :CTX]
+    dw_ctx = jnp.einsum("ton,ne->toe", ctx_grad, context[0], preferred_element_type=F32).astype(BF)
     mats = plan.pick(mats_own, mats_got)
-    dw_two = plan.pick(dw_two, after(grad_one, two_got))
+    dw_two = plan.pick(dw_two, two_got)
     early = jnp.concatenate(
         [dw_ctx[0], dw_ctx[1], *(mats[t * ch : (t + 1) * ch] for t in range(4)), dw_two], 1
     )
@@ -1052,13 +1058,9 @@
     input_got = plan.got(input_grad)
 
     output = output_product(
-        meta, w_out, full_heads, vectors[10].reshape(ch, 1), after(input_grad, hidden)
+        meta, w_out, full_heads, vectors[10].reshape(ch, 1), after((input_grad, one_got), hidden)
     )
     output_got = plan.got(output)
-    early, dw_one, one_got, sums_one = after((output, input_got), early, dw_one, one_got, sums_one)
-    dw_one, one_got, sums_one = after(early, dw_one, one_got, sums_one)
-    early = lax.all_gather(early, "dp", axis=0, tiled=True)
-    dw_one = plan.sum_owned(plan.pick(dw_one, one_got))
     ctx_sums = jnp.sum(ctx_own.astype(F32), axis=2)
     sums_two = sums_two[:, :5].T
     own_mod = sums_two[2:4].astype(BF).astype(F32)
@@ -1078,6 +1080,9 @@
             ]
         )
     )
+    early, dw_one, one_got = after((output, small), early, dw_one, one_got)
+    early = lax.all_gather(early, "dp", axis=0, tiled=True)
+    dw_one = plan.sum_owned(plan.pick(dw_one, one_got))
     mods = small[14:].reshape(plan.images, 2, ch)
     mods_low = mods.astype(BF)
     dw_emb = jnp.stack(
@@ -1086,9 +1091,10 @@
             for t in range(2)
         ]
     )
+    input_got, output_got = after((dw_one, small), input_got, output_got)
     input_grad = plan.pick(input_grad, input_got).astype(F32)
     output = plan.pick(output, output_got)
-    early = after((dw_one, small, input_grad), early)
+    early = after((dw_one, small, input_grad, output), early)
     dw_ctx = jnp.stack([early[:, n * CTX_EMB : (n + 1) * CTX_EMB] for n in range(2)])
     first = 2 * CTX_EMB
     mats = [early[:, first + n * C : first + (n + 1) * C].astype(F32) for n in range(4)]

time: 784 us -> 732 us (0.934)
  the two profiles are of different devices: /device:TPU:5 before, /device:TPU:1 now
where the time goes in v5:
time: 732 us; the launch traced here: 722 us
  Pallas kernels  434 us (59%)
  waiting for transfers between devices  109 us (15%)
  starting transfers between devices  79.3 us (11%)
  other arithmetic  38.1 us (5%)
  local copies, waits for them, and re-layouts  34.5 us (5%)
  between operations  16.9 us (2%)
  matrix products  10.3 us (1%)
    pallas_call x1, Pallas kernels, attention(): pl.pallas_call(functools.partial(attention_kernel, len(grads), unroll=unr...  234 us
    pallas_call x4, Pallas kernels, conv_call(): pl.pallas_call(functools.partial(kernel, len(pieces)), out_shape=[*outs,...  93.7 us
    ppermute x34, waiting for transfers between devices, over(): return lax.ppermute(x, 'dp', [(i, i ^ bit) for i in range(self.images)])  60.1 us
    ppermute x13, waiting for transfers between devices, got(): return lax.ppermute(x, ('dp', 'tensor'), self.far)  45.3 us
    ppermute x13, starting transfers between devices, got(): return lax.ppermute(x, ('dp', 'tensor'), self.far)  43.1 us
    ppermute x34, starting transfers between devices, over(): return lax.ppermute(x, 'dp', [(i, i ^ bit) for i in range(self.images)])  36 us
    pallas_call x2, Pallas kernels, conv_weight_grad(): pl.pallas_call(functools.partial(weight_grad_kernel, len(pieces)), out_sh...  32.9 us
    unnamed x70, local copies, waits for them, and re-layouts  17.2 us
  transfers between devices with their start and end apart: 50, of which 20 were waited for; matrix products, arithmetic and copies ran while one was open for 8% of the time, Pallas kernels for 27%

profile of v5, /device:TPU:1, one launch (start us, length us, event | category | flops | bytes accessed | tf_op | source)
XLA Modules:
  0.0 722.3 jit_solution(10443899847600182532)
XLA Ops:
  7.4 4.7 collective-permute-start
  12.9 2.0 fusion.15
  17.8 3.6 collective-permute-start.8
  26.2 11.2 %collective-permute-done.5 = f32[15,256]{0,1:T(8,128)S(1)} collective-permute-done((f32[15,256]{0,1:T(8,128)S(1)}, f32[15,256]{0,1:T(8,128)S(1)}, u32[]{:S(2)}, u32[]{:S(2)}) %collective-permute-start.5) | collective-permute-done | bytes 15392 | tf_op jit(solution)/shard_map/ppermute | solution.py:874
  37.4 2.4 collective-permute-start.4
  42.2 9.0 %act_one.1 = (bf16[256,4096]{1,0:T(8,128)(2,1)}, f32[256,128]{1,0:T(8,128)}, bf16[256,4096]{1,0:T(8,128)(2,1)}) custom-call(s32[2]{0:T(128)} %pad_add_fusion.meta, bf16[256,4096]{1,0:T(8,128)(2,1)} %bitcast.121, bf16[256,4096]{1,0:T(8,128)(2,1)} %collective-permute-done.got_ref, f32[256,2]{1,0:T(8,128)} %slice_bitcast_fusion.10.par_ref.refs_2_), custom_call_target="tpu_custom_call" | custom-call | flops 209715 | bytes 62914 | tf_op jit(solution)/shard_map/act_one/pallas_call | solution.py:187
  51.3 2.4 fusion
  53.7 4.8 collective-permute-start.6
  62.8 21.9 %conv_one.1 = (bf16[256,4096]{1,0:T(8,128)(2,1)}, f32[256,128]{1,0:T(8,128)}, f32[256,4096]{1,0:T(8,128)}, bf16[256,4608]{1,0:T(8,128)(2,1)}) custom-call(s32[2]{0:T(128)} %pad_add_fusion.meta, bf16[256,4608]{1,0:T(8,128)(2,1)} %w_own.2, bf16[256,4608]{1,0:T(8,128)(2,1)} %collective-permute-done.8.w_got, bf16[256,4096]{1,0:T(8,128)(2,1)} %get-tuple-element.82.refs_0_, ...), custom_call_target="tpu_custom_call" | custom-call | flops 96636768 | bytes 107530 | tf_op jit(solution)/shard_map/conv_one/pallas_call | solution.py:259
  84.8 3.6 collective-permute-start.11
  88.4 1.9 collective-permute-start.12
  91.1 19.4 %collective-permute-done.7.got_ref = bf16[256,4096]{1,0:T(8,128)(2,1)} collective-permute-done((bf16[256,4096]{1,0:T(8,128)(2,1)}, bf16[256,4096]{1,0:T(8,128)(2,1)}, u32[]{:S(2)}, u32[]{:S(2)}) %collective-permute-start.7) | collective-permute-done | bytes 2097184 | tf_op jit(solution)/shard_map/ppermute | solution.py:874
  110.5 22.3 %conv_two.1 = (bf16[256,4096]{1,0:T(8,128)(2,1)}, f32[256,128]{1,0:T(8,128)}, f32[256,4096]{1,0:T(8,128)}, bf16[256,4608]{1,0:T(8,128)(2,1)}) custom-call(s32[2]{0:T(128)} %pad_add_fusion.meta, bf16[256,4608]{1,0:T(8,128)(2,1)} %w_own.3, bf16[256,4608]{1,0:T(8,128)(2,1)} %collective-permute-done.6.w_got, bf16[256,4096]{1,0:T(8,128)(2,1)} %get-tuple-element.88.refs_0_, ...), custom_call_target="tpu_custom_call" | custom-call | flops 96636768 | bytes 128481 | tf_op jit(solution)/shard_map/conv_two/pallas_call | solution.py:259
  136.0 4.7 fold.1.refs_0_.refs_5_
  141.6 4.8 grad_heads.1
  153.3 7.7 %qkv.1 = bf16[768,4096]{1,0:T(8,128)(2,1)} custom-call(s32[2]{0:T(128)} %pad_add_fusion.meta, bf16[768,512]{1,0:T(8,128)(2,1)} %get-tuple-element.251.w_ref, bf16[256,4096]{1,0:T(8,128)(2,1)} %get-tuple-element.91.refs_0_.refs_3_, bf16[256,4096]{1,0:T(8,128)(2,1)} %collective-permute-done.13.refs_1_.refs_4_, f32[768,1]{1,0:T(8,128)} %bitcast.123), custom_call_target="tpu_custom_call" | custom-call | flops 32212254 | bytes 104857 | tf_op jit(solution)/shard_map/qkv/pallas_call | solution.py:524
  161.0 233.8 %attention.1 = (bf16[4,64,4096]{2,1,0:T(8,128)(2,1)}, bf16[4,64,4096]{2,1,0:T(8,128)(2,1)}, bf16[4,64,4096]{2,1,0:T(8,128)(2,1)}, bf16[4,64,4096]{2,1,0:T(8,128)...) custom-call(s32[1]{0:T(128)} %bitcast.21.lim_ref, bf16[3,4,64,4096]{3,2,1,0:T(8,128)(2,1)} %bitcast.103, ...), custom_call_target="tpu_custom_call" | custom-call | flops 1159641216 | bytes 167772 | tf_op jit(solution)/shard_map/attention/pallas_call | solution.py:766
  394.8 7.7 %grad_normed.1 = (bf16[256,4096]{1,0:T(8,128)(2,1)}, bf16[256,4096]{1,0:T(8,128)(2,1)}) custom-call(s32[2]{0:T(128)} %pad_add_fusion.meta, bf16[512,768]{1,0:T(8,128)(2,1)} %copy.127.w_ref, bf16[256,4096]{1,0:T(8,128)(2,1)} %bitcast.110, bf16[256,4096]{1,0:T(8,128)(2,1)} %bitcast.112, bf16[256,4096]{1,0:T(8,128)(2,1)} %bitcast.114), custom_call_target="tpu_custom_call" | custom-call | flops 32212254 | bytes 104857 | tf_op jit(solution)/shard_map/grad_normed/pallas_call | solution.py:558
  403.1 3.9 collective-permute-done.18.refs_1_
  407.0 10.2 %norm_three_back.1 = (f32[256,4096]{1,0:T(8,128)}, bf16[256,4096]{1,0:T(8,128)(2,1)}, f32[256,128]{1,0:T(8,128)}) custom-call(bf16[256,4096]{1,0:T(8,128)(2,1)} %get-tuple-element.108.refs_0_, bf16[256,4096]{1,0:T(8,128)(2,1)} %collective-permute-done.18.refs_1_, f32[256,4096]{1,0:T(8,128)} %get-tuple-element.129.refs_2_.refs_3_, ...), custom_call_target="tpu_custom_call" | custom-call | flops 209715 | bytes 167772 | tf_op jit(solution)/shard_map/norm_three_back/pallas_call | solution.py:494
  417.2 16.4 %conv_two_weight_grad.1 = bf16[256,4608]{1,0:T(8,128)(2,1)} custom-call(s32[2]{0:T(128)} %pad_add_fusion.meta, bf16[256,4096]{1,0:T(8,128)(2,1)} %get-tuple-element.113.grad_ref.refs_0_, bf16[256,4096]{1,0:T(8,128)(2,1)} %get-tuple-element.88.refs_0_, bf16[256,4096]{1,0:T(8,128)(2,1)} %collective-permute-done.10.refs_1_), custom_call_target="tpu_custom_call" | custom-call | flops 96636768 | bytes 86507 | tf_op jit(solution)/shard_map/conv_two_weight_grad/pallas_call | solution.py:417
  433.5 3.6 collective-permute-start.22
  437.2 8.5 %qkv_grad.1 = (bf16[768,512]{1,0:T(8,128)(2,1)}, f32[768,128]{1,0:T(8,128)}) custom-call(s32[2]{0:T(128)} %pad_add_fusion.meta, bf16[256,4096]{1,0:T(8,128)(2,1)} %bitcast.111, bf16[256,4096]{1,0:T(8,128)(2,1)} %bitcast.113, bf16[256,4096]{1,0:T(8,128)(2,1)} %bitcast.115, bf16[256,4096]{1,0:T(8,128)(2,1)} %get-tuple-element.91.refs_0_.refs_3_, ...), custom_call_target="tpu_custom_call" | custom-call | flops 32212254 | bytes 104857 | tf_op jit(solution)/shard_map/qkv_grad/pallas_call | solution.py:632
  445.7 2.1 constant_dynamic-update-slice_fusion.1
  447.8 5.3 out_grad.1
  454.7 2.1 collective-permute-start.20
  457.2 3.4 collective-permute-start.21
  460.7 4.5 turn.3.w_own.w_got
  465.2 24.7 %conv_two_back.1 = (bf16[256,4096]{1,0:T(8,128)(2,1)}, f32[256,128]{1,0:T(8,128)}) custom-call(s32[2]{0:T(128)} %pad_add_fusion.meta, bf16[256,4608]{1,0:T(8,128)(2,1)} %turn.3.w_own.w_got, bf16[256,4608]{1,0:T(8,128)(2,1)} %turn.3.w_own.w_got, bf16[256,4096]{1,0:T(8,128)(2,1)} %get-tuple-element.113.grad_ref.refs_0_, ...), custom_call_target="tpu_custom_call" | custom-call | flops 96636768 | bytes 150784 | tf_op jit(solution)/shard_map/conv_two_back/pallas_call | solution.py:259
  491.3 2.3 convolution_convert_fusion
  498.8 3.7 select_dynamic-update-slice_fusion
  503.8 16.6 %conv_one_weight_grad.1 = bf16[256,4608]{1,0:T(8,128)(2,1)} custom-call(s32[2]{0:T(128)} %pad_add_fusion.meta, bf16[256,4096]{1,0:T(8,128)(2,1)} %get-tuple-element.124.grad_ref.refs_0_, bf16[256,4096]{1,0:T(8,128)(2,1)} %get-tuple-element.82.refs_0_, bf16[256,4096]{1,0:T(8,128)(2,1)} %collective-permute-done.9.refs_1_), custom_call_target="tpu_custom_call" | custom-call | flops 96636768 | bytes 86507 | tf_op jit(solution)/shard_map/conv_one_weight_grad/pallas_call | solution.py:417
  520.3 2.1 collective-permute-start.24
  522.6 4.8 turn.2.w_own.w_got
  528.0 24.7 %conv_one_back.1 = (bf16[256,4096]{1,0:T(8,128)(2,1)}, f32[256,128]{1,0:T(8,128)}) custom-call(s32[2]{0:T(128)} %pad_add_fusion.meta, bf16[256,4608]{1,0:T(8,128)(2,1)} %turn.2.w_own.w_got, bf16[256,4608]{1,0:T(8,128)(2,1)} %turn.2.w_own.w_got, bf16[256,4096]{1,0:T(8,128)(2,1)} %get-tuple-element.124.grad_ref.refs_0_, ...), custom_call_target="tpu_custom_call" | custom-call | flops 96636768 | bytes 171724 | tf_op jit(solution)/shard_map/conv_one_back/pallas_call | solution.py:259
  554.2 3.6 collective-permute-done.25
  559.0 2.1 collective-permute-done.26
  564.2 2.4 collective-permute-start.28
  568.1 4.2 collective-permute-start.29
  573.0 4.6 collective-permute-start.46
  582.0 6.6 output.1
  588.5 1.9 broadcast_select_fusion
  592.9 2.3 pad_maximum_fusion
  600.1 5.2 collective-permute-done.31
  607.5 4.5 collective-permute-start.40
  612.0 6.8 collective-permute-done.32
  618.8 2.1 collective-permute-start.33
  621.9 8.7 %collective-permute-done.33 = bf16[8,4608]{1,0:T(8,128)(2,1)S(1)} collective-permute-done((bf16[8,4608]{1,0:T(8,128)(2,1)S(1)}, bf16[8,4608]{1,0:T(8,128)(2,1)S(1)}, u32[]{:S(2)}, u32[]{:S(2)}) %collective-permute-start.33) | collective-permute-done | bytes 73760 | tf_op jit(solution)/shard_map/ppermute | solution.py:880
  631.6 3.2 collective-permute-done.34
  635.0 1.9 collective-permute-start.43
  636.9 13.5 %collective-permute-done.35 = bf16[16,4608]{1,0:T(8,128)(2,1)S(1)} collective-permute-done((bf16[16,4608]{1,0:T(8,128)(2,1)S(1)}, bf16[16,4608]{1,0:T(8,128)(2,1)S(1)}, u32[]{:S(2)}, u32[]{:S(2)}) %collective-permute-start.35) | collective-permute-done | bytes 147488 | tf_op jit(solution)/shard_map/ppermute | solution.py:880
  650.4 2.4 collective-permute-start.36
  652.9 4.7 collective-permute-done.36
  657.7 3.2 collective-permute-start.37
  662.7 4.7 collective-permute-start.47
  667.4 3.5 collective-permute-done.44
  673.9 2.7 fusion.20
  676.6 14.2 %collective-permute-done.47 = bf16[256,4096]{1,0:T(8,128)(2,1)S(1)} collective-permute-done((bf16[256,4096]{1,0:T(8,128)(2,1)S(1)}, bf16[256,4096]{1,0:T(8,128)(2,1)S(1)}, u32[]{:S(2)}, u32[]{:S(2)}) %collective-permute-start.47) | collective-permute-done | bytes 2097184 | tf_op jit(solution)/shard_map/ppermute | solution.py:874
  690.8 2.9 select_convert_fusion
  693.7 6.3 copy.133
  700.1 3.1 broadcast_select_fusion.1
  704.9 2.1 slice_convert_fusion.1
  707.0 4.4 slice_convert_fusion
  711.4 2.3 maximum_convert_fusion
  (232 shorter events, 68.5 us)
Async XLA Ops:
  7.2 44.0 %copy-start = (bf16[1,260,2048]{2,1,0:T(8,128)(2,1)S(1)}, bf16[1,260,2048]{2,1,0:T(8,128)(2,1)}, u32[]{:S(2)}) copy-start(bf16[1,260,2048]{2,1,0:T(8,128)(2,1)} %param.26) | copy-start | bytes 3194884
  7.2 8.4 %copy-start.26 = (f32[256]{0:T(256)S(1)}, f32[256]{0:T(256)}, u32[]{:S(2)}) copy-start(f32[256]{0:T(256)} %param.38) | copy-start | bytes 3076
  7.2 8.4 %copy-start.27 = (f32[256]{0:T(256)S(1)}, f32[256]{0:T(256)}, u32[]{:S(2)}) copy-start(f32[256]{0:T(256)} %param.39) | copy-start | bytes 3076
  7.2 8.4 %copy-start.28 = (f32[256]{0:T(256)S(1)}, f32[256]{0:T(256)}, u32[]{:S(2)}) copy-start(f32[256]{0:T(256)} %param.45) | copy-start | bytes 3076
  7.3 8.4 %copy-start.20 = (f32[256]{0:T(256)S(1)}, f32[256]{0:T(256)}, u32[]{:S(2)}) copy-start(f32[256]{0:T(256)} %param.28) | copy-start | bytes 3076
  7.3 8.4 %copy-start.21 = (f32[256]{0:T(256)S(1)}, f32[256]{0:T(256)}, u32[]{:S(2)}) copy-start(f32[256]{0:T(256)} %param.29) | copy-start | bytes 3076
  7.3 8.4 %copy-start.22 = (f32[256]{0:T(256)S(1)}, f32[256]{0:T(256)}, u32[]{:S(2)}) copy-start(f32[256]{0:T(256)} %param.31) | copy-start | bytes 3076
  7.3 581.2 %reduce-scatter.2.cloned.1.call-start = ((), (), s32[]{:S(2)}) async-start(), calls=%async_computation.1 | async-start | bytes 5849088 | tf_op jit(solution)/shard_map/reduce_scatter | solution.py:1048
  7.4 34.8 %collective-permute-start = (bf16[256,4096]{1,0:T(8,128)(2,1)}, bf16[256,4096]{1,0:T(8,128)(2,1)}, u32[]{:S(2)}, u32[]{:S(2)}) collective-permute-start(bf16[256,4096]{1,0:T(8,128)(2,1)} %bitcast.120), channel_id=1, source_target_pairs={{1,2},{2,1},{5,6},{6,5},{9,10},{10,9},{13,14},{14,13},{17,18},{18,... | collective-permute-start | bytes 6291464 | tf_op jit(solution)/shard_map/ppermute | solution.py:874
  12.9 8.6 %collective-permute-start.1 = (bf16[16,2048]{1,0:T(8,128)(2,1)S(1)}, bf16[16,2048]{1,0:T(8,128)(2,1)S(1)}, u32[]{:S(2)}, u32[]{:S(2)}) collective-permute-start(bf16[16,2048]{1,0:T(8,128)(2,1)S(1)} %broadcast_select_fusion.5), channel_id=1, source_target_pairs={{0,2},{2,0},{4,6},{6,4},{8,10},{10,8},{12,14},{14,12},{16,18},{18,... | collective-permute-start | bytes 196616 | tf_op jit(solution)/shard_map/ppermute | solution.py:880
  15.9 21.5 %collective-permute-start.5 = (f32[15,256]{0,1:T(8,128)S(1)}, f32[15,256]{0,1:T(8,128)S(1)}, u32[]{:S(2)}, u32[]{:S(2)}) collective-permute-start(f32[15,256]{0,1:T(8,128)S(1)} %copy.120), channel_id=1, source_target_pairs={{1,2},{2,1},{5,6},{6,5},{9,10},{10,9},{13,14},{14,13},{17,18},{18,... | collective-permute-start | bytes 46088 | tf_op jit(solution)/shard_map/ppermute | solution.py:874
  17.8 45.0 %collective-permute-start.8 = (bf16[256,4608]{1,0:T(8,128)(2,1)}, bf16[256,4608]{1,0:T(8,128)(2,1)}, u32[]{:S(2)}, u32[]{:S(2)}) collective-permute-start(bf16[256,4608]{1,0:T(8,128)(2,1)} %w_own.2), channel_id=1, source_target_pairs={{1,2},{2,1},{5,6},{6,5},{9,10},{10,9},{13,14},{14,13},{17,18},{18,... | collective-permute-start | bytes 7077896 | tf_op jit(solution)/shard_map/ppermute | solution.py:874
  21.5 3.2 collective-permute-start.2
  24.8 12.6 %collective-permute-start.3 = (bf16[16,2048]{1,0:T(8,128)(2,1)S(1)}, bf16[16,2048]{1,0:T(8,128)(2,1)S(1)}, u32[]{:S(2)}, u32[]{:S(2)}) collective-permute-start(bf16[16,2048]{1,0:T(8,128)(2,1)S(1)} %fusion.30), channel_id=1, source_target_pairs={{0,8},{2,10},{4,12},{6,14},{8,0},{10,2},{12,4},{14,6},{16,24},{18,... | collective-permute-start | bytes 196616 | tf_op jit(solution)/shard_map/ppermute | solution.py:880
  37.4 4.1 collective-permute-start.4
  42.1 9.1 %copy-start.29 = (f32[2,256]{1,0:T(2,128)S(1)}, f32[2,256]{1,0:T(2,128)}, u32[]{:S(2)}) copy-start(f32[2,256]{1,0:T(2,128)} %param.43) | copy-start | bytes 6148
  51.2 11.6 %collective-permute-start.9 = (bf16[256,4096]{1,0:T(8,128)(2,1)}, bf16[256,4096]{1,0:T(8,128)(2,1)}, u32[]{:S(2)}, u32[]{:S(2)}) collective-permute-start(bf16[256,4096]{1,0:T(8,128)(2,1)} %get-tuple-element.82.refs_0_), channel_id=1, source_target_pairs={{0,2},{2,0},{4,6},{6,4},{8,10},{10,8},{12,14},{14,12},{16,18},{18,... | collective-permute-start | bytes 6291464 | tf_op jit(solution)/shard_map/ppermute | solution.py:880
  53.7 56.8 %collective-permute-start.6 = (bf16[256,4608]{1,0:T(8,128)(2,1)}, bf16[256,4608]{1,0:T(8,128)(2,1)}, u32[]{:S(2)}, u32[]{:S(2)}) collective-permute-start(bf16[256,4608]{1,0:T(8,128)(2,1)} %w_own.3), channel_id=1, source_target_pairs={{1,2},{2,1},{5,6},{6,5},{9,10},{10,9},{13,14},{14,13},{17,18},{18,... | collective-permute-start | bytes 7077896 | tf_op jit(solution)/shard_map/ppermute | solution.py:874
  60.3 50.2 %collective-permute-start.7 = (bf16[256,4096]{1,0:T(8,128)(2,1)}, bf16[256,4096]{1,0:T(8,128)(2,1)}, u32[]{:S(2)}, u32[]{:S(2)}) collective-permute-start(bf16[256,4096]{1,0:T(8,128)(2,1)} %bitcast.18.own_ref), channel_id=1, source_target_pairs={{1,2},{2,1},{5,6},{6,5},{9,10},{10,9},{13,14},{14,13},{17,18},{18,... | collective-permute-start | bytes 6291464 | tf_op jit(solution)/shard_map/ppermute | solution.py:874
  84.7 25.8 %collective-permute-start.10 = (bf16[256,4096]{1,0:T(8,128)(2,1)}, bf16[256,4096]{1,0:T(8,128)(2,1)}, u32[]{:S(2)}, u32[]{:S(2)}) collective-permute-start(bf16[256,4096]{1,0:T(8,128)(2,1)} %get-tuple-element.88.refs_0_), channel_id=1, source_target_pairs={{0,2},{2,0},{4,6},{6,4},{8,10},{10,8},{12,14},{14,12},{16,18},{18,... | collective-permute-start | bytes 6291464 | tf_op jit(solution)/shard_map/ppermute | solution.py:880
  84.8 48.1 %collective-permute-start.11 = (bf16[1024,512]{1,0:T(8,128)(2,1)}, bf16[1024,512]{1,0:T(8,128)(2,1)}, u32[]{:S(2)}, u32[]{:S(2)}) collective-permute-start(bf16[1024,512]{1,0:T(8,128)(2,1)} %pad_maximum_fusion.2), channel_id=1, source_target_pairs={{1,2},{2,1},{5,6},{6,5},{9,10},{10,9},{13,14},{14,13},{17,18},{18,... | collective-permute-start | bytes 3145736 | tf_op jit(solution)/shard_map/ppermute | solution.py:874
  88.4 44.5 %collective-permute-start.12 = (bf16[2,256,384]{1,2,0:T(8,128)(2,1)S(1)}, bf16[2,256,384]{1,2,0:T(8,128)(2,1)}, u32[]{:S(2)}, u32[]{:S(2)}) collective-permute-start(bf16[2,256,384]{1,2,0:T(8,128)(2,1)S(1)} %pad.4), channel_id=1, source_target_pairs={{1,2},{2,1},{5,6},{6,5},{9,10},{10,9},{13,14},{14,13},{17,18},{18,... | collective-permute-start | bytes 1179656 | tf_op jit(solution)/shard_map/ppermute | solution.py:874
  132.8 20.5 %collective-permute-start.13 = (bf16[256,4096]{1,0:T(8,128)(2,1)}, bf16[256,4096]{1,0:T(8,128)(2,1)}, u32[]{:S(2)}, u32[]{:S(2)}) collective-permute-start(bf16[256,4096]{1,0:T(8,128)(2,1)} %get-tuple-element.91.refs_0_.refs_3_), channel_id=1, source_target_pairs={{0,2},{2,0},{4,6},{6,4},{8,10},{10,8},{12,14},{14,12},{16,18},{18,... | collective-permute-start | bytes 6291464 | tf_op jit(solution)/shard_map/ppermute | solution.py:880
  146.3 14.7 %collective-permute-start.14 = (bf16[256,4096]{1,0:T(8,128)(2,1)}, bf16[256,4096]{1,0:T(8,128)(2,1)}, u32[]{:S(2)}, u32[]{:S(2)}) collective-permute-start(bf16[256,4096]{1,0:T(8,128)(2,1)} %get-tuple-element.97), channel_id=1, source_target_pairs={{0,2},{2,0},{4,6},{6,4},{8,10},{10,8},{12,14},{14,12},{16,18},{18,... | collective-permute-start | bytes 6291464 | tf_op jit(solution)/shard_map/ppermute | solution.py:880
  402.5 4.5 collective-permute-start.18
  402.5 45.3 %collective-permute-start.15 = (bf16[256,4096]{1,0:T(8,128)(2,1)}, bf16[256,4096]{1,0:T(8,128)(2,1)}, u32[]{:S(2)}, u32[]{:S(2)}) collective-permute-start(bf16[256,4096]{1,0:T(8,128)(2,1)} %bitcast.107), channel_id=1, source_target_pairs={{0,2},{2,0},{4,6},{6,4},{8,10},{10,8},{12,14},{14,12},{16,18},{18,... | collective-permute-start | bytes 6291464 | tf_op jit(solution)/shard_map/ppermute | solution.py:880
  403.0 57.7 %collective-permute-start.17 = (bf16[256,4608]{1,0:T(8,128)(2,1)}, bf16[256,4608]{1,0:T(8,128)(2,1)}, u32[]{:S(2)}, u32[]{:S(2)}) collective-permute-start(bf16[256,4608]{1,0:T(8,128)(2,1)} %get-tuple-element.104.own_ref), channel_id=1, source_target_pairs={{0,2},{2,0},{4,6},{6,4},{8,10},{10,8},{12,14},{14,12},{16,18},{18,... | collective-permute-start | bytes 7077896 | tf_op jit(solution)/shard_map/ppermute | solution.py:880
  433.5 56.4 %collective-permute-start.22 = (bf16[256,4608]{1,0:T(8,128)(2,1)}, bf16[256,4608]{1,0:T(8,128)(2,1)}, u32[]{:S(2)}, u32[]{:S(2)}) collective-permute-start(bf16[256,4608]{1,0:T(8,128)(2,1)} %conv_two_weight_grad.1), channel_id=1, source_target_pairs={{1,2},{2,1},{5,6},{6,5},{9,10},{10,9},{13,14},{14,13},{17,18},{18,... | collective-permute-start | bytes 7077896 | tf_op jit(solution)/shard_map/ppermute | solution.py:874
  437.1 28.0 %collective-permute-start.19 = (bf16[256,4096]{1,0:T(8,128)(2,1)}, bf16[256,4096]{1,0:T(8,128)(2,1)}, u32[]{:S(2)}, u32[]{:S(2)}) collective-permute-start(bf16[256,4096]{1,0:T(8,128)(2,1)} %get-tuple-element.113.grad_ref.refs_0_), channel_id=1, source_target_pairs={{0,2},{2,0},{4,6},{6,4},{8,10},{10,8},{12,14},{14,12},{16,18},{18,... | collective-permute-start | bytes 6291464 | tf_op jit(solution)/shard_map/ppermute | solution.py:880
  447.8 9.1 %copy-start.15 = (bf16[4,64,384]{2,1,0:T(8,128)(2,1)S(1)}, bf16[4,64,384]{2,1,0:T(8,128)(2,1)}, u32[]{:S(2)}) copy-start(bf16[4,64,384]{2,1,0:T(8,128)(2,1)} %get-tuple-element.101) | copy-start | bytes 589828
  447.8 9.3 %copy-start.14 = (bf16[4,64,384]{2,1,0:T(8,128)(2,1)S(1)}, bf16[4,64,384]{2,1,0:T(8,128)(2,1)}, u32[]{:S(2)}) copy-start(bf16[4,64,384]{2,1,0:T(8,128)(2,1)} %get-tuple-element.102) | copy-start | bytes 589828
  454.7 35.2 %collective-permute-start.20 = (bf16[1024,512]{1,0:T(8,128)(2,1)}, bf16[1024,512]{1,0:T(8,128)(2,1)}, u32[]{:S(2)}, u32[]{:S(2)}) collective-permute-start(bf16[1024,512]{1,0:T(8,128)(2,1)} %constant_dynamic-update-slice_fusion), channel_id=1, source_target_pairs={{1,2},{2,1},{5,6},{6,5},{9,10},{10,9},{13,14},{14,13},{17,18},{18,... | collective-permute-start | bytes 3145736 | tf_op jit(solution)/shard_map/ppermute | solution.py:874
  457.2 32.6 %collective-permute-start.21 = (bf16[2,256,384]{1,2,0:T(8,128)(2,1)S(1)}, bf16[2,256,384]{1,2,0:T(8,128)(2,1)}, u32[]{:S(2)}, u32[]{:S(2)}) collective-permute-start(bf16[2,256,384]{1,2,0:T(8,128)(2,1)S(1)} %pad_maximum_fusion.3), channel_id=1, source_target_pairs={{1,2},{2,1},{5,6},{6,5},{9,10},{10,9},{13,14},{14,13},{17,18},{18,... | collective-permute-start | bytes 1179656 | tf_op jit(solution)/shard_map/ppermute | solution.py:874
  502.5 200.7 %all-gather.2.cloned.1.call-start = ((), (), s32[]{:S(2)}) async-start(), calls=%async_computation.2 | async-start | bytes 5849088 | tf_op jit(solution)/shard_map/all_gather | solution.py:1084
  502.6 20.0 %collective-permute-start.16 = (bf16[256,4608]{1,0:T(8,128)(2,1)}, bf16[256,4608]{1,0:T(8,128)(2,1)}, u32[]{:S(2)}, u32[]{:S(2)}) collective-permute-start(bf16[256,4608]{1,0:T(8,128)(2,1)} %get-tuple-element.100.own_ref), channel_id=1, source_target_pairs={{0,2},{2,0},{4,6},{6,4},{8,10},{10,8},{12,14},{14,12},{16,18},{18,... | collective-permute-start | bytes 7077896 | tf_op jit(solution)/shard_map/ppermute | solution.py:880
  502.7 25.3 %collective-permute-start.23 = (bf16[256,4096]{1,0:T(8,128)(2,1)}, bf16[256,4096]{1,0:T(8,128)(2,1)}, u32[]{:S(2)}, u32[]{:S(2)}) collective-permute-start(bf16[256,4096]{1,0:T(8,128)(2,1)} %get-tuple-element.124.grad_ref.refs_0_), channel_id=1, source_target_pairs={{0,2},{2,0},{4,6},{6,4},{8,10},{10,8},{12,14},{14,12},{16,18},{18,... | collective-permute-start | bytes 6291464 | tf_op jit(solution)/shard_map/ppermute | solution.py:880
  503.8 18.7 %copy-start.16 = (f32[256,128]{1,0:T(8,128)S(1)}, f32[256,128]{1,0:T(8,128)}, u32[]{:S(2)}) copy-start(f32[256,128]{1,0:T(8,128)} %get-tuple-element.130) | copy-start | bytes 393220
  520.3 61.6 %collective-permute-start.24 = (bf16[256,4608]{1,0:T(8,128)(2,1)}, bf16[256,4608]{1,0:T(8,128)(2,1)}, u32[]{:S(2)}, u32[]{:S(2)}) collective-permute-start(bf16[256,4608]{1,0:T(8,128)(2,1)} %conv_one_weight_grad.1), channel_id=1, source_target_pairs={{1,2},{2,1},{5,6},{6,5},{9,10},{10,9},{13,14},{14,13},{17,18},{18,... | collective-permute-start | bytes 7077896 | tf_op jit(solution)/shard_map/ppermute | solution.py:874
  528.0 50.4 %copy-start.11 = (bf16[16,2048]{1,0:T(8,128)(2,1)S(1)}, bf16[16,2048]{1,0:T(8,128)(2,1)}, u32[]{:S(2)}) copy-start(bf16[16,2048]{1,0:T(8,128)(2,1)} %add.173) | copy-start | bytes 196612
  554.1 3.6 collective-permute-start.25
  557.7 3.4 collective-permute-start.26
  561.1 3.0 collective-permute-start.27
  564.2 3.9 collective-permute-start.28
  568.1 9.6 %collective-permute-start.29 = (f32[46,256]{1,0:T(8,128)S(1)}, f32[46,256]{1,0:T(8,128)S(1)}, u32[]{:S(2)}, u32[]{:S(2)}) collective-permute-start(f32[46,256]{1,0:T(8,128)S(1)} %add.186), channel_id=1, source_target_pairs={{0,2},{2,0},{4,6},{6,4},{8,10},{10,8},{12,14},{14,12},{16,18},{18,... | collective-permute-start | bytes 141320 | tf_op jit(solution)/shard_map/ppermute | solution.py:880
  573.0 103.6 %collective-permute-start.46 = (bf16[256,4096]{1,0:T(8,128)(2,1)}, bf16[256,4096]{1,0:T(8,128)(2,1)}, u32[]{:S(2)}, u32[]{:S(2)}) collective-permute-start(bf16[256,4096]{1,0:T(8,128)(2,1)} %get-tuple-element.128), channel_id=1, source_target_pairs={{1,2},{2,1},{5,6},{6,5},{9,10},{10,9},{13,14},{14,13},{17,18},{18,... | collective-permute-start | bytes 6291464 | tf_op jit(solution)/shard_map/ppermute | solution.py:874
  591.5 3.8 collective-permute-start.30
  595.2 3.1 collective-permute-start.38
  596.6 8.6 %collective-permute-start.31 = (bf16[32,4608]{1,0:T(8,128)(2,1)S(1)}, bf16[32,4608]{1,0:T(8,128)(2,1)S(1)}, u32[]{:S(2)}, u32[]{:S(2)}) collective-permute-start(bf16[32,4608]{1,0:T(8,128)(2,1)S(1)} %constant_dynamic-slice_fusion.6), channel_id=1, source_target_pairs={{0,4},{2,6},{4,0},{6,2},{8,12},{10,14},{12,8},{14,10},{16,20},{18,... | collective-permute-start | bytes 884744 | tf_op jit(solution)/shard_map/ppermute | solution.py:880
  599.6 7.8 %collective-permute-start.39 = (bf16[32,4608]{1,0:T(8,128)(2,1)S(1)}, bf16[32,4608]{1,0:T(8,128)(2,1)S(1)}, u32[]{:S(2)}, u32[]{:S(2)}) collective-permute-start(bf16[32,4608]{1,0:T(8,128)(2,1)S(1)} %constant_dynamic-slice_fusion.2), channel_id=1, source_target_pairs={{0,8},{2,10},{4,12},{6,14},{8,0},{10,2},{12,4},{14,6},{16,24},{18,... | collective-permute-start | bytes 884744 | tf_op jit(solution)/shard_map/ppermute | solution.py:880
  605.3 13.4 %collective-permute-start.32 = (bf16[16,4608]{1,0:T(8,128)(2,1)S(1)}, bf16[16,4608]{1,0:T(8,128)(2,1)S(1)}, u32[]{:S(2)}, u32[]{:S(2)}) collective-permute-start(bf16[16,4608]{1,0:T(8,128)(2,1)S(1)} %constant_dynamic-slice_fusion.5), channel_id=1, source_target_pairs={{0,8},{2,10},{4,12},{6,14},{8,0},{10,2},{12,4},{14,6},{16,24},{18,... | collective-permute-start | bytes 442376 | tf_op jit(solution)/shard_map/ppermute | solution.py:880
  607.5 13.5 %collective-permute-start.40 = (bf16[16,4608]{1,0:T(8,128)(2,1)S(1)}, bf16[16,4608]{1,0:T(8,128)(2,1)S(1)}, u32[]{:S(2)}, u32[]{:S(2)}) collective-permute-start(bf16[16,4608]{1,0:T(8,128)(2,1)S(1)} %constant_dynamic-slice_fusion.1), channel_id=1, source_target_pairs={{0,16},{2,18},{4,20},{6,22},{8,24},{10,26},{12,28},{14,30},{16,0},... | collective-permute-start | bytes 442376 | tf_op jit(solution)/shard_map/ppermute | solution.py:880
  618.8 43.9 %copy-start.3 = (bf16[256,4096]{1,0:T(8,128)(2,1)S(1)}, bf16[256,4096]{1,0:T(8,128)(2,1)}, u32[]{:S(2)}) copy-start(bf16[256,4096]{1,0:T(8,128)(2,1)} %output.1) | copy-start | bytes 6291460
  618.8 11.7 %collective-permute-start.33 = (bf16[8,4608]{1,0:T(8,128)(2,1)S(1)}, bf16[8,4608]{1,0:T(8,128)(2,1)S(1)}, u32[]{:S(2)}, u32[]{:S(2)}) collective-permute-start(bf16[8,4608]{1,0:T(8,128)(2,1)S(1)} %constant_dynamic-slice_fusion.4), channel_id=1, source_target_pairs={{0,16},{2,18},{4,20},{6,22},{8,24},{10,26},{12,28},{14,30},{16,0},... | collective-permute-start | bytes 221192 | tf_op jit(solution)/shard_map/ppermute | solution.py:880
  621.0 9.6 %collective-permute-start.41 = (bf16[8,4608]{1,0:T(8,128)(2,1)S(1)}, bf16[8,4608]{1,0:T(8,128)(2,1)S(1)}, u32[]{:S(2)}, u32[]{:S(2)}) collective-permute-start(bf16[8,4608]{1,0:T(8,128)(2,1)S(1)} %constant_dynamic-slice_fusion), channel_id=1, source_target_pairs={{0,4},{2,6},{4,0},{6,2},{8,12},{10,14},{12,8},{14,10},{16,20},{18,... | collective-permute-start | bytes 221192 | tf_op jit(solution)/shard_map/ppermute | solution.py:880
  630.5 4.3 collective-permute-start.34
  630.7 4.2 collective-permute-start.42
  634.8 15.5 %collective-permute-start.35 = (bf16[16,4608]{1,0:T(8,128)(2,1)S(1)}, bf16[16,4608]{1,0:T(8,128)(2,1)S(1)}, u32[]{:S(2)}, u32[]{:S(2)}) collective-permute-start(bf16[16,4608]{1,0:T(8,128)(2,1)S(1)} %maximum_select_fusion.6), channel_id=1, source_target_pairs={{0,8},{2,10},{4,12},{6,14},{8,0},{10,2},{12,4},{14,6},{16,24},{18,... | collective-permute-start | bytes 442376 | tf_op jit(solution)/shard_map/ppermute | solution.py:880
  635.0 17.8 %collective-permute-start.43 = (bf16[16,4608]{1,0:T(8,128)(2,1)S(1)}, bf16[16,4608]{1,0:T(8,128)(2,1)S(1)}, u32[]{:S(2)}, u32[]{:S(2)}) collective-permute-start(bf16[16,4608]{1,0:T(8,128)(2,1)S(1)} %maximum_select_fusion.7), channel_id=1, source_target_pairs={{0,16},{2,18},{4,20},{6,22},{8,24},{10,26},{12,28},{14,30},{16,0},... | collective-permute-start | bytes 442376 | tf_op jit(solution)/shard_map/ppermute | solution.py:880
  650.4 7.2 collective-permute-start.36
  652.8 18.1 %collective-permute-start.44 = (bf16[32,4608]{1,0:T(8,128)(2,1)S(1)}, bf16[32,4608]{1,0:T(8,128)(2,1)S(1)}, u32[]{:S(2)}, u32[]{:S(2)}) collective-permute-start(bf16[32,4608]{1,0:T(8,128)(2,1)S(1)} %maximum_select_fusion.5), channel_id=1, source_target_pairs={{0,8},{2,10},{4,12},{6,14},{8,0},{10,2},{12,4},{14,6},{16,24},{18,... | collective-permute-start | bytes 884744 | tf_op jit(solution)/shard_map/ppermute | solution.py:880
  657.7 14.4 %collective-permute-start.37 = (bf16[64,4608]{1,0:T(8,128)(2,1)S(1)}, bf16[64,4608]{1,0:T(8,128)(2,1)S(1)}, u32[]{:S(2)}, u32[]{:S(2)}) collective-permute-start(bf16[64,4608]{1,0:T(8,128)(2,1)S(1)} %maximum_select_fusion.2), channel_id=1, source_target_pairs={{0,2},{2,0},{4,6},{6,4},{8,10},{10,8},{12,14},{14,12},{16,18},{18,... | collective-permute-start | bytes 1769480 | tf_op jit(solution)/shard_map/ppermute | solution.py:880
  662.7 28.2 %collective-permute-start.47 = (bf16[256,4096]{1,0:T(8,128)(2,1)S(1)}, bf16[256,4096]{1,0:T(8,128)(2,1)S(1)}, u32[]{:S(2)}, u32[]{:S(2)}) collective-permute-start(bf16[256,4096]{1,0:T(8,128)(2,1)S(1)} %copy-done.3), channel_id=1, source_target_pairs={{1,2},{2,1},{5,6},{6,5},{9,10},{10,9},{13,14},{14,13},{17,18},{18,... | collective-permute-start | bytes 6291464 | tf_op jit(solution)/shard_map/ppermute | solution.py:874
  671.0 2.7 collective-permute-start.45
  673.9 17.0 %copy-start.9 = (bf16[256,4096]{1,0:T(8,128)(2,1)S(1)}, bf16[256,4096]{1,0:T(8,128)(2,1)}, u32[]{:S(2)}) copy-start(bf16[256,4096]{1,0:T(8,128)(2,1)} %get-tuple-element.128) | copy-start | bytes 6291460
  (16 other events, 82.3 us)
Sparse Core Ops, SparseCore 0:
  502.6 80.3 reduce-scatter.1
  595.5 76.1 all-gather.1

commit v6 on v5

--- a/solution.py
+++ b/solution.py
@@ -748,7 +748,7 @@
         dvc_ref[0] = dv_acc[:, HW : HW + CTXP].astype(BF)
 
 
-def attention(limit, qkv, ctx_kv, grads, width=1024, unroll=6, back=512):
+def attention(limit, qkv, ctx_kv, grads, width=1024, unroll=6, back=256):
     heads = qkv.shape[1]
     keys = KEYS
 
@@ -841,7 +841,7 @@
     def everywhere(self, x):
         return lax.psum(x, "dp")
 
-    def sum_owned(self, x):
+    def sum_owned(self, x, late):
         return lax.psum(x, "dp")
 
 
@@ -899,7 +899,7 @@
             x = x + self.over(x, bit)
         return x
 
-    def sum_owned(self, x):
+    def sum_owned(self, x, late):
         rows = x.shape[0] // 2
         order = (self.bits, [self.bits[0], *self.bits[2:], self.bits[1]])
         parts = [lax.slice_in_dim(x, at * rows, (at + 1) * rows) for at in range(2)]
@@ -914,6 +914,7 @@
                 keep = lax.dynamic_slice_in_dim(parts[at], upper(bit) * size, size)
                 send = lax.dynamic_slice_in_dim(parts[at], (1 - upper(bit)) * size, size)
                 parts[at] = (keep.astype(F32) + self.over(send, bit).astype(F32)).astype(BF)
+        parts = list(after(late, *parts))
         for step in reversed(range(len(self.bits))):
             for at in range(2):
                 bit = order[at][step]
@@ -976,10 +977,9 @@
     act_one, stat_one, f_low = first_activation(meta, f_own, f_got, par_one)
     full_one = plan.gather(act_one)
     mats_own = jnp.concatenate([qkv_weight.reshape(3 * ch, C), out_weight])
-    mats_own, ctx_own, cot_own = after(
-        act_one, mats_own, ctx_kv, cotangent.reshape(ch, pixels)
-    )
+    mats_own, ctx_own = after(act_one, mats_own, ctx_kv)
     mats_got, ctx_got = plan.got(mats_own), plan.got(ctx_own)
+    cot_own = after((mats_got, ctx_got), cotangent.reshape(ch, pixels))
     cot_got = plan.got(cot_own)
 
     low, stat, wide = struct((ch, HW), BF), struct((ch, 128), F32), struct((ch, HW), F32)
@@ -990,13 +990,13 @@
     )
     full_two = plan.gather(act_two)
     if moved:
-        full_two = after(cot_got, *full_two)
+        full_two = after((mats_got, ctx_got), *full_two)
     normed, stat_three, hidden, w2 = conv_call(
         conv_two_kernel, meta, (conv2_weight, w2_got), full_two, (par_three, f_low), (),
         [low, stat], [wide, weight], [], "conv_two",
     )
     full_three = plan.gather(normed)
-    mats_got, ctx_got, cot_got = after(normed, mats_got, ctx_got, cot_got)
+    cot_got = after(normed, cot_got)
     mats = plan.pick(mats_own, mats_got)
     w_qkv, w_out = mats[: 3 * ch], mats[3 * ch :]
     cot = folded(meta, cot_own, cot_got)
@@ -1082,7 +1082,7 @@
     )
     early, dw_one, one_got = after((output, small), early, dw_one, one_got)
     early = lax.all_gather(early, "dp", axis=0, tiled=True)
-    dw_one = plan.sum_owned(plan.pick(dw_one, one_got))
+    dw_one = plan.sum_owned(plan.pick(dw_one, one_got), (input_got, output_got))
     mods = small[14:].reshape(plan.images, 2, ch)
     mods_low = mods.astype(BF)
     dw_emb = jnp.stack(
@@ -1091,7 +1091,6 @@
             for t in range(2)
         ]
     )
-    input_got, output_got = after((dw_one, small), input_got, output_got)
     input_grad = plan.pick(input_grad, input_got).astype(F32)
     output = plan.pick(output, output_got)
     early = after((dw_one, small, input_grad, output), early)

time: 732 us -> 700 us (0.956)
  the two profiles are of different devices: /device:TPU:1 before, /device:TPU:5 now
where the time goes in v6:
time: 700 us; the launch traced here: 690 us
  Pallas kernels  426 us (61%)
  starting transfers between devices  106 us (15%)
  waiting for transfers between devices  66.5 us (10%)
  local copies, waits for them, and re-layouts  34.9 us (5%)
  other arithmetic  32.3 us (5%)
  between operations  16.7 us (2%)
  matrix products  7.57 us (1%)
    pallas_call x1, Pallas kernels, attention(): pl.pallas_call(functools.partial(attention_kernel, len(grads), unroll=unr...  225 us
    pallas_call x4, Pallas kernels, conv_call(): pl.pallas_call(functools.partial(kernel, len(pieces)), out_shape=[*outs,...  93.6 us
    ppermute x34, starting transfers between devices, over(): return lax.ppermute(x, 'dp', [(i, i ^ bit) for i in range(self.images)])  81 us
    ppermute x34, waiting for transfers between devices, over(): return lax.ppermute(x, 'dp', [(i, i ^ bit) for i in range(self.images)])  64.1 us
    pallas_call x2, Pallas kernels, conv_weight_grad(): pl.pallas_call(functools.partial(weight_grad_kernel, len(pieces)), out_sh...  33.3 us
    ppermute x13, starting transfers between devices, got(): return lax.ppermute(x, ('dp', 'tensor'), self.far)  22.7 us
    unnamed x68, local copies, waits for them, and re-layouts  15.4 us
  transfers between devices with their start and end apart: 50, of which 18 were waited for; matrix products, arithmetic and copies ran while one was open for 7% of the time, Pallas kernels for 28%

profile of v6, /device:TPU:5, one launch (start us, length us, event | category | flops | bytes accessed | tf_op | source)
XLA Modules:
  0.0 689.8 jit_solution(17648800632894930220)
XLA Ops:
  7.4 2.1 collective-permute-start
  11.0 2.0 fusion.15
  14.6 2.1 collective-permute-start.9
  21.8 2.2 collective-permute-done.3
  24.0 2.4 collective-permute-start.4
  28.9 9.0 %act_one.1 = (bf16[256,4096]{1,0:T(8,128)(2,1)}, f32[256,128]{1,0:T(8,128)}, bf16[256,4096]{1,0:T(8,128)(2,1)}) custom-call(s32[2]{0:T(128)} %pad_add_fusion.meta, bf16[256,4096]{1,0:T(8,128)(2,1)} %bitcast.123, bf16[256,4096]{1,0:T(8,128)(2,1)} %collective-permute-done.got_ref, f32[256,2]{1,0:T(8,128)} %slice_bitcast_fusion.10.par_ref.refs_2_), custom_call_target="tpu_custom_call" | custom-call | flops 209715 | bytes 62914 | tf_op jit(solution)/shard_map/act_one/pallas_call | solution.py:187
  37.9 14.3 %collective-permute-start.10 = (bf16[256,4096]{1,0:T(8,128)(2,1)}, bf16[256,4096]{1,0:T(8,128)(2,1)}, u32[]{:S(2)}, u32[]{:S(2)}) collective-permute-start(bf16[256,4096]{1,0:T(8,128)(2,1)} %get-tuple-element.80.refs_0_), channel_id=1, source_target_pairs={{0,2},{2,0},{4,6},{6,4},{8,10},{10,8},{12,14},{14,12},{16,18},{18,... | collective-permute-start | bytes 6291464 | tf_op jit(solution)/shard_map/ppermute | solution.py:880
  52.2 2.4 fusion
  57.3 2.0 collective-permute-start.7
  60.8 21.9 %conv_one.1 = (bf16[256,4096]{1,0:T(8,128)(2,1)}, f32[256,128]{1,0:T(8,128)}, f32[256,4096]{1,0:T(8,128)}, bf16[256,4608]{1,0:T(8,128)(2,1)}) custom-call(s32[2]{0:T(128)} %pad_add_fusion.meta, bf16[256,4608]{1,0:T(8,128)(2,1)} %w_own.2, bf16[256,4608]{1,0:T(8,128)(2,1)} %collective-permute-done.9.w_got, bf16[256,4096]{1,0:T(8,128)(2,1)} %get-tuple-element.80.refs_0_, ...), custom_call_target="tpu_custom_call" | custom-call | flops 96636768 | bytes 107530 | tf_op jit(solution)/shard_map/conv_one/pallas_call | solution.py:259
  82.7 3.3 collective-permute-start.11
  86.8 2.0 collective-permute-start.13
  89.5 2.3 broadcast_select_fusion.3
  91.8 22.3 %conv_two.1 = (bf16[256,4096]{1,0:T(8,128)(2,1)}, f32[256,128]{1,0:T(8,128)}, f32[256,4096]{1,0:T(8,128)}, bf16[256,4608]{1,0:T(8,128)(2,1)}) custom-call(s32[2]{0:T(128)} %pad_add_fusion.meta, bf16[256,4608]{1,0:T(8,128)(2,1)} %w_own.3, bf16[256,4608]{1,0:T(8,128)(2,1)} %collective-permute-done.7.w_got, bf16[256,4096]{1,0:T(8,128)(2,1)} %get-tuple-element.86.refs_0_, ...), custom_call_target="tpu_custom_call" | custom-call | flops 96636768 | bytes 128481 | tf_op jit(solution)/shard_map/conv_two/pallas_call | solution.py:259
  114.1 17.2 %collective-permute-start.12 = (bf16[256,4096]{1,0:T(8,128)(2,1)}, bf16[256,4096]{1,0:T(8,128)(2,1)}, u32[]{:S(2)}, u32[]{:S(2)}) collective-permute-start(bf16[256,4096]{1,0:T(8,128)(2,1)} %get-tuple-element.89.refs_0_.refs_3_), channel_id=1, source_target_pairs={{0,2},{2,0},{4,6},{6,4},{8,10},{10,8},{12,14},{14,12},{16,18},{18,... | collective-permute-start | bytes 6291464 | tf_op jit(solution)/shard_map/ppermute | solution.py:880
  133.8 4.7 fold.1.refs_0_.refs_5_
  138.6 4.8 grad_heads.1
  148.9 7.7 %qkv.1 = bf16[768,4096]{1,0:T(8,128)(2,1)} custom-call(s32[2]{0:T(128)} %pad_add_fusion.meta, bf16[768,512]{1,0:T(8,128)(2,1)} %get-tuple-element.245.w_ref, bf16[256,4096]{1,0:T(8,128)(2,1)} %get-tuple-element.89.refs_0_.refs_3_, bf16[256,4096]{1,0:T(8,128)(2,1)} %collective-permute-done.12.refs_1_.refs_4_, f32[768,1]{1,0:T(8,128)} %bitcast.125), custom_call_target="tpu_custom_call" | custom-call | flops 32212254 | bytes 104857 | tf_op jit(solution)/shard_map/qkv/pallas_call | solution.py:524
  156.6 225.2 %attention.1 = (bf16[4,64,4096]{2,1,0:T(8,128)(2,1)}, bf16[4,64,4096]{2,1,0:T(8,128)(2,1)}, bf16[4,64,4096]{2,1,0:T(8,128)(2,1)}, bf16[4,64,4096]{2,1,0:T(8,128)...) custom-call(s32[1]{0:T(128)} %bitcast.18.lim_ref, bf16[3,4,64,4096]{3,2,1,0:T(8,128)(2,1)} %bitcast.103, ...), custom_call_target="tpu_custom_call" | custom-call | flops 1159641216 | bytes 167772 | tf_op jit(solution)/shard_map/attention/pallas_call | solution.py:766
  381.9 7.7 %grad_normed.1 = (bf16[256,4096]{1,0:T(8,128)(2,1)}, bf16[256,4096]{1,0:T(8,128)(2,1)}) custom-call(s32[2]{0:T(128)} %pad_add_fusion.meta, bf16[512,768]{1,0:T(8,128)(2,1)} %copy.127.w_ref, bf16[256,4096]{1,0:T(8,128)(2,1)} %bitcast.110, bf16[256,4096]{1,0:T(8,128)(2,1)} %bitcast.112, bf16[256,4096]{1,0:T(8,128)(2,1)} %bitcast.114), custom_call_target="tpu_custom_call" | custom-call | flops 32212254 | bytes 104857 | tf_op jit(solution)/shard_map/grad_normed/pallas_call | solution.py:558
  391.5 3.6 collective-permute-done.18.refs_1_
  395.1 10.2 %norm_three_back.1 = (f32[256,4096]{1,0:T(8,128)}, bf16[256,4096]{1,0:T(8,128)(2,1)}, f32[256,128]{1,0:T(8,128)}) custom-call(bf16[256,4096]{1,0:T(8,128)(2,1)} %get-tuple-element.104.refs_0_, bf16[256,4096]{1,0:T(8,128)(2,1)} %collective-permute-done.18.refs_1_, f32[256,4096]{1,0:T(8,128)} %get-tuple-element.125.refs_2_.refs_3_, ...), custom_call_target="tpu_custom_call" | custom-call | flops 209715 | bytes 167772 | tf_op jit(solution)/shard_map/norm_three_back/pallas_call | solution.py:494
  405.3 16.4 %conv_two_weight_grad.1 = bf16[256,4608]{1,0:T(8,128)(2,1)} custom-call(s32[2]{0:T(128)} %pad_add_fusion.meta, bf16[256,4096]{1,0:T(8,128)(2,1)} %get-tuple-element.109.grad_ref.refs_0_, bf16[256,4096]{1,0:T(8,128)(2,1)} %get-tuple-element.86.refs_0_, bf16[256,4096]{1,0:T(8,128)(2,1)} %collective-permute-done.11.refs_1_), custom_call_target="tpu_custom_call" | custom-call | flops 96636768 | bytes 86507 | tf_op jit(solution)/shard_map/conv_two_weight_grad/pallas_call | solution.py:417
  421.7 2.1 collective-permute-start.22
  423.7 2.0 collective-permute-start.19
  425.8 8.4 %qkv_grad.1 = (bf16[768,512]{1,0:T(8,128)(2,1)}, f32[768,128]{1,0:T(8,128)}) custom-call(s32[2]{0:T(128)} %pad_add_fusion.meta, bf16[256,4096]{1,0:T(8,128)(2,1)} %bitcast.111, bf16[256,4096]{1,0:T(8,128)(2,1)} %bitcast.113, bf16[256,4096]{1,0:T(8,128)(2,1)} %bitcast.115, bf16[256,4096]{1,0:T(8,128)(2,1)} %get-tuple-element.89.refs_0_.refs_3_, ...), custom_call_target="tpu_custom_call" | custom-call | flops 32212254 | bytes 104857 | tf_op jit(solution)/shard_map/qkv_grad/pallas_call | solution.py:632
  434.2 2.1 constant_dynamic-update-slice_fusion.1
  436.3 5.3 out_grad.1
  446.7 4.5 turn.3.w_own.w_got
  451.2 24.6 %conv_two_back.1 = (bf16[256,4096]{1,0:T(8,128)(2,1)}, f32[256,128]{1,0:T(8,128)}) custom-call(s32[2]{0:T(128)} %pad_add_fusion.meta, bf16[256,4608]{1,0:T(8,128)(2,1)} %turn.3.w_own.w_got, bf16[256,4608]{1,0:T(8,128)(2,1)} %turn.3.w_own.w_got, bf16[256,4096]{1,0:T(8,128)(2,1)} %get-tuple-element.109.grad_ref.refs_0_, ...), custom_call_target="tpu_custom_call" | custom-call | flops 96636768 | bytes 150784 | tf_op jit(solution)/shard_map/conv_two_back/pallas_call | solution.py:259
  477.2 2.3 convolution_convert_fusion
  484.6 2.0 select_dynamic-update-slice_fusion
  486.7 4.3 collective-permute-start.16
  491.7 3.9 collective-permute-done.16.other_ref
  495.6 4.6 turn.2.w_own.w_got
  500.3 16.9 %conv_one_weight_grad.1 = bf16[256,4608]{1,0:T(8,128)(2,1)} custom-call(s32[2]{0:T(128)} %pad_add_fusion.meta, bf16[256,4096]{1,0:T(8,128)(2,1)} %get-tuple-element.120.grad_ref.refs_0_, bf16[256,4096]{1,0:T(8,128)(2,1)} %get-tuple-element.80.refs_0_, bf16[256,4096]{1,0:T(8,128)(2,1)} %collective-permute-done.10.refs_1_), custom_call_target="tpu_custom_call" | custom-call | flops 96636768 | bytes 86507 | tf_op jit(solution)/shard_map/conv_one_weight_grad/pallas_call | solution.py:417
  517.2 2.1 collective-permute-start.24
  519.8 24.7 %conv_one_back.1 = (bf16[256,4096]{1,0:T(8,128)(2,1)}, f32[256,128]{1,0:T(8,128)}) custom-call(s32[2]{0:T(128)} %pad_add_fusion.meta, bf16[256,4608]{1,0:T(8,128)(2,1)} %turn.2.w_own.w_got, bf16[256,4608]{1,0:T(8,128)(2,1)} %turn.2.w_own.w_got, bf16[256,4096]{1,0:T(8,128)(2,1)} %get-tuple-element.120.grad_ref.refs_0_, ...), custom_call_target="tpu_custom_call" | custom-call | flops 96636768 | bytes 171724 | tf_op jit(solution)/shard_map/conv_one_back/pallas_call | solution.py:259
  545.8 2.4 collective-permute-start.27
  548.2 2.4 collective-permute-done.27
  556.7 2.2 collective-permute-start.30
  558.9 4.4 collective-permute-done.30
  563.2 4.9 collective-permute-start.31
  568.9 2.0 collective-permute-start.26
  572.6 2.3 pad_maximum_fusion
  574.8 6.5 output.1
  586.7 2.3 collective-permute-start.25
  596.1 5.7 collective-permute-done.37
  602.0 2.6 collective-permute-start.38
  604.7 2.0 collective-permute-start.34
  606.7 11.5 %collective-permute-done.38 = bf16[16,4608]{1,0:T(8,128)(2,1)S(1)} collective-permute-done((bf16[16,4608]{1,0:T(8,128)(2,1)S(1)}, bf16[16,4608]{1,0:T(8,128)(2,1)S(1)}, u32[]{:S(2)}, u32[]{:S(2)}) %collective-permute-start.38) | collective-permute-done | bytes 147488 | tf_op jit(solution)/shard_map/ppermute | solution.py:880
  621.9 3.3 collective-permute-done.35
  625.6 6.3 copy.133
  632.6 3.1 collective-permute-start.41
  637.1 2.4 collective-permute-start.45
  639.5 10.7 %collective-permute-done.41 = bf16[16,4608]{1,0:T(8,128)(2,1)S(1)} collective-permute-done((bf16[16,4608]{1,0:T(8,128)(2,1)S(1)}, bf16[16,4608]{1,0:T(8,128)(2,1)S(1)}, u32[]{:S(2)}, u32[]{:S(2)}) %collective-permute-start.41) | collective-permute-done | bytes 147488 | tf_op jit(solution)/shard_map/ppermute | solution.py:880
  650.5 5.8 collective-permute-done.42
  656.4 3.9 collective-permute-start.43
  661.8 2.1 collective-permute-done.46
  664.0 2.2 collective-permute-start.47
  668.0 2.7 fusion.20
  672.4 2.1 slice_convert_fusion.1
  674.5 4.4 slice_convert_fusion
  678.9 2.3 maximum_convert_fusion
  (230 shorter events, 73.0 us)
Async XLA Ops:
  7.2 45.0 %copy-start = (bf16[1,260,2048]{2,1,0:T(8,128)(2,1)S(1)}, bf16[1,260,2048]{2,1,0:T(8,128)(2,1)}, u32[]{:S(2)}) copy-start(bf16[1,260,2048]{2,1,0:T(8,128)(2,1)} %param.26) | copy-start | bytes 3194884
  7.2 6.4 copy-start.25
  7.2 6.4 copy-start.26
  7.2 6.4 copy-start.27
  7.3 6.4 copy-start.19
  7.3 574.1 %reduce-scatter.2.cloned.1.call-start = ((), (), s32[]{:S(2)}) async-start(), calls=%async_computation.1 | async-start | bytes 5849088 | tf_op jit(solution)/shard_map/reduce_scatter | solution.py:1048
  7.4 21.5 %collective-permute-start = (bf16[256,4096]{1,0:T(8,128)(2,1)}, bf16[256,4096]{1,0:T(8,128)(2,1)}, u32[]{:S(2)}, u32[]{:S(2)}) collective-permute-start(bf16[256,4096]{1,0:T(8,128)(2,1)} %bitcast.122), channel_id=1, source_target_pairs={{1,2},{2,1},{5,6},{6,5},{9,10},{10,9},{13,14},{14,13},{17,18},{18,... | collective-permute-start | bytes 6291464 | tf_op jit(solution)/shard_map/ppermute | solution.py:874
  10.3 6.4 collective-permute-start.1
  13.9 7.9 %collective-permute-start.5 = (f32[15,256]{0,1:T(8,128)S(1)}, f32[15,256]{0,1:T(8,128)S(1)}, u32[]{:S(2)}, u32[]{:S(2)}) collective-permute-start(f32[15,256]{0,1:T(8,128)S(1)} %copy.120), channel_id=1, source_target_pairs={{1,2},{2,1},{5,6},{6,5},{9,10},{10,9},{13,14},{14,13},{17,18},{18,... | collective-permute-start | bytes 46088 | tf_op jit(solution)/shard_map/ppermute | solution.py:874
  14.6 46.2 %collective-permute-start.9 = (bf16[256,4608]{1,0:T(8,128)(2,1)}, bf16[256,4608]{1,0:T(8,128)(2,1)}, u32[]{:S(2)}, u32[]{:S(2)}) collective-permute-start(bf16[256,4608]{1,0:T(8,128)(2,1)} %w_own.2), channel_id=1, source_target_pairs={{1,2},{2,1},{5,6},{6,5},{9,10},{10,9},{13,14},{14,13},{17,18},{18,... | collective-permute-start | bytes 7077896 | tf_op jit(solution)/shard_map/ppermute | solution.py:874
  16.7 3.6 collective-permute-start.2
  20.4 3.6 collective-permute-start.3
  24.0 4.2 collective-permute-start.4
  28.9 23.3 %copy-start.28 = (f32[2,256]{1,0:T(2,128)S(1)}, f32[2,256]{1,0:T(2,128)}, u32[]{:S(2)}) copy-start(f32[2,256]{1,0:T(2,128)} %param.43) | copy-start | bytes 6148
  37.8 16.7 %copy-start.8 = (bf16[3,256,512]{2,1,0:T(8,128)(2,1)S(1)}, bf16[3,256,512]{2,1,0:T(8,128)(2,1)}, u32[]{:S(2)}) copy-start(bf16[3,256,512]{2,1,0:T(8,128)(2,1)} %param.40) | copy-start | bytes 2359300
  37.9 16.7 %copy-start.12 = (bf16[256,512]{1,0:T(8,128)(2,1)S(1)}, bf16[256,512]{1,0:T(8,128)(2,1)}, u32[]{:S(2)}) copy-start(bf16[256,512]{1,0:T(8,128)(2,1)} %param.44) | copy-start | bytes 786436
  37.9 22.9 %collective-permute-start.10 = (bf16[256,4096]{1,0:T(8,128)(2,1)}, bf16[256,4096]{1,0:T(8,128)(2,1)}, u32[]{:S(2)}, u32[]{:S(2)}) collective-permute-start(bf16[256,4096]{1,0:T(8,128)(2,1)} %get-tuple-element.80.refs_0_), channel_id=1, source_target_pairs={{0,2},{2,0},{4,6},{6,4},{8,10},{10,8},{12,14},{14,12},{16,18},{18,... | collective-permute-start | bytes 6291464 | tf_op jit(solution)/shard_map/ppermute | solution.py:880
  55.6 30.4 %collective-permute-start.6 = (bf16[1024,512]{1,0:T(8,128)(2,1)}, bf16[1024,512]{1,0:T(8,128)(2,1)}, u32[]{:S(2)}, u32[]{:S(2)}) collective-permute-start(bf16[1024,512]{1,0:T(8,128)(2,1)} %pad_maximum_fusion.2), channel_id=1, source_target_pairs={{1,2},{2,1},{5,6},{6,5},{9,10},{10,9},{13,14},{14,13},{17,18},{18,... | collective-permute-start | bytes 3145736 | tf_op jit(solution)/shard_map/ppermute | solution.py:874
  57.3 34.5 %collective-permute-start.7 = (bf16[256,4608]{1,0:T(8,128)(2,1)}, bf16[256,4608]{1,0:T(8,128)(2,1)}, u32[]{:S(2)}, u32[]{:S(2)}) collective-permute-start(bf16[256,4608]{1,0:T(8,128)(2,1)} %w_own.3), channel_id=1, source_target_pairs={{1,2},{2,1},{5,6},{6,5},{9,10},{10,9},{13,14},{14,13},{17,18},{18,... | collective-permute-start | bytes 7077896 | tf_op jit(solution)/shard_map/ppermute | solution.py:874
  59.3 26.7 %collective-permute-start.8 = (bf16[2,256,384]{1,2,0:T(8,128)(2,1)S(1)}, bf16[2,256,384]{1,2,0:T(8,128)(2,1)S(1)}, u32[]{:S(2)}, u32[]{:S(2)}) collective-permute-start(bf16[2,256,384]{1,2,0:T(8,128)(2,1)S(1)} %pad.4), channel_id=1, source_target_pairs={{1,2},{2,1},{5,6},{6,5},{9,10},{10,9},{13,14},{14,13},{17,18},{18,... | collective-permute-start | bytes 1179656 | tf_op jit(solution)/shard_map/ppermute | solution.py:874
  82.7 9.1 %collective-permute-start.11 = (bf16[256,4096]{1,0:T(8,128)(2,1)}, bf16[256,4096]{1,0:T(8,128)(2,1)}, u32[]{:S(2)}, u32[]{:S(2)}) collective-permute-start(bf16[256,4096]{1,0:T(8,128)(2,1)} %get-tuple-element.86.refs_0_), channel_id=1, source_target_pairs={{0,2},{2,0},{4,6},{6,4},{8,10},{10,8},{12,14},{14,12},{16,18},{18,... | collective-permute-start | bytes 6291464 | tf_op jit(solution)/shard_map/ppermute | solution.py:880
  86.8 47.1 %collective-permute-start.13 = (bf16[256,4096]{1,0:T(8,128)(2,1)}, bf16[256,4096]{1,0:T(8,128)(2,1)}, u32[]{:S(2)}, u32[]{:S(2)}) collective-permute-start(bf16[256,4096]{1,0:T(8,128)(2,1)} %bitcast.118), channel_id=1, source_target_pairs={{1,2},{2,1},{5,6},{6,5},{9,10},{10,9},{13,14},{14,13},{17,18},{18,... | collective-permute-start | bytes 6291464 | tf_op jit(solution)/shard_map/ppermute | solution.py:874
  114.1 34.8 %collective-permute-start.12 = (bf16[256,4096]{1,0:T(8,128)(2,1)}, bf16[256,4096]{1,0:T(8,128)(2,1)}, u32[]{:S(2)}, u32[]{:S(2)}) collective-permute-start(bf16[256,4096]{1,0:T(8,128)(2,1)} %get-tuple-element.89.refs_0_.refs_3_), channel_id=1, source_target_pairs={{0,2},{2,0},{4,6},{6,4},{8,10},{10,8},{12,14},{14,12},{16,18},{18,... | collective-permute-start | bytes 6291464 | tf_op jit(solution)/shard_map/ppermute | solution.py:880
  143.4 13.3 %collective-permute-start.14 = (bf16[256,4096]{1,0:T(8,128)(2,1)}, bf16[256,4096]{1,0:T(8,128)(2,1)}, u32[]{:S(2)}, u32[]{:S(2)}) collective-permute-start(bf16[256,4096]{1,0:T(8,128)(2,1)} %get-tuple-element.93), channel_id=1, source_target_pairs={{0,2},{2,0},{4,6},{6,4},{8,10},{10,8},{12,14},{14,12},{16,18},{18,... | collective-permute-start | bytes 6291464 | tf_op jit(solution)/shard_map/ppermute | solution.py:880
  389.5 5.6 collective-permute-start.18
  391.0 45.3 %collective-permute-start.15 = (bf16[256,4096]{1,0:T(8,128)(2,1)}, bf16[256,4096]{1,0:T(8,128)(2,1)}, u32[]{:S(2)}, u32[]{:S(2)}) collective-permute-start(bf16[256,4096]{1,0:T(8,128)(2,1)} %bitcast.107), channel_id=1, source_target_pairs={{0,2},{2,0},{4,6},{6,4},{8,10},{10,8},{12,14},{14,12},{16,18},{18,... | collective-permute-start | bytes 6291464 | tf_op jit(solution)/shard_map/ppermute | solution.py:880
  391.1 55.6 %collective-permute-start.17 = (bf16[256,4608]{1,0:T(8,128)(2,1)}, bf16[256,4608]{1,0:T(8,128)(2,1)}, u32[]{:S(2)}, u32[]{:S(2)}) collective-permute-start(bf16[256,4608]{1,0:T(8,128)(2,1)} %get-tuple-element.100.own_ref), channel_id=1, source_target_pairs={{0,2},{2,0},{4,6},{6,4},{8,10},{10,8},{12,14},{14,12},{16,18},{18,... | collective-permute-start | bytes 7077896 | tf_op jit(solution)/shard_map/ppermute | solution.py:880
  421.7 54.2 %collective-permute-start.22 = (bf16[256,4608]{1,0:T(8,128)(2,1)}, bf16[256,4608]{1,0:T(8,128)(2,1)}, u32[]{:S(2)}, u32[]{:S(2)}) collective-permute-start(bf16[256,4608]{1,0:T(8,128)(2,1)} %conv_two_weight_grad.1), channel_id=1, source_target_pairs={{1,2},{2,1},{5,6},{6,5},{9,10},{10,9},{13,14},{14,13},{17,18},{18,... | collective-permute-start | bytes 7077896 | tf_op jit(solution)/shard_map/ppermute | solution.py:874
  423.7 27.4 %collective-permute-start.19 = (bf16[256,4096]{1,0:T(8,128)(2,1)}, bf16[256,4096]{1,0:T(8,128)(2,1)}, u32[]{:S(2)}, u32[]{:S(2)}) collective-permute-start(bf16[256,4096]{1,0:T(8,128)(2,1)} %get-tuple-element.109.grad_ref.refs_0_), channel_id=1, source_target_pairs={{0,2},{2,0},{4,6},{6,4},{8,10},{10,8},{12,14},{14,12},{16,18},{18,... | collective-permute-start | bytes 6291464 | tf_op jit(solution)/shard_map/ppermute | solution.py:880
  436.3 8.6 %copy-start.14 = (bf16[4,64,384]{2,1,0:T(8,128)(2,1)S(1)}, bf16[4,64,384]{2,1,0:T(8,128)(2,1)}, u32[]{:S(2)}) copy-start(bf16[4,64,384]{2,1,0:T(8,128)(2,1)} %get-tuple-element.97) | copy-start | bytes 589828
  436.3 8.8 %copy-start.13 = (bf16[4,64,384]{2,1,0:T(8,128)(2,1)S(1)}, bf16[4,64,384]{2,1,0:T(8,128)(2,1)}, u32[]{:S(2)}) copy-start(bf16[4,64,384]{2,1,0:T(8,128)(2,1)} %get-tuple-element.98) | copy-start | bytes 589828
  443.3 32.6 %collective-permute-start.20 = (bf16[1024,512]{1,0:T(8,128)(2,1)}, bf16[1024,512]{1,0:T(8,128)(2,1)}, u32[]{:S(2)}, u32[]{:S(2)}) collective-permute-start(bf16[1024,512]{1,0:T(8,128)(2,1)} %constant_dynamic-update-slice_fusion), channel_id=1, source_target_pairs={{1,2},{2,1},{5,6},{6,5},{9,10},{10,9},{13,14},{14,13},{17,18},{18,... | collective-permute-start | bytes 3145736 | tf_op jit(solution)/shard_map/ppermute | solution.py:874
  445.3 30.6 %collective-permute-start.21 = (bf16[2,256,384]{1,2,0:T(8,128)(2,1)S(1)}, bf16[2,256,384]{1,2,0:T(8,128)(2,1)}, u32[]{:S(2)}, u32[]{:S(2)}) collective-permute-start(bf16[2,256,384]{1,2,0:T(8,128)(2,1)S(1)} %pad_maximum_fusion.3), channel_id=1, source_target_pairs={{1,2},{2,1},{5,6},{6,5},{9,10},{10,9},{13,14},{14,13},{17,18},{18,... | collective-permute-start | bytes 1179656 | tf_op jit(solution)/shard_map/ppermute | solution.py:874
  486.7 184.1 %all-gather.2.cloned.1.call-start = ((), (), s32[]{:S(2)}) async-start(), calls=%async_computation.2 | async-start | bytes 5849088 | tf_op jit(solution)/shard_map/all_gather | solution.py:1084
  486.7 8.8 %collective-permute-start.16 = (bf16[256,4608]{1,0:T(8,128)(2,1)}, bf16[256,4608]{1,0:T(8,128)(2,1)}, u32[]{:S(2)}, u32[]{:S(2)}) collective-permute-start(bf16[256,4608]{1,0:T(8,128)(2,1)} %get-tuple-element.96.own_ref), channel_id=1, source_target_pairs={{0,2},{2,0},{4,6},{6,4},{8,10},{10,8},{12,14},{14,12},{16,18},{18,... | collective-permute-start | bytes 7077896 | tf_op jit(solution)/shard_map/ppermute | solution.py:880
  491.1 28.7 %collective-permute-start.23 = (bf16[256,4096]{1,0:T(8,128)(2,1)}, bf16[256,4096]{1,0:T(8,128)(2,1)}, u32[]{:S(2)}, u32[]{:S(2)}) collective-permute-start(bf16[256,4096]{1,0:T(8,128)(2,1)} %get-tuple-element.120.grad_ref.refs_0_), channel_id=1, source_target_pairs={{0,2},{2,0},{4,6},{6,4},{8,10},{10,8},{12,14},{14,12},{16,18},{18,... | collective-permute-start | bytes 6291464 | tf_op jit(solution)/shard_map/ppermute | solution.py:880
  491.7 8.5 %copy-start.16 = (f32[256,128]{1,0:T(8,128)S(1)}, f32[256,128]{1,0:T(8,128)}, u32[]{:S(2)}) copy-start(f32[256,128]{1,0:T(8,128)} %get-tuple-element.128) | copy-start | bytes 393220
  517.2 57.6 %collective-permute-start.24 = (bf16[256,4608]{1,0:T(8,128)(2,1)}, bf16[256,4608]{1,0:T(8,128)(2,1)}, u32[]{:S(2)}, u32[]{:S(2)}) collective-permute-start(bf16[256,4608]{1,0:T(8,128)(2,1)} %conv_one_weight_grad.1), channel_id=1, source_target_pairs={{1,2},{2,1},{5,6},{6,5},{9,10},{10,9},{13,14},{14,13},{17,18},{18,... | collective-permute-start | bytes 7077896 | tf_op jit(solution)/shard_map/ppermute | solution.py:874
  519.8 51.8 %copy-start.9 = (bf16[16,2048]{1,0:T(8,128)(2,1)S(1)}, bf16[16,2048]{1,0:T(8,128)(2,1)}, u32[]{:S(2)}) copy-start(bf16[16,2048]{1,0:T(8,128)(2,1)} %add.173) | copy-start | bytes 196612
  545.8 4.8 collective-permute-start.27
  550.6 3.0 collective-permute-start.28
  553.6 3.0 collective-permute-start.29
  556.7 6.6 collective-permute-start.30
  563.2 7.7 %collective-permute-start.31 = (f32[46,256]{1,0:T(8,128)S(1)}, f32[46,256]{1,0:T(8,128)S(1)}, u32[]{:S(2)}, u32[]{:S(2)}) collective-permute-start(f32[46,256]{1,0:T(8,128)S(1)} %add.183), channel_id=1, source_target_pairs={{0,2},{2,0},{4,6},{6,4},{8,10},{10,8},{12,14},{14,12},{16,18},{18,... | collective-permute-start | bytes 141320 | tf_op jit(solution)/shard_map/ppermute | solution.py:880
  568.9 56.3 %collective-permute-start.26 = (bf16[256,4096]{1,0:T(8,128)(2,1)}, bf16[256,4096]{1,0:T(8,128)(2,1)}, u32[]{:S(2)}, u32[]{:S(2)}) collective-permute-start(bf16[256,4096]{1,0:T(8,128)(2,1)} %get-tuple-element.124), channel_id=1, source_target_pairs={{1,2},{2,1},{5,6},{6,5},{9,10},{10,9},{13,14},{14,13},{17,18},{18,... | collective-permute-start | bytes 6291464 | tf_op jit(solution)/shard_map/ppermute | solution.py:874
  584.5 7.1 %collective-permute-start.36 = (bf16[64,4608]{1,0:T(8,128)(2,1)S(1)}, bf16[64,4608]{1,0:T(8,128)(2,1)}, u32[]{:S(2)}, u32[]{:S(2)}) collective-permute-start(bf16[64,4608]{1,0:T(8,128)(2,1)S(1)} %constant_dynamic-slice_fusion.3), channel_id=1, source_target_pairs={{0,2},{2,0},{4,6},{6,4},{8,10},{10,8},{12,14},{14,12},{16,18},{18,... | collective-permute-start | bytes 1769480 | tf_op jit(solution)/shard_map/ppermute | solution.py:880
  586.7 38.6 %collective-permute-start.25 = (bf16[256,4096]{1,0:T(8,128)(2,1)S(1)}, bf16[256,4096]{1,0:T(8,128)(2,1)}, u32[]{:S(2)}, u32[]{:S(2)}) collective-permute-start(bf16[256,4096]{1,0:T(8,128)(2,1)S(1)} %copy-done.3), channel_id=1, source_target_pairs={{1,2},{2,1},{5,6},{6,5},{9,10},{10,9},{13,14},{14,13},{17,18},{18,... | collective-permute-start | bytes 6291464 | tf_op jit(solution)/shard_map/ppermute | solution.py:874
  590.1 3.2 collective-permute-start.32
  593.1 8.8 %collective-permute-start.37 = (bf16[32,4608]{1,0:T(8,128)(2,1)S(1)}, bf16[32,4608]{1,0:T(8,128)(2,1)S(1)}, u32[]{:S(2)}, u32[]{:S(2)}) collective-permute-start(bf16[32,4608]{1,0:T(8,128)(2,1)S(1)} %constant_dynamic-slice_fusion.2), channel_id=1, source_target_pairs={{0,8},{2,10},{4,12},{6,14},{8,0},{10,2},{12,4},{14,6},{16,24},{18,... | collective-permute-start | bytes 884744 | tf_op jit(solution)/shard_map/ppermute | solution.py:880
  594.6 30.7 %copy-start.7 = (bf16[256,4096]{1,0:T(8,128)(2,1)S(1)}, bf16[256,4096]{1,0:T(8,128)(2,1)}, u32[]{:S(2)}) copy-start(bf16[256,4096]{1,0:T(8,128)(2,1)} %get-tuple-element.124) | copy-start | bytes 6291460
  594.6 10.0 %collective-permute-start.33 = (bf16[32,4608]{1,0:T(8,128)(2,1)S(1)}, bf16[32,4608]{1,0:T(8,128)(2,1)S(1)}, u32[]{:S(2)}, u32[]{:S(2)}) collective-permute-start(bf16[32,4608]{1,0:T(8,128)(2,1)S(1)} %constant_dynamic-slice_fusion.6), channel_id=1, source_target_pairs={{0,4},{2,6},{4,0},{6,2},{8,12},{10,14},{12,8},{14,10},{16,20},{18,... | collective-permute-start | bytes 884744 | tf_op jit(solution)/shard_map/ppermute | solution.py:880
  602.0 16.3 %collective-permute-start.38 = (bf16[16,4608]{1,0:T(8,128)(2,1)S(1)}, bf16[16,4608]{1,0:T(8,128)(2,1)S(1)}, u32[]{:S(2)}, u32[]{:S(2)}) collective-permute-start(bf16[16,4608]{1,0:T(8,128)(2,1)S(1)} %constant_dynamic-slice_fusion.1), channel_id=1, source_target_pairs={{0,16},{2,18},{4,20},{6,22},{8,24},{10,26},{12,28},{14,30},{16,0},... | collective-permute-start | bytes 442376 | tf_op jit(solution)/shard_map/ppermute | solution.py:880
  604.7 15.5 %collective-permute-start.34 = (bf16[16,4608]{1,0:T(8,128)(2,1)S(1)}, bf16[16,4608]{1,0:T(8,128)(2,1)S(1)}, u32[]{:S(2)}, u32[]{:S(2)}) collective-permute-start(bf16[16,4608]{1,0:T(8,128)(2,1)S(1)} %constant_dynamic-slice_fusion.5), channel_id=1, source_target_pairs={{0,8},{2,10},{4,12},{6,14},{8,0},{10,2},{12,4},{14,6},{16,24},{18,... | collective-permute-start | bytes 442376 | tf_op jit(solution)/shard_map/ppermute | solution.py:880
  618.3 3.6 collective-permute-start.39
  620.2 5.0 collective-permute-start.35
  625.2 7.4 %collective-permute-start.40 = (bf16[8,4608]{1,0:T(8,128)(2,1)S(1)}, bf16[8,4608]{1,0:T(8,128)(2,1)S(1)}, u32[]{:S(2)}, u32[]{:S(2)}) collective-permute-start(bf16[8,4608]{1,0:T(8,128)(2,1)S(1)} %add_convert_fusion.7), channel_id=1, source_target_pairs={{0,16},{2,18},{4,20},{6,22},{8,24},{10,26},{12,28},{14,30},{16,0},... | collective-permute-start | bytes 221192 | tf_op jit(solution)/shard_map/ppermute | solution.py:880
  631.9 28.3 %copy-start.4 = (bf16[256,4096]{1,0:T(8,128)(2,1)S(1)}, bf16[256,4096]{1,0:T(8,128)(2,1)}, u32[]{:S(2)}) copy-start(bf16[256,4096]{1,0:T(8,128)(2,1)} %output.1) | copy-start | bytes 6291460
  631.9 5.2 collective-permute-start.44
  632.6 17.6 %collective-permute-start.41 = (bf16[16,4608]{1,0:T(8,128)(2,1)S(1)}, bf16[16,4608]{1,0:T(8,128)(2,1)S(1)}, u32[]{:S(2)}, u32[]{:S(2)}) collective-permute-start(bf16[16,4608]{1,0:T(8,128)(2,1)S(1)} %maximum_select_fusion.6), channel_id=1, source_target_pairs={{0,8},{2,10},{4,12},{6,14},{8,0},{10,2},{12,4},{14,6},{16,24},{18,... | collective-permute-start | bytes 442376 | tf_op jit(solution)/shard_map/ppermute | solution.py:880
  637.1 13.2 %collective-permute-start.45 = (bf16[16,4608]{1,0:T(8,128)(2,1)S(1)}, bf16[16,4608]{1,0:T(8,128)(2,1)S(1)}, u32[]{:S(2)}, u32[]{:S(2)}) collective-permute-start(bf16[16,4608]{1,0:T(8,128)(2,1)S(1)} %maximum_select_fusion.7), channel_id=1, source_target_pairs={{0,16},{2,18},{4,20},{6,22},{8,24},{10,26},{12,28},{14,30},{16,0},... | collective-permute-start | bytes 442376 | tf_op jit(solution)/shard_map/ppermute | solution.py:880
  650.3 6.0 collective-permute-start.42
  650.4 13.5 %collective-permute-start.46 = (bf16[32,4608]{1,0:T(8,128)(2,1)S(1)}, bf16[32,4608]{1,0:T(8,128)(2,1)S(1)}, u32[]{:S(2)}, u32[]{:S(2)}) collective-permute-start(bf16[32,4608]{1,0:T(8,128)(2,1)S(1)} %maximum_select_fusion.5), channel_id=1, source_target_pairs={{0,8},{2,10},{4,12},{6,14},{8,0},{10,2},{12,4},{14,6},{16,24},{18,... | collective-permute-start | bytes 884744 | tf_op jit(solution)/shard_map/ppermute | solution.py:880
  656.4 9.8 %collective-permute-start.43 = (bf16[64,4608]{1,0:T(8,128)(2,1)S(1)}, bf16[64,4608]{1,0:T(8,128)(2,1)S(1)}, u32[]{:S(2)}, u32[]{:S(2)}) collective-permute-start(bf16[64,4608]{1,0:T(8,128)(2,1)S(1)} %maximum_select_fusion.2), channel_id=1, source_target_pairs={{0,2},{2,0},{4,6},{6,4},{8,10},{10,8},{12,14},{14,12},{16,18},{18,... | collective-permute-start | bytes 1769480 | tf_op jit(solution)/shard_map/ppermute | solution.py:880
  664.0 3.8 collective-permute-start.47
  (15 other events, 70.4 us)
Sparse Core Ops, SparseCore 0:
  486.8 87.2 reduce-scatter.1
  589.1 73.4 all-gather.1

commit v7 on v6

--- a/solution.py
+++ b/solution.py
@@ -835,7 +835,7 @@
         turned = lax.all_to_all(cut, "tensor", split_axis=2, concat_axis=0, tiled=True)
         return turned[:, ::-1].transpose(2, 1, 0).reshape(ch, 9 * C)
 
-    def total(self, x):
+    def total(self, x, beside):
         return lax.psum(x, "dp")
 
     def everywhere(self, x):
@@ -888,8 +888,8 @@
     def turn(self, meta, w):
         return turned_pair(meta, w, self.over(w, 1))
 
-    def total(self, x):
-        x = x + lax.ppermute(x, "tensor", [(0, 1), (1, 0)])
+    def total(self, x, beside):
+        x = after(beside, x + lax.ppermute(x, "tensor", [(0, 1), (1, 0)]))
         for bit in self.bits[1:]:
             x = x + self.over(x, bit)
         return self.pick(x, self.over(x, 1))
@@ -972,16 +972,20 @@
     emb_all = plan.everywhere(emb_all)
     length = vectors[14, :1].astype(jnp.int32)
     par_one, par_two, par_three = vectors[0:2].T, vectors[2:7].T, vectors[7:10].T
+    bias_qkv, bias_out = vectors[11:14].reshape(3 * ch, 1), vectors[10].reshape(ch, 1)
     par_one = after(emb_all, par_one)
     w2_got = plan.got(after(vectors, conv2_weight))
     act_one, stat_one, f_low = first_activation(meta, f_own, f_got, par_one)
     full_one = plan.gather(act_one)
     mats_own = jnp.concatenate([qkv_weight.reshape(3 * ch, C), out_weight])
-    mats_own, ctx_own = after(act_one, mats_own, ctx_kv)
+    mats_own, ctx_own, cot_own = after(
+        act_one, mats_own, ctx_kv, cotangent.reshape(ch, pixels)
+    )
     mats_got, ctx_got = plan.got(mats_own), plan.got(ctx_own)
-    cot_own = after((mats_got, ctx_got), cotangent.reshape(ch, pixels))
     cot_got = plan.got(cot_own)
 
+    par_two, par_three, bias_qkv, bias_out = after(act_one, par_two, par_three, bias_qkv, bias_out)
+    par_two = after((par_three, bias_qkv, bias_out), par_two)
     low, stat, wide = struct((ch, HW), BF), struct((ch, 128), F32), struct((ch, HW), F32)
     weight = struct((ch, 9 * C), BF)
     act_two, stat_two, conv_one, w1 = conv_call(
@@ -989,21 +993,19 @@
         [low, stat], [wide, weight], [], "conv_one",
     )
     full_two = plan.gather(act_two)
-    if moved:
-        full_two = after((mats_got, ctx_got), *full_two)
     normed, stat_three, hidden, w2 = conv_call(
         conv_two_kernel, meta, (conv2_weight, w2_got), full_two, (par_three, f_low), (),
         [low, stat], [wide, weight], [], "conv_two",
     )
     full_three = plan.gather(normed)
-    cot_got = after(normed, cot_got)
+    mats_got, ctx_got, cot_got = after(normed, mats_got, ctx_got, cot_got)
     mats = plan.pick(mats_own, mats_got)
     w_qkv, w_out = mats[: 3 * ch], mats[3 * ch :]
     cot = folded(meta, cot_own, cot_got)
     grad_heads = plan.scatter(
         parts_product(meta, w_out.T, (cot,), plan.parts, name="grad_heads")
     )
-    qkv = inputs_product(meta, w_qkv, full_three, vectors[11:14].reshape(3 * ch, 1), name="qkv")
+    qkv = inputs_product(meta, w_qkv, full_three, bias_qkv, name="qkv")
     ctx_kv = plan.pick(ctx_own, ctx_got)
     mixed, dq, dk, dv, dkc, dvc = attention(
         4 + length,
@@ -1057,8 +1059,9 @@
     )
     input_got = plan.got(input_grad)
 
+    one_got = after(input_grad, one_got)
     output = output_product(
-        meta, w_out, full_heads, vectors[10].reshape(ch, 1), after((input_grad, one_got), hidden)
+        meta, w_out, full_heads, bias_out, after(input_grad, hidden)
     )
     output_got = plan.got(output)
     ctx_sums = jnp.sum(ctx_own.astype(F32), axis=2)
@@ -1078,11 +1081,12 @@
                 sums_one[:, :2].T,
                 mods,
             ]
-        )
-    )
-    early, dw_one, one_got = after((output, small), early, dw_one, one_got)
+        ),
+        output,
+    )
+    early, dw_one, one_got = after(small, early, dw_one, one_got)
+    dw_one = plan.sum_owned(plan.pick(dw_one, one_got), (input_got, output_got))
     early = lax.all_gather(early, "dp", axis=0, tiled=True)
-    dw_one = plan.sum_owned(plan.pick(dw_one, one_got), (input_got, output_got))
     mods = small[14:].reshape(plan.images, 2, ch)
     mods_low = mods.astype(BF)
     dw_emb = jnp.stack(

time: 700 us -> 705 us (level)
    unnamed x68 -> x79, local copies, waits for them, and re-layouts: 15.4 us -> 17.4 us
where the time goes in v7:
time: 705 us; the launch traced here: 692 us
  Pallas kernels  426 us (60%)
  starting transfers between devices  108 us (15%)
  waiting for transfers between devices  68.8 us (10%)
  local copies, waits for them, and re-layouts  34.8 us (5%)
  other arithmetic  29.4 us (4%)
  between operations  16.7 us (2%)
  matrix products  8.28 us (1%)
    pallas_call x1, Pallas kernels, attention(): pl.pallas_call(functools.partial(attention_kernel, len(grads), unroll=unr...  225 us
    pallas_call x4, Pallas kernels, conv_call(): pl.pallas_call(functools.partial(kernel, len(pieces)), out_shape=[*outs,...  93.5 us
    ppermute x34, starting transfers between devices, over(): return lax.ppermute(x, 'dp', [(i, i ^ bit) for i in range(self.images)])  83.7 us
    ppermute x34, waiting for transfers between devices, over(): return lax.ppermute(x, 'dp', [(i, i ^ bit) for i in range(self.images)])  68.8 us
    pallas_call x2, Pallas kernels, conv_weight_grad(): pl.pallas_call(functools.partial(weight_grad_kernel, len(pieces)), out_sh...  33.3 us
    ppermute x13, starting transfers between devices, got(): return lax.ppermute(x, ('dp', 'tensor'), self.far)  22.8 us
    unnamed x79, local copies, waits for them, and re-layouts  17.4 us
  transfers between devices with their start and end apart: 50, of which 18 were waited for; matrix products, arithmetic and copies ran while one was open for 7% of the time, Pallas kernels for 28%

profile of v7, /device:TPU:5, one launch (start us, length us, event | category | flops | bytes accessed | tf_op | source)
XLA Modules:
  0.0 692.0 jit_solution(10895542611298122304)
XLA Ops:
  7.4 2.1 collective-permute-start
  11.0 2.0 fusion.15
  14.6 2.1 collective-permute-start.7
  21.8 2.2 collective-permute-done.3
  24.0 2.4 collective-permute-start.4
  28.8 9.0 %act_one.1 = (bf16[256,4096]{1,0:T(8,128)(2,1)}, f32[256,128]{1,0:T(8,128)}, bf16[256,4096]{1,0:T(8,128)(2,1)}) custom-call(s32[2]{0:T(128)} %pad_add_fusion.meta, bf16[256,4096]{1,0:T(8,128)(2,1)} %bitcast.121, bf16[256,4096]{1,0:T(8,128)(2,1)} %collective-permute-done.got_ref, f32[256,2]{1,0:T(8,128)} %slice_bitcast_fusion.10.par_ref.refs_2_), custom_call_target="tpu_custom_call" | custom-call | flops 209715 | bytes 62914 | tf_op jit(solution)/shard_map/act_one/pallas_call | solution.py:187
  37.8 14.3 %collective-permute-start.8 = (bf16[256,4096]{1,0:T(8,128)(2,1)}, bf16[256,4096]{1,0:T(8,128)(2,1)}, u32[]{:S(2)}, u32[]{:S(2)}) collective-permute-start(bf16[256,4096]{1,0:T(8,128)(2,1)} %get-tuple-element.87.refs_0_), channel_id=1, source_target_pairs={{0,2},{2,0},{4,6},{6,4},{8,10},{10,8},{12,14},{14,12},{16,18},{18,... | collective-permute-start | bytes 6291464 | tf_op jit(solution)/shard_map/ppermute | solution.py:880
  52.1 3.1 fusion
  56.1 2.1 collective-permute-start.6
  59.6 22.0 %conv_one.1 = (bf16[256,4096]{1,0:T(8,128)(2,1)}, f32[256,128]{1,0:T(8,128)}, f32[256,4096]{1,0:T(8,128)}, bf16[256,4608]{1,0:T(8,128)(2,1)}) custom-call(s32[2]{0:T(128)} %pad_add_fusion.meta, bf16[256,4608]{1,0:T(8,128)(2,1)} %w_own.2, bf16[256,4608]{1,0:T(8,128)(2,1)} %collective-permute-done.7.w_got, bf16[256,4096]{1,0:T(8,128)(2,1)} %get-tuple-element.87.refs_0_, ...), custom_call_target="tpu_custom_call" | custom-call | flops 96636768 | bytes 107530 | tf_op jit(solution)/shard_map/conv_one/pallas_call | solution.py:259
  81.7 2.9 collective-permute-start.9
  84.6 2.0 pad_maximum_fusion.2
  90.9 22.3 %conv_two.1 = (bf16[256,4096]{1,0:T(8,128)(2,1)}, f32[256,128]{1,0:T(8,128)}, f32[256,4096]{1,0:T(8,128)}, bf16[256,4608]{1,0:T(8,128)(2,1)}) custom-call(s32[2]{0:T(128)} %pad_add_fusion.meta, bf16[256,4608]{1,0:T(8,128)(2,1)} %w_own.3, bf16[256,4608]{1,0:T(8,128)(2,1)} %collective-permute-done.6.w_got, bf16[256,4096]{1,0:T(8,128)(2,1)} %get-tuple-element.96.refs_0_, ...), custom_call_target="tpu_custom_call" | custom-call | flops 96636768 | bytes 128481 | tf_op jit(solution)/shard_map/conv_two/pallas_call | solution.py:259
  113.3 3.3 collective-permute-start.13
  120.4 4.8 fold.1.refs_0_.refs_5_
  126.0 4.9 grad_heads.1
  130.8 13.1 %collective-permute-start.14 = (bf16[256,4096]{1,0:T(8,128)(2,1)}, bf16[256,4096]{1,0:T(8,128)(2,1)}, u32[]{:S(2)}, u32[]{:S(2)}) collective-permute-start(bf16[256,4096]{1,0:T(8,128)(2,1)} %get-tuple-element.105), channel_id=1, source_target_pairs={{0,2},{2,0},{4,6},{6,4},{8,10},{10,8},{12,14},{14,12},{16,18},{18,... | collective-permute-start | bytes 6291464 | tf_op jit(solution)/shard_map/ppermute | solution.py:880
  149.3 7.7 %qkv.1 = bf16[768,4096]{1,0:T(8,128)(2,1)} custom-call(s32[2]{0:T(128)} %pad_add_fusion.meta, bf16[768,512]{1,0:T(8,128)(2,1)} %get-tuple-element.259.w_ref, bf16[256,4096]{1,0:T(8,128)(2,1)} %get-tuple-element.98.refs_0_.refs_3_, bf16[256,4096]{1,0:T(8,128)(2,1)} %collective-permute-done.13.refs_1_.refs_4_, f32[768,1]{1,0:T(8,128)} %copy.122.refs_2_), custom_call_target="tpu_custom_call" | custom-call | flops 32212254 | bytes 104857 | tf_op jit(solution)/shard_map/qkv/pallas_call | solution.py:524
  156.9 225.2 %attention.1 = (bf16[4,64,4096]{2,1,0:T(8,128)(2,1)}, bf16[4,64,4096]{2,1,0:T(8,128)(2,1)}, bf16[4,64,4096]{2,1,0:T(8,128)(2,1)}, bf16[4,64,4096]{2,1,0:T(8,128)...) custom-call(s32[1]{0:T(128)} %bitcast.22.lim_ref, bf16[3,4,64,4096]{3,2,1,0:T(8,128)(2,1)} %bitcast.103, ...), custom_call_target="tpu_custom_call" | custom-call | flops 1159641216 | bytes 167772 | tf_op jit(solution)/shard_map/attention/pallas_call | solution.py:766
  382.2 7.7 %grad_normed.1 = (bf16[256,4096]{1,0:T(8,128)(2,1)}, bf16[256,4096]{1,0:T(8,128)(2,1)}) custom-call(s32[2]{0:T(128)} %pad_add_fusion.meta, bf16[512,768]{1,0:T(8,128)(2,1)} %copy.127.w_ref, bf16[256,4096]{1,0:T(8,128)(2,1)} %bitcast.110, bf16[256,4096]{1,0:T(8,128)(2,1)} %bitcast.112, bf16[256,4096]{1,0:T(8,128)(2,1)} %bitcast.114), custom_call_target="tpu_custom_call" | custom-call | flops 32212254 | bytes 104857 | tf_op jit(solution)/shard_map/grad_normed/pallas_call | solution.py:558
  390.4 3.9 collective-permute-done.18.refs_1_
  394.4 10.2 %norm_three_back.1 = (f32[256,4096]{1,0:T(8,128)}, bf16[256,4096]{1,0:T(8,128)(2,1)}, f32[256,128]{1,0:T(8,128)}) custom-call(bf16[256,4096]{1,0:T(8,128)(2,1)} %get-tuple-element.116.refs_0_, bf16[256,4096]{1,0:T(8,128)(2,1)} %collective-permute-done.18.refs_1_, f32[256,4096]{1,0:T(8,128)} %get-tuple-element.137.refs_2_.refs_3_, ...), custom_call_target="tpu_custom_call" | custom-call | flops 209715 | bytes 167772 | tf_op jit(solution)/shard_map/norm_three_back/pallas_call | solution.py:494
  404.5 16.4 %conv_two_weight_grad.1 = bf16[256,4608]{1,0:T(8,128)(2,1)} custom-call(s32[2]{0:T(128)} %pad_add_fusion.meta, bf16[256,4096]{1,0:T(8,128)(2,1)} %get-tuple-element.121.grad_ref.refs_0_, bf16[256,4096]{1,0:T(8,128)(2,1)} %get-tuple-element.96.refs_0_, bf16[256,4096]{1,0:T(8,128)(2,1)} %collective-permute-done.9.refs_1_), custom_call_target="tpu_custom_call" | custom-call | flops 96636768 | bytes 86507 | tf_op jit(solution)/shard_map/conv_two_weight_grad/pallas_call | solution.py:417
  420.9 2.1 collective-permute-start.22
  423.0 8.4 %qkv_grad.1 = (bf16[768,512]{1,0:T(8,128)(2,1)}, f32[768,128]{1,0:T(8,128)}) custom-call(s32[2]{0:T(128)} %pad_add_fusion.meta, bf16[256,4096]{1,0:T(8,128)(2,1)} %bitcast.111, bf16[256,4096]{1,0:T(8,128)(2,1)} %bitcast.113, bf16[256,4096]{1,0:T(8,128)(2,1)} %bitcast.115, bf16[256,4096]{1,0:T(8,128)(2,1)} %get-tuple-element.98.refs_0_.refs_3_, ...), custom_call_target="tpu_custom_call" | custom-call | flops 32212254 | bytes 104857 | tf_op jit(solution)/shard_map/qkv_grad/pallas_call | solution.py:632
  431.5 2.1 constant_dynamic-update-slice_fusion.1
  433.6 5.3 out_grad.1
  444.0 4.5 turn.3.w_own.w_got
  448.4 24.7 %conv_two_back.1 = (bf16[256,4096]{1,0:T(8,128)(2,1)}, f32[256,128]{1,0:T(8,128)}) custom-call(s32[2]{0:T(128)} %pad_add_fusion.meta, bf16[256,4608]{1,0:T(8,128)(2,1)} %turn.3.w_own.w_got, bf16[256,4608]{1,0:T(8,128)(2,1)} %turn.3.w_own.w_got, bf16[256,4096]{1,0:T(8,128)(2,1)} %get-tuple-element.121.grad_ref.refs_0_, ...), custom_call_target="tpu_custom_call" | custom-call | flops 96636768 | bytes 150784 | tf_op jit(solution)/shard_map/conv_two_back/pallas_call | solution.py:259
  474.5 2.3 convolution_convert_fusion
  482.0 2.0 select_dynamic-update-slice_fusion
  485.7 4.7 collective-permute-start.16
  490.9 7.0 %collective-permute-done.16.other_ref = bf16[256,4608]{1,0:T(8,128)(2,1)} collective-permute-done((bf16[256,4608]{1,0:T(8,128)(2,1)S(1)}, bf16[256,4608]{1,0:T(8,128)(2,1)}, u32[]{:S(2)}, u32[]{:S(2)}) %collective-permute-start.16) | collective-permute-done | bytes 2359328 | tf_op jit(solution)/shard_map/ppermute | solution.py:880
  498.0 4.8 turn.2.w_own.w_got
  502.8 17.0 %conv_one_weight_grad.1 = bf16[256,4608]{1,0:T(8,128)(2,1)} custom-call(s32[2]{0:T(128)} %pad_add_fusion.meta, bf16[256,4096]{1,0:T(8,128)(2,1)} %get-tuple-element.132.grad_ref.refs_0_, bf16[256,4096]{1,0:T(8,128)(2,1)} %get-tuple-element.87.refs_0_, bf16[256,4096]{1,0:T(8,128)(2,1)} %collective-permute-done.8.refs_1_), custom_call_target="tpu_custom_call" | custom-call | flops 96636768 | bytes 86507 | tf_op jit(solution)/shard_map/conv_one_weight_grad/pallas_call | solution.py:417
  519.8 2.1 collective-permute-start.31
  522.5 24.5 %conv_one_back.1 = (bf16[256,4096]{1,0:T(8,128)(2,1)}, f32[256,128]{1,0:T(8,128)}) custom-call(s32[2]{0:T(128)} %pad_add_fusion.meta, bf16[256,4608]{1,0:T(8,128)(2,1)} %turn.2.w_own.w_got, bf16[256,4608]{1,0:T(8,128)(2,1)} %turn.2.w_own.w_got, bf16[256,4096]{1,0:T(8,128)(2,1)} %get-tuple-element.132.grad_ref.refs_0_, ...), custom_call_target="tpu_custom_call" | custom-call | flops 96636768 | bytes 171724 | tf_op jit(solution)/shard_map/conv_one_back/pallas_call | solution.py:259
  549.9 6.6 output.1
  557.7 3.2 collective-permute-done.27
  562.3 2.7 collective-permute-done.28
  565.0 2.9 collective-permute-start.29
  567.9 3.7 collective-permute-done.29
  571.6 2.4 collective-permute-start.30
  574.0 2.1 collective-permute-start.25
  576.1 2.2 collective-permute-start.24
  580.0 2.3 pad_maximum_fusion
  583.1 3.8 collective-permute-start.36
  591.0 2.1 collective-permute-start.33
  593.1 5.3 collective-permute-done.37
  598.5 2.1 collective-permute-start.38
  601.8 12.4 %collective-permute-done.38 = bf16[16,4608]{1,0:T(8,128)(2,1)S(1)} collective-permute-done((bf16[16,4608]{1,0:T(8,128)(2,1)S(1)}, bf16[16,4608]{1,0:T(8,128)(2,1)S(1)}, u32[]{:S(2)}, u32[]{:S(2)}) %collective-permute-start.38) | collective-permute-done | bytes 147488 | tf_op jit(solution)/shard_map/ppermute | solution.py:880
  614.3 2.3 collective-permute-start.39
  616.7 2.0 collective-permute-done.39
  618.7 2.9 collective-permute-done.35
  622.3 4.4 collective-permute-done.40
  627.1 3.9 collective-permute-start.45
  630.9 9.7 %collective-permute-done.41 = bf16[16,4608]{1,0:T(8,128)(2,1)S(1)} collective-permute-done((bf16[16,4608]{1,0:T(8,128)(2,1)S(1)}, bf16[16,4608]{1,0:T(8,128)(2,1)S(1)}, u32[]{:S(2)}, u32[]{:S(2)}) %collective-permute-start.41) | collective-permute-done | bytes 147488 | tf_op jit(solution)/shard_map/ppermute | solution.py:880
  642.7 4.0 collective-permute-done.42
  646.8 12.0 %collective-permute-start.43 = (bf16[64,4608]{1,0:T(8,128)(2,1)S(1)}, bf16[64,4608]{1,0:T(8,128)(2,1)S(1)}, u32[]{:S(2)}, u32[]{:S(2)}) collective-permute-start(bf16[64,4608]{1,0:T(8,128)(2,1)S(1)} %maximum_select_fusion.2), channel_id=1, source_target_pairs={{0,2},{2,0},{4,6},{6,4},{8,10},{10,8},{12,14},{14,12},{16,18},{18,... | collective-permute-start | bytes 1769480 | tf_op jit(solution)/shard_map/ppermute | solution.py:880
  660.3 6.3 copy.133
  670.3 2.7 fusion.20
  674.7 2.1 slice_convert_fusion.1
  676.8 4.4 slice_convert_fusion
  681.2 2.3 maximum_convert_fusion
  (242 shorter events, 66.0 us)
Async XLA Ops:
  7.2 44.9 %copy-start = (bf16[1,260,2048]{2,1,0:T(8,128)(2,1)S(1)}, bf16[1,260,2048]{2,1,0:T(8,128)(2,1)}, u32[]{:S(2)}) copy-start(bf16[1,260,2048]{2,1,0:T(8,128)(2,1)} %param.26) | copy-start | bytes 3194884
  7.3 575.0 %reduce-scatter.2.cloned.1.call-start = ((), (), s32[]{:S(2)}) async-start(), calls=%async_computation.1 | async-start | bytes 5849088 | tf_op jit(solution)/shard_map/reduce_scatter | solution.py:1050
  7.4 21.5 %collective-permute-start = (bf16[256,4096]{1,0:T(8,128)(2,1)}, bf16[256,4096]{1,0:T(8,128)(2,1)}, u32[]{:S(2)}, u32[]{:S(2)}) collective-permute-start(bf16[256,4096]{1,0:T(8,128)(2,1)} %bitcast.120), channel_id=1, source_target_pairs={{1,2},{2,1},{5,6},{6,5},{9,10},{10,9},{13,14},{14,13},{17,18},{18,... | collective-permute-start | bytes 6291464 | tf_op jit(solution)/shard_map/ppermute | solution.py:874
  10.3 6.3 collective-permute-start.1
  13.9 7.9 %collective-permute-start.5 = (f32[15,256]{0,1:T(8,128)S(1)}, f32[15,256]{0,1:T(8,128)S(1)}, u32[]{:S(2)}, u32[]{:S(2)}) collective-permute-start(f32[15,256]{0,1:T(8,128)S(1)} %copy.120), channel_id=1, source_target_pairs={{1,2},{2,1},{5,6},{6,5},{9,10},{10,9},{13,14},{14,13},{17,18},{18,... | collective-permute-start | bytes 46088 | tf_op jit(solution)/shard_map/ppermute | solution.py:874
  14.6 45.1 %collective-permute-start.7 = (bf16[256,4608]{1,0:T(8,128)(2,1)}, bf16[256,4608]{1,0:T(8,128)(2,1)}, u32[]{:S(2)}, u32[]{:S(2)}) collective-permute-start(bf16[256,4608]{1,0:T(8,128)(2,1)} %w_own.2), channel_id=1, source_target_pairs={{1,2},{2,1},{5,6},{6,5},{9,10},{10,9},{13,14},{14,13},{17,18},{18,... | collective-permute-start | bytes 7077896 | tf_op jit(solution)/shard_map/ppermute | solution.py:874
  16.7 3.6 collective-permute-start.2
  20.4 3.6 collective-permute-start.3
  24.0 4.2 collective-permute-start.4
  28.8 23.3 %copy-start.34 = (f32[2,256]{1,0:T(2,128)S(1)}, f32[2,256]{1,0:T(2,128)}, u32[]{:S(2)}) copy-start(f32[2,256]{1,0:T(2,128)} %param.43) | copy-start | bytes 6148
  37.8 21.8 %collective-permute-start.8 = (bf16[256,4096]{1,0:T(8,128)(2,1)}, bf16[256,4096]{1,0:T(8,128)(2,1)}, u32[]{:S(2)}, u32[]{:S(2)}) collective-permute-start(bf16[256,4096]{1,0:T(8,128)(2,1)} %get-tuple-element.87.refs_0_), channel_id=1, source_target_pairs={{0,2},{2,0},{4,6},{6,4},{8,10},{10,8},{12,14},{14,12},{16,18},{18,... | collective-permute-start | bytes 6291464 | tf_op jit(solution)/shard_map/ppermute | solution.py:880
  56.1 34.8 %collective-permute-start.6 = (bf16[256,4608]{1,0:T(8,128)(2,1)}, bf16[256,4608]{1,0:T(8,128)(2,1)}, u32[]{:S(2)}, u32[]{:S(2)}) collective-permute-start(bf16[256,4608]{1,0:T(8,128)(2,1)} %w_own.3), channel_id=1, source_target_pairs={{1,2},{2,1},{5,6},{6,5},{9,10},{10,9},{13,14},{14,13},{17,18},{18,... | collective-permute-start | bytes 7077896 | tf_op jit(solution)/shard_map/ppermute | solution.py:874
  59.6 24.9 %copy-start.13 = (bf16[3,256,512]{2,1,0:T(8,128)(2,1)S(1)}, bf16[3,256,512]{2,1,0:T(8,128)(2,1)}, u32[]{:S(2)}) copy-start(bf16[3,256,512]{2,1,0:T(8,128)(2,1)} %param.40) | copy-start | bytes 2359300
  81.7 9.2 %collective-permute-start.9 = (bf16[256,4096]{1,0:T(8,128)(2,1)}, bf16[256,4096]{1,0:T(8,128)(2,1)}, u32[]{:S(2)}, u32[]{:S(2)}) collective-permute-start(bf16[256,4096]{1,0:T(8,128)(2,1)} %get-tuple-element.96.refs_0_), channel_id=1, source_target_pairs={{0,2},{2,0},{4,6},{6,4},{8,10},{10,8},{12,14},{14,12},{16,18},{18,... | collective-permute-start | bytes 6291464 | tf_op jit(solution)/shard_map/ppermute | solution.py:880
  86.6 30.0 %collective-permute-start.12 = (bf16[256,4096]{1,0:T(8,128)(2,1)}, bf16[256,4096]{1,0:T(8,128)(2,1)}, u32[]{:S(2)}, u32[]{:S(2)}) collective-permute-start(bf16[256,4096]{1,0:T(8,128)(2,1)} %bitcast.18.own_ref), channel_id=1, source_target_pairs={{1,2},{2,1},{5,6},{6,5},{9,10},{10,9},{13,14},{14,13},{17,18},{18,... | collective-permute-start | bytes 6291464 | tf_op jit(solution)/shard_map/ppermute | solution.py:874
  88.6 28.0 %collective-permute-start.10 = (bf16[1024,512]{1,0:T(8,128)(2,1)}, bf16[1024,512]{1,0:T(8,128)(2,1)}, u32[]{:S(2)}, u32[]{:S(2)}) collective-permute-start(bf16[1024,512]{1,0:T(8,128)(2,1)} %pad_maximum_fusion.2), channel_id=1, source_target_pairs={{1,2},{2,1},{5,6},{6,5},{9,10},{10,9},{13,14},{14,13},{17,18},{18,... | collective-permute-start | bytes 3145736 | tf_op jit(solution)/shard_map/ppermute | solution.py:874
  90.2 26.4 %collective-permute-start.11 = (bf16[2,256,384]{1,2,0:T(8,128)(2,1)S(1)}, bf16[2,256,384]{1,2,0:T(8,128)(2,1)S(1)}, u32[]{:S(2)}, u32[]{:S(2)}) collective-permute-start(bf16[2,256,384]{1,2,0:T(8,128)(2,1)S(1)} %pad.4), channel_id=1, source_target_pairs={{1,2},{2,1},{5,6},{6,5},{9,10},{10,9},{13,14},{14,13},{17,18},{18,... | collective-permute-start | bytes 1179656 | tf_op jit(solution)/shard_map/ppermute | solution.py:874
  113.3 36.0 %collective-permute-start.13 = (bf16[256,4096]{1,0:T(8,128)(2,1)}, bf16[256,4096]{1,0:T(8,128)(2,1)}, u32[]{:S(2)}, u32[]{:S(2)}) collective-permute-start(bf16[256,4096]{1,0:T(8,128)(2,1)} %get-tuple-element.98.refs_0_.refs_3_), channel_id=1, source_target_pairs={{0,2},{2,0},{4,6},{6,4},{8,10},{10,8},{12,14},{14,12},{16,18},{18,... | collective-permute-start | bytes 6291464 | tf_op jit(solution)/shard_map/ppermute | solution.py:880
  126.0 20.1 %copy-start.17 = (bf16[2,256,384]{1,2,0:T(8,128)(2,1)S(1)}, bf16[2,256,384]{1,2,0:T(8,128)(2,1)}, u32[]{:S(2)}) copy-start(bf16[2,256,384]{1,2,0:T(8,128)(2,1)} %copy-done.16) | copy-start | bytes 1179652
  130.8 16.2 %copy-start.6 = (bf16[1024,512]{1,0:T(8,128)(2,1)S(1)}, bf16[1024,512]{1,0:T(8,128)(2,1)}, u32[]{:S(2)}) copy-start(bf16[1024,512]{1,0:T(8,128)(2,1)} %copy-done.5) | copy-start | bytes 3145732
  130.8 26.1 %collective-permute-start.14 = (bf16[256,4096]{1,0:T(8,128)(2,1)}, bf16[256,4096]{1,0:T(8,128)(2,1)}, u32[]{:S(2)}, u32[]{:S(2)}) collective-permute-start(bf16[256,4096]{1,0:T(8,128)(2,1)} %get-tuple-element.105), channel_id=1, source_target_pairs={{0,2},{2,0},{4,6},{6,4},{8,10},{10,8},{12,14},{14,12},{16,18},{18,... | collective-permute-start | bytes 6291464 | tf_op jit(solution)/shard_map/ppermute | solution.py:880
  389.9 4.5 collective-permute-start.18
  389.9 43.7 %collective-permute-start.15 = (bf16[256,4096]{1,0:T(8,128)(2,1)}, bf16[256,4096]{1,0:T(8,128)(2,1)}, u32[]{:S(2)}, u32[]{:S(2)}) collective-permute-start(bf16[256,4096]{1,0:T(8,128)(2,1)} %bitcast.107), channel_id=1, source_target_pairs={{0,2},{2,0},{4,6},{6,4},{8,10},{10,8},{12,14},{14,12},{16,18},{18,... | collective-permute-start | bytes 6291464 | tf_op jit(solution)/shard_map/ppermute | solution.py:880
  390.4 53.6 %collective-permute-start.17 = (bf16[256,4608]{1,0:T(8,128)(2,1)}, bf16[256,4608]{1,0:T(8,128)(2,1)}, u32[]{:S(2)}, u32[]{:S(2)}) collective-permute-start(bf16[256,4608]{1,0:T(8,128)(2,1)} %get-tuple-element.112.own_ref), channel_id=1, source_target_pairs={{0,2},{2,0},{4,6},{6,4},{8,10},{10,8},{12,14},{14,12},{16,18},{18,... | collective-permute-start | bytes 7077896 | tf_op jit(solution)/shard_map/ppermute | solution.py:880
  420.9 52.2 %collective-permute-start.22 = (bf16[256,4608]{1,0:T(8,128)(2,1)}, bf16[256,4608]{1,0:T(8,128)(2,1)}, u32[]{:S(2)}, u32[]{:S(2)}) collective-permute-start(bf16[256,4608]{1,0:T(8,128)(2,1)} %conv_two_weight_grad.1), channel_id=1, source_target_pairs={{1,2},{2,1},{5,6},{6,5},{9,10},{10,9},{13,14},{14,13},{17,18},{18,... | collective-permute-start | bytes 7077896 | tf_op jit(solution)/shard_map/ppermute | solution.py:874
  423.0 25.5 %collective-permute-start.19 = (bf16[256,4096]{1,0:T(8,128)(2,1)}, bf16[256,4096]{1,0:T(8,128)(2,1)}, u32[]{:S(2)}, u32[]{:S(2)}) collective-permute-start(bf16[256,4096]{1,0:T(8,128)(2,1)} %get-tuple-element.121.grad_ref.refs_0_), channel_id=1, source_target_pairs={{0,2},{2,0},{4,6},{6,4},{8,10},{10,8},{12,14},{14,12},{16,18},{18,... | collective-permute-start | bytes 6291464 | tf_op jit(solution)/shard_map/ppermute | solution.py:880
  433.5 8.6 %copy-start.20 = (bf16[4,64,384]{2,1,0:T(8,128)(2,1)S(1)}, bf16[4,64,384]{2,1,0:T(8,128)(2,1)}, u32[]{:S(2)}) copy-start(bf16[4,64,384]{2,1,0:T(8,128)(2,1)} %get-tuple-element.109) | copy-start | bytes 589828
  433.5 8.8 %copy-start.19 = (bf16[4,64,384]{2,1,0:T(8,128)(2,1)S(1)}, bf16[4,64,384]{2,1,0:T(8,128)(2,1)}, u32[]{:S(2)}) copy-start(bf16[4,64,384]{2,1,0:T(8,128)(2,1)} %get-tuple-element.110) | copy-start | bytes 589828
  440.5 32.6 %collective-permute-start.20 = (bf16[1024,512]{1,0:T(8,128)(2,1)}, bf16[1024,512]{1,0:T(8,128)(2,1)}, u32[]{:S(2)}, u32[]{:S(2)}) collective-permute-start(bf16[1024,512]{1,0:T(8,128)(2,1)} %constant_dynamic-update-slice_fusion), channel_id=1, source_target_pairs={{1,2},{2,1},{5,6},{6,5},{9,10},{10,9},{13,14},{14,13},{17,18},{18,... | collective-permute-start | bytes 3145736 | tf_op jit(solution)/shard_map/ppermute | solution.py:874
  442.3 32.2 %copy-start.9 = (bf16[1,256,384]{1,2,0:T(8,128)(2,1)}, bf16[1,256,384]{1,2,0:T(8,128)(2,1)S(1)}, u32[]{:S(2)}) copy-start(bf16[1,256,384]{1,2,0:T(8,128)(2,1)S(1)} %copy.125) | copy-start | bytes 589828
  442.5 32.0 %copy-start.11 = (bf16[1,256,384]{1,2,0:T(8,128)(2,1)}, bf16[1,256,384]{1,2,0:T(8,128)(2,1)S(1)}, u32[]{:S(2)}) copy-start(bf16[1,256,384]{1,2,0:T(8,128)(2,1)S(1)} %copy.126) | copy-start | bytes 589828
  442.5 30.6 %collective-permute-start.21 = (bf16[2,256,384]{1,2,0:T(8,128)(2,1)S(1)}, bf16[2,256,384]{1,2,0:T(8,128)(2,1)}, u32[]{:S(2)}, u32[]{:S(2)}) collective-permute-start(bf16[2,256,384]{1,2,0:T(8,128)(2,1)S(1)} %pad_maximum_fusion.3), channel_id=1, source_target_pairs={{1,2},{2,1},{5,6},{6,5},{9,10},{10,9},{13,14},{14,13},{17,18},{18,... | collective-permute-start | bytes 1179656 | tf_op jit(solution)/shard_map/ppermute | solution.py:874
  484.0 6.8 copy-start.21
  484.0 189.0 %all-gather.2.cloned.1.call-start = ((), (), s32[]{:S(2)}) async-start(), calls=%async_computation.2 | async-start | bytes 5849088 | tf_op jit(solution)/shard_map/all_gather | solution.py:1089
  485.7 12.3 %collective-permute-start.16 = (bf16[256,4608]{1,0:T(8,128)(2,1)S(1)}, bf16[256,4608]{1,0:T(8,128)(2,1)}, u32[]{:S(2)}, u32[]{:S(2)}) collective-permute-start(bf16[256,4608]{1,0:T(8,128)(2,1)S(1)} %copy-done.7), channel_id=1, source_target_pairs={{0,2},{2,0},{4,6},{6,4},{8,10},{10,8},{12,14},{14,12},{16,18},{18,... | collective-permute-start | bytes 7077896 | tf_op jit(solution)/shard_map/ppermute | solution.py:880
  490.3 32.1 %collective-permute-start.23 = (bf16[256,4096]{1,0:T(8,128)(2,1)}, bf16[256,4096]{1,0:T(8,128)(2,1)}, u32[]{:S(2)}, u32[]{:S(2)}) collective-permute-start(bf16[256,4096]{1,0:T(8,128)(2,1)} %get-tuple-element.132.grad_ref.refs_0_), channel_id=1, source_target_pairs={{0,2},{2,0},{4,6},{6,4},{8,10},{10,8},{12,14},{14,12},{16,18},{18,... | collective-permute-start | bytes 6291464 | tf_op jit(solution)/shard_map/ppermute | solution.py:880
  502.8 19.1 %copy-start.22 = (f32[256,128]{1,0:T(8,128)S(1)}, f32[256,128]{1,0:T(8,128)}, u32[]{:S(2)}) copy-start(f32[256,128]{1,0:T(8,128)} %get-tuple-element.140) | copy-start | bytes 393220
  519.8 62.5 %collective-permute-start.31 = (bf16[256,4608]{1,0:T(8,128)(2,1)}, bf16[256,4608]{1,0:T(8,128)(2,1)}, u32[]{:S(2)}, u32[]{:S(2)}) collective-permute-start(bf16[256,4608]{1,0:T(8,128)(2,1)} %conv_one_weight_grad.1), channel_id=1, source_target_pairs={{1,2},{2,1},{5,6},{6,5},{9,10},{10,9},{13,14},{14,13},{17,18},{18,... | collective-permute-start | bytes 7077896 | tf_op jit(solution)/shard_map/ppermute | solution.py:874
  548.3 8.2 %collective-permute-start.26 = (f32[46,256]{1,0:T(8,128)S(1)}, f32[46,256]{1,0:T(8,128)S(1)}, u32[]{:S(2)}, u32[]{:S(2)}) collective-permute-start(f32[46,256]{1,0:T(8,128)S(1)} %concatenate.74), channel_id=1, source_target_pairs={{0,1},{1,0},{2,3},{3,2},{4,5},{5,4},{6,7},{7,6},{8,9},{9,8},{10,11... | collective-permute-start | bytes 141320 | tf_op jit(solution)/shard_map/ppermute | solution.py:892
  549.9 29.1 %copy-start.14 = (bf16[16,2048]{1,0:T(8,128)(2,1)S(1)}, bf16[16,2048]{1,0:T(8,128)(2,1)}, u32[]{:S(2)}) copy-start(bf16[16,2048]{1,0:T(8,128)(2,1)} %add.173) | copy-start | bytes 196612
  556.5 4.4 collective-permute-start.27
  560.9 4.1 collective-permute-start.28
  565.0 6.6 collective-permute-start.29
  571.6 6.7 collective-permute-start.30
  574.0 47.6 %collective-permute-start.25 = (bf16[256,4096]{1,0:T(8,128)(2,1)}, bf16[256,4096]{1,0:T(8,128)(2,1)}, u32[]{:S(2)}, u32[]{:S(2)}) collective-permute-start(bf16[256,4096]{1,0:T(8,128)(2,1)} %get-tuple-element.136), channel_id=1, source_target_pairs={{1,2},{2,1},{5,6},{6,5},{9,10},{10,9},{13,14},{14,13},{17,18},{18,... | collective-permute-start | bytes 6291464 | tf_op jit(solution)/shard_map/ppermute | solution.py:874
  576.1 45.6 %collective-permute-start.24 = (bf16[256,4096]{1,0:T(8,128)(2,1)}, bf16[256,4096]{1,0:T(8,128)(2,1)}, u32[]{:S(2)}, u32[]{:S(2)}) collective-permute-start(bf16[256,4096]{1,0:T(8,128)(2,1)} %output.1), channel_id=1, source_target_pairs={{1,2},{2,1},{5,6},{6,5},{9,10},{10,9},{13,14},{14,13},{17,18},{18,... | collective-permute-start | bytes 6291464 | tf_op jit(solution)/shard_map/ppermute | solution.py:874
  583.1 5.7 collective-permute-start.36
  588.8 2.1 collective-permute-start.32
  590.1 8.3 %collective-permute-start.37 = (bf16[32,4608]{1,0:T(8,128)(2,1)S(1)}, bf16[32,4608]{1,0:T(8,128)(2,1)S(1)}, u32[]{:S(2)}, u32[]{:S(2)}) collective-permute-start(bf16[32,4608]{1,0:T(8,128)(2,1)S(1)} %constant_dynamic-slice_fusion.2), channel_id=1, source_target_pairs={{0,8},{2,10},{4,12},{6,14},{8,0},{10,2},{12,4},{14,6},{16,24},{18,... | collective-permute-start | bytes 884744 | tf_op jit(solution)/shard_map/ppermute | solution.py:880
  591.0 30.7 %copy-start.8 = (bf16[256,4096]{1,0:T(8,128)(2,1)S(1)}, bf16[256,4096]{1,0:T(8,128)(2,1)}, u32[]{:S(2)}) copy-start(bf16[256,4096]{1,0:T(8,128)(2,1)} %get-tuple-element.136) | copy-start | bytes 6291460
  591.0 9.5 %collective-permute-start.33 = (bf16[32,4608]{1,0:T(8,128)(2,1)S(1)}, bf16[32,4608]{1,0:T(8,128)(2,1)S(1)}, u32[]{:S(2)}, u32[]{:S(2)}) collective-permute-start(bf16[32,4608]{1,0:T(8,128)(2,1)S(1)} %constant_dynamic-slice_fusion.6), channel_id=1, source_target_pairs={{0,4},{2,6},{4,0},{6,2},{8,12},{10,14},{12,8},{14,10},{16,20},{18,... | collective-permute-start | bytes 884744 | tf_op jit(solution)/shard_map/ppermute | solution.py:880
  598.5 15.8 %collective-permute-start.38 = (bf16[16,4608]{1,0:T(8,128)(2,1)S(1)}, bf16[16,4608]{1,0:T(8,128)(2,1)S(1)}, u32[]{:S(2)}, u32[]{:S(2)}) collective-permute-start(bf16[16,4608]{1,0:T(8,128)(2,1)S(1)} %constant_dynamic-slice_fusion.1), channel_id=1, source_target_pairs={{0,16},{2,18},{4,20},{6,22},{8,24},{10,26},{12,28},{14,30},{16,0},... | collective-permute-start | bytes 442376 | tf_op jit(solution)/shard_map/ppermute | solution.py:880
  600.6 15.9 %collective-permute-start.34 = (bf16[16,4608]{1,0:T(8,128)(2,1)S(1)}, bf16[16,4608]{1,0:T(8,128)(2,1)S(1)}, u32[]{:S(2)}, u32[]{:S(2)}) collective-permute-start(bf16[16,4608]{1,0:T(8,128)(2,1)S(1)} %constant_dynamic-slice_fusion.5), channel_id=1, source_target_pairs={{0,8},{2,10},{4,12},{6,14},{8,0},{10,2},{12,4},{14,6},{16,24},{18,... | collective-permute-start | bytes 442376 | tf_op jit(solution)/shard_map/ppermute | solution.py:880
  614.3 4.4 collective-permute-start.39
  616.6 5.0 collective-permute-start.35
  621.6 5.1 collective-permute-start.40
  622.0 36.8 %copy-start.4 = (bf16[256,4096]{1,0:T(8,128)(2,1)S(1)}, bf16[256,4096]{1,0:T(8,128)(2,1)}, u32[]{:S(2)}) copy-start(bf16[256,4096]{1,0:T(8,128)(2,1)} %output.1) | copy-start | bytes 6291460
  622.0 5.0 collective-permute-start.44
  626.7 13.9 %collective-permute-start.41 = (bf16[16,4608]{1,0:T(8,128)(2,1)S(1)}, bf16[16,4608]{1,0:T(8,128)(2,1)S(1)}, u32[]{:S(2)}, u32[]{:S(2)}) collective-permute-start(bf16[16,4608]{1,0:T(8,128)(2,1)S(1)} %maximum_select_fusion.6), channel_id=1, source_target_pairs={{0,8},{2,10},{4,12},{6,14},{8,0},{10,2},{12,4},{14,6},{16,24},{18,... | collective-permute-start | bytes 442376 | tf_op jit(solution)/shard_map/ppermute | solution.py:880
  627.1 14.7 %collective-permute-start.45 = (bf16[16,4608]{1,0:T(8,128)(2,1)S(1)}, bf16[16,4608]{1,0:T(8,128)(2,1)S(1)}, u32[]{:S(2)}, u32[]{:S(2)}) collective-permute-start(bf16[16,4608]{1,0:T(8,128)(2,1)S(1)} %maximum_select_fusion.7), channel_id=1, source_target_pairs={{0,16},{2,18},{4,20},{6,22},{8,24},{10,26},{12,28},{14,30},{16,0},... | collective-permute-start | bytes 442376 | tf_op jit(solution)/shard_map/ppermute | solution.py:880
  640.7 6.0 collective-permute-start.42
  641.8 24.9 %collective-permute-start.46 = (bf16[32,4608]{1,0:T(8,128)(2,1)S(1)}, bf16[32,4608]{1,0:T(8,128)(2,1)S(1)}, u32[]{:S(2)}, u32[]{:S(2)}) collective-permute-start(bf16[32,4608]{1,0:T(8,128)(2,1)S(1)} %maximum_select_fusion.5), channel_id=1, source_target_pairs={{0,8},{2,10},{4,12},{6,14},{8,0},{10,2},{12,4},{14,6},{16,24},{18,... | collective-permute-start | bytes 884744 | tf_op jit(solution)/shard_map/ppermute | solution.py:880
  646.8 21.7 %collective-permute-start.43 = (bf16[64,4608]{1,0:T(8,128)(2,1)S(1)}, bf16[64,4608]{1,0:T(8,128)(2,1)S(1)}, u32[]{:S(2)}, u32[]{:S(2)}) collective-permute-start(bf16[64,4608]{1,0:T(8,128)(2,1)S(1)} %maximum_select_fusion.2), channel_id=1, source_target_pairs={{0,2},{2,0},{4,6},{6,4},{8,10},{10,8},{12,14},{14,12},{16,18},{18,... | collective-permute-start | bytes 1769480 | tf_op jit(solution)/shard_map/ppermute | solution.py:880
  666.8 3.3 collective-permute-start.47
  (21 other events, 108.5 us)
Sparse Core Ops, SparseCore 0:
  484.2 88.8 reduce-scatter.1
  588.8 72.2 all-gather.1

commit v8 on v7

--- a/solution.py
+++ b/solution.py
@@ -841,8 +841,8 @@
     def everywhere(self, x):
         return lax.psum(x, "dp")
 
-    def sum_owned(self, x, late):
-        return lax.psum(x, "dp")
+    def sum_owned(self, x, beside):
+        return lax.psum(x, "dp"), beside(x)
 
 
 class Paired:
@@ -899,7 +899,7 @@
             x = x + self.over(x, bit)
         return x
 
-    def sum_owned(self, x, late):
+    def sum_owned(self, x, beside):
         rows = x.shape[0] // 2
         order = (self.bits, [self.bits[0], *self.bits[2:], self.bits[1]])
         parts = [lax.slice_in_dim(x, at * rows, (at + 1) * rows) for at in range(2)]
@@ -914,8 +914,10 @@
                 keep = lax.dynamic_slice_in_dim(parts[at], upper(bit) * size, size)
                 send = lax.dynamic_slice_in_dim(parts[at], (1 - upper(bit)) * size, size)
                 parts[at] = (keep.astype(F32) + self.over(send, bit).astype(F32)).astype(BF)
-        parts = list(after(late, *parts))
+        held = beside(parts[0])
         for step in reversed(range(len(self.bits))):
+            if step == 0:
+                parts = list(after(held, *parts))
             for at in range(2):
                 bit = order[at][step]
                 other = self.over(parts[at], bit)
@@ -924,7 +926,7 @@
                     jnp.concatenate([parts[at], other]),
                     jnp.concatenate([other, parts[at]]),
                 )
-        return jnp.concatenate(parts)
+        return jnp.concatenate(parts), held
 
 
 def after(first, *later):
@@ -1023,6 +1025,7 @@
     ctx_own = jnp.concatenate([a.reshape(1, ch, CTXP) for a in (dkc, dvc)])
     ctx_got = plan.got(ctx_own)
     turned_two = plan.turn(meta, after(mixed, w2))
+    turned_one = plan.turn(meta, after(mixed, w1))
     dw_qkv, db_qkv = outer(meta, (dq, dk, dv), full_three, name="qkv_grad")
     dw_out, _ = outer(meta, (cot,), full_heads, name="out_grad")
     mats_own = jnp.concatenate([dw_qkv, dw_out])
@@ -1031,13 +1034,12 @@
     full_grad_two = plan.gather(grad_two)
     dw_two = conv_weight_grad(meta, grad_two, full_two, "conv_two_weight_grad")
     two_got = plan.got(dw_two)
-    full_grad_two = after(dw_two, *full_grad_two) if moved else full_grad_two
+    full_grad_two = after((dw_two, turned_one), *full_grad_two) if moved else full_grad_two
     grad_one, sums_two = conv_call(
         conv_two_back_kernel, meta, (turned_two, turned_two), full_grad_two, (par_two, stat_two),
         (conv_one,), [low, stat], [], [pltpu.VMEM((ch, HW), F32)], "conv_two_back",
     )
     full_grad_one = plan.gather(grad_one)
-    turned_one = plan.turn(meta, after(mixed, w1))
     mats_got, ctx_got, two_got = after(grad_one, mats_got, ctx_got, two_got)
     ctx_grad = plan.pick(ctx_own, ctx_got)[:, :, :CTX]
     dw_ctx = jnp.einsum("ton,ne->toe", ctx_grad, context[0], preferred_element_type=F32).astype(BF)
@@ -1085,18 +1087,25 @@
         output,
     )
     early, dw_one, one_got = after(small, early, dw_one, one_got)
-    dw_one = plan.sum_owned(plan.pick(dw_one, one_got), (input_got, output_got))
+
+    def finish(token):
+        out_got, in_got, sums = after(token, output_got, input_got, small)
+        per_image = sums[14:].reshape(plan.images, 2, ch).astype(BF)
+        return (
+            plan.pick(input_grad, in_got).astype(F32).reshape(ch, images, pixels),
+            plan.pick(output, out_got),
+            jnp.stack(
+                [
+                    jnp.einsum("ie,io->eo", emb_all, per_image[:, t], preferred_element_type=F32)
+                    for t in range(2)
+                ]
+            ),
+        )
+
+    dw_one, done = plan.sum_owned(plan.pick(dw_one, one_got), finish)
     early = lax.all_gather(early, "dp", axis=0, tiled=True)
     mods = small[14:].reshape(plan.images, 2, ch)
-    mods_low = mods.astype(BF)
-    dw_emb = jnp.stack(
-        [
-            jnp.einsum("ie,io->eo", emb_all, mods_low[:, t], preferred_element_type=F32)
-            for t in range(2)
-        ]
-    )
-    input_grad = plan.pick(input_grad, input_got).astype(F32)
-    output = plan.pick(output, output_got)
+    input_grad, output, dw_emb = done
     early = after((dw_one, small, input_grad, output), early)
     dw_ctx = jnp.stack([early[:, n * CTX_EMB : (n + 1) * CTX_EMB] for n in range(2)])
     first = 2 * CTX_EMB
@@ -1105,7 +1114,7 @@
 
     return (
         output.reshape(ch, images, pixels),
-        input_grad.reshape(ch, images, pixels),
+        input_grad,
         small[12],
         small[13],
         dw_one.astype(F32),

time: 705 us -> 709 us (level)
  starting transfers between devices: 108 us -> 91.5 us
  waiting for transfers between devices: 68.8 us -> 84.6 us
    ppermute x34, starting transfers between devices: 83.7 us -> 67.4 us  [over(): return lax.ppermute(x, 'dp', [(i, i ^ bit) for i in range(self.images)])]
    reduce_scatter x1, waiting for transfers between devices: 0.01 us -> 11.5 us  [local(): early = lax.psum_scatter(early, 'dp', scatter_dimension=0, tiled=True)]
    unnamed x79 -> x69, local copies, waits for them, and re-layouts: 17.4 us -> 19.4 us
  transfers between devices with their start and end apart: 50 -> 50, of which waited for: 18 -> 19; matrix products, arithmetic and copies ran while one was open for 7% -> 7% of each run, Pallas kernels for 28% -> 28%
where the time goes in v8:
time: 709 us; the launch traced here: 700 us
  Pallas kernels  425 us (60%)
  starting transfers between devices  91.5 us (13%)
  waiting for transfers between devices  84.6 us (12%)
  local copies, waits for them, and re-layouts  38.9 us (5%)
  other arithmetic  34.3 us (5%)
  between operations  16.7 us (2%)
  matrix products  8.28 us (1%)
    pallas_call x1, Pallas kernels, attention(): pl.pallas_call(functools.partial(attention_kernel, len(grads), unroll=unr...  225 us
    pallas_call x4, Pallas kernels, conv_call(): pl.pallas_call(functools.partial(kernel, len(pieces)), out_shape=[*outs,...  93.7 us
    ppermute x34, waiting for transfers between devices, over(): return lax.ppermute(x, 'dp', [(i, i ^ bit) for i in range(self.images)])  73 us
    ppermute x34, starting transfers between devices, over(): return lax.ppermute(x, 'dp', [(i, i ^ bit) for i in range(self.images)])  67.4 us
    pallas_call x2, Pallas kernels, conv_weight_grad(): pl.pallas_call(functools.partial(weight_grad_kernel, len(pieces)), out_sh...  32.8 us
    ppermute x13, starting transfers between devices, got(): return lax.ppermute(x, ('dp', 'tensor'), self.far)  22.8 us
    unnamed x69, local copies, waits for them, and re-layouts  19.4 us
  transfers between devices with their start and end apart: 50, of which 19 were waited for; matrix products, arithmetic and copies ran while one was open for 7% of the time, Pallas kernels for 28%

profile of v8, /device:TPU:5, one launch (start us, length us, event | category | flops | bytes accessed | tf_op | source)
XLA Modules:
  0.0 699.6 jit_solution(11667555919155640849)
XLA Ops:
  7.4 2.1 collective-permute-start
  11.0 2.0 fusion.15
  14.6 2.1 collective-permute-start.7
  21.8 2.2 collective-permute-done.3
  24.0 2.4 collective-permute-start.4
  28.9 9.0 %act_one.1 = (bf16[256,4096]{1,0:T(8,128)(2,1)}, f32[256,128]{1,0:T(8,128)}, bf16[256,4096]{1,0:T(8,128)(2,1)}) custom-call(s32[2]{0:T(128)} %pad_add_fusion.meta, bf16[256,4096]{1,0:T(8,128)(2,1)} %bitcast.122, bf16[256,4096]{1,0:T(8,128)(2,1)} %collective-permute-done.got_ref, f32[256,2]{1,0:T(8,128)} %slice_bitcast_fusion.10.par_ref.refs_2_), custom_call_target="tpu_custom_call" | custom-call | flops 209715 | bytes 62914 | tf_op jit(solution)/shard_map/act_one/pallas_call | solution.py:187
  37.8 14.3 %collective-permute-start.8 = (bf16[256,4096]{1,0:T(8,128)(2,1)}, bf16[256,4096]{1,0:T(8,128)(2,1)}, u32[]{:S(2)}, u32[]{:S(2)}) collective-permute-start(bf16[256,4096]{1,0:T(8,128)(2,1)} %get-tuple-element.90.refs_0_), channel_id=1, source_target_pairs={{0,2},{2,0},{4,6},{6,4},{8,10},{10,8},{12,14},{14,12},{16,18},{18,... | collective-permute-start | bytes 6291464 | tf_op jit(solution)/shard_map/ppermute | solution.py:880
  52.1 3.1 fusion
  56.1 2.1 collective-permute-start.6
  59.7 22.0 %conv_one.1 = (bf16[256,4096]{1,0:T(8,128)(2,1)}, f32[256,128]{1,0:T(8,128)}, f32[256,4096]{1,0:T(8,128)}, bf16[256,4608]{1,0:T(8,128)(2,1)}) custom-call(s32[2]{0:T(128)} %pad_add_fusion.meta, bf16[256,4608]{1,0:T(8,128)(2,1)} %w_own.2, bf16[256,4608]{1,0:T(8,128)(2,1)} %collective-permute-done.7.w_got, bf16[256,4096]{1,0:T(8,128)(2,1)} %get-tuple-element.90.refs_0_, ...), custom_call_target="tpu_custom_call" | custom-call | flops 96636768 | bytes 107530 | tf_op jit(solution)/shard_map/conv_one/pallas_call | solution.py:259
  81.7 2.9 collective-permute-start.9
  84.6 2.0 pad_maximum_fusion.2
  86.6 2.0 collective-permute-start.12
  90.9 22.3 %conv_two.1 = (bf16[256,4096]{1,0:T(8,128)(2,1)}, f32[256,128]{1,0:T(8,128)}, f32[256,4096]{1,0:T(8,128)}, bf16[256,4608]{1,0:T(8,128)(2,1)}) custom-call(s32[2]{0:T(128)} %pad_add_fusion.meta, bf16[256,4608]{1,0:T(8,128)(2,1)} %w_own.3, bf16[256,4608]{1,0:T(8,128)(2,1)} %collective-permute-done.6.w_got, bf16[256,4096]{1,0:T(8,128)(2,1)} %get-tuple-element.99.refs_0_, ...), custom_call_target="tpu_custom_call" | custom-call | flops 96636768 | bytes 128481 | tf_op jit(solution)/shard_map/conv_two/pallas_call | solution.py:259
  113.2 3.3 collective-permute-start.13
  120.3 4.7 fold.1.refs_0_.refs_5_
  125.8 5.0 grad_heads.1
  130.8 13.1 %collective-permute-start.14 = (bf16[256,4096]{1,0:T(8,128)(2,1)}, bf16[256,4096]{1,0:T(8,128)(2,1)}, u32[]{:S(2)}, u32[]{:S(2)}) collective-permute-start(bf16[256,4096]{1,0:T(8,128)(2,1)} %get-tuple-element.108), channel_id=1, source_target_pairs={{0,2},{2,0},{4,6},{6,4},{8,10},{10,8},{12,14},{14,12},{16,18},{18,... | collective-permute-start | bytes 6291464 | tf_op jit(solution)/shard_map/ppermute | solution.py:880
  149.3 7.7 %qkv.1 = bf16[768,4096]{1,0:T(8,128)(2,1)} custom-call(s32[2]{0:T(128)} %pad_add_fusion.meta, bf16[768,512]{1,0:T(8,128)(2,1)} %get-tuple-element.265.w_ref, bf16[256,4096]{1,0:T(8,128)(2,1)} %get-tuple-element.101.refs_0_.refs_3_, bf16[256,4096]{1,0:T(8,128)(2,1)} %collective-permute-done.13.refs_1_.refs_4_, f32[768,1]{1,0:T(8,128)} %copy.122.refs_2_), custom_call_target="tpu_custom_call" | custom-call | flops 32212254 | bytes 104857 | tf_op jit(solution)/shard_map/qkv/pallas_call | solution.py:524
  157.1 225.2 %attention.1 = (bf16[4,64,4096]{2,1,0:T(8,128)(2,1)}, bf16[4,64,4096]{2,1,0:T(8,128)(2,1)}, bf16[4,64,4096]{2,1,0:T(8,128)(2,1)}, bf16[4,64,4096]{2,1,0:T(8,128)...) custom-call(s32[1]{0:T(128)} %bitcast.22.lim_ref, bf16[3,4,64,4096]{3,2,1,0:T(8,128)(2,1)} %bitcast.105, ...), custom_call_target="tpu_custom_call" | custom-call | flops 1159641216 | bytes 167772 | tf_op jit(solution)/shard_map/attention/pallas_call | solution.py:766
  382.2 7.7 %grad_normed.1 = (bf16[256,4096]{1,0:T(8,128)(2,1)}, bf16[256,4096]{1,0:T(8,128)(2,1)}) custom-call(s32[2]{0:T(128)} %pad_add_fusion.meta, bf16[512,768]{1,0:T(8,128)(2,1)} %copy.127.w_ref, bf16[256,4096]{1,0:T(8,128)(2,1)} %bitcast.111, bf16[256,4096]{1,0:T(8,128)(2,1)} %bitcast.113, bf16[256,4096]{1,0:T(8,128)(2,1)} %bitcast.115), custom_call_target="tpu_custom_call" | custom-call | flops 32212254 | bytes 104857 | tf_op jit(solution)/shard_map/grad_normed/pallas_call | solution.py:558
  390.9 3.5 collective-permute-done.18.refs_1_
  394.4 10.2 %norm_three_back.1 = (f32[256,4096]{1,0:T(8,128)}, bf16[256,4096]{1,0:T(8,128)(2,1)}, f32[256,128]{1,0:T(8,128)}) custom-call(bf16[256,4096]{1,0:T(8,128)(2,1)} %get-tuple-element.119.refs_0_, bf16[256,4096]{1,0:T(8,128)(2,1)} %collective-permute-done.18.refs_1_, f32[256,4096]{1,0:T(8,128)} %get-tuple-element.140.refs_2_.refs_3_, ...), custom_call_target="tpu_custom_call" | custom-call | flops 209715 | bytes 167772 | tf_op jit(solution)/shard_map/norm_three_back/pallas_call | solution.py:494
  404.6 16.3 %conv_two_weight_grad.1 = bf16[256,4608]{1,0:T(8,128)(2,1)} custom-call(s32[2]{0:T(128)} %pad_add_fusion.meta, bf16[256,4096]{1,0:T(8,128)(2,1)} %get-tuple-element.124.grad_ref.refs_0_, bf16[256,4096]{1,0:T(8,128)(2,1)} %get-tuple-element.99.refs_0_, bf16[256,4096]{1,0:T(8,128)(2,1)} %collective-permute-done.9.refs_1_), custom_call_target="tpu_custom_call" | custom-call | flops 96636768 | bytes 86507 | tf_op jit(solution)/shard_map/conv_two_weight_grad/pallas_call | solution.py:417
  420.9 2.1 collective-permute-start.22
  423.0 8.4 %qkv_grad.1 = (bf16[768,512]{1,0:T(8,128)(2,1)}, f32[768,128]{1,0:T(8,128)}) custom-call(s32[2]{0:T(128)} %pad_add_fusion.meta, bf16[256,4096]{1,0:T(8,128)(2,1)} %bitcast.112, bf16[256,4096]{1,0:T(8,128)(2,1)} %bitcast.114, bf16[256,4096]{1,0:T(8,128)(2,1)} %bitcast.116, bf16[256,4096]{1,0:T(8,128)(2,1)} %get-tuple-element.101.refs_0_.refs_3_, ...), custom_call_target="tpu_custom_call" | custom-call | flops 32212254 | bytes 104857 | tf_op jit(solution)/shard_map/qkv_grad/pallas_call | solution.py:632
  431.5 2.1 constant_dynamic-update-slice_fusion.1
  433.5 5.3 out_grad.1
  443.9 4.5 turn.2.w_own.w_got
  448.4 4.5 turn.3.w_own.w_got
  452.9 24.7 %conv_two_back.1 = (bf16[256,4096]{1,0:T(8,128)(2,1)}, f32[256,128]{1,0:T(8,128)}) custom-call(s32[2]{0:T(128)} %pad_add_fusion.meta, bf16[256,4608]{1,0:T(8,128)(2,1)} %turn.3.w_own.w_got, bf16[256,4608]{1,0:T(8,128)(2,1)} %turn.3.w_own.w_got, bf16[256,4096]{1,0:T(8,128)(2,1)} %get-tuple-element.124.grad_ref.refs_0_, ...), custom_call_target="tpu_custom_call" | custom-call | flops 96636768 | bytes 150784 | tf_op jit(solution)/shard_map/conv_two_back/pallas_call | solution.py:259
  479.0 2.3 convolution_convert_fusion
  486.4 2.0 select_dynamic-update-slice_fusion
  488.5 4.8 collective-permute-start.23
  493.4 16.5 %conv_one_weight_grad.1 = bf16[256,4608]{1,0:T(8,128)(2,1)} custom-call(s32[2]{0:T(128)} %pad_add_fusion.meta, bf16[256,4096]{1,0:T(8,128)(2,1)} %get-tuple-element.135.grad_ref.refs_0_, bf16[256,4096]{1,0:T(8,128)(2,1)} %get-tuple-element.90.refs_0_, bf16[256,4096]{1,0:T(8,128)(2,1)} %collective-permute-done.8.refs_1_), custom_call_target="tpu_custom_call" | custom-call | flops 96636768 | bytes 86507 | tf_op jit(solution)/shard_map/conv_one_weight_grad/pallas_call | solution.py:417
  509.9 2.1 collective-permute-start.29
  513.1 24.8 %conv_one_back.1 = (bf16[256,4096]{1,0:T(8,128)(2,1)}, f32[256,128]{1,0:T(8,128)}) custom-call(s32[2]{0:T(128)} %pad_add_fusion.meta, bf16[256,4608]{1,0:T(8,128)(2,1)} %turn.2.w_own.w_got, bf16[256,4608]{1,0:T(8,128)(2,1)} %turn.2.w_own.w_got, bf16[256,4096]{1,0:T(8,128)(2,1)} %get-tuple-element.135.grad_ref.refs_0_, ...), custom_call_target="tpu_custom_call" | custom-call | flops 96636768 | bytes 171724 | tf_op jit(solution)/shard_map/conv_one_back/pallas_call | solution.py:259
  540.4 6.6 output.1
  548.4 2.0 collective-permute-done.25
  553.6 2.1 collective-permute-start.27
  555.7 1.8 collective-permute-done.27
  557.5 3.4 collective-permute-start.28
  561.8 11.5 %reduce-scatter.2.cloned.1.call-done = bf16[16,10752]{1,0:T(8,128)(2,1)} async-done(((bf16[256,10752]{1,0:T(8,128)(2,1)}), bf16[16,10752]{1,0:T(8,128)(2,1)}) %reduce-scatter.2.cloned.1.call-update) | async-done | bytes 344080 | tf_op jit(solution)/shard_map/reduce_scatter | solution.py:1052
  573.3 1.9 broadcast_select_fusion
  577.4 2.1 collective-permute-start.30
  579.5 2.1 collective-permute-start.34
  581.6 2.2 collective-permute-start.35
  585.0 1.8 collective-permute-start.39
  591.3 7.1 %collective-permute-done.31 = bf16[32,4608]{1,0:T(8,128)(2,1)S(1)} collective-permute-done((bf16[32,4608]{1,0:T(8,128)(2,1)S(1)}, bf16[32,4608]{1,0:T(8,128)(2,1)S(1)}, u32[]{:S(2)}, u32[]{:S(2)}) %collective-permute-start.31) | collective-permute-done | bytes 294944 | tf_op jit(solution)/shard_map/ppermute | solution.py:880
  598.7 6.7 collective-permute-done.40
  605.6 6.8 collective-permute-done.32
  613.6 6.7 collective-permute-done.41
  622.0 2.0 collective-permute-done.42
  627.5 2.3 bitcast_convert_fusion
  629.8 2.3 pad_maximum_fusion
  633.1 11.7 %collective-permute-done.44 = bf16[16,4608]{1,0:T(8,128)(2,1)S(1)} collective-permute-done((bf16[16,4608]{1,0:T(8,128)(2,1)S(1)}, bf16[16,4608]{1,0:T(8,128)(2,1)S(1)}, u32[]{:S(2)}, u32[]{:S(2)}) %collective-permute-start.44) | collective-permute-done | bytes 147488 | tf_op jit(solution)/shard_map/ppermute | solution.py:880
  646.7 13.2 %collective-permute-done.45 = bf16[32,4608]{1,0:T(8,128)(2,1)S(1)} collective-permute-done((bf16[32,4608]{1,0:T(8,128)(2,1)S(1)}, bf16[32,4608]{1,0:T(8,128)(2,1)S(1)}, u32[]{:S(2)}, u32[]{:S(2)}) %collective-permute-start.45) | collective-permute-done | bytes 294944 | tf_op jit(solution)/shard_map/ppermute | solution.py:880
  660.2 4.4 collective-permute-start.46
  667.1 8.5 %copy.133 = f32[256,1,4096]{2,1,0:T(1,128)} copy(f32[256,1,4096]{2,0,1:T(8,128)} %bitcast_convert_fusion) | data formatting | bytes 8388608
  675.8 1.8 collective-permute-done.47
  677.8 2.7 fusion.20
  682.2 2.1 slice_convert_fusion.1
  684.3 4.4 slice_convert_fusion
  688.7 2.3 maximum_convert_fusion
  (234 shorter events, 69.4 us)
Async XLA Ops:
  7.2 44.9 %copy-start = (bf16[1,260,2048]{2,1,0:T(8,128)(2,1)S(1)}, bf16[1,260,2048]{2,1,0:T(8,128)(2,1)}, u32[]{:S(2)}) copy-start(bf16[1,260,2048]{2,1,0:T(8,128)(2,1)} %param.26) | copy-start | bytes 3194884
  7.2 6.4 copy-start.26
  7.2 6.4 copy-start.27
  7.2 6.4 copy-start.28
  7.3 565.9 %reduce-scatter.2.cloned.1.call-start = ((), (), s32[]{:S(2)}) async-start(), calls=%async_computation.1 | async-start | bytes 5849088 | tf_op jit(solution)/shard_map/reduce_scatter | solution.py:1052
  7.4 21.5 %collective-permute-start = (bf16[256,4096]{1,0:T(8,128)(2,1)}, bf16[256,4096]{1,0:T(8,128)(2,1)}, u32[]{:S(2)}, u32[]{:S(2)}) collective-permute-start(bf16[256,4096]{1,0:T(8,128)(2,1)} %bitcast.121), channel_id=1, source_target_pairs={{1,2},{2,1},{5,6},{6,5},{9,10},{10,9},{13,14},{14,13},{17,18},{18,... | collective-permute-start | bytes 6291464 | tf_op jit(solution)/shard_map/ppermute | solution.py:874
  10.3 6.3 collective-permute-start.1
  13.9 7.9 %collective-permute-start.5 = (f32[15,256]{0,1:T(8,128)S(1)}, f32[15,256]{0,1:T(8,128)S(1)}, u32[]{:S(2)}, u32[]{:S(2)}) collective-permute-start(f32[15,256]{0,1:T(8,128)S(1)} %copy.120), channel_id=1, source_target_pairs={{1,2},{2,1},{5,6},{6,5},{9,10},{10,9},{13,14},{14,13},{17,18},{18,... | collective-permute-start | bytes 46088 | tf_op jit(solution)/shard_map/ppermute | solution.py:874
  14.6 45.1 %collective-permute-start.7 = (bf16[256,4608]{1,0:T(8,128)(2,1)}, bf16[256,4608]{1,0:T(8,128)(2,1)}, u32[]{:S(2)}, u32[]{:S(2)}) collective-permute-start(bf16[256,4608]{1,0:T(8,128)(2,1)} %w_own.2), channel_id=1, source_target_pairs={{1,2},{2,1},{5,6},{6,5},{9,10},{10,9},{13,14},{14,13},{17,18},{18,... | collective-permute-start | bytes 7077896 | tf_op jit(solution)/shard_map/ppermute | solution.py:874
  16.7 3.6 collective-permute-start.2
  20.4 3.6 collective-permute-start.3
  24.0 4.2 collective-permute-start.4
  28.8 23.3 %copy-start.29 = (f32[2,256]{1,0:T(2,128)S(1)}, f32[2,256]{1,0:T(2,128)}, u32[]{:S(2)}) copy-start(f32[2,256]{1,0:T(2,128)} %param.43) | copy-start | bytes 6148
  37.8 21.8 %collective-permute-start.8 = (bf16[256,4096]{1,0:T(8,128)(2,1)}, bf16[256,4096]{1,0:T(8,128)(2,1)}, u32[]{:S(2)}, u32[]{:S(2)}) collective-permute-start(bf16[256,4096]{1,0:T(8,128)(2,1)} %get-tuple-element.90.refs_0_), channel_id=1, source_target_pairs={{0,2},{2,0},{4,6},{6,4},{8,10},{10,8},{12,14},{14,12},{16,18},{18,... | collective-permute-start | bytes 6291464 | tf_op jit(solution)/shard_map/ppermute | solution.py:880
  56.1 34.9 %collective-permute-start.6 = (bf16[256,4608]{1,0:T(8,128)(2,1)}, bf16[256,4608]{1,0:T(8,128)(2,1)}, u32[]{:S(2)}, u32[]{:S(2)}) collective-permute-start(bf16[256,4608]{1,0:T(8,128)(2,1)} %w_own.3), channel_id=1, source_target_pairs={{1,2},{2,1},{5,6},{6,5},{9,10},{10,9},{13,14},{14,13},{17,18},{18,... | collective-permute-start | bytes 7077896 | tf_op jit(solution)/shard_map/ppermute | solution.py:874
  59.7 24.9 %copy-start.8 = (bf16[3,256,512]{2,1,0:T(8,128)(2,1)S(1)}, bf16[3,256,512]{2,1,0:T(8,128)(2,1)}, u32[]{:S(2)}) copy-start(bf16[3,256,512]{2,1,0:T(8,128)(2,1)} %param.40) | copy-start | bytes 2359300
  81.7 9.2 %collective-permute-start.9 = (bf16[256,4096]{1,0:T(8,128)(2,1)}, bf16[256,4096]{1,0:T(8,128)(2,1)}, u32[]{:S(2)}, u32[]{:S(2)}) collective-permute-start(bf16[256,4096]{1,0:T(8,128)(2,1)} %get-tuple-element.99.refs_0_), channel_id=1, source_target_pairs={{0,2},{2,0},{4,6},{6,4},{8,10},{10,8},{12,14},{14,12},{16,18},{18,... | collective-permute-start | bytes 6291464 | tf_op jit(solution)/shard_map/ppermute | solution.py:880
  86.6 29.9 %collective-permute-start.12 = (bf16[256,4096]{1,0:T(8,128)(2,1)}, bf16[256,4096]{1,0:T(8,128)(2,1)}, u32[]{:S(2)}, u32[]{:S(2)}) collective-permute-start(bf16[256,4096]{1,0:T(8,128)(2,1)} %bitcast.18.own_ref), channel_id=1, source_target_pairs={{1,2},{2,1},{5,6},{6,5},{9,10},{10,9},{13,14},{14,13},{17,18},{18,... | collective-permute-start | bytes 6291464 | tf_op jit(solution)/shard_map/ppermute | solution.py:874
  88.6 27.9 %collective-permute-start.10 = (bf16[1024,512]{1,0:T(8,128)(2,1)}, bf16[1024,512]{1,0:T(8,128)(2,1)}, u32[]{:S(2)}, u32[]{:S(2)}) collective-permute-start(bf16[1024,512]{1,0:T(8,128)(2,1)} %pad_maximum_fusion.2), channel_id=1, source_target_pairs={{1,2},{2,1},{5,6},{6,5},{9,10},{10,9},{13,14},{14,13},{17,18},{18,... | collective-permute-start | bytes 3145736 | tf_op jit(solution)/shard_map/ppermute | solution.py:874
  90.2 26.3 %collective-permute-start.11 = (bf16[2,256,384]{1,2,0:T(8,128)(2,1)S(1)}, bf16[2,256,384]{1,2,0:T(8,128)(2,1)S(1)}, u32[]{:S(2)}, u32[]{:S(2)}) collective-permute-start(bf16[2,256,384]{1,2,0:T(8,128)(2,1)S(1)} %pad.4), channel_id=1, source_target_pairs={{1,2},{2,1},{5,6},{6,5},{9,10},{10,9},{13,14},{14,13},{17,18},{18,... | collective-permute-start | bytes 1179656 | tf_op jit(solution)/shard_map/ppermute | solution.py:874
  113.2 36.1 %collective-permute-start.13 = (bf16[256,4096]{1,0:T(8,128)(2,1)}, bf16[256,4096]{1,0:T(8,128)(2,1)}, u32[]{:S(2)}, u32[]{:S(2)}) collective-permute-start(bf16[256,4096]{1,0:T(8,128)(2,1)} %get-tuple-element.101.refs_0_.refs_3_), channel_id=1, source_target_pairs={{0,2},{2,0},{4,6},{6,4},{8,10},{10,8},{12,14},{14,12},{16,18},{18,... | collective-permute-start | bytes 6291464 | tf_op jit(solution)/shard_map/ppermute | solution.py:880
  125.8 20.3 %copy-start.12 = (bf16[2,256,384]{1,2,0:T(8,128)(2,1)S(1)}, bf16[2,256,384]{1,2,0:T(8,128)(2,1)}, u32[]{:S(2)}) copy-start(bf16[2,256,384]{1,2,0:T(8,128)(2,1)} %copy-done.11) | copy-start | bytes 1179652
  130.8 16.3 %copy-start.6 = (bf16[1024,512]{1,0:T(8,128)(2,1)S(1)}, bf16[1024,512]{1,0:T(8,128)(2,1)}, u32[]{:S(2)}) copy-start(bf16[1024,512]{1,0:T(8,128)(2,1)} %copy-done.5) | copy-start | bytes 3145732
  130.8 26.2 %collective-permute-start.14 = (bf16[256,4096]{1,0:T(8,128)(2,1)}, bf16[256,4096]{1,0:T(8,128)(2,1)}, u32[]{:S(2)}, u32[]{:S(2)}) collective-permute-start(bf16[256,4096]{1,0:T(8,128)(2,1)} %get-tuple-element.108), channel_id=1, source_target_pairs={{0,2},{2,0},{4,6},{6,4},{8,10},{10,8},{12,14},{14,12},{16,18},{18,... | collective-permute-start | bytes 6291464 | tf_op jit(solution)/shard_map/ppermute | solution.py:880
  389.9 4.5 collective-permute-start.18
  389.9 43.6 %collective-permute-start.15 = (bf16[256,4096]{1,0:T(8,128)(2,1)}, bf16[256,4096]{1,0:T(8,128)(2,1)}, u32[]{:S(2)}, u32[]{:S(2)}) collective-permute-start(bf16[256,4096]{1,0:T(8,128)(2,1)} %bitcast.108), channel_id=1, source_target_pairs={{0,2},{2,0},{4,6},{6,4},{8,10},{10,8},{12,14},{14,12},{16,18},{18,... | collective-permute-start | bytes 6291464 | tf_op jit(solution)/shard_map/ppermute | solution.py:880
  390.4 52.1 %collective-permute-start.16 = (bf16[256,4608]{1,0:T(8,128)(2,1)}, bf16[256,4608]{1,0:T(8,128)(2,1)}, u32[]{:S(2)}, u32[]{:S(2)}) collective-permute-start(bf16[256,4608]{1,0:T(8,128)(2,1)} %get-tuple-element.111.own_ref), channel_id=1, source_target_pairs={{0,2},{2,0},{4,6},{6,4},{8,10},{10,8},{12,14},{14,12},{16,18},{18,... | collective-permute-start | bytes 7077896 | tf_op jit(solution)/shard_map/ppermute | solution.py:880
  390.5 57.9 %collective-permute-start.17 = (bf16[256,4608]{1,0:T(8,128)(2,1)}, bf16[256,4608]{1,0:T(8,128)(2,1)}, u32[]{:S(2)}, u32[]{:S(2)}) collective-permute-start(bf16[256,4608]{1,0:T(8,128)(2,1)} %get-tuple-element.115.own_ref), channel_id=1, source_target_pairs={{0,2},{2,0},{4,6},{6,4},{8,10},{10,8},{12,14},{14,12},{16,18},{18,... | collective-permute-start | bytes 7077896 | tf_op jit(solution)/shard_map/ppermute | solution.py:880
  420.9 56.7 %collective-permute-start.22 = (bf16[256,4608]{1,0:T(8,128)(2,1)}, bf16[256,4608]{1,0:T(8,128)(2,1)}, u32[]{:S(2)}, u32[]{:S(2)}) collective-permute-start(bf16[256,4608]{1,0:T(8,128)(2,1)} %conv_two_weight_grad.1), channel_id=1, source_target_pairs={{1,2},{2,1},{5,6},{6,5},{9,10},{10,9},{13,14},{14,13},{17,18},{18,... | collective-permute-start | bytes 7077896 | tf_op jit(solution)/shard_map/ppermute | solution.py:874
  423.0 29.9 %collective-permute-start.19 = (bf16[256,4096]{1,0:T(8,128)(2,1)}, bf16[256,4096]{1,0:T(8,128)(2,1)}, u32[]{:S(2)}, u32[]{:S(2)}) collective-permute-start(bf16[256,4096]{1,0:T(8,128)(2,1)} %get-tuple-element.124.grad_ref.refs_0_), channel_id=1, source_target_pairs={{0,2},{2,0},{4,6},{6,4},{8,10},{10,8},{12,14},{14,12},{16,18},{18,... | collective-permute-start | bytes 6291464 | tf_op jit(solution)/shard_map/ppermute | solution.py:880
  433.5 8.6 %copy-start.15 = (bf16[4,64,384]{2,1,0:T(8,128)(2,1)S(1)}, bf16[4,64,384]{2,1,0:T(8,128)(2,1)}, u32[]{:S(2)}) copy-start(bf16[4,64,384]{2,1,0:T(8,128)(2,1)} %get-tuple-element.112) | copy-start | bytes 589828
  433.5 8.8 %copy-start.14 = (bf16[4,64,384]{2,1,0:T(8,128)(2,1)S(1)}, bf16[4,64,384]{2,1,0:T(8,128)(2,1)}, u32[]{:S(2)}) copy-start(bf16[4,64,384]{2,1,0:T(8,128)(2,1)} %get-tuple-element.113) | copy-start | bytes 589828
  440.5 37.1 %collective-permute-start.20 = (bf16[1024,512]{1,0:T(8,128)(2,1)}, bf16[1024,512]{1,0:T(8,128)(2,1)}, u32[]{:S(2)}, u32[]{:S(2)}) collective-permute-start(bf16[1024,512]{1,0:T(8,128)(2,1)} %constant_dynamic-update-slice_fusion), channel_id=1, source_target_pairs={{1,2},{2,1},{5,6},{6,5},{9,10},{10,9},{13,14},{14,13},{17,18},{18,... | collective-permute-start | bytes 3145736 | tf_op jit(solution)/shard_map/ppermute | solution.py:874
  442.5 35.1 %collective-permute-start.21 = (bf16[2,256,384]{1,2,0:T(8,128)(2,1)S(1)}, bf16[2,256,384]{1,2,0:T(8,128)(2,1)}, u32[]{:S(2)}, u32[]{:S(2)}) collective-permute-start(bf16[2,256,384]{1,2,0:T(8,128)(2,1)S(1)} %pad_maximum_fusion.3), channel_id=1, source_target_pairs={{1,2},{2,1},{5,6},{6,5},{9,10},{10,9},{13,14},{14,13},{17,18},{18,... | collective-permute-start | bytes 1179656 | tf_op jit(solution)/shard_map/ppermute | solution.py:874
  488.5 23.7 %copy-start.10 = (f32[768,128]{1,0:T(8,128)S(1)}, f32[768,128]{1,0:T(8,128)}, u32[]{:S(2)}) copy-start(f32[768,128]{1,0:T(8,128)} %get-tuple-element.142) | copy-start | bytes 1179652
  488.5 23.9 %copy-start.16 = (f32[256,128]{1,0:T(8,128)S(1)}, f32[256,128]{1,0:T(8,128)}, u32[]{:S(2)}) copy-start(f32[256,128]{1,0:T(8,128)} %get-tuple-element.141) | copy-start | bytes 393220
  488.5 24.0 %copy-start.17 = (f32[256,128]{1,0:T(8,128)S(1)}, f32[256,128]{1,0:T(8,128)}, u32[]{:S(2)}) copy-start(f32[256,128]{1,0:T(8,128)} %get-tuple-element.143) | copy-start | bytes 393220
  488.5 192.0 %all-gather.2.cloned.1.call-start = ((), (), s32[]{:S(2)}) async-start(), calls=%async_computation.2 | async-start | bytes 5849088 | tf_op jit(solution)/shard_map/all_gather | solution.py:1106
  488.5 24.6 %collective-permute-start.23 = (bf16[256,4096]{1,0:T(8,128)(2,1)}, bf16[256,4096]{1,0:T(8,128)(2,1)}, u32[]{:S(2)}, u32[]{:S(2)}) collective-permute-start(bf16[256,4096]{1,0:T(8,128)(2,1)} %get-tuple-element.135.grad_ref.refs_0_), channel_id=1, source_target_pairs={{0,2},{2,0},{4,6},{6,4},{8,10},{10,8},{12,14},{14,12},{16,18},{18,... | collective-permute-start | bytes 6291464 | tf_op jit(solution)/shard_map/ppermute | solution.py:880
  509.9 51.9 %collective-permute-start.29 = (bf16[256,4608]{1,0:T(8,128)(2,1)}, bf16[256,4608]{1,0:T(8,128)(2,1)}, u32[]{:S(2)}, u32[]{:S(2)}) collective-permute-start(bf16[256,4608]{1,0:T(8,128)(2,1)} %conv_one_weight_grad.1), channel_id=1, source_target_pairs={{1,2},{2,1},{5,6},{6,5},{9,10},{10,9},{13,14},{14,13},{17,18},{18,... | collective-permute-start | bytes 7077896 | tf_op jit(solution)/shard_map/ppermute | solution.py:874
  539.2 7.8 %collective-permute-start.24 = (f32[46,256]{1,0:T(8,128)S(1)}, f32[46,256]{1,0:T(8,128)S(1)}, u32[]{:S(2)}, u32[]{:S(2)}) collective-permute-start(f32[46,256]{1,0:T(8,128)S(1)} %concatenate.74), channel_id=1, source_target_pairs={{0,1},{1,0},{2,3},{3,2},{4,5},{5,4},{6,7},{7,6},{8,9},{9,8},{10,11... | collective-permute-start | bytes 141320 | tf_op jit(solution)/shard_map/ppermute | solution.py:892
  547.0 3.4 collective-permute-start.25
  550.4 3.1 collective-permute-start.26
  553.6 3.9 collective-permute-start.27
  557.5 4.3 collective-permute-start.28
  577.4 9.3 %collective-permute-start.30 = (bf16[64,4608]{1,0:T(8,128)(2,1)S(1)}, bf16[64,4608]{1,0:T(8,128)(2,1)}, u32[]{:S(2)}, u32[]{:S(2)}) collective-permute-start(bf16[64,4608]{1,0:T(8,128)(2,1)S(1)} %constant_dynamic-slice_fusion.7), channel_id=1, source_target_pairs={{0,2},{2,0},{4,6},{6,4},{8,10},{10,8},{12,14},{14,12},{16,18},{18,... | collective-permute-start | bytes 1769480 | tf_op jit(solution)/shard_map/ppermute | solution.py:880
  579.5 42.4 %collective-permute-start.34 = (bf16[256,4096]{1,0:T(8,128)(2,1)S(1)}, bf16[256,4096]{1,0:T(8,128)(2,1)}, u32[]{:S(2)}, u32[]{:S(2)}) collective-permute-start(bf16[256,4096]{1,0:T(8,128)(2,1)S(1)} %copy-done.3), channel_id=1, source_target_pairs={{1,2},{2,1},{5,6},{6,5},{9,10},{10,9},{13,14},{14,13},{17,18},{18,... | collective-permute-start | bytes 6291464 | tf_op jit(solution)/shard_map/ppermute | solution.py:874
  581.6 40.3 %collective-permute-start.35 = (bf16[256,4096]{1,0:T(8,128)(2,1)}, bf16[256,4096]{1,0:T(8,128)(2,1)}, u32[]{:S(2)}, u32[]{:S(2)}) collective-permute-start(bf16[256,4096]{1,0:T(8,128)(2,1)} %get-tuple-element.139), channel_id=1, source_target_pairs={{1,2},{2,1},{5,6},{6,5},{9,10},{10,9},{13,14},{14,13},{17,18},{18,... | collective-permute-start | bytes 6291464 | tf_op jit(solution)/shard_map/ppermute | solution.py:874
  585.0 4.5 collective-permute-start.39
  588.2 10.2 %collective-permute-start.31 = (bf16[32,4608]{1,0:T(8,128)(2,1)S(1)}, bf16[32,4608]{1,0:T(8,128)(2,1)S(1)}, u32[]{:S(2)}, u32[]{:S(2)}) collective-permute-start(bf16[32,4608]{1,0:T(8,128)(2,1)S(1)} %constant_dynamic-slice_fusion.6), channel_id=1, source_target_pairs={{0,4},{2,6},{4,0},{6,2},{8,12},{10,14},{12,8},{14,10},{16,20},{18,... | collective-permute-start | bytes 884744 | tf_op jit(solution)/shard_map/ppermute | solution.py:880
  590.8 33.4 %copy-start.9 = (bf16[16,2048]{1,0:T(8,128)(2,1)S(1)}, bf16[16,2048]{1,0:T(8,128)(2,1)}, u32[]{:S(2)}) copy-start(bf16[16,2048]{1,0:T(8,128)(2,1)} %add.173) | copy-start | bytes 196612
  590.8 14.6 %collective-permute-start.40 = (bf16[32,4608]{1,0:T(8,128)(2,1)S(1)}, bf16[32,4608]{1,0:T(8,128)(2,1)S(1)}, u32[]{:S(2)}, u32[]{:S(2)}) collective-permute-start(bf16[32,4608]{1,0:T(8,128)(2,1)S(1)} %constant_dynamic-slice_fusion.2), channel_id=1, source_target_pairs={{0,8},{2,10},{4,12},{6,14},{8,0},{10,2},{12,4},{14,6},{16,24},{18,... | collective-permute-start | bytes 884744 | tf_op jit(solution)/shard_map/ppermute | solution.py:880
  598.4 13.9 %collective-permute-start.32 = (bf16[16,4608]{1,0:T(8,128)(2,1)S(1)}, bf16[16,4608]{1,0:T(8,128)(2,1)S(1)}, u32[]{:S(2)}, u32[]{:S(2)}) collective-permute-start(bf16[16,4608]{1,0:T(8,128)(2,1)S(1)} %constant_dynamic-slice_fusion.5), channel_id=1, source_target_pairs={{0,8},{2,10},{4,12},{6,14},{8,0},{10,2},{12,4},{14,6},{16,24},{18,... | collective-permute-start | bytes 442376 | tf_op jit(solution)/shard_map/ppermute | solution.py:880
  605.5 14.7 %collective-permute-start.41 = (bf16[16,4608]{1,0:T(8,128)(2,1)S(1)}, bf16[16,4608]{1,0:T(8,128)(2,1)S(1)}, u32[]{:S(2)}, u32[]{:S(2)}) collective-permute-start(bf16[16,4608]{1,0:T(8,128)(2,1)S(1)} %constant_dynamic-slice_fusion.1), channel_id=1, source_target_pairs={{0,16},{2,18},{4,20},{6,22},{8,24},{10,26},{12,28},{14,30},{16,0},... | collective-permute-start | bytes 442376 | tf_op jit(solution)/shard_map/ppermute | solution.py:880
  612.4 9.4 %collective-permute-start.33 = (bf16[8,4608]{1,0:T(8,128)(2,1)S(1)}, bf16[8,4608]{1,0:T(8,128)(2,1)S(1)}, u32[]{:S(2)}, u32[]{:S(2)}) collective-permute-start(bf16[8,4608]{1,0:T(8,128)(2,1)S(1)} %constant_dynamic-slice_fusion.4), channel_id=1, source_target_pairs={{0,16},{2,18},{4,20},{6,22},{8,24},{10,26},{12,28},{14,30},{16,0},... | collective-permute-start | bytes 221192 | tf_op jit(solution)/shard_map/ppermute | solution.py:880
  620.3 3.7 collective-permute-start.42
  621.9 11.1 %collective-permute-start.36 = (bf16[8,4608]{1,0:T(8,128)(2,1)S(1)}, bf16[8,4608]{1,0:T(8,128)(2,1)S(1)}, u32[]{:S(2)}, u32[]{:S(2)}) collective-permute-start(bf16[8,4608]{1,0:T(8,128)(2,1)S(1)} %add_convert_fusion.7), channel_id=1, source_target_pairs={{0,16},{2,18},{4,20},{6,22},{8,24},{10,26},{12,28},{14,30},{16,0},... | collective-permute-start | bytes 221192 | tf_op jit(solution)/shard_map/ppermute | solution.py:880
  624.0 8.1 %collective-permute-start.43 = (bf16[8,4608]{1,0:T(8,128)(2,1)S(1)}, bf16[8,4608]{1,0:T(8,128)(2,1)S(1)}, u32[]{:S(2)}, u32[]{:S(2)}) collective-permute-start(bf16[8,4608]{1,0:T(8,128)(2,1)S(1)} %add_convert_fusion.6), channel_id=1, source_target_pairs={{0,4},{2,6},{4,0},{6,2},{8,12},{10,14},{12,8},{14,10},{16,20},{18,... | collective-permute-start | bytes 221192 | tf_op jit(solution)/shard_map/ppermute | solution.py:880
  632.1 12.7 %collective-permute-start.44 = (bf16[16,4608]{1,0:T(8,128)(2,1)S(1)}, bf16[16,4608]{1,0:T(8,128)(2,1)S(1)}, u32[]{:S(2)}, u32[]{:S(2)}) collective-permute-start(bf16[16,4608]{1,0:T(8,128)(2,1)S(1)} %maximum_select_fusion.7), channel_id=1, source_target_pairs={{0,16},{2,18},{4,20},{6,22},{8,24},{10,26},{12,28},{14,30},{16,0},... | collective-permute-start | bytes 442376 | tf_op jit(solution)/shard_map/ppermute | solution.py:880
  633.0 11.9 %collective-permute-start.37 = (bf16[16,4608]{1,0:T(8,128)(2,1)S(1)}, bf16[16,4608]{1,0:T(8,128)(2,1)S(1)}, u32[]{:S(2)}, u32[]{:S(2)}) collective-permute-start(bf16[16,4608]{1,0:T(8,128)(2,1)S(1)} %maximum_select_fusion.6), channel_id=1, source_target_pairs={{0,8},{2,10},{4,12},{6,14},{8,0},{10,2},{12,4},{14,6},{16,24},{18,... | collective-permute-start | bytes 442376 | tf_op jit(solution)/shard_map/ppermute | solution.py:880
  644.8 15.2 %collective-permute-start.45 = (bf16[32,4608]{1,0:T(8,128)(2,1)S(1)}, bf16[32,4608]{1,0:T(8,128)(2,1)S(1)}, u32[]{:S(2)}, u32[]{:S(2)}) collective-permute-start(bf16[32,4608]{1,0:T(8,128)(2,1)S(1)} %maximum_select_fusion.5), channel_id=1, source_target_pairs={{0,8},{2,10},{4,12},{6,14},{8,0},{10,2},{12,4},{14,6},{16,24},{18,... | collective-permute-start | bytes 884744 | tf_op jit(solution)/shard_map/ppermute | solution.py:880
  645.0 15.1 %collective-permute-start.38 = (bf16[32,4608]{1,0:T(8,128)(2,1)S(1)}, bf16[32,4608]{1,0:T(8,128)(2,1)S(1)}, u32[]{:S(2)}, u32[]{:S(2)}) collective-permute-start(bf16[32,4608]{1,0:T(8,128)(2,1)S(1)} %maximum_select_fusion.4), channel_id=1, source_target_pairs={{0,4},{2,6},{4,0},{6,2},{8,12},{10,14},{12,8},{14,10},{16,20},{18,... | collective-permute-start | bytes 884744 | tf_op jit(solution)/shard_map/ppermute | solution.py:880
  660.2 15.4 %collective-permute-start.46 = (bf16[64,4608]{1,0:T(8,128)(2,1)S(1)}, bf16[64,4608]{1,0:T(8,128)(2,1)S(1)}, u32[]{:S(2)}, u32[]{:S(2)}) collective-permute-start(bf16[64,4608]{1,0:T(8,128)(2,1)S(1)} %maximum_select_fusion.2), channel_id=1, source_target_pairs={{0,2},{2,0},{4,6},{6,4},{8,10},{10,8},{12,14},{14,12},{16,18},{18,... | collective-permute-start | bytes 1769480 | tf_op jit(solution)/shard_map/ppermute | solution.py:880
  675.6 2.0 collective-permute-start.47
  (16 other events, 72.7 us)
Sparse Core Ops, SparseCore 0:
  488.6 84.6 reduce-scatter.1
  584.0 74.6 all-gather.1

commit v9 on v8

--- a/solution.py
+++ b/solution.py
@@ -1086,13 +1086,15 @@
         ),
         output,
     )
-    early, dw_one, one_got = after(small, early, dw_one, one_got)
+    early, dw_one, one_got = after((small, input_got), early, dw_one, one_got)
 
     def finish(token):
         out_got, in_got, sums = after(token, output_got, input_got, small)
         per_image = sums[14:].reshape(plan.images, 2, ch).astype(BF)
         return (
-            plan.pick(input_grad, in_got).astype(F32).reshape(ch, images, pixels),
+            plan.pick(
+                input_grad.reshape(ch, images, pixels), in_got.reshape(ch, images, pixels)
+            ).astype(F32),
             plan.pick(output, out_got),
             jnp.stack(
                 [

time: 709 us -> 712 us (level)
    ppermute x1, waiting for transfers between devices: 0.01 us -> 16.8 us  [total(): x = after(beside, x + lax.ppermute(x, 'tensor', [(0, 1), (1, 0)]))]
    reduce_scatter x1, waiting for transfers between devices: 11.5 us -> 0.02 us  [local(): early = lax.psum_scatter(early, 'dp', scatter_dimension=0, tiled=True)]
    ppermute x34, waiting for transfers between devices: 73 us -> 64.6 us  [over(): return lax.ppermute(x, 'dp', [(i, i ^ bit) for i in range(self.images)])]
    unnamed x69 -> x71, local copies, waits for them, and re-layouts: 19.4 us -> 19.6 us
  transfers between devices with their start and end apart: 50 -> 50, of which waited for: 19 -> 16; matrix products, arithmetic and copies ran while one was open for 7% -> 7% of each run, Pallas kernels for 28% -> 27%
where the time goes in v9:
time: 712 us; the launch traced here: 703 us
  Pallas kernels  425 us (60%)
  starting transfers between devices  98.2 us (14%)
  waiting for transfers between devices  81.5 us (11%)
  local copies, waits for them, and re-layouts  38.1 us (5%)
  other arithmetic  34.3 us (5%)
  between operations  16.7 us (2%)
  matrix products  8.27 us (1%)
    pallas_call x1, Pallas kernels, attention(): pl.pallas_call(functools.partial(attention_kernel, len(grads), unroll=unr...  225 us
    pallas_call x4, Pallas kernels, conv_call(): pl.pallas_call(functools.partial(kernel, len(pieces)), out_shape=[*outs,...  93.9 us
    ppermute x34, starting transfers between devices, over(): return lax.ppermute(x, 'dp', [(i, i ^ bit) for i in range(self.images)])  72.8 us
    ppermute x34, waiting for transfers between devices, over(): return lax.ppermute(x, 'dp', [(i, i ^ bit) for i in range(self.images)])  64.6 us
    pallas_call x2, Pallas kernels, conv_weight_grad(): pl.pallas_call(functools.partial(weight_grad_kernel, len(pieces)), out_sh...  32.8 us
    ppermute x13, starting transfers between devices, got(): return lax.ppermute(x, ('dp', 'tensor'), self.far)  23.1 us
    unnamed x71, local copies, waits for them, and re-layouts  19.6 us
    ppermute x1, waiting for transfers between devices, total(): x = after(beside, x + lax.ppermute(x, 'tensor', [(0, 1), (1, 0)]))  16.8 us
  transfers between devices with their start and end apart: 50, of which 16 were waited for; matrix products, arithmetic and copies ran while one was open for 7% of the time, Pallas kernels for 27%

profile of v9, /device:TPU:5, one launch (start us, length us, event | category | flops | bytes accessed | tf_op | source)
XLA Modules:
  0.0 702.5 jit_solution(7051873198130658534)
XLA Ops:
  7.4 2.2 collective-permute-start
  11.0 2.0 fusion.15
  14.6 2.1 collective-permute-start.7
  21.8 2.2 collective-permute-done.3
  24.0 2.4 collective-permute-start.4
  28.9 9.0 %act_one.1 = (bf16[256,4096]{1,0:T(8,128)(2,1)}, f32[256,128]{1,0:T(8,128)}, bf16[256,4096]{1,0:T(8,128)(2,1)}) custom-call(s32[2]{0:T(128)} %pad_add_fusion.meta, bf16[256,4096]{1,0:T(8,128)(2,1)} %bitcast.122, bf16[256,4096]{1,0:T(8,128)(2,1)} %collective-permute-done.got_ref, f32[256,2]{1,0:T(8,128)} %slice_bitcast_fusion.10.par_ref.refs_2_), custom_call_target="tpu_custom_call" | custom-call | flops 209715 | bytes 62914 | tf_op jit(solution)/shard_map/act_one/pallas_call | solution.py:187
  37.9 14.3 %collective-permute-start.8 = (bf16[256,4096]{1,0:T(8,128)(2,1)}, bf16[256,4096]{1,0:T(8,128)(2,1)}, u32[]{:S(2)}, u32[]{:S(2)}) collective-permute-start(bf16[256,4096]{1,0:T(8,128)(2,1)} %get-tuple-element.90.refs_0_), channel_id=1, source_target_pairs={{0,2},{2,0},{4,6},{6,4},{8,10},{10,8},{12,14},{14,12},{16,18},{18,... | collective-permute-start | bytes 6291464 | tf_op jit(solution)/shard_map/ppermute | solution.py:880
  52.1 3.1 fusion
  56.0 2.1 collective-permute-start.6
  59.7 22.0 %conv_one.1 = (bf16[256,4096]{1,0:T(8,128)(2,1)}, f32[256,128]{1,0:T(8,128)}, f32[256,4096]{1,0:T(8,128)}, bf16[256,4608]{1,0:T(8,128)(2,1)}) custom-call(s32[2]{0:T(128)} %pad_add_fusion.meta, bf16[256,4608]{1,0:T(8,128)(2,1)} %w_own.2, bf16[256,4608]{1,0:T(8,128)(2,1)} %collective-permute-done.7.w_got, bf16[256,4096]{1,0:T(8,128)(2,1)} %get-tuple-element.90.refs_0_, ...), custom_call_target="tpu_custom_call" | custom-call | flops 96636768 | bytes 107530 | tf_op jit(solution)/shard_map/conv_one/pallas_call | solution.py:259
  81.7 2.9 collective-permute-start.9
  84.6 2.0 pad_maximum_fusion.2
  86.6 2.0 collective-permute-start.12
  90.9 22.3 %conv_two.1 = (bf16[256,4096]{1,0:T(8,128)(2,1)}, f32[256,128]{1,0:T(8,128)}, f32[256,4096]{1,0:T(8,128)}, bf16[256,4608]{1,0:T(8,128)(2,1)}) custom-call(s32[2]{0:T(128)} %pad_add_fusion.meta, bf16[256,4608]{1,0:T(8,128)(2,1)} %w_own.3, bf16[256,4608]{1,0:T(8,128)(2,1)} %collective-permute-done.6.w_got, bf16[256,4096]{1,0:T(8,128)(2,1)} %get-tuple-element.99.refs_0_, ...), custom_call_target="tpu_custom_call" | custom-call | flops 96636768 | bytes 128481 | tf_op jit(solution)/shard_map/conv_two/pallas_call | solution.py:259
  113.2 3.3 collective-permute-start.13
  120.3 4.7 fold.1.refs_0_.refs_5_
  125.8 4.9 grad_heads.1
  130.8 13.1 %collective-permute-start.14 = (bf16[256,4096]{1,0:T(8,128)(2,1)}, bf16[256,4096]{1,0:T(8,128)(2,1)}, u32[]{:S(2)}, u32[]{:S(2)}) collective-permute-start(bf16[256,4096]{1,0:T(8,128)(2,1)} %get-tuple-element.108), channel_id=1, source_target_pairs={{0,2},{2,0},{4,6},{6,4},{8,10},{10,8},{12,14},{14,12},{16,18},{18,... | collective-permute-start | bytes 6291464 | tf_op jit(solution)/shard_map/ppermute | solution.py:880
  149.3 7.7 %qkv.1 = bf16[768,4096]{1,0:T(8,128)(2,1)} custom-call(s32[2]{0:T(128)} %pad_add_fusion.meta, bf16[768,512]{1,0:T(8,128)(2,1)} %get-tuple-element.265.w_ref, bf16[256,4096]{1,0:T(8,128)(2,1)} %get-tuple-element.101.refs_0_.refs_3_, bf16[256,4096]{1,0:T(8,128)(2,1)} %collective-permute-done.13.refs_1_.refs_4_, f32[768,1]{1,0:T(8,128)} %copy.122.refs_2_), custom_call_target="tpu_custom_call" | custom-call | flops 32212254 | bytes 104857 | tf_op jit(solution)/shard_map/qkv/pallas_call | solution.py:524
  157.0 225.2 %attention.1 = (bf16[4,64,4096]{2,1,0:T(8,128)(2,1)}, bf16[4,64,4096]{2,1,0:T(8,128)(2,1)}, bf16[4,64,4096]{2,1,0:T(8,128)(2,1)}, bf16[4,64,4096]{2,1,0:T(8,128)...) custom-call(s32[1]{0:T(128)} %bitcast.22.lim_ref, bf16[3,4,64,4096]{3,2,1,0:T(8,128)(2,1)} %bitcast.105, ...), custom_call_target="tpu_custom_call" | custom-call | flops 1159641216 | bytes 167772 | tf_op jit(solution)/shard_map/attention/pallas_call | solution.py:766
  382.2 7.7 %grad_normed.1 = (bf16[256,4096]{1,0:T(8,128)(2,1)}, bf16[256,4096]{1,0:T(8,128)(2,1)}) custom-call(s32[2]{0:T(128)} %pad_add_fusion.meta, bf16[512,768]{1,0:T(8,128)(2,1)} %copy.127.w_ref, bf16[256,4096]{1,0:T(8,128)(2,1)} %bitcast.111, bf16[256,4096]{1,0:T(8,128)(2,1)} %bitcast.113, bf16[256,4096]{1,0:T(8,128)(2,1)} %bitcast.115), custom_call_target="tpu_custom_call" | custom-call | flops 32212254 | bytes 104857 | tf_op jit(solution)/shard_map/grad_normed/pallas_call | solution.py:558
  390.9 3.5 collective-permute-done.18.refs_1_
  394.4 10.2 %norm_three_back.1 = (f32[256,4096]{1,0:T(8,128)}, bf16[256,4096]{1,0:T(8,128)(2,1)}, f32[256,128]{1,0:T(8,128)}) custom-call(bf16[256,4096]{1,0:T(8,128)(2,1)} %get-tuple-element.119.refs_0_, bf16[256,4096]{1,0:T(8,128)(2,1)} %collective-permute-done.18.refs_1_, f32[256,4096]{1,0:T(8,128)} %get-tuple-element.140.refs_2_.refs_3_, ...), custom_call_target="tpu_custom_call" | custom-call | flops 209715 | bytes 167772 | tf_op jit(solution)/shard_map/norm_three_back/pallas_call | solution.py:494
  404.5 16.3 %conv_two_weight_grad.1 = bf16[256,4608]{1,0:T(8,128)(2,1)} custom-call(s32[2]{0:T(128)} %pad_add_fusion.meta, bf16[256,4096]{1,0:T(8,128)(2,1)} %get-tuple-element.124.grad_ref.refs_0_, bf16[256,4096]{1,0:T(8,128)(2,1)} %get-tuple-element.99.refs_0_, bf16[256,4096]{1,0:T(8,128)(2,1)} %collective-permute-done.9.refs_1_), custom_call_target="tpu_custom_call" | custom-call | flops 96636768 | bytes 86507 | tf_op jit(solution)/shard_map/conv_two_weight_grad/pallas_call | solution.py:417
  420.8 2.1 collective-permute-start.22
  422.9 8.5 %qkv_grad.1 = (bf16[768,512]{1,0:T(8,128)(2,1)}, f32[768,128]{1,0:T(8,128)}) custom-call(s32[2]{0:T(128)} %pad_add_fusion.meta, bf16[256,4096]{1,0:T(8,128)(2,1)} %bitcast.112, bf16[256,4096]{1,0:T(8,128)(2,1)} %bitcast.114, bf16[256,4096]{1,0:T(8,128)(2,1)} %bitcast.116, bf16[256,4096]{1,0:T(8,128)(2,1)} %get-tuple-element.101.refs_0_.refs_3_, ...), custom_call_target="tpu_custom_call" | custom-call | flops 32212254 | bytes 104857 | tf_op jit(solution)/shard_map/qkv_grad/pallas_call | solution.py:632
  431.4 2.1 constant_dynamic-update-slice_fusion.1
  433.4 5.3 out_grad.1
  443.9 4.5 turn.2.w_own.w_got
  448.4 4.5 turn.3.w_own.w_got
  452.9 24.6 %conv_two_back.1 = (bf16[256,4096]{1,0:T(8,128)(2,1)}, f32[256,128]{1,0:T(8,128)}) custom-call(s32[2]{0:T(128)} %pad_add_fusion.meta, bf16[256,4608]{1,0:T(8,128)(2,1)} %turn.3.w_own.w_got, bf16[256,4608]{1,0:T(8,128)(2,1)} %turn.3.w_own.w_got, bf16[256,4096]{1,0:T(8,128)(2,1)} %get-tuple-element.124.grad_ref.refs_0_, ...), custom_call_target="tpu_custom_call" | custom-call | flops 96636768 | bytes 150784 | tf_op jit(solution)/shard_map/conv_two_back/pallas_call | solution.py:259
  478.9 2.3 convolution_convert_fusion
  486.4 1.9 select_dynamic-update-slice_fusion
  488.5 4.8 collective-permute-start.23
  493.2 16.5 %conv_one_weight_grad.1 = bf16[256,4608]{1,0:T(8,128)(2,1)} custom-call(s32[2]{0:T(128)} %pad_add_fusion.meta, bf16[256,4096]{1,0:T(8,128)(2,1)} %get-tuple-element.135.grad_ref.refs_0_, bf16[256,4096]{1,0:T(8,128)(2,1)} %get-tuple-element.90.refs_0_, bf16[256,4096]{1,0:T(8,128)(2,1)} %collective-permute-done.8.refs_1_), custom_call_target="tpu_custom_call" | custom-call | flops 96636768 | bytes 86507 | tf_op jit(solution)/shard_map/conv_one_weight_grad/pallas_call | solution.py:417
  509.8 2.2 collective-permute-start.30
  511.9 25.0 %conv_one_back.1 = (bf16[256,4096]{1,0:T(8,128)(2,1)}, f32[256,128]{1,0:T(8,128)}) custom-call(s32[2]{0:T(128)} %pad_add_fusion.meta, bf16[256,4608]{1,0:T(8,128)(2,1)} %turn.2.w_own.w_got, bf16[256,4608]{1,0:T(8,128)(2,1)} %turn.2.w_own.w_got, bf16[256,4096]{1,0:T(8,128)(2,1)} %get-tuple-element.135.grad_ref.refs_0_, ...), custom_call_target="tpu_custom_call" | custom-call | flops 96636768 | bytes 171724 | tf_op jit(solution)/shard_map/conv_one_back/pallas_call | solution.py:259
  536.9 2.2 collective-permute-start.29
  540.7 2.2 collective-permute-start.24
  542.9 6.6 output.1
  549.6 16.8 %collective-permute-done.24 = f32[46,256]{1,0:T(8,128)S(1)} collective-permute-done((f32[46,256]{1,0:T(8,128)S(1)}, f32[46,256]{1,0:T(8,128)S(1)}, u32[]{:S(2)}, u32[]{:S(2)}) %collective-permute-start.24) | collective-permute-done | bytes 47136 | tf_op jit(solution)/shard_map/ppermute | solution.py:892
  567.6 2.1 collective-permute-done.25
  571.1 2.8 collective-permute-done.26
  573.9 2.0 collective-permute-start.27
  575.9 1.9 collective-permute-done.27
  577.8 2.5 collective-permute-start.28
  581.2 1.9 broadcast_select_fusion
  585.8 2.3 collective-permute-start.35
  595.4 4.9 collective-permute-done.32
  601.8 3.6 collective-permute-done.40
  605.5 4.0 collective-permute-start.41
  609.5 5.0 collective-permute-done.33
  614.5 3.5 collective-permute-start.34
  618.1 7.4 %collective-permute-done.34 = bf16[8,4608]{1,0:T(8,128)(2,1)S(1)} collective-permute-done((bf16[8,4608]{1,0:T(8,128)(2,1)S(1)}, bf16[8,4608]{1,0:T(8,128)(2,1)S(1)}, u32[]{:S(2)}, u32[]{:S(2)}) %collective-permute-start.34) | collective-permute-done | bytes 73760 | tf_op jit(solution)/shard_map/ppermute | solution.py:880
  629.6 2.3 bitcast_convert_fusion
  631.9 2.3 pad_maximum_fusion
  634.2 2.4 collective-permute-start.44
  638.6 11.4 %collective-permute-done.44 = bf16[16,4608]{1,0:T(8,128)(2,1)S(1)} collective-permute-done((bf16[16,4608]{1,0:T(8,128)(2,1)S(1)}, bf16[16,4608]{1,0:T(8,128)(2,1)S(1)}, u32[]{:S(2)}, u32[]{:S(2)}) %collective-permute-start.44) | collective-permute-done | bytes 147488 | tf_op jit(solution)/shard_map/ppermute | solution.py:880
  652.0 14.2 %collective-permute-done.45 = bf16[32,4608]{1,0:T(8,128)(2,1)S(1)} collective-permute-done((bf16[32,4608]{1,0:T(8,128)(2,1)S(1)}, bf16[32,4608]{1,0:T(8,128)(2,1)S(1)}, u32[]{:S(2)}, u32[]{:S(2)}) %collective-permute-start.45) | collective-permute-done | bytes 294944 | tf_op jit(solution)/shard_map/ppermute | solution.py:880
  670.0 8.5 %copy.133 = f32[256,1,4096]{2,1,0:T(1,128)} copy(f32[256,1,4096]{2,0,1:T(8,128)} %bitcast_convert_fusion) | data formatting | bytes 8388608
  680.8 2.7 fusion.20
  685.2 2.1 slice_convert_fusion.1
  687.3 4.4 slice_convert_fusion
  691.7 2.3 maximum_convert_fusion
  (236 shorter events, 70.5 us)
Async XLA Ops:
  7.2 44.9 %copy-start = (bf16[1,260,2048]{2,1,0:T(8,128)(2,1)S(1)}, bf16[1,260,2048]{2,1,0:T(8,128)(2,1)}, u32[]{:S(2)}) copy-start(bf16[1,260,2048]{2,1,0:T(8,128)(2,1)} %param.26) | copy-start | bytes 3194884
  7.2 6.4 copy-start.27
  7.2 6.4 copy-start.28
  7.2 6.4 copy-start.29
  7.3 573.9 %reduce-scatter.2.cloned.1.call-start = ((), (), s32[]{:S(2)}) async-start(), calls=%async_computation.1 | async-start | bytes 5849088 | tf_op jit(solution)/shard_map/reduce_scatter | solution.py:1052
  7.4 21.5 %collective-permute-start = (bf16[256,4096]{1,0:T(8,128)(2,1)}, bf16[256,4096]{1,0:T(8,128)(2,1)}, u32[]{:S(2)}, u32[]{:S(2)}) collective-permute-start(bf16[256,4096]{1,0:T(8,128)(2,1)} %bitcast.121), channel_id=1, source_target_pairs={{1,2},{2,1},{5,6},{6,5},{9,10},{10,9},{13,14},{14,13},{17,18},{18,... | collective-permute-start | bytes 6291464 | tf_op jit(solution)/shard_map/ppermute | solution.py:874
  10.4 6.3 collective-permute-start.1
  13.9 7.9 %collective-permute-start.5 = (f32[15,256]{0,1:T(8,128)S(1)}, f32[15,256]{0,1:T(8,128)S(1)}, u32[]{:S(2)}, u32[]{:S(2)}) collective-permute-start(f32[15,256]{0,1:T(8,128)S(1)} %copy.120), channel_id=1, source_target_pairs={{1,2},{2,1},{5,6},{6,5},{9,10},{10,9},{13,14},{14,13},{17,18},{18,... | collective-permute-start | bytes 46088 | tf_op jit(solution)/shard_map/ppermute | solution.py:874
  14.6 45.1 %collective-permute-start.7 = (bf16[256,4608]{1,0:T(8,128)(2,1)}, bf16[256,4608]{1,0:T(8,128)(2,1)}, u32[]{:S(2)}, u32[]{:S(2)}) collective-permute-start(bf16[256,4608]{1,0:T(8,128)(2,1)} %w_own.2), channel_id=1, source_target_pairs={{1,2},{2,1},{5,6},{6,5},{9,10},{10,9},{13,14},{14,13},{17,18},{18,... | collective-permute-start | bytes 7077896 | tf_op jit(solution)/shard_map/ppermute | solution.py:874
  16.8 3.6 collective-permute-start.2
  20.4 3.6 collective-permute-start.3
  24.0 4.2 collective-permute-start.4
  28.9 23.3 %copy-start.30 = (f32[2,256]{1,0:T(2,128)S(1)}, f32[2,256]{1,0:T(2,128)}, u32[]{:S(2)}) copy-start(f32[2,256]{1,0:T(2,128)} %param.43) | copy-start | bytes 6148
  37.9 21.8 %collective-permute-start.8 = (bf16[256,4096]{1,0:T(8,128)(2,1)}, bf16[256,4096]{1,0:T(8,128)(2,1)}, u32[]{:S(2)}, u32[]{:S(2)}) collective-permute-start(bf16[256,4096]{1,0:T(8,128)(2,1)} %get-tuple-element.90.refs_0_), channel_id=1, source_target_pairs={{0,2},{2,0},{4,6},{6,4},{8,10},{10,8},{12,14},{14,12},{16,18},{18,... | collective-permute-start | bytes 6291464 | tf_op jit(solution)/shard_map/ppermute | solution.py:880
  56.0 34.9 %collective-permute-start.6 = (bf16[256,4608]{1,0:T(8,128)(2,1)}, bf16[256,4608]{1,0:T(8,128)(2,1)}, u32[]{:S(2)}, u32[]{:S(2)}) collective-permute-start(bf16[256,4608]{1,0:T(8,128)(2,1)} %w_own.3), channel_id=1, source_target_pairs={{1,2},{2,1},{5,6},{6,5},{9,10},{10,9},{13,14},{14,13},{17,18},{18,... | collective-permute-start | bytes 7077896 | tf_op jit(solution)/shard_map/ppermute | solution.py:874
  59.7 24.9 %copy-start.8 = (bf16[3,256,512]{2,1,0:T(8,128)(2,1)S(1)}, bf16[3,256,512]{2,1,0:T(8,128)(2,1)}, u32[]{:S(2)}) copy-start(bf16[3,256,512]{2,1,0:T(8,128)(2,1)} %param.40) | copy-start | bytes 2359300
  81.7 9.2 %collective-permute-start.9 = (bf16[256,4096]{1,0:T(8,128)(2,1)}, bf16[256,4096]{1,0:T(8,128)(2,1)}, u32[]{:S(2)}, u32[]{:S(2)}) collective-permute-start(bf16[256,4096]{1,0:T(8,128)(2,1)} %get-tuple-element.99.refs_0_), channel_id=1, source_target_pairs={{0,2},{2,0},{4,6},{6,4},{8,10},{10,8},{12,14},{14,12},{16,18},{18,... | collective-permute-start | bytes 6291464 | tf_op jit(solution)/shard_map/ppermute | solution.py:880
  86.6 29.9 %collective-permute-start.12 = (bf16[256,4096]{1,0:T(8,128)(2,1)}, bf16[256,4096]{1,0:T(8,128)(2,1)}, u32[]{:S(2)}, u32[]{:S(2)}) collective-permute-start(bf16[256,4096]{1,0:T(8,128)(2,1)} %bitcast.18.own_ref), channel_id=1, source_target_pairs={{1,2},{2,1},{5,6},{6,5},{9,10},{10,9},{13,14},{14,13},{17,18},{18,... | collective-permute-start | bytes 6291464 | tf_op jit(solution)/shard_map/ppermute | solution.py:874
  88.5 28.0 %collective-permute-start.10 = (bf16[1024,512]{1,0:T(8,128)(2,1)}, bf16[1024,512]{1,0:T(8,128)(2,1)}, u32[]{:S(2)}, u32[]{:S(2)}) collective-permute-start(bf16[1024,512]{1,0:T(8,128)(2,1)} %pad_maximum_fusion.2), channel_id=1, source_target_pairs={{1,2},{2,1},{5,6},{6,5},{9,10},{10,9},{13,14},{14,13},{17,18},{18,... | collective-permute-start | bytes 3145736 | tf_op jit(solution)/shard_map/ppermute | solution.py:874
  90.2 26.3 %collective-permute-start.11 = (bf16[2,256,384]{1,2,0:T(8,128)(2,1)S(1)}, bf16[2,256,384]{1,2,0:T(8,128)(2,1)S(1)}, u32[]{:S(2)}, u32[]{:S(2)}) collective-permute-start(bf16[2,256,384]{1,2,0:T(8,128)(2,1)S(1)} %pad.4), channel_id=1, source_target_pairs={{1,2},{2,1},{5,6},{6,5},{9,10},{10,9},{13,14},{14,13},{17,18},{18,... | collective-permute-start | bytes 1179656 | tf_op jit(solution)/shard_map/ppermute | solution.py:874
  113.2 36.1 %collective-permute-start.13 = (bf16[256,4096]{1,0:T(8,128)(2,1)}, bf16[256,4096]{1,0:T(8,128)(2,1)}, u32[]{:S(2)}, u32[]{:S(2)}) collective-permute-start(bf16[256,4096]{1,0:T(8,128)(2,1)} %get-tuple-element.101.refs_0_.refs_3_), channel_id=1, source_target_pairs={{0,2},{2,0},{4,6},{6,4},{8,10},{10,8},{12,14},{14,12},{16,18},{18,... | collective-permute-start | bytes 6291464 | tf_op jit(solution)/shard_map/ppermute | solution.py:880
  125.8 20.2 %copy-start.12 = (bf16[2,256,384]{1,2,0:T(8,128)(2,1)S(1)}, bf16[2,256,384]{1,2,0:T(8,128)(2,1)}, u32[]{:S(2)}) copy-start(bf16[2,256,384]{1,2,0:T(8,128)(2,1)} %copy-done.11) | copy-start | bytes 1179652
  130.8 16.3 %copy-start.6 = (bf16[1024,512]{1,0:T(8,128)(2,1)S(1)}, bf16[1024,512]{1,0:T(8,128)(2,1)}, u32[]{:S(2)}) copy-start(bf16[1024,512]{1,0:T(8,128)(2,1)} %copy-done.5) | copy-start | bytes 3145732
  130.8 26.2 %collective-permute-start.14 = (bf16[256,4096]{1,0:T(8,128)(2,1)}, bf16[256,4096]{1,0:T(8,128)(2,1)}, u32[]{:S(2)}, u32[]{:S(2)}) collective-permute-start(bf16[256,4096]{1,0:T(8,128)(2,1)} %get-tuple-element.108), channel_id=1, source_target_pairs={{0,2},{2,0},{4,6},{6,4},{8,10},{10,8},{12,14},{14,12},{16,18},{18,... | collective-permute-start | bytes 6291464 | tf_op jit(solution)/shard_map/ppermute | solution.py:880
  389.9 4.5 collective-permute-start.18
  389.9 43.6 %collective-permute-start.15 = (bf16[256,4096]{1,0:T(8,128)(2,1)}, bf16[256,4096]{1,0:T(8,128)(2,1)}, u32[]{:S(2)}, u32[]{:S(2)}) collective-permute-start(bf16[256,4096]{1,0:T(8,128)(2,1)} %bitcast.108), channel_id=1, source_target_pairs={{0,2},{2,0},{4,6},{6,4},{8,10},{10,8},{12,14},{14,12},{16,18},{18,... | collective-permute-start | bytes 6291464 | tf_op jit(solution)/shard_map/ppermute | solution.py:880
  390.4 52.1 %collective-permute-start.16 = (bf16[256,4608]{1,0:T(8,128)(2,1)}, bf16[256,4608]{1,0:T(8,128)(2,1)}, u32[]{:S(2)}, u32[]{:S(2)}) collective-permute-start(bf16[256,4608]{1,0:T(8,128)(2,1)} %get-tuple-element.111.own_ref), channel_id=1, source_target_pairs={{0,2},{2,0},{4,6},{6,4},{8,10},{10,8},{12,14},{14,12},{16,18},{18,... | collective-permute-start | bytes 7077896 | tf_op jit(solution)/shard_map/ppermute | solution.py:880
  390.4 58.0 %collective-permute-start.17 = (bf16[256,4608]{1,0:T(8,128)(2,1)}, bf16[256,4608]{1,0:T(8,128)(2,1)}, u32[]{:S(2)}, u32[]{:S(2)}) collective-permute-start(bf16[256,4608]{1,0:T(8,128)(2,1)} %get-tuple-element.115.own_ref), channel_id=1, source_target_pairs={{0,2},{2,0},{4,6},{6,4},{8,10},{10,8},{12,14},{14,12},{16,18},{18,... | collective-permute-start | bytes 7077896 | tf_op jit(solution)/shard_map/ppermute | solution.py:880
  420.8 56.8 %collective-permute-start.22 = (bf16[256,4608]{1,0:T(8,128)(2,1)}, bf16[256,4608]{1,0:T(8,128)(2,1)}, u32[]{:S(2)}, u32[]{:S(2)}) collective-permute-start(bf16[256,4608]{1,0:T(8,128)(2,1)} %conv_two_weight_grad.1), channel_id=1, source_target_pairs={{1,2},{2,1},{5,6},{6,5},{9,10},{10,9},{13,14},{14,13},{17,18},{18,... | collective-permute-start | bytes 7077896 | tf_op jit(solution)/shard_map/ppermute | solution.py:874
  422.9 30.0 %collective-permute-start.19 = (bf16[256,4096]{1,0:T(8,128)(2,1)}, bf16[256,4096]{1,0:T(8,128)(2,1)}, u32[]{:S(2)}, u32[]{:S(2)}) collective-permute-start(bf16[256,4096]{1,0:T(8,128)(2,1)} %get-tuple-element.124.grad_ref.refs_0_), channel_id=1, source_target_pairs={{0,2},{2,0},{4,6},{6,4},{8,10},{10,8},{12,14},{14,12},{16,18},{18,... | collective-permute-start | bytes 6291464 | tf_op jit(solution)/shard_map/ppermute | solution.py:880
  433.4 8.7 %copy-start.15 = (bf16[4,64,384]{2,1,0:T(8,128)(2,1)S(1)}, bf16[4,64,384]{2,1,0:T(8,128)(2,1)}, u32[]{:S(2)}) copy-start(bf16[4,64,384]{2,1,0:T(8,128)(2,1)} %get-tuple-element.112) | copy-start | bytes 589828
  433.4 8.8 %copy-start.14 = (bf16[4,64,384]{2,1,0:T(8,128)(2,1)S(1)}, bf16[4,64,384]{2,1,0:T(8,128)(2,1)}, u32[]{:S(2)}) copy-start(bf16[4,64,384]{2,1,0:T(8,128)(2,1)} %get-tuple-element.113) | copy-start | bytes 589828
  440.4 37.1 %collective-permute-start.20 = (bf16[1024,512]{1,0:T(8,128)(2,1)}, bf16[1024,512]{1,0:T(8,128)(2,1)}, u32[]{:S(2)}, u32[]{:S(2)}) collective-permute-start(bf16[1024,512]{1,0:T(8,128)(2,1)} %constant_dynamic-update-slice_fusion), channel_id=1, source_target_pairs={{1,2},{2,1},{5,6},{6,5},{9,10},{10,9},{13,14},{14,13},{17,18},{18,... | collective-permute-start | bytes 3145736 | tf_op jit(solution)/shard_map/ppermute | solution.py:874
  442.5 35.1 %collective-permute-start.21 = (bf16[2,256,384]{1,2,0:T(8,128)(2,1)S(1)}, bf16[2,256,384]{1,2,0:T(8,128)(2,1)}, u32[]{:S(2)}, u32[]{:S(2)}) collective-permute-start(bf16[2,256,384]{1,2,0:T(8,128)(2,1)S(1)} %pad_maximum_fusion.3), channel_id=1, source_target_pairs={{1,2},{2,1},{5,6},{6,5},{9,10},{10,9},{13,14},{14,13},{17,18},{18,... | collective-permute-start | bytes 1179656 | tf_op jit(solution)/shard_map/ppermute | solution.py:874
  488.4 195.1 %all-gather.2.cloned.1.call-start = ((), (), s32[]{:S(2)}) async-start(), calls=%async_computation.2 | async-start | bytes 5849088 | tf_op jit(solution)/shard_map/all_gather | solution.py:1108
  488.5 23.5 %collective-permute-start.23 = (bf16[256,4096]{1,0:T(8,128)(2,1)}, bf16[256,4096]{1,0:T(8,128)(2,1)}, u32[]{:S(2)}, u32[]{:S(2)}) collective-permute-start(bf16[256,4096]{1,0:T(8,128)(2,1)} %get-tuple-element.135.grad_ref.refs_0_), channel_id=1, source_target_pairs={{0,2},{2,0},{4,6},{6,4},{8,10},{10,8},{12,14},{14,12},{16,18},{18,... | collective-permute-start | bytes 6291464 | tf_op jit(solution)/shard_map/ppermute | solution.py:880
  509.8 71.4 %collective-permute-start.30 = (bf16[256,4608]{1,0:T(8,128)(2,1)}, bf16[256,4608]{1,0:T(8,128)(2,1)}, u32[]{:S(2)}, u32[]{:S(2)}) collective-permute-start(bf16[256,4608]{1,0:T(8,128)(2,1)} %conv_one_weight_grad.1), channel_id=1, source_target_pairs={{1,2},{2,1},{5,6},{6,5},{9,10},{10,9},{13,14},{14,13},{17,18},{18,... | collective-permute-start | bytes 7077896 | tf_op jit(solution)/shard_map/ppermute | solution.py:874
  511.9 27.3 %copy-start.10 = (f32[768,128]{1,0:T(8,128)S(1)}, f32[768,128]{1,0:T(8,128)}, u32[]{:S(2)}) copy-start(f32[768,128]{1,0:T(8,128)} %get-tuple-element.142) | copy-start | bytes 1179652
  511.9 27.6 %copy-start.16 = (f32[256,128]{1,0:T(8,128)S(1)}, f32[256,128]{1,0:T(8,128)}, u32[]{:S(2)}) copy-start(f32[256,128]{1,0:T(8,128)} %get-tuple-element.141) | copy-start | bytes 393220
  511.9 27.7 %copy-start.17 = (f32[256,128]{1,0:T(8,128)S(1)}, f32[256,128]{1,0:T(8,128)}, u32[]{:S(2)}) copy-start(f32[256,128]{1,0:T(8,128)} %get-tuple-element.143) | copy-start | bytes 393220
  536.9 44.3 %collective-permute-start.29 = (bf16[256,4096]{1,0:T(8,128)(2,1)}, bf16[256,4096]{1,0:T(8,128)(2,1)}, u32[]{:S(2)}, u32[]{:S(2)}) collective-permute-start(bf16[256,4096]{1,0:T(8,128)(2,1)} %get-tuple-element.139), channel_id=1, source_target_pairs={{1,2},{2,1},{5,6},{6,5},{9,10},{10,9},{13,14},{14,13},{17,18},{18,... | collective-permute-start | bytes 6291464 | tf_op jit(solution)/shard_map/ppermute | solution.py:874
  540.7 25.6 %collective-permute-start.24 = (f32[46,256]{1,0:T(8,128)S(1)}, f32[46,256]{1,0:T(8,128)S(1)}, u32[]{:S(2)}, u32[]{:S(2)}) collective-permute-start(f32[46,256]{1,0:T(8,128)S(1)} %concatenate.74), channel_id=1, source_target_pairs={{0,1},{1,0},{2,3},{3,2},{4,5},{5,4},{6,7},{7,6},{8,9},{9,8},{10,11... | collective-permute-start | bytes 141320 | tf_op jit(solution)/shard_map/ppermute | solution.py:892
  566.3 3.4 collective-permute-start.25
  569.7 4.2 collective-permute-start.26
  573.9 3.9 collective-permute-start.27
  577.8 3.3 collective-permute-start.28
  585.4 4.8 collective-permute-start.31
  585.8 39.8 %collective-permute-start.35 = (bf16[256,4096]{1,0:T(8,128)(2,1)S(1)}, bf16[256,4096]{1,0:T(8,128)(2,1)}, u32[]{:S(2)}, u32[]{:S(2)}) collective-permute-start(bf16[256,4096]{1,0:T(8,128)(2,1)S(1)} %copy-done.3), channel_id=1, source_target_pairs={{1,2},{2,1},{5,6},{6,5},{9,10},{10,9},{13,14},{14,13},{17,18},{18,... | collective-permute-start | bytes 6291464 | tf_op jit(solution)/shard_map/ppermute | solution.py:874
  589.2 3.6 collective-permute-start.39
  591.6 8.8 %collective-permute-start.32 = (bf16[32,4608]{1,0:T(8,128)(2,1)S(1)}, bf16[32,4608]{1,0:T(8,128)(2,1)S(1)}, u32[]{:S(2)}, u32[]{:S(2)}) collective-permute-start(bf16[32,4608]{1,0:T(8,128)(2,1)S(1)} %constant_dynamic-slice_fusion.6), channel_id=1, source_target_pairs={{0,4},{2,6},{4,0},{6,2},{8,12},{10,14},{12,8},{14,10},{16,20},{18,... | collective-permute-start | bytes 884744 | tf_op jit(solution)/shard_map/ppermute | solution.py:880
  594.1 32.1 %copy-start.9 = (bf16[16,2048]{1,0:T(8,128)(2,1)S(1)}, bf16[16,2048]{1,0:T(8,128)(2,1)}, u32[]{:S(2)}) copy-start(bf16[16,2048]{1,0:T(8,128)(2,1)} %add.173) | copy-start | bytes 196612
  594.1 11.3 %collective-permute-start.40 = (bf16[32,4608]{1,0:T(8,128)(2,1)S(1)}, bf16[32,4608]{1,0:T(8,128)(2,1)S(1)}, u32[]{:S(2)}, u32[]{:S(2)}) collective-permute-start(bf16[32,4608]{1,0:T(8,128)(2,1)S(1)} %constant_dynamic-slice_fusion.2), channel_id=1, source_target_pairs={{0,8},{2,10},{4,12},{6,14},{8,0},{10,2},{12,4},{14,6},{16,24},{18,... | collective-permute-start | bytes 884744 | tf_op jit(solution)/shard_map/ppermute | solution.py:880
  600.5 13.9 %collective-permute-start.33 = (bf16[16,4608]{1,0:T(8,128)(2,1)S(1)}, bf16[16,4608]{1,0:T(8,128)(2,1)S(1)}, u32[]{:S(2)}, u32[]{:S(2)}) collective-permute-start(bf16[16,4608]{1,0:T(8,128)(2,1)S(1)} %constant_dynamic-slice_fusion.5), channel_id=1, source_target_pairs={{0,8},{2,10},{4,12},{6,14},{8,0},{10,2},{12,4},{14,6},{16,24},{18,... | collective-permute-start | bytes 442376 | tf_op jit(solution)/shard_map/ppermute | solution.py:880
  605.5 12.4 %collective-permute-start.41 = (bf16[16,4608]{1,0:T(8,128)(2,1)S(1)}, bf16[16,4608]{1,0:T(8,128)(2,1)S(1)}, u32[]{:S(2)}, u32[]{:S(2)}) collective-permute-start(bf16[16,4608]{1,0:T(8,128)(2,1)S(1)} %constant_dynamic-slice_fusion.1), channel_id=1, source_target_pairs={{0,16},{2,18},{4,20},{6,22},{8,24},{10,26},{12,28},{14,30},{16,0},... | collective-permute-start | bytes 442376 | tf_op jit(solution)/shard_map/ppermute | solution.py:880
  614.5 11.0 %collective-permute-start.34 = (bf16[8,4608]{1,0:T(8,128)(2,1)S(1)}, bf16[8,4608]{1,0:T(8,128)(2,1)S(1)}, u32[]{:S(2)}, u32[]{:S(2)}) collective-permute-start(bf16[8,4608]{1,0:T(8,128)(2,1)S(1)} %constant_dynamic-slice_fusion.4), channel_id=1, source_target_pairs={{0,16},{2,18},{4,20},{6,22},{8,24},{10,26},{12,28},{14,30},{16,0},... | collective-permute-start | bytes 221192 | tf_op jit(solution)/shard_map/ppermute | solution.py:880
  618.0 7.6 %collective-permute-start.42 = (bf16[8,4608]{1,0:T(8,128)(2,1)S(1)}, bf16[8,4608]{1,0:T(8,128)(2,1)S(1)}, u32[]{:S(2)}, u32[]{:S(2)}) collective-permute-start(bf16[8,4608]{1,0:T(8,128)(2,1)S(1)} %constant_dynamic-slice_fusion), channel_id=1, source_target_pairs={{0,4},{2,6},{4,0},{6,2},{8,12},{10,14},{12,8},{14,10},{16,20},{18,... | collective-permute-start | bytes 221192 | tf_op jit(solution)/shard_map/ppermute | solution.py:880
  625.5 11.2 %collective-permute-start.36 = (bf16[8,4608]{1,0:T(8,128)(2,1)S(1)}, bf16[8,4608]{1,0:T(8,128)(2,1)S(1)}, u32[]{:S(2)}, u32[]{:S(2)}) collective-permute-start(bf16[8,4608]{1,0:T(8,128)(2,1)S(1)} %add_convert_fusion.7), channel_id=1, source_target_pairs={{0,16},{2,18},{4,20},{6,22},{8,24},{10,26},{12,28},{14,30},{16,0},... | collective-permute-start | bytes 221192 | tf_op jit(solution)/shard_map/ppermute | solution.py:880
  625.6 8.6 %collective-permute-start.43 = (bf16[8,4608]{1,0:T(8,128)(2,1)S(1)}, bf16[8,4608]{1,0:T(8,128)(2,1)S(1)}, u32[]{:S(2)}, u32[]{:S(2)}) collective-permute-start(bf16[8,4608]{1,0:T(8,128)(2,1)S(1)} %add_convert_fusion.6), channel_id=1, source_target_pairs={{0,4},{2,6},{4,0},{6,2},{8,12},{10,14},{12,8},{14,10},{16,20},{18,... | collective-permute-start | bytes 221192 | tf_op jit(solution)/shard_map/ppermute | solution.py:880
  634.2 15.7 %collective-permute-start.44 = (bf16[16,4608]{1,0:T(8,128)(2,1)S(1)}, bf16[16,4608]{1,0:T(8,128)(2,1)S(1)}, u32[]{:S(2)}, u32[]{:S(2)}) collective-permute-start(bf16[16,4608]{1,0:T(8,128)(2,1)S(1)} %maximum_select_fusion.7), channel_id=1, source_target_pairs={{0,16},{2,18},{4,20},{6,22},{8,24},{10,26},{12,28},{14,30},{16,0},... | collective-permute-start | bytes 442376 | tf_op jit(solution)/shard_map/ppermute | solution.py:880
  636.7 13.9 %collective-permute-start.37 = (bf16[16,4608]{1,0:T(8,128)(2,1)S(1)}, bf16[16,4608]{1,0:T(8,128)(2,1)S(1)}, u32[]{:S(2)}, u32[]{:S(2)}) collective-permute-start(bf16[16,4608]{1,0:T(8,128)(2,1)S(1)} %maximum_select_fusion.6), channel_id=1, source_target_pairs={{0,8},{2,10},{4,12},{6,14},{8,0},{10,2},{12,4},{14,6},{16,24},{18,... | collective-permute-start | bytes 442376 | tf_op jit(solution)/shard_map/ppermute | solution.py:880
  650.0 16.3 %collective-permute-start.45 = (bf16[32,4608]{1,0:T(8,128)(2,1)S(1)}, bf16[32,4608]{1,0:T(8,128)(2,1)S(1)}, u32[]{:S(2)}, u32[]{:S(2)}) collective-permute-start(bf16[32,4608]{1,0:T(8,128)(2,1)S(1)} %maximum_select_fusion.5), channel_id=1, source_target_pairs={{0,8},{2,10},{4,12},{6,14},{8,0},{10,2},{12,4},{14,6},{16,24},{18,... | collective-permute-start | bytes 884744 | tf_op jit(solution)/shard_map/ppermute | solution.py:880
  650.7 15.7 %collective-permute-start.38 = (bf16[32,4608]{1,0:T(8,128)(2,1)S(1)}, bf16[32,4608]{1,0:T(8,128)(2,1)S(1)}, u32[]{:S(2)}, u32[]{:S(2)}) collective-permute-start(bf16[32,4608]{1,0:T(8,128)(2,1)S(1)} %maximum_select_fusion.4), channel_id=1, source_target_pairs={{0,4},{2,6},{4,0},{6,2},{8,12},{10,14},{12,8},{14,10},{16,20},{18,... | collective-permute-start | bytes 884744 | tf_op jit(solution)/shard_map/ppermute | solution.py:880
  666.5 12.0 %collective-permute-start.46 = (bf16[64,4608]{1,0:T(8,128)(2,1)S(1)}, bf16[64,4608]{1,0:T(8,128)(2,1)S(1)}, u32[]{:S(2)}, u32[]{:S(2)}) collective-permute-start(bf16[64,4608]{1,0:T(8,128)(2,1)S(1)} %maximum_select_fusion.2), channel_id=1, source_target_pairs={{0,2},{2,0},{4,6},{6,4},{8,10},{10,8},{12,14},{14,12},{16,18},{18,... | collective-permute-start | bytes 1769480 | tf_op jit(solution)/shard_map/ppermute | solution.py:880
  678.5 2.0 collective-permute-start.47
  (17 other events, 74.4 us)
Sparse Core Ops, SparseCore 0:
  488.5 84.4 reduce-scatter.1
  588.2 76.2 all-gather.1

commit v10 on v7

--- a/solution.py
+++ b/solution.py
@@ -835,7 +835,7 @@
         turned = lax.all_to_all(cut, "tensor", split_axis=2, concat_axis=0, tiled=True)
         return turned[:, ::-1].transpose(2, 1, 0).reshape(ch, 9 * C)
 
-    def total(self, x, beside):
+    def total(self, x):
         return lax.psum(x, "dp")
 
     def everywhere(self, x):
@@ -888,8 +888,8 @@
     def turn(self, meta, w):
         return turned_pair(meta, w, self.over(w, 1))
 
-    def total(self, x, beside):
-        x = after(beside, x + lax.ppermute(x, "tensor", [(0, 1), (1, 0)]))
+    def total(self, x):
+        x = x + lax.ppermute(x, "tensor", [(0, 1), (1, 0)])
         for bit in self.bits[1:]:
             x = x + self.over(x, bit)
         return self.pick(x, self.over(x, 1))
@@ -1023,6 +1023,7 @@
     ctx_own = jnp.concatenate([a.reshape(1, ch, CTXP) for a in (dkc, dvc)])
     ctx_got = plan.got(ctx_own)
     turned_two = plan.turn(meta, after(mixed, w2))
+    turned_one = plan.turn(meta, after(mixed, w1))
     dw_qkv, db_qkv = outer(meta, (dq, dk, dv), full_three, name="qkv_grad")
     dw_out, _ = outer(meta, (cot,), full_heads, name="out_grad")
     mats_own = jnp.concatenate([dw_qkv, dw_out])
@@ -1031,13 +1032,12 @@
     full_grad_two = plan.gather(grad_two)
     dw_two = conv_weight_grad(meta, grad_two, full_two, "conv_two_weight_grad")
     two_got = plan.got(dw_two)
-    full_grad_two = after(dw_two, *full_grad_two) if moved else full_grad_two
+    full_grad_two = after((dw_two, turned_one), *full_grad_two) if moved else full_grad_two
     grad_one, sums_two = conv_call(
         conv_two_back_kernel, meta, (turned_two, turned_two), full_grad_two, (par_two, stat_two),
         (conv_one,), [low, stat], [], [pltpu.VMEM((ch, HW), F32)], "conv_two_back",
     )
     full_grad_one = plan.gather(grad_one)
-    turned_one = plan.turn(meta, after(mixed, w1))
     mats_got, ctx_got, two_got = after(grad_one, mats_got, ctx_got, two_got)
     ctx_grad = plan.pick(ctx_own, ctx_got)[:, :, :CTX]
     dw_ctx = jnp.einsum("ton,ne->toe", ctx_grad, context[0], preferred_element_type=F32).astype(BF)
@@ -1059,9 +1059,8 @@
     )
     input_got = plan.got(input_grad)
 
-    one_got = after(input_grad, one_got)
     output = output_product(
-        meta, w_out, full_heads, bias_out, after(input_grad, hidden)
+        meta, w_out, full_heads, bias_out, after((input_grad, one_got), hidden)
     )
     output_got = plan.got(output)
     ctx_sums = jnp.sum(ctx_own.astype(F32), axis=2)
@@ -1081,12 +1080,11 @@
                 sums_one[:, :2].T,
                 mods,
             ]
-        ),
-        output,
-    )
-    early, dw_one, one_got = after(small, early, dw_one, one_got)
+        )
+    )
+    early, dw_one, one_got = after((output, small), early, dw_one, one_got)
+    early = lax.all_gather(early, "dp", axis=0, tiled=True)
     dw_one = plan.sum_owned(plan.pick(dw_one, one_got), (input_got, output_got))
-    early = lax.all_gather(early, "dp", axis=0, tiled=True)
     mods = small[14:].reshape(plan.images, 2, ch)
     mods_low = mods.astype(BF)
     dw_emb = jnp.stack(

time: 705 us -> 694 us (0.984)
  starting transfers between devices: 108 us -> 86.6 us
  waiting for transfers between devices: 68.8 us -> 78.8 us
    ppermute x34, starting transfers between devices: 83.7 us -> 62.1 us  [over(): return lax.ppermute(x, 'dp', [(i, i ^ bit) for i in range(self.images)])]
    unnamed x79 -> x71, local copies, waits for them, and re-layouts: 17.4 us -> 15.4 us
where the time goes in v10:
time: 694 us; the launch traced here: 683 us
  Pallas kernels  426 us (61%)
  starting transfers between devices  86.6 us (12%)
  waiting for transfers between devices  78.8 us (11%)
  local copies, waits for them, and re-layouts  34.9 us (5%)
  other arithmetic  32.2 us (5%)
  between operations  16.7 us (2%)
  matrix products  8.28 us (1%)
    pallas_call x1, Pallas kernels, attention(): pl.pallas_call(functools.partial(attention_kernel, len(grads), unroll=unr...  225 us
    pallas_call x4, Pallas kernels, conv_call(): pl.pallas_call(functools.partial(kernel, len(pieces)), out_shape=[*outs,...  94 us
    ppermute x34, waiting for transfers between devices, over(): return lax.ppermute(x, 'dp', [(i, i ^ bit) for i in range(self.images)])  75.5 us
    ppermute x34, starting transfers between devices, over(): return lax.ppermute(x, 'dp', [(i, i ^ bit) for i in range(self.images)])  62.1 us
    pallas_call x2, Pallas kernels, conv_weight_grad(): pl.pallas_call(functools.partial(weight_grad_kernel, len(pieces)), out_sh...  32.9 us
    ppermute x13, starting transfers between devices, got(): return lax.ppermute(x, ('dp', 'tensor'), self.far)  22.8 us
    unnamed x71, local copies, waits for them, and re-layouts  15.4 us
  transfers between devices with their start and end apart: 50, of which 18 were waited for; matrix products, arithmetic and copies ran while one was open for 7% of the time, Pallas kernels for 28%

profile of v10, /device:TPU:5, one launch (start us, length us, event | category | flops | bytes accessed | tf_op | source)
XLA Modules:
  0.0 683.1 jit_solution(4303395646741687326)
XLA Ops:
  7.4 2.1 collective-permute-start
  11.0 2.0 fusion.15
  14.6 2.1 collective-permute-start.7
  18.6 1.7 collective-permute-done.2
  21.8 2.2 collective-permute-done.3
  24.0 2.4 collective-permute-start.4
  28.9 9.0 %act_one.1 = (bf16[256,4096]{1,0:T(8,128)(2,1)}, f32[256,128]{1,0:T(8,128)}, bf16[256,4096]{1,0:T(8,128)(2,1)}) custom-call(s32[2]{0:T(128)} %pad_add_fusion.meta, bf16[256,4096]{1,0:T(8,128)(2,1)} %bitcast.121, bf16[256,4096]{1,0:T(8,128)(2,1)} %collective-permute-done.got_ref, f32[256,2]{1,0:T(8,128)} %slice_bitcast_fusion.10.par_ref.refs_2_), custom_call_target="tpu_custom_call" | custom-call | flops 209715 | bytes 62914 | tf_op jit(solution)/shard_map/act_one/pallas_call | solution.py:187
  37.9 14.3 %collective-permute-start.8 = (bf16[256,4096]{1,0:T(8,128)(2,1)}, bf16[256,4096]{1,0:T(8,128)(2,1)}, u32[]{:S(2)}, u32[]{:S(2)}) collective-permute-start(bf16[256,4096]{1,0:T(8,128)(2,1)} %get-tuple-element.85.refs_0_), channel_id=1, source_target_pairs={{0,2},{2,0},{4,6},{6,4},{8,10},{10,8},{12,14},{14,12},{16,18},{18,... | collective-permute-start | bytes 6291464 | tf_op jit(solution)/shard_map/ppermute | solution.py:880
  52.1 3.1 fusion
  56.1 2.1 collective-permute-start.6
  59.7 22.0 %conv_one.1 = (bf16[256,4096]{1,0:T(8,128)(2,1)}, f32[256,128]{1,0:T(8,128)}, f32[256,4096]{1,0:T(8,128)}, bf16[256,4608]{1,0:T(8,128)(2,1)}) custom-call(s32[2]{0:T(128)} %pad_add_fusion.meta, bf16[256,4608]{1,0:T(8,128)(2,1)} %w_own.2, bf16[256,4608]{1,0:T(8,128)(2,1)} %collective-permute-done.7.w_got, bf16[256,4096]{1,0:T(8,128)(2,1)} %get-tuple-element.85.refs_0_, ...), custom_call_target="tpu_custom_call" | custom-call | flops 96636768 | bytes 107530 | tf_op jit(solution)/shard_map/conv_one/pallas_call | solution.py:259
  81.7 2.8 collective-permute-start.9
  84.6 2.0 pad_maximum_fusion.2
  86.6 2.0 collective-permute-start.12
  90.9 22.3 %conv_two.1 = (bf16[256,4096]{1,0:T(8,128)(2,1)}, f32[256,128]{1,0:T(8,128)}, f32[256,4096]{1,0:T(8,128)}, bf16[256,4608]{1,0:T(8,128)(2,1)}) custom-call(s32[2]{0:T(128)} %pad_add_fusion.meta, bf16[256,4608]{1,0:T(8,128)(2,1)} %w_own.3, bf16[256,4608]{1,0:T(8,128)(2,1)} %collective-permute-done.6.w_got, bf16[256,4096]{1,0:T(8,128)(2,1)} %get-tuple-element.94.refs_0_, ...), custom_call_target="tpu_custom_call" | custom-call | flops 96636768 | bytes 128481 | tf_op jit(solution)/shard_map/conv_two/pallas_call | solution.py:259
  113.2 3.3 collective-permute-start.13
  120.3 4.7 fold.1.refs_0_.refs_5_
  125.8 5.0 grad_heads.1
  130.8 13.1 %collective-permute-start.14 = (bf16[256,4096]{1,0:T(8,128)(2,1)}, bf16[256,4096]{1,0:T(8,128)(2,1)}, u32[]{:S(2)}, u32[]{:S(2)}) collective-permute-start(bf16[256,4096]{1,0:T(8,128)(2,1)} %get-tuple-element.103), channel_id=1, source_target_pairs={{0,2},{2,0},{4,6},{6,4},{8,10},{10,8},{12,14},{14,12},{16,18},{18,... | collective-permute-start | bytes 6291464 | tf_op jit(solution)/shard_map/ppermute | solution.py:880
  149.3 7.6 %qkv.1 = bf16[768,4096]{1,0:T(8,128)(2,1)} custom-call(s32[2]{0:T(128)} %pad_add_fusion.meta, bf16[768,512]{1,0:T(8,128)(2,1)} %get-tuple-element.255.w_ref, bf16[256,4096]{1,0:T(8,128)(2,1)} %get-tuple-element.96.refs_0_.refs_3_, bf16[256,4096]{1,0:T(8,128)(2,1)} %collective-permute-done.13.refs_1_.refs_4_, f32[768,1]{1,0:T(8,128)} %copy.122.refs_2_), custom_call_target="tpu_custom_call" | custom-call | flops 32212254 | bytes 104857 | tf_op jit(solution)/shard_map/qkv/pallas_call | solution.py:524
  156.9 225.2 %attention.1 = (bf16[4,64,4096]{2,1,0:T(8,128)(2,1)}, bf16[4,64,4096]{2,1,0:T(8,128)(2,1)}, bf16[4,64,4096]{2,1,0:T(8,128)(2,1)}, bf16[4,64,4096]{2,1,0:T(8,128)...) custom-call(s32[1]{0:T(128)} %bitcast.22.lim_ref, bf16[3,4,64,4096]{3,2,1,0:T(8,128)(2,1)} %bitcast.103, ...), custom_call_target="tpu_custom_call" | custom-call | flops 1159641216 | bytes 167772 | tf_op jit(solution)/shard_map/attention/pallas_call | solution.py:766
  382.1 7.7 %grad_normed.1 = (bf16[256,4096]{1,0:T(8,128)(2,1)}, bf16[256,4096]{1,0:T(8,128)(2,1)}) custom-call(s32[2]{0:T(128)} %pad_add_fusion.meta, bf16[512,768]{1,0:T(8,128)(2,1)} %copy.127.w_ref, bf16[256,4096]{1,0:T(8,128)(2,1)} %bitcast.110, bf16[256,4096]{1,0:T(8,128)(2,1)} %bitcast.112, bf16[256,4096]{1,0:T(8,128)(2,1)} %bitcast.114), custom_call_target="tpu_custom_call" | custom-call | flops 32212254 | bytes 104857 | tf_op jit(solution)/shard_map/grad_normed/pallas_call | solution.py:558
  390.8 3.5 collective-permute-done.18.refs_1_
  394.3 10.2 %norm_three_back.1 = (f32[256,4096]{1,0:T(8,128)}, bf16[256,4096]{1,0:T(8,128)(2,1)}, f32[256,128]{1,0:T(8,128)}) custom-call(bf16[256,4096]{1,0:T(8,128)(2,1)} %get-tuple-element.114.refs_0_, bf16[256,4096]{1,0:T(8,128)(2,1)} %collective-permute-done.18.refs_1_, f32[256,4096]{1,0:T(8,128)} %get-tuple-element.135.refs_2_.refs_3_, ...), custom_call_target="tpu_custom_call" | custom-call | flops 209715 | bytes 167772 | tf_op jit(solution)/shard_map/norm_three_back/pallas_call | solution.py:494
  404.5 16.3 %conv_two_weight_grad.1 = bf16[256,4608]{1,0:T(8,128)(2,1)} custom-call(s32[2]{0:T(128)} %pad_add_fusion.meta, bf16[256,4096]{1,0:T(8,128)(2,1)} %get-tuple-element.119.grad_ref.refs_0_, bf16[256,4096]{1,0:T(8,128)(2,1)} %get-tuple-element.94.refs_0_, bf16[256,4096]{1,0:T(8,128)(2,1)} %collective-permute-done.9.refs_1_), custom_call_target="tpu_custom_call" | custom-call | flops 96636768 | bytes 86507 | tf_op jit(solution)/shard_map/conv_two_weight_grad/pallas_call | solution.py:417
  420.8 2.1 collective-permute-start.22
  422.9 8.4 %qkv_grad.1 = (bf16[768,512]{1,0:T(8,128)(2,1)}, f32[768,128]{1,0:T(8,128)}) custom-call(s32[2]{0:T(128)} %pad_add_fusion.meta, bf16[256,4096]{1,0:T(8,128)(2,1)} %bitcast.111, bf16[256,4096]{1,0:T(8,128)(2,1)} %bitcast.113, bf16[256,4096]{1,0:T(8,128)(2,1)} %bitcast.115, bf16[256,4096]{1,0:T(8,128)(2,1)} %get-tuple-element.96.refs_0_.refs_3_, ...), custom_call_target="tpu_custom_call" | custom-call | flops 32212254 | bytes 104857 | tf_op jit(solution)/shard_map/qkv_grad/pallas_call | solution.py:632
  431.4 2.1 constant_dynamic-update-slice_fusion.1
  433.4 5.3 out_grad.1
  443.8 4.5 turn.2.w_own.w_got
  448.4 4.5 turn.3.w_own.w_got
  452.8 24.7 %conv_two_back.1 = (bf16[256,4096]{1,0:T(8,128)(2,1)}, f32[256,128]{1,0:T(8,128)}) custom-call(s32[2]{0:T(128)} %pad_add_fusion.meta, bf16[256,4608]{1,0:T(8,128)(2,1)} %turn.3.w_own.w_got, bf16[256,4608]{1,0:T(8,128)(2,1)} %turn.3.w_own.w_got, bf16[256,4096]{1,0:T(8,128)(2,1)} %get-tuple-element.119.grad_ref.refs_0_, ...), custom_call_target="tpu_custom_call" | custom-call | flops 96636768 | bytes 150784 | tf_op jit(solution)/shard_map/conv_two_back/pallas_call | solution.py:259
  478.9 2.3 convolution_convert_fusion
  486.4 1.9 select_dynamic-update-slice_fusion
  488.4 4.8 collective-permute-start.23
  493.8 16.6 %conv_one_weight_grad.1 = bf16[256,4608]{1,0:T(8,128)(2,1)} custom-call(s32[2]{0:T(128)} %pad_add_fusion.meta, bf16[256,4096]{1,0:T(8,128)(2,1)} %get-tuple-element.130.grad_ref.refs_0_, bf16[256,4096]{1,0:T(8,128)(2,1)} %get-tuple-element.85.refs_0_, bf16[256,4096]{1,0:T(8,128)(2,1)} %collective-permute-done.8.refs_1_), custom_call_target="tpu_custom_call" | custom-call | flops 96636768 | bytes 86507 | tf_op jit(solution)/shard_map/conv_one_weight_grad/pallas_call | solution.py:417
  510.3 2.1 collective-permute-start.24
  513.0 25.1 %conv_one_back.1 = (bf16[256,4096]{1,0:T(8,128)(2,1)}, f32[256,128]{1,0:T(8,128)}) custom-call(s32[2]{0:T(128)} %pad_add_fusion.meta, bf16[256,4608]{1,0:T(8,128)(2,1)} %turn.2.w_own.w_got, bf16[256,4608]{1,0:T(8,128)(2,1)} %turn.2.w_own.w_got, bf16[256,4096]{1,0:T(8,128)(2,1)} %get-tuple-element.130.grad_ref.refs_0_, ...), custom_call_target="tpu_custom_call" | custom-call | flops 96636768 | bytes 171724 | tf_op jit(solution)/shard_map/conv_one_back/pallas_call | solution.py:259
  539.4 1.7 collective-permute-start.27
  543.8 2.3 collective-permute-done.28
  547.3 5.5 collective-permute-done.29
  553.0 4.2 collective-permute-done.30
  557.3 2.6 collective-permute-start.31
  559.8 2.0 collective-permute-start.26
  563.5 2.3 pad_maximum_fusion
  565.8 6.6 output.1
  574.0 1.9 broadcast_select_fusion
  580.5 2.2 collective-permute-start.25
  589.0 9.1 %collective-permute-done.37 = bf16[32,4608]{1,0:T(8,128)(2,1)S(1)} collective-permute-done((bf16[32,4608]{1,0:T(8,128)(2,1)S(1)}, bf16[32,4608]{1,0:T(8,128)(2,1)S(1)}, u32[]{:S(2)}, u32[]{:S(2)}) %collective-permute-start.37) | collective-permute-done | bytes 294944 | tf_op jit(solution)/shard_map/ppermute | solution.py:880
  600.3 12.8 %collective-permute-done.38 = bf16[16,4608]{1,0:T(8,128)(2,1)S(1)} collective-permute-done((bf16[16,4608]{1,0:T(8,128)(2,1)S(1)}, bf16[16,4608]{1,0:T(8,128)(2,1)S(1)}, u32[]{:S(2)}, u32[]{:S(2)}) %collective-permute-start.38) | collective-permute-done | bytes 147488 | tf_op jit(solution)/shard_map/ppermute | solution.py:880
  614.3 2.2 collective-permute-done.39
  616.5 3.2 collective-permute-done.35
  620.1 6.3 copy.133
  626.9 4.6 collective-permute-done.40
  631.7 2.3 collective-permute-start.45
  634.0 12.4 %collective-permute-done.41 = bf16[16,4608]{1,0:T(8,128)(2,1)S(1)} collective-permute-done((bf16[16,4608]{1,0:T(8,128)(2,1)S(1)}, bf16[16,4608]{1,0:T(8,128)(2,1)S(1)}, u32[]{:S(2)}, u32[]{:S(2)}) %collective-permute-start.41) | collective-permute-done | bytes 147488 | tf_op jit(solution)/shard_map/ppermute | solution.py:880
  646.7 7.6 %collective-permute-done.42 = bf16[32,4608]{1,0:T(8,128)(2,1)S(1)} collective-permute-done((bf16[32,4608]{1,0:T(8,128)(2,1)S(1)}, bf16[32,4608]{1,0:T(8,128)(2,1)S(1)}, u32[]{:S(2)}, u32[]{:S(2)}) %collective-permute-start.42) | collective-permute-done | bytes 294944 | tf_op jit(solution)/shard_map/ppermute | solution.py:880
  654.5 1.7 collective-permute-start.43
  657.8 1.7 collective-permute-start.47
  661.3 2.7 fusion.20
  664.1 1.7 slice_bitcast_fusion.3
  665.7 2.1 slice_convert_fusion.1
  667.8 4.4 slice_convert_fusion
  672.2 2.3 maximum_convert_fusion
  (234 shorter events, 65.0 us)
Async XLA Ops:
  7.2 45.0 %copy-start = (bf16[1,260,2048]{2,1,0:T(8,128)(2,1)S(1)}, bf16[1,260,2048]{2,1,0:T(8,128)(2,1)}, u32[]{:S(2)}) copy-start(bf16[1,260,2048]{2,1,0:T(8,128)(2,1)} %param.26) | copy-start | bytes 3194884
  7.2 6.4 copy-start.27
  7.2 6.4 copy-start.28
  7.2 6.4 copy-start.29
  7.3 566.7 %reduce-scatter.2.cloned.1.call-start = ((), (), s32[]{:S(2)}) async-start(), calls=%async_computation.1 | async-start | bytes 5849088 | tf_op jit(solution)/shard_map/reduce_scatter | solution.py:1050
  7.4 21.5 %collective-permute-start = (bf16[256,4096]{1,0:T(8,128)(2,1)}, bf16[256,4096]{1,0:T(8,128)(2,1)}, u32[]{:S(2)}, u32[]{:S(2)}) collective-permute-start(bf16[256,4096]{1,0:T(8,128)(2,1)} %bitcast.120), channel_id=1, source_target_pairs={{1,2},{2,1},{5,6},{6,5},{9,10},{10,9},{13,14},{14,13},{17,18},{18,... | collective-permute-start | bytes 6291464 | tf_op jit(solution)/shard_map/ppermute | solution.py:874
  10.3 6.3 collective-permute-start.1
  13.9 7.9 %collective-permute-start.5 = (f32[15,256]{0,1:T(8,128)S(1)}, f32[15,256]{0,1:T(8,128)S(1)}, u32[]{:S(2)}, u32[]{:S(2)}) collective-permute-start(f32[15,256]{0,1:T(8,128)S(1)} %copy.120), channel_id=1, source_target_pairs={{1,2},{2,1},{5,6},{6,5},{9,10},{10,9},{13,14},{14,13},{17,18},{18,... | collective-permute-start | bytes 46088 | tf_op jit(solution)/shard_map/ppermute | solution.py:874
  14.6 45.1 %collective-permute-start.7 = (bf16[256,4608]{1,0:T(8,128)(2,1)}, bf16[256,4608]{1,0:T(8,128)(2,1)}, u32[]{:S(2)}, u32[]{:S(2)}) collective-permute-start(bf16[256,4608]{1,0:T(8,128)(2,1)} %w_own.2), channel_id=1, source_target_pairs={{1,2},{2,1},{5,6},{6,5},{9,10},{10,9},{13,14},{14,13},{17,18},{18,... | collective-permute-start | bytes 7077896 | tf_op jit(solution)/shard_map/ppermute | solution.py:874
  16.8 3.6 collective-permute-start.2
  20.4 3.6 collective-permute-start.3
  24.0 4.2 collective-permute-start.4
  28.9 23.3 %copy-start.30 = (f32[2,256]{1,0:T(2,128)S(1)}, f32[2,256]{1,0:T(2,128)}, u32[]{:S(2)}) copy-start(f32[2,256]{1,0:T(2,128)} %param.43) | copy-start | bytes 6148
  37.9 21.8 %collective-permute-start.8 = (bf16[256,4096]{1,0:T(8,128)(2,1)}, bf16[256,4096]{1,0:T(8,128)(2,1)}, u32[]{:S(2)}, u32[]{:S(2)}) collective-permute-start(bf16[256,4096]{1,0:T(8,128)(2,1)} %get-tuple-element.85.refs_0_), channel_id=1, source_target_pairs={{0,2},{2,0},{4,6},{6,4},{8,10},{10,8},{12,14},{14,12},{16,18},{18,... | collective-permute-start | bytes 6291464 | tf_op jit(solution)/shard_map/ppermute | solution.py:880
  56.1 34.8 %collective-permute-start.6 = (bf16[256,4608]{1,0:T(8,128)(2,1)}, bf16[256,4608]{1,0:T(8,128)(2,1)}, u32[]{:S(2)}, u32[]{:S(2)}) collective-permute-start(bf16[256,4608]{1,0:T(8,128)(2,1)} %w_own.3), channel_id=1, source_target_pairs={{1,2},{2,1},{5,6},{6,5},{9,10},{10,9},{13,14},{14,13},{17,18},{18,... | collective-permute-start | bytes 7077896 | tf_op jit(solution)/shard_map/ppermute | solution.py:874
  59.7 24.9 %copy-start.9 = (bf16[3,256,512]{2,1,0:T(8,128)(2,1)S(1)}, bf16[3,256,512]{2,1,0:T(8,128)(2,1)}, u32[]{:S(2)}) copy-start(bf16[3,256,512]{2,1,0:T(8,128)(2,1)} %param.40) | copy-start | bytes 2359300
  81.7 9.2 %collective-permute-start.9 = (bf16[256,4096]{1,0:T(8,128)(2,1)}, bf16[256,4096]{1,0:T(8,128)(2,1)}, u32[]{:S(2)}, u32[]{:S(2)}) collective-permute-start(bf16[256,4096]{1,0:T(8,128)(2,1)} %get-tuple-element.94.refs_0_), channel_id=1, source_target_pairs={{0,2},{2,0},{4,6},{6,4},{8,10},{10,8},{12,14},{14,12},{16,18},{18,... | collective-permute-start | bytes 6291464 | tf_op jit(solution)/shard_map/ppermute | solution.py:880
  86.6 29.9 %collective-permute-start.12 = (bf16[256,4096]{1,0:T(8,128)(2,1)}, bf16[256,4096]{1,0:T(8,128)(2,1)}, u32[]{:S(2)}, u32[]{:S(2)}) collective-permute-start(bf16[256,4096]{1,0:T(8,128)(2,1)} %bitcast.18.own_ref), channel_id=1, source_target_pairs={{1,2},{2,1},{5,6},{6,5},{9,10},{10,9},{13,14},{14,13},{17,18},{18,... | collective-permute-start | bytes 6291464 | tf_op jit(solution)/shard_map/ppermute | solution.py:874
  88.6 27.9 %collective-permute-start.10 = (bf16[1024,512]{1,0:T(8,128)(2,1)}, bf16[1024,512]{1,0:T(8,128)(2,1)}, u32[]{:S(2)}, u32[]{:S(2)}) collective-permute-start(bf16[1024,512]{1,0:T(8,128)(2,1)} %pad_maximum_fusion.2), channel_id=1, source_target_pairs={{1,2},{2,1},{5,6},{6,5},{9,10},{10,9},{13,14},{14,13},{17,18},{18,... | collective-permute-start | bytes 3145736 | tf_op jit(solution)/shard_map/ppermute | solution.py:874
  90.2 26.3 %collective-permute-start.11 = (bf16[2,256,384]{1,2,0:T(8,128)(2,1)S(1)}, bf16[2,256,384]{1,2,0:T(8,128)(2,1)S(1)}, u32[]{:S(2)}, u32[]{:S(2)}) collective-permute-start(bf16[2,256,384]{1,2,0:T(8,128)(2,1)S(1)} %pad.4), channel_id=1, source_target_pairs={{1,2},{2,1},{5,6},{6,5},{9,10},{10,9},{13,14},{14,13},{17,18},{18,... | collective-permute-start | bytes 1179656 | tf_op jit(solution)/shard_map/ppermute | solution.py:874
  113.2 36.1 %collective-permute-start.13 = (bf16[256,4096]{1,0:T(8,128)(2,1)}, bf16[256,4096]{1,0:T(8,128)(2,1)}, u32[]{:S(2)}, u32[]{:S(2)}) collective-permute-start(bf16[256,4096]{1,0:T(8,128)(2,1)} %get-tuple-element.96.refs_0_.refs_3_), channel_id=1, source_target_pairs={{0,2},{2,0},{4,6},{6,4},{8,10},{10,8},{12,14},{14,12},{16,18},{18,... | collective-permute-start | bytes 6291464 | tf_op jit(solution)/shard_map/ppermute | solution.py:880
  125.8 20.3 %copy-start.13 = (bf16[2,256,384]{1,2,0:T(8,128)(2,1)S(1)}, bf16[2,256,384]{1,2,0:T(8,128)(2,1)}, u32[]{:S(2)}) copy-start(bf16[2,256,384]{1,2,0:T(8,128)(2,1)} %copy-done.12) | copy-start | bytes 1179652
  130.8 16.3 %copy-start.7 = (bf16[1024,512]{1,0:T(8,128)(2,1)S(1)}, bf16[1024,512]{1,0:T(8,128)(2,1)}, u32[]{:S(2)}) copy-start(bf16[1024,512]{1,0:T(8,128)(2,1)} %copy-done.6) | copy-start | bytes 3145732
  130.8 26.1 %collective-permute-start.14 = (bf16[256,4096]{1,0:T(8,128)(2,1)}, bf16[256,4096]{1,0:T(8,128)(2,1)}, u32[]{:S(2)}, u32[]{:S(2)}) collective-permute-start(bf16[256,4096]{1,0:T(8,128)(2,1)} %get-tuple-element.103), channel_id=1, source_target_pairs={{0,2},{2,0},{4,6},{6,4},{8,10},{10,8},{12,14},{14,12},{16,18},{18,... | collective-permute-start | bytes 6291464 | tf_op jit(solution)/shard_map/ppermute | solution.py:880
  389.8 4.5 collective-permute-start.18
  389.8 43.6 %collective-permute-start.15 = (bf16[256,4096]{1,0:T(8,128)(2,1)}, bf16[256,4096]{1,0:T(8,128)(2,1)}, u32[]{:S(2)}, u32[]{:S(2)}) collective-permute-start(bf16[256,4096]{1,0:T(8,128)(2,1)} %bitcast.107), channel_id=1, source_target_pairs={{0,2},{2,0},{4,6},{6,4},{8,10},{10,8},{12,14},{14,12},{16,18},{18,... | collective-permute-start | bytes 6291464 | tf_op jit(solution)/shard_map/ppermute | solution.py:880
  390.3 52.1 %collective-permute-start.16 = (bf16[256,4608]{1,0:T(8,128)(2,1)}, bf16[256,4608]{1,0:T(8,128)(2,1)}, u32[]{:S(2)}, u32[]{:S(2)}) collective-permute-start(bf16[256,4608]{1,0:T(8,128)(2,1)} %get-tuple-element.106.own_ref), channel_id=1, source_target_pairs={{0,2},{2,0},{4,6},{6,4},{8,10},{10,8},{12,14},{14,12},{16,18},{18,... | collective-permute-start | bytes 7077896 | tf_op jit(solution)/shard_map/ppermute | solution.py:880
  390.4 58.0 %collective-permute-start.17 = (bf16[256,4608]{1,0:T(8,128)(2,1)}, bf16[256,4608]{1,0:T(8,128)(2,1)}, u32[]{:S(2)}, u32[]{:S(2)}) collective-permute-start(bf16[256,4608]{1,0:T(8,128)(2,1)} %get-tuple-element.110.own_ref), channel_id=1, source_target_pairs={{0,2},{2,0},{4,6},{6,4},{8,10},{10,8},{12,14},{14,12},{16,18},{18,... | collective-permute-start | bytes 7077896 | tf_op jit(solution)/shard_map/ppermute | solution.py:880
  420.8 56.8 %collective-permute-start.22 = (bf16[256,4608]{1,0:T(8,128)(2,1)}, bf16[256,4608]{1,0:T(8,128)(2,1)}, u32[]{:S(2)}, u32[]{:S(2)}) collective-permute-start(bf16[256,4608]{1,0:T(8,128)(2,1)} %conv_two_weight_grad.1), channel_id=1, source_target_pairs={{1,2},{2,1},{5,6},{6,5},{9,10},{10,9},{13,14},{14,13},{17,18},{18,... | collective-permute-start | bytes 7077896 | tf_op jit(solution)/shard_map/ppermute | solution.py:874
  422.9 30.0 %collective-permute-start.19 = (bf16[256,4096]{1,0:T(8,128)(2,1)}, bf16[256,4096]{1,0:T(8,128)(2,1)}, u32[]{:S(2)}, u32[]{:S(2)}) collective-permute-start(bf16[256,4096]{1,0:T(8,128)(2,1)} %get-tuple-element.119.grad_ref.refs_0_), channel_id=1, source_target_pairs={{0,2},{2,0},{4,6},{6,4},{8,10},{10,8},{12,14},{14,12},{16,18},{18,... | collective-permute-start | bytes 6291464 | tf_op jit(solution)/shard_map/ppermute | solution.py:880
  433.4 8.6 %copy-start.16 = (bf16[4,64,384]{2,1,0:T(8,128)(2,1)S(1)}, bf16[4,64,384]{2,1,0:T(8,128)(2,1)}, u32[]{:S(2)}) copy-start(bf16[4,64,384]{2,1,0:T(8,128)(2,1)} %get-tuple-element.107) | copy-start | bytes 589828
  433.4 8.8 %copy-start.15 = (bf16[4,64,384]{2,1,0:T(8,128)(2,1)S(1)}, bf16[4,64,384]{2,1,0:T(8,128)(2,1)}, u32[]{:S(2)}) copy-start(bf16[4,64,384]{2,1,0:T(8,128)(2,1)} %get-tuple-element.108) | copy-start | bytes 589828
  440.4 37.1 %collective-permute-start.20 = (bf16[1024,512]{1,0:T(8,128)(2,1)}, bf16[1024,512]{1,0:T(8,128)(2,1)}, u32[]{:S(2)}, u32[]{:S(2)}) collective-permute-start(bf16[1024,512]{1,0:T(8,128)(2,1)} %constant_dynamic-update-slice_fusion), channel_id=1, source_target_pairs={{1,2},{2,1},{5,6},{6,5},{9,10},{10,9},{13,14},{14,13},{17,18},{18,... | collective-permute-start | bytes 3145736 | tf_op jit(solution)/shard_map/ppermute | solution.py:874
  442.4 35.1 %collective-permute-start.21 = (bf16[2,256,384]{1,2,0:T(8,128)(2,1)S(1)}, bf16[2,256,384]{1,2,0:T(8,128)(2,1)}, u32[]{:S(2)}, u32[]{:S(2)}) collective-permute-start(bf16[2,256,384]{1,2,0:T(8,128)(2,1)S(1)} %pad_maximum_fusion.3), channel_id=1, source_target_pairs={{1,2},{2,1},{5,6},{6,5},{9,10},{10,9},{13,14},{14,13},{17,18},{18,... | collective-permute-start | bytes 1179656 | tf_op jit(solution)/shard_map/ppermute | solution.py:874
  488.3 175.7 %all-gather.2.cloned.1.call-start = ((), (), s32[]{:S(2)}) async-start(), calls=%async_computation.2 | async-start | bytes 5849088 | tf_op jit(solution)/shard_map/all_gather | solution.py:1086
  488.4 24.6 %collective-permute-start.23 = (bf16[256,4096]{1,0:T(8,128)(2,1)}, bf16[256,4096]{1,0:T(8,128)(2,1)}, u32[]{:S(2)}, u32[]{:S(2)}) collective-permute-start(bf16[256,4096]{1,0:T(8,128)(2,1)} %get-tuple-element.130.grad_ref.refs_0_), channel_id=1, source_target_pairs={{0,2},{2,0},{4,6},{6,4},{8,10},{10,8},{12,14},{14,12},{16,18},{18,... | collective-permute-start | bytes 6291464 | tf_op jit(solution)/shard_map/ppermute | solution.py:880
  493.8 18.7 %copy-start.18 = (f32[256,128]{1,0:T(8,128)S(1)}, f32[256,128]{1,0:T(8,128)}, u32[]{:S(2)}) copy-start(f32[256,128]{1,0:T(8,128)} %get-tuple-element.138) | copy-start | bytes 393220
  510.3 55.5 %collective-permute-start.24 = (bf16[256,4608]{1,0:T(8,128)(2,1)}, bf16[256,4608]{1,0:T(8,128)(2,1)}, u32[]{:S(2)}, u32[]{:S(2)}) collective-permute-start(bf16[256,4608]{1,0:T(8,128)(2,1)} %conv_one_weight_grad.1), channel_id=1, source_target_pairs={{1,2},{2,1},{5,6},{6,5},{9,10},{10,9},{13,14},{14,13},{17,18},{18,... | collective-permute-start | bytes 7077896 | tf_op jit(solution)/shard_map/ppermute | solution.py:874
  513.0 49.5 %copy-start.10 = (bf16[16,2048]{1,0:T(8,128)(2,1)S(1)}, bf16[16,2048]{1,0:T(8,128)(2,1)}, u32[]{:S(2)}) copy-start(bf16[16,2048]{1,0:T(8,128)(2,1)} %add.173) | copy-start | bytes 196612
  539.4 3.3 collective-permute-start.27
  542.7 3.4 collective-permute-start.28
  546.1 6.7 collective-permute-start.29
  552.9 4.4 collective-permute-start.30
  557.3 4.6 collective-permute-start.31
  559.8 59.9 %collective-permute-start.26 = (bf16[256,4096]{1,0:T(8,128)(2,1)}, bf16[256,4096]{1,0:T(8,128)(2,1)}, u32[]{:S(2)}, u32[]{:S(2)}) collective-permute-start(bf16[256,4096]{1,0:T(8,128)(2,1)} %get-tuple-element.134), channel_id=1, source_target_pairs={{1,2},{2,1},{5,6},{6,5},{9,10},{10,9},{13,14},{14,13},{17,18},{18,... | collective-permute-start | bytes 6291464 | tf_op jit(solution)/shard_map/ppermute | solution.py:874
  577.1 7.4 %collective-permute-start.36 = (bf16[64,4608]{1,0:T(8,128)(2,1)S(1)}, bf16[64,4608]{1,0:T(8,128)(2,1)}, u32[]{:S(2)}, u32[]{:S(2)}) collective-permute-start(bf16[64,4608]{1,0:T(8,128)(2,1)S(1)} %constant_dynamic-slice_fusion.3), channel_id=1, source_target_pairs={{0,2},{2,0},{4,6},{6,4},{8,10},{10,8},{12,14},{14,12},{16,18},{18,... | collective-permute-start | bytes 1769480 | tf_op jit(solution)/shard_map/ppermute | solution.py:880
  580.5 39.2 %collective-permute-start.25 = (bf16[256,4096]{1,0:T(8,128)(2,1)S(1)}, bf16[256,4096]{1,0:T(8,128)(2,1)}, u32[]{:S(2)}, u32[]{:S(2)}) collective-permute-start(bf16[256,4096]{1,0:T(8,128)(2,1)S(1)} %copy-done.3), channel_id=1, source_target_pairs={{1,2},{2,1},{5,6},{6,5},{9,10},{10,9},{13,14},{14,13},{17,18},{18,... | collective-permute-start | bytes 6291464 | tf_op jit(solution)/shard_map/ppermute | solution.py:874
  583.9 2.8 collective-permute-start.32
  586.0 12.1 %collective-permute-start.37 = (bf16[32,4608]{1,0:T(8,128)(2,1)S(1)}, bf16[32,4608]{1,0:T(8,128)(2,1)S(1)}, u32[]{:S(2)}, u32[]{:S(2)}) collective-permute-start(bf16[32,4608]{1,0:T(8,128)(2,1)S(1)} %constant_dynamic-slice_fusion.2), channel_id=1, source_target_pairs={{0,8},{2,10},{4,12},{6,14},{8,0},{10,2},{12,4},{14,6},{16,24},{18,... | collective-permute-start | bytes 884744 | tf_op jit(solution)/shard_map/ppermute | solution.py:880
  587.9 31.9 %copy-start.8 = (bf16[256,4096]{1,0:T(8,128)(2,1)S(1)}, bf16[256,4096]{1,0:T(8,128)(2,1)}, u32[]{:S(2)}) copy-start(bf16[256,4096]{1,0:T(8,128)(2,1)} %get-tuple-element.134) | copy-start | bytes 6291460
  587.9 11.7 %collective-permute-start.33 = (bf16[32,4608]{1,0:T(8,128)(2,1)S(1)}, bf16[32,4608]{1,0:T(8,128)(2,1)S(1)}, u32[]{:S(2)}, u32[]{:S(2)}) collective-permute-start(bf16[32,4608]{1,0:T(8,128)(2,1)S(1)} %constant_dynamic-slice_fusion.6), channel_id=1, source_target_pairs={{0,4},{2,6},{4,0},{6,2},{8,12},{10,14},{12,8},{14,10},{16,20},{18,... | collective-permute-start | bytes 884744 | tf_op jit(solution)/shard_map/ppermute | solution.py:880
  598.2 14.9 %collective-permute-start.38 = (bf16[16,4608]{1,0:T(8,128)(2,1)S(1)}, bf16[16,4608]{1,0:T(8,128)(2,1)S(1)}, u32[]{:S(2)}, u32[]{:S(2)}) collective-permute-start(bf16[16,4608]{1,0:T(8,128)(2,1)S(1)} %constant_dynamic-slice_fusion.1), channel_id=1, source_target_pairs={{0,16},{2,18},{4,20},{6,22},{8,24},{10,26},{12,28},{14,30},{16,0},... | collective-permute-start | bytes 442376 | tf_op jit(solution)/shard_map/ppermute | solution.py:880
  599.8 14.3 %collective-permute-start.34 = (bf16[16,4608]{1,0:T(8,128)(2,1)S(1)}, bf16[16,4608]{1,0:T(8,128)(2,1)S(1)}, u32[]{:S(2)}, u32[]{:S(2)}) collective-permute-start(bf16[16,4608]{1,0:T(8,128)(2,1)S(1)} %constant_dynamic-slice_fusion.5), channel_id=1, source_target_pairs={{0,8},{2,10},{4,12},{6,14},{8,0},{10,2},{12,4},{14,6},{16,24},{18,... | collective-permute-start | bytes 442376 | tf_op jit(solution)/shard_map/ppermute | solution.py:880
  613.2 3.3 collective-permute-start.39
  614.2 5.5 collective-permute-start.35
  619.7 11.8 %collective-permute-start.40 = (bf16[8,4608]{1,0:T(8,128)(2,1)S(1)}, bf16[8,4608]{1,0:T(8,128)(2,1)S(1)}, u32[]{:S(2)}, u32[]{:S(2)}) collective-permute-start(bf16[8,4608]{1,0:T(8,128)(2,1)S(1)} %add_convert_fusion.7), channel_id=1, source_target_pairs={{0,16},{2,18},{4,20},{6,22},{8,24},{10,26},{12,28},{14,30},{16,0},... | collective-permute-start | bytes 221192 | tf_op jit(solution)/shard_map/ppermute | solution.py:880
  626.4 29.7 %copy-start.4 = (bf16[256,4096]{1,0:T(8,128)(2,1)S(1)}, bf16[256,4096]{1,0:T(8,128)(2,1)}, u32[]{:S(2)}) copy-start(bf16[256,4096]{1,0:T(8,128)(2,1)} %output.1) | copy-start | bytes 6291460
  626.4 5.2 collective-permute-start.44
  631.6 14.9 %collective-permute-start.41 = (bf16[16,4608]{1,0:T(8,128)(2,1)S(1)}, bf16[16,4608]{1,0:T(8,128)(2,1)S(1)}, u32[]{:S(2)}, u32[]{:S(2)}) collective-permute-start(bf16[16,4608]{1,0:T(8,128)(2,1)S(1)} %maximum_select_fusion.6), channel_id=1, source_target_pairs={{0,8},{2,10},{4,12},{6,14},{8,0},{10,2},{12,4},{14,6},{16,24},{18,... | collective-permute-start | bytes 442376 | tf_op jit(solution)/shard_map/ppermute | solution.py:880
  631.7 14.9 %collective-permute-start.45 = (bf16[16,4608]{1,0:T(8,128)(2,1)S(1)}, bf16[16,4608]{1,0:T(8,128)(2,1)S(1)}, u32[]{:S(2)}, u32[]{:S(2)}) collective-permute-start(bf16[16,4608]{1,0:T(8,128)(2,1)S(1)} %maximum_select_fusion.7), channel_id=1, source_target_pairs={{0,16},{2,18},{4,20},{6,22},{8,24},{10,26},{12,28},{14,30},{16,0},... | collective-permute-start | bytes 442376 | tf_op jit(solution)/shard_map/ppermute | solution.py:880
  646.5 7.9 %collective-permute-start.42 = (bf16[32,4608]{1,0:T(8,128)(2,1)S(1)}, bf16[32,4608]{1,0:T(8,128)(2,1)S(1)}, u32[]{:S(2)}, u32[]{:S(2)}) collective-permute-start(bf16[32,4608]{1,0:T(8,128)(2,1)S(1)} %maximum_select_fusion.4), channel_id=1, source_target_pairs={{0,4},{2,6},{4,0},{6,2},{8,12},{10,14},{12,8},{14,10},{16,20},{18,... | collective-permute-start | bytes 884744 | tf_op jit(solution)/shard_map/ppermute | solution.py:880
  646.6 11.1 %collective-permute-start.46 = (bf16[32,4608]{1,0:T(8,128)(2,1)S(1)}, bf16[32,4608]{1,0:T(8,128)(2,1)S(1)}, u32[]{:S(2)}, u32[]{:S(2)}) collective-permute-start(bf16[32,4608]{1,0:T(8,128)(2,1)S(1)} %maximum_select_fusion.5), channel_id=1, source_target_pairs={{0,8},{2,10},{4,12},{6,14},{8,0},{10,2},{12,4},{14,6},{16,24},{18,... | collective-permute-start | bytes 884744 | tf_op jit(solution)/shard_map/ppermute | solution.py:880
  654.5 5.0 collective-permute-start.43
  657.8 3.3 collective-permute-start.47
  (17 other events, 82.7 us)
Sparse Core Ops, SparseCore 0:
  488.5 85.4 reduce-scatter.1
  582.9 71.1 all-gather.1
